TPU v7x, 32 devices: a whole 2x2x4 slice. The times are simulated.
32 devices in a mesh: dom: 8 (over z, y), samp: 4 (over x, core).
Axes of the slice: x: 2, y: 2, z: 4, core: 2. Of those that a mesh axis runs over, the one named last changes fastest.
Arguments:
- residual: float32 [256, 32768], P('samp', 'dom'), may hold values from -60 to 60
- conductance: float32 [256, 32768], P('samp', 'dom'), may hold values from 0.2 to 2
- capacitance: float32 [256, 32768], P('samp', 'dom'), may hold values from 0.2 to 2
- stamps: float32 [512, 4, 64, 128], P('dom'), may hold values from -0.375 to 0.375
- block_cols: int32 [512, 4], P('dom'), may hold values from 0 to 95, as said below
- send_blocks: int32 [8, 8, 4], P('dom'), may hold values from 0 to 63
Outputs:
- update: float32 [256, 32768], P('samp', 'dom')
Inputs may be any that keep to these rules, and one draw needn't show every extreme that they name: `block_cols`: entries below 64 name the partition's own block rows; an entry 64 + s * 4 + j names slot j that partition s sends to this partition, s never the partition itself; entry 0 of a row is the row's own block.
All inputs are finite; a program needn't handle non-finite values.
Results may differ from a plain program's by a relative error of at most 0.00005.
Values sent between devices are 32-bit elements; how exact they have to be, the bound alone decides.
No kernel may reach another device: no remote copies, remote signals or barrier semaphores. Data moves between devices by JAX's collectives and lax.ppermute only.
A program may use at most 64 MiB of HBM per device.

v0:
```python
import functools

import jax
import jax.numpy as jnp
from jax import lax
from jax.experimental import pallas as pl
from jax.experimental.pallas import tpu as pltpu
from jax.sharding import PartitionSpec as P


LANES = 128
HALF = 64
GROUP = 4


LIMIT = 24 * 1024 * 1024


def whole():
    return pl.BlockSpec(memory_space=pltpu.VMEM)


def scalars():
    return pl.BlockSpec(memory_space=pltpu.SMEM)


def near_memory(x):
    return pltpu.with_memory_space_constraint(x, pltpu.VMEM)


def far_memory(x):
    return pltpu.with_memory_space_constraint(x, pltpu.HBM)


def kernel_call(kernel, inputs, outputs, aliases=None, table_copied=False, scratch=(), far_first=False):
    specs = []
    operands = []
    for x in inputs:
        if x.dtype == jnp.int32 and table_copied:
            specs.append(pl.BlockSpec(memory_space=pl.ANY))
            operands.append(near_memory(x))
            scratch = (*scratch, pltpu.SMEM(x.shape, x.dtype), pltpu.SemaphoreType.DMA)
        elif x.dtype == jnp.int32:
            specs.append(scalars())
            operands.append(x)
        elif far_first and not specs:
            specs.append(pl.BlockSpec(memory_space=pl.ANY))
            operands.append(far_memory(x))
        else:
            specs.append(whole())
            operands.append(near_memory(x))
    integer = [dtype == jnp.int32 for _, dtype in outputs]
    out = [
        jax.ShapeDtypeStruct(shape, dtype) if number else pltpu.VMEM(shape, dtype)
        for (shape, dtype), number in zip(outputs, integer)
    ]
    return pl.pallas_call(
        kernel,
        in_specs=specs,
        out_specs=[scalars() if number else whole() for number in integer],
        out_shape=out,
        input_output_aliases=aliases or {},
        scratch_shapes=scratch,
        compiler_params=pltpu.CompilerParams(vmem_limit_bytes=LIMIT),
    )(*operands)


def split(x):
    high = x.astype(jnp.bfloat16)
    low = (x - high.astype(jnp.float32)).astype(jnp.bfloat16)
    return high, low


def spectral_rows(me, sources, samples, period):
    row = me * samples + lax.broadcasted_iota(jnp.int32, (samples, samples), 0)
    column = lax.broadcasted_iota(jnp.int32, (samples, samples), 1)
    blocks = []
    for source in sources:
        offset = row - (source * samples + column)
        sign = (1 - 2 * (offset & 1)).astype(jnp.float32)
        angle = jnp.pi / period * offset.astype(jnp.float32)
        nonzero = offset != 0
        safe = jnp.where(nonzero, angle, 0.5)
        value = sign * jnp.cos(safe) / jnp.sin(safe) / period
        blocks.append(jnp.where(nonzero, value, 0.0))
    high, low = split(jnp.concatenate(blocks, axis=1))
    return jnp.concatenate([high, low], axis=0)


def tables_kernel(groups, near_ref, far_ref):
    samples = near_ref.shape[1] // 2
    me = lax.axis_index("samp")
    partner = me + 1 - 2 * (me & 1)
    near_ref[...] = spectral_rows(me, [me, partner], samples, samples * groups)
    far = []
    for k in range(2, groups, 2):
        for source in (me - k, partner - k):
            far.append(jnp.where(source < 0, source + groups, source))
    far_ref[...] = spectral_rows(me, far, samples, samples * groups)


def load_stamps(first_row, stamps_hbm, perm_ref, out_ref, buffer, sems, meanwhile=None):
    rows, _, width = out_ref.shape
    copies = []
    for n in range(rows):
        source = stamps_hbm.at[perm_ref[first_row + n]]
        copies.append(pltpu.make_async_copy(source, buffer.at[n], sems.at[n]))
        copies[-1].start()
    if meanwhile is not None:
        meanwhile()
    for n, copy in enumerate(copies):
        copy.wait()
        high, low = split(buffer[n])
        out_ref[n, :, : width // 2] = high
        out_ref[n, :, width // 2 :] = low


def prepare_first_kernel(stamps_hbm, perm_ref, inv_ref, cols_ref, send_ref, out_ref, new_cols, new_send, buffer, sems):
    per_entry, rows = cols_ref.shape

    def tables():
        def one_row(i, carry):
            for k in range(per_entry):
                entry = cols_ref[k, perm_ref[i]]
                own = inv_ref[jnp.minimum(entry, rows - 1)]
                new_cols[k, i] = jnp.where(entry < rows, own, entry)
            return carry

        lax.fori_loop(0, rows, one_row, 0, unroll=2)
        for j in range(send_ref.shape[0]):
            for d in range(send_ref.shape[1]):
                new_send[j, d] = inv_ref[send_ref[j, d]]

    load_stamps(0, stamps_hbm, perm_ref, out_ref, buffer, sems, tables)


def prepare_rest_kernel(first_row, stamps_hbm, perm_ref, out_ref, buffer, sems):
    load_stamps(first_row, stamps_hbm, perm_ref, out_ref, buffer, sems)


def pair_tile(ref, first, second):
    samples = ref.shape[0]
    lane = lax.broadcasted_iota(jnp.int32, (samples, LANES), 1)

    def placed(block, upper):
        start = pl.multiple_of((block // 2) * LANES, LANES)
        tile = ref[:, pl.ds(start, LANES)]
        turned = pltpu.roll(tile, HALF, 1)
        return jnp.where((block & 1) == upper, tile, turned)

    return jnp.where(lane < HALF, placed(first, 0), placed(second, 1))


def gather_blocks(targets, send_ref, field_ref, out_refs):
    slots = send_ref.shape[0]
    for d, out_ref in zip(targets, out_refs):
        for j in range(0, slots, 2):
            out_ref[:, j * HALF : j * HALF + LANES] = pair_tile(field_ref, send_ref[j, d], send_ref[j + 1, d])


def halo_offsets(domains):
    return sorted(range(1, domains), key=lambda k: (-(k >= domains // 2), k if k >= domains // 2 else -k))


def few(domains):
    return domains <= 8 and domains & (domains - 1) == 0


def gather_all(domains, send_ref, field_ref, out_refs):
    if few(domains):
        me = lax.axis_index("dom")
        gather_blocks([me ^ k for k in halo_offsets(domains)], send_ref, field_ref, out_refs)
    else:
        gather_blocks(range(domains), send_ref, field_ref, [out_refs[0].at[d] for d in range(domains)])


COPIES = 4


def order_rows(domains, send_ref, perm_ref, inv_ref, flags):
    rows = perm_ref.shape[0]
    if not few(domains):

        def keep(row, carry):
            perm_ref[row] = row
            inv_ref[row] = row
            return carry

        lax.fori_loop(0, rows, keep, 0)
        return
    me = lax.axis_index("dom")

    def clear(row, carry):
        flags[row] = 0
        return carry

    lax.fori_loop(0, rows + 1, clear, 0, unroll=5)
    for d in range(domains):
        for j in range(send_ref.shape[0]):
            flags[jnp.where(d == me, rows, send_ref[j, d])] = 1

    sent = lax.fori_loop(0, rows, lambda row, total: total + flags[row], 0, unroll=4)

    def place(row, carry):
        first, later = carry
        flag = flags[row]
        position = jnp.where(flag == 1, first, later)
        inv_ref[row] = position
        perm_ref[position] = row
        return first + flag, later + 1 - flag

    lax.fori_loop(0, rows, place, (jnp.int32(0), sent), unroll=4)


def gather_kernel(domains, send_hbm, field_hbm, field_ref, perm_ref, inv_ref, *refs):
    *out_refs, field_sem, send_ref, send_sem, flags = refs
    table = pltpu.make_async_copy(send_hbm, send_ref, send_sem)
    table.start()
    width = field_ref.shape[1] // COPIES
    copies = []
    for n in range(COPIES):
        inside = pl.ds(n * width, width)
        copies.append(pltpu.make_async_copy(field_hbm.at[:, inside], field_ref.at[:, inside], field_sem.at[n]))
        copies[-1].start()
    table.wait()
    order_rows(domains, send_ref, perm_ref, inv_ref, flags)
    for copy in copies:
        copy.wait()
    gather_all(domains, send_ref, field_ref, out_refs)


def gather(send, field, rows, domains, outputs):
    table = jax.ShapeDtypeStruct((rows,), jnp.int32)
    return pl.pallas_call(
        functools.partial(gather_kernel, domains),
        in_specs=[pl.BlockSpec(memory_space=pl.ANY)] * 2,
        out_specs=[whole(), scalars(), scalars()] + [whole()] * len(outputs),
        out_shape=[
            pltpu.VMEM(field.shape, field.dtype),
            table,
            table,
            *[pltpu.VMEM(shape, dtype) for shape, dtype in outputs],
        ],
        scratch_shapes=[
            pltpu.SemaphoreType.DMA((COPIES,)),
            pltpu.SMEM(send.shape, send.dtype),
            pltpu.SemaphoreType.DMA,
            pltpu.SMEM((rows + 8,), jnp.int32),
        ],
        compiler_params=pltpu.CompilerParams(vmem_limit_bytes=LIMIT),
        name="gather",
    )(far_memory(send), far_memory(field))


def store_tile(ext, index, x):
    high, low = split(x)
    ext[0, index] = jnp.concatenate([high, low], axis=0)
    high, low = split(pltpu.roll(x, HALF, 1))
    ext[1, index] = jnp.concatenate([high, low], axis=0)


def arrange_kernel(perm_ref, field_ref, g_ref, c_ref, field_out, g_out, c_out, ext):
    for i in range(field_ref.shape[1] // LANES):
        inside = slice(i * LANES, (i + 1) * LANES)
        first, second = perm_ref[2 * i], perm_ref[2 * i + 1]
        tile = pair_tile(field_ref, first, second)
        field_out[:, inside] = tile
        store_tile(ext, i, tile)
        g_out[:, inside] = pair_tile(g_ref, first, second)
        c_out[:, inside] = pair_tile(c_ref, first, second)


def extend_kernel(field_ref, ext):
    for i in range(field_ref.shape[1] // LANES):
        store_tile(ext, i, field_ref[:, i * LANES : (i + 1) * LANES])


def extend_arrived(domains, own_tiles, inc_refs, ext):
    if few(domains):
        me = lax.axis_index("dom")
        arrived = [(me ^ k, ref) for k, ref in zip(halo_offsets(domains), inc_refs)]
    else:
        arrived = [(d, inc_refs[0].at[d]) for d in range(domains)]
    for source, ref in arrived:
        per_domain = ref.shape[1] // LANES
        for j in range(per_domain):
            store_tile(ext, own_tiles + source * per_domain + j, ref[:, j * LANES : (j + 1) * LANES])


def first_product_kernel(domains, cols_hbm, field_ref, own_ref, g_ref, c_ref, w_ref, *refs):
    *inc_refs, ext, p_ref, q_ref, cols_ref, cols_sem = refs
    table = pltpu.make_async_copy(cols_hbm, cols_ref, cols_sem)
    table.start()
    extend_arrived(domains, field_ref.shape[1] // LANES, inc_refs, ext)
    table.wait()
    product_kernel(0, 0, cols_ref, field_ref, ext, g_ref, c_ref, w_ref, p_ref, q_ref)


def product_kernel(first_row, weight_row, cols_ref, field_ref, ext, g_ref, c_ref, w_ref, p_ref, q_ref):
    samples = field_ref.shape[0]
    per_entry = cols_ref.shape[0]
    lane = lax.broadcasted_iota(jnp.int32, (2 * samples, LANES), 1)
    low_lane = lax.broadcasted_iota(jnp.int32, (samples, LANES), 1) < HALF

    def row_product(row):
        parts = []
        for k in range(0, per_entry, 2):
            first = cols_ref[k, row]
            second = cols_ref[k + 1, row]
            a = ext[first & 1, first // 2]
            b = ext[1 - (second & 1), second // 2]
            parts.append(jnp.where(lane < HALF, a, b))
        left = jnp.concatenate(parts, axis=1)
        full = jnp.dot(left, w_ref[row - weight_row], preferred_element_type=jnp.float32)
        width = full.shape[1] // 2
        rows = full[:, :width] + full[:, width:]
        return rows[:samples] + rows[samples:]

    def block(step, carry):
        for pair in range(GROUP // 2):
            row = first_row + step * GROUP + 2 * pair
            first = row_product(row)
            second = row_product(row + 1)
            direct = jnp.where(low_lane, first, pltpu.roll(second, HALF, 1))
            charge = jnp.where(low_lane, pltpu.roll(first, HALF, 1), second)
            here = pl.ds(pl.multiple_of(step * GROUP * HALF + pair * LANES, LANES), LANES)
            there = pl.ds(pl.multiple_of(first_row * HALF + step * GROUP * HALF + pair * LANES, LANES), LANES)
            own = field_ref[:, there]
            p_ref[:, here] = direct + g_ref[:, there] * own
            q_ref[:, here] = charge + c_ref[:, there] * own
        return carry

    lax.fori_loop(0, p_ref.shape[1] // (GROUP * HALF), block, 0)


def slope_columns(matrix, charges):
    samples = charges[0].shape[0]
    parts = [split(x) for x in charges]
    high = jnp.concatenate([h for h, _ in parts], axis=0)
    low = jnp.concatenate([l for _, l in parts], axis=0)
    first = jnp.dot(matrix, high, preferred_element_type=jnp.float32)
    second = jnp.dot(matrix[:samples], low, preferred_element_type=jnp.float32)
    return first[:samples] + first[samples:] + second


CHUNK = 256


def near_kernel(chunks, *refs):
    matrix = refs[0][...]
    p_refs, q_refs, mate_refs, out_refs = [refs[1 + n * chunks : 1 + (n + 1) * chunks] for n in range(4)]
    for p_ref, q_ref, mate_ref, out_ref in zip(p_refs, q_refs, mate_refs, out_refs):
        for start in range(0, p_ref.shape[1], CHUNK):
            inside = slice(start, start + CHUNK)
            out_ref[:, inside] = p_ref[:, inside] + slope_columns(matrix, [q_ref[:, inside], mate_ref[:, inside]])


def far_columns(matrix, p_ref, charge_refs):
    for start in range(0, p_ref.shape[1], CHUNK):
        inside = slice(start, start + CHUNK)
        yield start, p_ref[:, inside] + slope_columns(matrix, [c[:, inside] for c in charge_refs])


def far_kernel(count, base, chunks, *refs):
    matrix = refs[0][...]
    out_ref = refs[-1]
    size = 1 + count
    for n in range(chunks):
        p_ref, *charge_refs = refs[1 + n * size : 1 + (n + 1) * size]
        for start, value in far_columns(matrix, p_ref, charge_refs):
            out_ref[:, base + start : base + start + CHUNK] = value
        base += p_ref.shape[1]


def far_send_kernel(count, chunks, domains, send_near, *refs):
    size = 1 + count
    u_ref, *out_refs, send_ref, send_sem = refs[1 + chunks * size :]
    table = pltpu.make_async_copy(send_near, send_ref, send_sem)
    table.start()
    far_kernel(count, 0, chunks, *refs[: 1 + chunks * size], u_ref)
    table.wait()
    gather_all(domains, send_ref, u_ref, out_refs)


def dot_totals(totals, r_ref, u_ref, base, v):
    for i in range(0, v.shape[1], LANES):
        vv = v[:, i : i + LANES]
        rr = r_ref[:, base + i : base + i + LANES]
        uu = u_ref[:, base + i : base + i + LANES]
        for n, (a, b) in enumerate(((uu, uu), (uu, vv), (vv, vv), (rr, uu), (rr, vv))):
            totals[n] = totals[n] + a * b


def far_dots_kernel(count, base, chunks, *refs):
    matrix = refs[0][...]
    out_ref = refs[-1]
    size = 1 + count
    r_ref, u_ref, *before = refs[1 + chunks * size : -1]
    samples = r_ref.shape[0]
    totals = [before[0][n] if before else jnp.zeros((samples, LANES), jnp.float32) for n in range(5)]
    for n in range(chunks):
        p_ref, *charge_refs = refs[1 + n * size : 1 + (n + 1) * size]
        for start, value in far_columns(matrix, p_ref, charge_refs):
            dot_totals(totals, r_ref, u_ref, base + start, value)
        base += p_ref.shape[1]
    if base < u_ref.shape[1]:
        for n in range(5):
            out_ref[n] = totals[n]
        return
    lane = lax.broadcasted_iota(jnp.int32, (1, LANES), 1)
    packed = jnp.zeros((1, LANES), jnp.float32)
    for n, total in enumerate(totals):
        packed = jnp.where(lane == n, jnp.sum(total), packed)
    for d in range(out_ref.shape[0]):
        out_ref[d] = packed


def update_kernel(inv_near, sums_ref, r_ref, u_ref, out_hbm, out_ref, sems, inv_ref, inv_sem):
    table = pltpu.make_async_copy(inv_near, inv_ref, inv_sem)
    table.start()
    total = jnp.sum(sums_ref[...], axis=0)
    lane = lax.broadcasted_iota(jnp.int32, total.shape, 1)
    uu, uv, vv, ru, rv = [jnp.sum(jnp.where(lane == n, total, 0.0), axis=1, keepdims=True) for n in range(5)]
    length_u = jnp.sqrt(uu)
    length_v = jnp.sqrt(vv)
    cross = uv / length_u / length_v
    target_u = ru / length_u
    target_v = rv / length_v
    determinant = 1.0 - cross * cross
    weight_r = (target_u - cross * target_v) / determinant / length_u
    weight_u = (target_v - cross * target_u) / determinant / length_v
    table.wait()
    width = r_ref.shape[1] // COPIES
    copies = []
    for n in range(COPIES):
        for start in range(n * width, (n + 1) * width, LANES):
            inside = slice(start, start + LANES)
            tile = pair_tile(u_ref, inv_ref[start // HALF], inv_ref[start // HALF + 1])
            out_ref[:, inside] = weight_r * r_ref[:, inside] + weight_u * tile
        inside = pl.ds(n * width, width)
        copies.append(pltpu.make_async_copy(out_ref.at[:, inside], out_hbm.at[:, inside], sems.at[n]))
        copies[-1].start()
    for copy in copies:
        copy.wait()


def update(inv, sums, r, u):
    return pl.pallas_call(
        update_kernel,
        in_specs=[pl.BlockSpec(memory_space=pl.ANY)] + [whole()] * 3,
        out_specs=pl.BlockSpec(memory_space=pl.ANY),
        out_shape=jax.ShapeDtypeStruct(r.shape, r.dtype),
        scratch_shapes=[
            pltpu.VMEM(r.shape, r.dtype),
            pltpu.SemaphoreType.DMA((COPIES,)),
            pltpu.SMEM(inv.shape, inv.dtype),
            pltpu.SemaphoreType.DMA,
        ],
        compiler_params=pltpu.CompilerParams(vmem_limit_bytes=LIMIT),
        name="update",
    )(near_memory(inv), near_memory(sums), near_memory(r), near_memory(u))


CHUNKS = 4


def chunk_sizes(rows, domains, slots):
    unit = rows // 8
    early = (domains - 1) * slots if few(domains) else 3 * unit
    return [unit, early - unit, rows - unit - early, unit]


def body(residual, conductance, capacitance, stamps, block_cols, send_blocks):
    samples, unknowns = residual.shape
    rows, per_entry = block_cols.shape
    width = stamps.shape[2]
    slots = send_blocks.shape[2]
    domains = lax.axis_size("dom")
    groups = lax.axis_size("samp")
    pairs = [(i, i ^ 1) for i in range(groups)]
    shifts = range(2, groups, 2)
    count = 2 * len(shifts)
    sizes = chunk_sizes(rows, domains, slots)
    f32 = jnp.float32
    if few(domains):
        outgoing_shapes = [((samples, slots * width), f32)] * (domains - 1)
    else:
        outgoing_shapes = [((domains, samples, slots * width), f32)]
    field_shape = ((samples, unknowns), f32)
    tiles = unknowns // LANES + domains * slots * width // LANES
    ext_shape = ((2, tiles, 2 * samples, LANES), jnp.bfloat16)

    def exchange(outgoing):
        if not few(domains):
            return [lax.all_to_all(outgoing[0], "dom", split_axis=0, concat_axis=0, tiled=True)]
        incoming = []
        for k, x in zip(halo_offsets(domains), outgoing):
            incoming.append(lax.ppermute(x, "dom", [(i, i ^ k) for i in range(domains)]))
        return incoming

    def charges_of(field, ext, incoming, cols, g, c, weights):
        direct, charge, mates, far = [], [], [], []
        first = 0
        for n, size in enumerate(sizes):
            shape = ((samples, size * width), f32)
            weight_row, weight = next((at, w) for at, w in reversed(weights) if at <= first)
            operands = (cols, field, ext, g, c, weight)
            if n == 0:
                ext, p, q = kernel_call(
                    functools.partial(first_product_kernel, domains),
                    operands + tuple(incoming),
                    [ext_shape, shape, shape],
                    aliases={2: 0},
                    table_copied=True,
                )
            else:
                p, q = kernel_call(functools.partial(product_kernel, first, weight_row), operands, [shape, shape])
            first += size
            direct.append(p)
            charge.append(q)
            far.append([lax.ppermute(q, "samp", [(i, (i + k) % groups) for i in range(groups)]) for k in shifts])
            mates.append(lax.ppermute(q, "samp", pairs))
        half = []
        for low, high in ((0, 2), (2, CHUNKS)):
            half += kernel_call(
                functools.partial(near_kernel, high - low),
                (near_matrix, *direct[low:high], *charge[low:high], *mates[low:high]),
                [(p.shape, f32) for p in direct[low:high]],
            )
        pieces = []
        for n, there in enumerate(far):
            charges = []
            for x in there:
                charges += [x, lax.ppermute(x, "samp", pairs)]
            pieces.append((half[n], *charges))
        return pieces

    starts = [sum(sizes[:n]) * width for n in range(CHUNKS)]

    cols = block_cols.T
    send = send_blocks[0].T
    field, perm, inv, *outgoing = gather(send, residual, rows, domains, outgoing_shapes)
    incoming = exchange(outgoing)
    blocks = stamps.reshape(rows, per_entry * width, 2 * width)
    early = sizes[0] + sizes[1]
    loading = lambda n: (pltpu.VMEM((n, *blocks.shape[1:]), f32), pltpu.SemaphoreType.DMA((n,)))
    weight_shape = lambda n: ((n, per_entry * width, 4 * width), jnp.bfloat16)
    first_weights, cols, send = kernel_call(
        prepare_first_kernel,
        (blocks, perm, inv, cols, send),
        [weight_shape(early), (cols.shape, jnp.int32), (send.shape, jnp.int32)],
        scratch=loading(early),
        far_first=True,
    )
    (other_weights,) = kernel_call(
        functools.partial(prepare_rest_kernel, early),
        (blocks, perm),
        [weight_shape(rows - early)],
        scratch=loading(rows - early),
        far_first=True,
    )
    weights = [(0, first_weights), (early, other_weights)]
    near_matrix, far_matrix = kernel_call(
        functools.partial(tables_kernel, groups),
        (),
        [((2 * samples, 2 * samples), jnp.bfloat16), ((2 * samples, count * samples), jnp.bfloat16)],
    )
    ordered, g, c, ext = kernel_call(
        arrange_kernel, (perm, field, conductance, capacitance), [field_shape] * 3 + [ext_shape]
    )
    pieces = charges_of(ordered, ext, incoming, cols, g, c, weights)
    ready = 2 if few(domains) else CHUNKS
    u, *outgoing = kernel_call(
        functools.partial(far_send_kernel, count, ready, domains),
        (send, far_matrix, *[x for piece in pieces[:ready] for x in piece]),
        [field_shape, *outgoing_shapes],
        table_copied=True,
    )
    incoming = exchange(outgoing)
    if ready < CHUNKS:
        operands = [far_matrix, *[x for piece in pieces[ready:] for x in piece]]
        (u,) = kernel_call(
            functools.partial(far_kernel, count, starts[ready], CHUNKS - ready),
            operands + [u],
            [field_shape],
            aliases={len(operands): 0},
        )
    (ext,) = kernel_call(extend_kernel, (u,), [ext_shape])
    pieces = charges_of(u, ext, incoming, cols, g, c, weights)
    sums = None
    steps = [(0, CHUNKS - 2), (CHUNKS - 2, CHUNKS - 1), (CHUNKS - 1, CHUNKS)]
    for n, (low, high) in enumerate(steps):
        operands = [far_matrix, *[x for piece in pieces[low:high] for x in piece], ordered, u]
        final = n == len(steps) - 1
        (sums,) = kernel_call(
            functools.partial(far_dots_kernel, count, starts[low], high - low),
            operands + [sums] * (n > 0),
            [((domains * groups, 1, LANES) if final else (5, samples, LANES), f32)],
        )
    sums = lax.all_to_all(sums, ("dom", "samp"), split_axis=0, concat_axis=0, tiled=True)
    return update(inv, sums, field, u)


def solution(mesh):
    in_specs = (
        P("samp", "dom"),
        P("samp", "dom"),
        P("samp", "dom"),
        P("dom", None, None, None),
        P("dom", None),
        P("dom", None, None),
    )
    out_specs = P("samp", "dom")
    return jax.shard_map(body, mesh=mesh, in_specs=in_specs, out_specs=out_specs, check_vma=False)
```

profile of v0, /device:TPU:0, one launch (start us, length us, event | category | flops | bytes accessed | tf_op | source)
XLA Modules:
  0.0 131.1 jit_solution(14952912605527869985)
XLA Ops:
  0.0 2.3 %gather.1 = (f32[64,4096]{1,0:T(8,128)S(1)}, s32[64]{0:T(128)S(1)}, s32[64]{0:T(128)S(1)}, f32[64,256]{1,0:T(8,128)S(1)}, f32[64,256]{1,0:T(8,128)S(1)}, /*index...) custom-call(s32[4,8]{1,0:T(4,128)} %bitcast.5, ...), custom_call_target="tpu_custom_call" | custom-call | tf_op jit(solution)/shard_map/gather/pallas_call | solution.py:234
  2.3 4.1 %collective-permute-start = (f32[64,256]{1,0:T(8,128)S(1)}, f32[64,256]{1,0:T(8,128)S(1)}, u32[]{:S(2)}, u32[]{:S(2)}) collective-permute-start(f32[64,256]{1,0:T(8,128)S(1)} %get-tuple-element.69), channel_id=1, source_target_pairs={{0,16},{4,20},{8,24},{12,28},{16,0},{20,4},{24,8},{28,12},{1,17},{... | collective-permute-start | bytes 196616 | tf_op jit(solution)/shard_map/ppermute | solution.py:498
  6.4 1.3 collective-permute-start.1
  7.7 3.6 %collective-permute-start.2 = (f32[64,256]{1,0:T(8,128)S(1)}, f32[64,256]{1,0:T(8,128)S(1)}, u32[]{:S(2)}, u32[]{:S(2)}) collective-permute-start(f32[64,256]{1,0:T(8,128)S(1)} %get-tuple-element.71), channel_id=1, source_target_pairs={{0,24},{4,28},{8,16},{12,20},{16,8},{20,12},{24,0},{28,4},{1,25},{... | collective-permute-start | bytes 196616 | tf_op jit(solution)/shard_map/ppermute | solution.py:498
  11.3 0.9 collective-permute-start.4
  12.2 2.2 %collective-permute-start.5 = (f32[64,256]{1,0:T(8,128)S(1)}, f32[64,256]{1,0:T(8,128)S(1)}, u32[]{:S(2)}, u32[]{:S(2)}) collective-permute-start(f32[64,256]{1,0:T(8,128)S(1)} %get-tuple-element.74), channel_id=1, source_target_pairs={{0,8},{4,12},{8,0},{12,4},{16,24},{20,28},{24,16},{28,20},{1,9},{5... | collective-permute-start | bytes 196616 | tf_op jit(solution)/shard_map/ppermute | solution.py:498
  14.4 2.0 %collective-permute-done.1.refs_1_ = f32[64,256]{1,0:T(8,128)S(1)} collective-permute-done((f32[64,256]{1,0:T(8,128)S(1)}, f32[64,256]{1,0:T(8,128)S(1)}, u32[]{:S(2)}, u32[]{:S(2)}) %collective-permute-start.1) | collective-permute-done | bytes 65568 | tf_op jit(solution)/shard_map/ppermute | solution.py:498
  16.4 1.5 %collective-permute-start.6 = (f32[64,256]{1,0:T(8,128)S(1)}, f32[64,256]{1,0:T(8,128)S(1)}, u32[]{:S(2)}, u32[]{:S(2)}) collective-permute-start(f32[64,256]{1,0:T(8,128)S(1)} %get-tuple-element.75), channel_id=1, source_target_pairs={{0,4},{4,0},{8,12},{12,8},{16,20},{20,16},{24,28},{28,24},{1,5},{5... | collective-permute-start | bytes 196616 | tf_op jit(solution)/shard_map/ppermute | solution.py:498
  17.9 3.3 %shard_map.68.w_ref = bf16[36,256,256]{2,1,0:T(8,128)(2,1)S(1)} custom-call(f32[64,256,128]{2,1,0:T(8,128)} %bitcast.8, s32[64]{0:T(128)S(1)} %get-tuple-element.61.perm_ref), custom_call_target="tpu_custom_call" | custom-call | tf_op jit(solution)/shard_map/pallas_call | solution.py:57
  21.2 3.6 %shard_map.65 = (bf16[28,256,256]{2,1,0:T(8,128)(2,1)S(1)}, s32[4,64]{1,0:T(4,128)S(1)}, s32[4,8]{1,0:T(4,128)S(1)}) custom-call(f32[64,256,128]{2,1,0:T(8,128)} %bitcast.9, s32[64]{0:T(128)S(1)} %get-tuple-element.61.perm_ref, s32[64]{0:T(128)S(1)} %get-tuple-element.58.inv_ref.inv_near, s32[4,64]{1,0:T(4,128)S(1)} %bitcast.7, s32[4,8]{1,0:T(4,128)S(1)} %bitcast.6), custom_call_target="tpu_custom_call" | custom-call | tf_op jit(solution)/shard_map/pallas_call | solution.py:57
  24.8 4.4 %shard_map.66 = (f32[64,4096]{1,0:T(8,128)S(1)}, f32[64,4096]{1,0:T(8,128)S(1)}, f32[64,4096]{1,0:T(8,128)S(1)}, bf16[2,48,128,128]{3,2,1,0:T(8,128)(2,1)S(1)}) custom-call(s32[64]{0:T(128)S(1)} %get-tuple-element.61.perm_ref, f32[64,4096]{1,0:T(8,128)S(1)} %get-tuple-element.63.field_ref.r_ref, f32[64,4096]{1,0:T(8,128)S(1)} %copy-done, ...), custom_call_target="tpu_custom_call" | custom-call | tf_op jit(solution)/shard_map/pallas_call | solution.py:57
  29.2 1.3 shard_map.67
  30.5 3.0 %shard_map.69 = (f32[64,1792]{1,0:T(8,128)S(1)}, f32[64,1792]{1,0:T(8,128)S(1)}) custom-call(s32[4,64]{1,0:T(4,128)S(1)} %get-tuple-element.62.cols_hbm.cols_ref, f32[64,4096]{1,0:T(8,128)S(1)} %get-tuple-element.64.field_ref.refs_7_.refs_4_, bf16[2,48,128,128]{3,2,1,0:T(8,128)(2,1)S(1)} %get-tuple-element.76.ext, f32[64,4096]{1,0:T(8,128)S(1)} %get-tuple-element.66.g_ref, ...), custom_call_target="tpu_custom_call" | custom-call | tf_op jit(solution)/shard_map/pallas_call | solution.py:57
  33.6 1.6 %collective-permute-start.9 = (f32[64,1792]{1,0:T(8,128)S(1)}, f32[64,1792]{1,0:T(8,128)S(1)}, u32[]{:S(2)}, u32[]{:S(2)}) collective-permute-start(f32[64,1792]{1,0:T(8,128)S(1)} %get-tuple-element.79.refs_3_), channel_id=1, source_target_pairs={{0,2},{1,3},{2,0},{3,1},{4,6},{5,7},{6,4},{7,5},{8,10},{9,11},{10,... | collective-permute-start | bytes 1376264 | tf_op jit(solution)/shard_map/ppermute | solution.py:521
  35.2 2.3 %shard_map.72 = (f32[64,1280]{1,0:T(8,128)S(1)}, f32[64,1280]{1,0:T(8,128)S(1)}) custom-call(s32[4,64]{1,0:T(4,128)S(1)} %get-tuple-element.62.cols_hbm.cols_ref, f32[64,4096]{1,0:T(8,128)S(1)} %get-tuple-element.64.field_ref.refs_7_.refs_4_, bf16[2,48,128,128]{3,2,1,0:T(8,128)(2,1)S(1)} %get-tuple-element.76.ext, f32[64,4096]{1,0:T(8,128)S(1)} %get-tuple-element.66.g_ref, ...), custom_call_target="tpu_custom_call" | custom-call | tf_op jit(solution)/shard_map/pallas_call | solution.py:57
  37.5 0.6 collective-permute-start.17
  38.1 1.5 %collective-permute-start.15 = (f32[64,512]{1,0:T(8,128)S(1)}, f32[64,512]{1,0:T(8,128)S(1)}, u32[]{:S(2)}, u32[]{:S(2)}) collective-permute-start(f32[64,512]{1,0:T(8,128)S(1)} %get-tuple-element.86.refs_3_), channel_id=1, source_target_pairs={{0,2},{1,3},{2,0},{3,1},{4,6},{5,7},{6,4},{7,5},{8,10},{9,11},{10,... | collective-permute-start | bytes 393224 | tf_op jit(solution)/shard_map/ppermute | solution.py:521
  39.6 0.5 collective-permute-start.14
  40.1 1.3 shard_map.70
  41.4 11.9 %collective-permute-done.15.refs_2_ = f32[64,512]{1,0:T(8,128)S(1)} collective-permute-done((f32[64,512]{1,0:T(8,128)S(1)}, f32[64,512]{1,0:T(8,128)S(1)}, u32[]{:S(2)}, u32[]{:S(2)}) %collective-permute-start.15) | collective-permute-done | bytes 131104 | tf_op jit(solution)/shard_map/ppermute | solution.py:521
  53.3 1.5 %collective-permute-start.11 = (f32[64,512]{1,0:T(8,128)S(1)}, f32[64,512]{1,0:T(8,128)S(1)}, u32[]{:S(2)}, u32[]{:S(2)}) collective-permute-start(f32[64,512]{1,0:T(8,128)S(1)} %get-tuple-element.80.refs_4_), channel_id=1, source_target_pairs={{0,2},{1,3},{2,0},{3,1},{4,6},{5,7},{6,4},{7,5},{8,10},{9,11},{10,... | collective-permute-start | bytes 393224 | tf_op jit(solution)/shard_map/ppermute | solution.py:521
  54.8 0.2 collective-permute-start.10
  55.0 0.3 collective-permute-start.18
  55.3 3.9 %collective-permute-done.11.refs_5_ = f32[64,512]{1,0:T(8,128)S(1)} collective-permute-done((f32[64,512]{1,0:T(8,128)S(1)}, f32[64,512]{1,0:T(8,128)S(1)}, u32[]{:S(2)}, u32[]{:S(2)}) %collective-permute-start.11) | collective-permute-done | bytes 131104 | tf_op jit(solution)/shard_map/ppermute | solution.py:521
  59.2 1.3 %collective-permute-done.16.refs_3_ = f32[64,512]{1,0:T(8,128)S(1)} collective-permute-done((f32[64,512]{1,0:T(8,128)S(1)}, f32[64,512]{1,0:T(8,128)S(1)}, u32[]{:S(2)}, u32[]{:S(2)}) %collective-permute-start.16) | collective-permute-done | bytes 131104 | tf_op jit(solution)/shard_map/ppermute | solution.py:534
  60.6 0.1 collective-permute-start.8
  60.7 0.4 collective-permute-start.12
  61.1 0.5 shard_map.64
  61.6 0.4 shard_map.73
  62.0 0.9 shard_map.74
  62.9 3.1 %collective-permute-start.19 = (f32[64,256]{1,0:T(8,128)S(1)}, f32[64,256]{1,0:T(8,128)S(1)}, u32[]{:S(2)}, u32[]{:S(2)}) collective-permute-start(f32[64,256]{1,0:T(8,128)S(1)} %get-tuple-element.91), channel_id=1, source_target_pairs={{0,16},{4,20},{8,24},{12,28},{16,0},{20,4},{24,8},{28,12},{1,17},{... | collective-permute-start | bytes 196616 | tf_op jit(solution)/shard_map/ppermute | solution.py:498
  66.0 1.1 collective-permute-start.20
  67.1 4.8 %collective-permute-start.21 = (f32[64,256]{1,0:T(8,128)S(1)}, f32[64,256]{1,0:T(8,128)S(1)}, u32[]{:S(2)}, u32[]{:S(2)}) collective-permute-start(f32[64,256]{1,0:T(8,128)S(1)} %get-tuple-element.93), channel_id=1, source_target_pairs={{0,24},{4,28},{8,16},{12,20},{16,8},{20,12},{24,0},{28,4},{1,25},{... | collective-permute-start | bytes 196616 | tf_op jit(solution)/shard_map/ppermute | solution.py:498
  71.9 0.6 collective-permute-start.23
  72.6 3.1 %collective-permute-done.20.refs_1_ = f32[64,256]{1,0:T(8,128)S(1)} collective-permute-done((f32[64,256]{1,0:T(8,128)S(1)}, f32[64,256]{1,0:T(8,128)S(1)}, u32[]{:S(2)}, u32[]{:S(2)}) %collective-permute-start.20) | collective-permute-done | bytes 65568 | tf_op jit(solution)/shard_map/ppermute | solution.py:498
  75.7 0.9 collective-permute-start.25
  76.6 0.4 shard_map.71
  77.0 0.4 shard_map.75.field_ref.refs_8_.refs_5_.u_ref
  77.4 0.3 shard_map.76.own_ref
  77.7 1.3 %collective-permute-done.22.refs_3_ = f32[64,256]{1,0:T(8,128)S(1)} collective-permute-done((f32[64,256]{1,0:T(8,128)S(1)}, f32[64,256]{1,0:T(8,128)S(1)}, u32[]{:S(2)}, u32[]{:S(2)}) %collective-permute-start.22) | collective-permute-done | bytes 65568 | tf_op jit(solution)/shard_map/ppermute | solution.py:498
  79.2 0.7 collective-permute-done.24.refs_5_
  79.9 0.5 collective-permute-done.25.refs_6_
  80.5 1.3 shard_map.77
  81.8 3.0 %shard_map.78 = (f32[64,1792]{1,0:T(8,128)S(1)}, f32[64,1792]{1,0:T(8,128)S(1)}) custom-call(s32[4,64]{1,0:T(4,128)S(1)} %get-tuple-element.62.cols_hbm.cols_ref, f32[64,4096]{1,0:T(8,128)S(1)} %shard_map.75.field_ref.refs_8_.refs_5_.u_ref, bf16[2,48,128,128]{3,2,1,0:T(8,128)(2,1)S(1)} %get-tuple-element.98.ext, f32[64,4096]{1,0:T(8,128)S(1)} %get-tuple-element.66.g_ref, ...), custom_call_target="tpu_custom_call" | custom-call | tf_op jit(solution)/shard_map/pallas_call | solution.py:57
  84.8 1.6 %collective-permute-start.30 = (f32[64,1792]{1,0:T(8,128)S(1)}, f32[64,1792]{1,0:T(8,128)S(1)}, u32[]{:S(2)}, u32[]{:S(2)}) collective-permute-start(f32[64,1792]{1,0:T(8,128)S(1)} %get-tuple-element.101.refs_3_), channel_id=1, source_target_pairs={{0,2},{1,3},{2,0},{3,1},{4,6},{5,7},{6,4},{7,5},{8,10},{9,11},{10,... | collective-permute-start | bytes 1376264 | tf_op jit(solution)/shard_map/ppermute | solution.py:521
  86.4 2.5 %shard_map.81 = (f32[64,1280]{1,0:T(8,128)S(1)}, f32[64,1280]{1,0:T(8,128)S(1)}) custom-call(s32[4,64]{1,0:T(4,128)S(1)} %get-tuple-element.62.cols_hbm.cols_ref, f32[64,4096]{1,0:T(8,128)S(1)} %shard_map.75.field_ref.refs_8_.refs_5_.u_ref, bf16[2,48,128,128]{3,2,1,0:T(8,128)(2,1)S(1)} %get-tuple-element.98.ext, f32[64,4096]{1,0:T(8,128)S(1)} %get-tuple-element.66.g_ref, ...), custom_call_target="tpu_custom_call" | custom-call | tf_op jit(solution)/shard_map/pallas_call | solution.py:57
  88.9 0.6 collective-permute-start.36
  89.5 1.5 %collective-permute-start.34 = (f32[64,512]{1,0:T(8,128)S(1)}, f32[64,512]{1,0:T(8,128)S(1)}, u32[]{:S(2)}, u32[]{:S(2)}) collective-permute-start(f32[64,512]{1,0:T(8,128)S(1)} %get-tuple-element.107.refs_3_), channel_id=1, source_target_pairs={{0,2},{1,3},{2,0},{3,1},{4,6},{5,7},{6,4},{7,5},{8,10},{9,11},{10,... | collective-permute-start | bytes 393224 | tf_op jit(solution)/shard_map/ppermute | solution.py:521
  91.0 0.5 collective-permute-start.26
  91.5 6.8 %collective-permute-done.30.refs_2_ = f32[64,1792]{1,0:T(8,128)S(1)} collective-permute-done((f32[64,1792]{1,0:T(8,128)S(1)}, f32[64,1792]{1,0:T(8,128)S(1)}, u32[]{:S(2)}, u32[]{:S(2)}) %collective-permute-start.30) | collective-permute-done | bytes 458784 | tf_op jit(solution)/shard_map/ppermute | solution.py:521
  98.3 8.8 %collective-permute-done.34.refs_2_ = f32[64,512]{1,0:T(8,128)S(1)} collective-permute-done((f32[64,512]{1,0:T(8,128)S(1)}, f32[64,512]{1,0:T(8,128)S(1)}, u32[]{:S(2)}, u32[]{:S(2)}) %collective-permute-start.34) | collective-permute-done | bytes 131104 | tf_op jit(solution)/shard_map/ppermute | solution.py:521
  107.1 1.3 shard_map.79
  108.4 1.6 %collective-permute-start.28 = (f32[64,512]{1,0:T(8,128)S(1)}, f32[64,512]{1,0:T(8,128)S(1)}, u32[]{:S(2)}, u32[]{:S(2)}) collective-permute-start(f32[64,512]{1,0:T(8,128)S(1)} %get-tuple-element.102.refs_4_), channel_id=1, source_target_pairs={{0,2},{1,3},{2,0},{3,1},{4,6},{5,7},{6,4},{7,5},{8,10},{9,11},{10,... | collective-permute-start | bytes 393224 | tf_op jit(solution)/shard_map/ppermute | solution.py:521
  109.9 0.2 collective-permute-start.37
  110.2 4.2 %collective-permute-done.28.refs_2_ = f32[64,512]{1,0:T(8,128)S(1)} collective-permute-done((f32[64,512]{1,0:T(8,128)S(1)}, f32[64,512]{1,0:T(8,128)S(1)}, u32[]{:S(2)}, u32[]{:S(2)}) %collective-permute-start.28) | collective-permute-done | bytes 131104 | tf_op jit(solution)/shard_map/ppermute | solution.py:521
  114.4 1.3 %collective-permute-done.27.refs_6_ = f32[64,512]{1,0:T(8,128)S(1)} collective-permute-done((f32[64,512]{1,0:T(8,128)S(1)}, f32[64,512]{1,0:T(8,128)S(1)}, u32[]{:S(2)}, u32[]{:S(2)}) %collective-permute-start.27) | collective-permute-done | bytes 131104 | tf_op jit(solution)/shard_map/ppermute | solution.py:522
  115.9 0.4 collective-permute-start.29
  116.2 0.3 shard_map.82
  116.6 0.4 shard_map.80
  117.1 0.4 shard_map.83.refs_6_
  117.5 0.4 shard_map.84.refs_6_
  117.9 0.4 shard_map.85
  118.3 10.7 %all_to_all.5.sums_ref = f32[32,1,128]{2,1,0:T(1,128)S(1)} all-to-all(f32[32,1,128]{2,1,0:T(1,128)S(1)} %shard_map.85), channel_id=1, replica_groups=mesh['dom'=8,'samp'=4] {'dom','samp'}, dimensions={0} | all-to-all | bytes 32768 | tf_op jit(solution)/shard_map/all_to_all | solution.py:600
  129.0 1.9 %update.1 = f32[64,4096]{1,0:T(8,128)} custom-call(s32[64]{0:T(128)S(1)} %get-tuple-element.58.inv_ref.inv_near, f32[32,1,128]{2,1,0:T(1,128)S(1)} %all_to_all.5.sums_ref, f32[64,4096]{1,0:T(8,128)S(1)} %get-tuple-element.63.field_ref.r_ref, f32[64,4096]{1,0:T(8,128)S(1)} %shard_map.75.field_ref.refs_8_.refs_5_.u_ref), custom_call_target="tpu_custom_call" | custom-call | tf_op jit(solution)/shard_map/update/pallas_call | solution.py:448
  (45 shorter events, 0.5 us)
Async XLA Ops:
  2.3 9.9 %collective-permute-start = (f32[64,256]{1,0:T(8,128)S(1)}, f32[64,256]{1,0:T(8,128)S(1)}, u32[]{:S(2)}, u32[]{:S(2)}) collective-permute-start(f32[64,256]{1,0:T(8,128)S(1)} %get-tuple-element.69), channel_id=1, source_target_pairs={{0,16},{4,20},{8,24},{12,28},{16,0},{20,4},{24,8},{28,12},{1,17},{... | collective-permute-start | bytes 196616 | tf_op jit(solution)/shard_map/ppermute | solution.py:498
  6.4 10.0 %collective-permute-start.1 = (f32[64,256]{1,0:T(8,128)S(1)}, f32[64,256]{1,0:T(8,128)S(1)}, u32[]{:S(2)}, u32[]{:S(2)}) collective-permute-start(f32[64,256]{1,0:T(8,128)S(1)} %get-tuple-element.70), channel_id=1, source_target_pairs={{0,20},{4,16},{8,28},{12,24},{16,4},{20,0},{24,12},{28,8},{1,21},{... | collective-permute-start | bytes 196616 | tf_op jit(solution)/shard_map/ppermute | solution.py:498
  7.7 21.5 %collective-permute-start.2 = (f32[64,256]{1,0:T(8,128)S(1)}, f32[64,256]{1,0:T(8,128)S(1)}, u32[]{:S(2)}, u32[]{:S(2)}) collective-permute-start(f32[64,256]{1,0:T(8,128)S(1)} %get-tuple-element.71), channel_id=1, source_target_pairs={{0,24},{4,28},{8,16},{12,20},{16,8},{20,12},{24,0},{28,4},{1,25},{... | collective-permute-start | bytes 196616 | tf_op jit(solution)/shard_map/ppermute | solution.py:498
  11.3 17.9 %collective-permute-start.3 = (f32[64,256]{1,0:T(8,128)S(1)}, f32[64,256]{1,0:T(8,128)S(1)}, u32[]{:S(2)}, u32[]{:S(2)}) collective-permute-start(f32[64,256]{1,0:T(8,128)S(1)} %get-tuple-element.72), channel_id=1, source_target_pairs={{0,28},{4,24},{8,20},{12,16},{16,12},{20,8},{24,4},{28,0},{1,29},{... | collective-permute-start | bytes 196616 | tf_op jit(solution)/shard_map/ppermute | solution.py:498
  11.3 17.9 %collective-permute-start.4 = (f32[64,256]{1,0:T(8,128)S(1)}, f32[64,256]{1,0:T(8,128)S(1)}, u32[]{:S(2)}, u32[]{:S(2)}) collective-permute-start(f32[64,256]{1,0:T(8,128)S(1)} %get-tuple-element.73), channel_id=1, source_target_pairs={{0,12},{4,8},{8,4},{12,0},{16,28},{20,24},{24,20},{28,16},{1,13},{... | collective-permute-start | bytes 196616 | tf_op jit(solution)/shard_map/ppermute | solution.py:498
  12.2 17.0 %collective-permute-start.5 = (f32[64,256]{1,0:T(8,128)S(1)}, f32[64,256]{1,0:T(8,128)S(1)}, u32[]{:S(2)}, u32[]{:S(2)}) collective-permute-start(f32[64,256]{1,0:T(8,128)S(1)} %get-tuple-element.74), channel_id=1, source_target_pairs={{0,8},{4,12},{8,0},{12,4},{16,24},{20,28},{24,16},{28,20},{1,9},{5... | collective-permute-start | bytes 196616 | tf_op jit(solution)/shard_map/ppermute | solution.py:498
  16.4 12.8 %collective-permute-start.6 = (f32[64,256]{1,0:T(8,128)S(1)}, f32[64,256]{1,0:T(8,128)S(1)}, u32[]{:S(2)}, u32[]{:S(2)}) collective-permute-start(f32[64,256]{1,0:T(8,128)S(1)} %get-tuple-element.75), channel_id=1, source_target_pairs={{0,4},{4,0},{8,12},{12,8},{16,20},{20,16},{24,28},{28,24},{1,5},{5... | collective-permute-start | bytes 196616 | tf_op jit(solution)/shard_map/ppermute | solution.py:498
  17.9 3.3 %copy-start.2 = (s32[1,8,4]{1,2,0:T(4,128)S(1)}, s32[1,8,4]{1,2,0:T(4,128)}, u32[]{:S(2)}) copy-start(s32[1,8,4]{1,2,0:T(4,128)} %param.11) | copy-start | bytes 388
  17.9 3.3 %copy-start.3 = (s32[64,4]{0,1:T(4,128)S(1)}, s32[64,4]{0,1:T(4,128)}, u32[]{:S(2)}) copy-start(s32[64,4]{0,1:T(4,128)} %param.10) | copy-start | bytes 3076
  21.2 3.6 %copy-start = (f32[64,4096]{1,0:T(8,128)S(1)}, f32[64,4096]{1,0:T(8,128)}, u32[]{:S(2)}) copy-start(f32[64,4096]{1,0:T(8,128)} %g_ref.1) | copy-start | bytes 3145732
  21.2 3.6 %copy-start.1 = (f32[64,4096]{1,0:T(8,128)S(1)}, f32[64,4096]{1,0:T(8,128)}, u32[]{:S(2)}) copy-start(f32[64,4096]{1,0:T(8,128)} %c_ref.1) | copy-start | bytes 3145732
  33.6 21.2 %collective-permute-start.9 = (f32[64,1792]{1,0:T(8,128)S(1)}, f32[64,1792]{1,0:T(8,128)S(1)}, u32[]{:S(2)}, u32[]{:S(2)}) collective-permute-start(f32[64,1792]{1,0:T(8,128)S(1)} %get-tuple-element.79.refs_3_), channel_id=1, source_target_pairs={{0,2},{1,3},{2,0},{3,1},{4,6},{5,7},{6,4},{7,5},{8,10},{9,11},{10,... | collective-permute-start | bytes 1376264 | tf_op jit(solution)/shard_map/ppermute | solution.py:521
  37.5 17.5 %collective-permute-start.17 = (f32[64,1280]{1,0:T(8,128)S(1)}, f32[64,1280]{1,0:T(8,128)S(1)}, u32[]{:S(2)}, u32[]{:S(2)}) collective-permute-start(f32[64,1280]{1,0:T(8,128)S(1)} %get-tuple-element.87.refs_4_), channel_id=1, source_target_pairs={{0,2},{1,3},{2,0},{3,1},{4,6},{5,7},{6,4},{7,5},{8,10},{9,11},{10,... | collective-permute-start | bytes 983048 | tf_op jit(solution)/shard_map/ppermute | solution.py:521
  38.1 15.2 %collective-permute-start.15 = (f32[64,512]{1,0:T(8,128)S(1)}, f32[64,512]{1,0:T(8,128)S(1)}, u32[]{:S(2)}, u32[]{:S(2)}) collective-permute-start(f32[64,512]{1,0:T(8,128)S(1)} %get-tuple-element.86.refs_3_), channel_id=1, source_target_pairs={{0,2},{1,3},{2,0},{3,1},{4,6},{5,7},{6,4},{7,5},{8,10},{9,11},{10,... | collective-permute-start | bytes 393224 | tf_op jit(solution)/shard_map/ppermute | solution.py:521
  39.6 13.7 %collective-permute-start.13 = (f32[64,512]{1,0:T(8,128)S(1)}, f32[64,512]{1,0:T(8,128)S(1)}, u32[]{:S(2)}, u32[]{:S(2)}) collective-permute-start(f32[64,512]{1,0:T(8,128)S(1)} %get-tuple-element.86.refs_3_), channel_id=1, source_target_pairs={{0,1},{1,0},{2,3},{3,2},{4,5},{5,4},{6,7},{7,6},{8,9},{9,8},{10,11... | collective-permute-start | bytes 393224 | tf_op jit(solution)/shard_map/ppermute | solution.py:522
  39.6 21.1 %collective-permute-start.14 = (f32[64,1280]{1,0:T(8,128)S(1)}, f32[64,1280]{1,0:T(8,128)S(1)}, u32[]{:S(2)}, u32[]{:S(2)}) collective-permute-start(f32[64,1280]{1,0:T(8,128)S(1)} %get-tuple-element.87.refs_4_), channel_id=1, source_target_pairs={{0,1},{1,0},{2,3},{3,2},{4,5},{5,4},{6,7},{7,6},{8,9},{9,8},{10,11... | collective-permute-start | bytes 983048 | tf_op jit(solution)/shard_map/ppermute | solution.py:522
  53.3 18.6 %collective-permute-start.7 = (f32[64,1792]{1,0:T(8,128)S(1)}, f32[64,1792]{1,0:T(8,128)S(1)}, u32[]{:S(2)}, u32[]{:S(2)}) collective-permute-start(f32[64,1792]{1,0:T(8,128)S(1)} %get-tuple-element.79.refs_3_), channel_id=1, source_target_pairs={{0,1},{1,0},{2,3},{3,2},{4,5},{5,4},{6,7},{7,6},{8,9},{9,8},{10,11... | collective-permute-start | bytes 1376264 | tf_op jit(solution)/shard_map/ppermute | solution.py:522
  53.3 5.9 %collective-permute-start.11 = (f32[64,512]{1,0:T(8,128)S(1)}, f32[64,512]{1,0:T(8,128)S(1)}, u32[]{:S(2)}, u32[]{:S(2)}) collective-permute-start(f32[64,512]{1,0:T(8,128)S(1)} %get-tuple-element.80.refs_4_), channel_id=1, source_target_pairs={{0,2},{1,3},{2,0},{3,1},{4,6},{5,7},{6,4},{7,5},{8,10},{9,11},{10,... | collective-permute-start | bytes 393224 | tf_op jit(solution)/shard_map/ppermute | solution.py:521
  54.8 20.9 %collective-permute-start.10 = (f32[64,1792]{1,0:T(8,128)S(1)}, f32[64,1792]{1,0:T(8,128)S(1)}, u32[]{:S(2)}, u32[]{:S(2)}) collective-permute-start(f32[64,1792]{1,0:T(8,128)S(1)} %collective-permute-done.9.refs_2_), channel_id=1, source_target_pairs={{0,1},{1,0},{2,3},{3,2},{4,5},{5,4},{6,7},{7,6},{8,9},{9,8},{10,11... | collective-permute-start | bytes 1376264 | tf_op jit(solution)/shard_map/ppermute | solution.py:534
  55.0 7.0 %collective-permute-start.18 = (f32[64,1280]{1,0:T(8,128)S(1)}, f32[64,1280]{1,0:T(8,128)S(1)}, u32[]{:S(2)}, u32[]{:S(2)}) collective-permute-start(f32[64,1280]{1,0:T(8,128)S(1)} %collective-permute-done.17.refs_5_), channel_id=1, source_target_pairs={{0,1},{1,0},{2,3},{3,2},{4,5},{5,4},{6,7},{7,6},{8,9},{9,8},{10,11... | collective-permute-start | bytes 983048 | tf_op jit(solution)/shard_map/ppermute | solution.py:534
  59.2 1.3 %collective-permute-start.16 = (f32[64,512]{1,0:T(8,128)S(1)}, f32[64,512]{1,0:T(8,128)S(1)}, u32[]{:S(2)}, u32[]{:S(2)}) collective-permute-start(f32[64,512]{1,0:T(8,128)S(1)} %collective-permute-done.15.refs_2_), channel_id=1, source_target_pairs={{0,1},{1,0},{2,3},{3,2},{4,5},{5,4},{6,7},{7,6},{8,9},{9,8},{10,11... | collective-permute-start | bytes 393224 | tf_op jit(solution)/shard_map/ppermute | solution.py:534
  60.6 5.4 %collective-permute-start.8 = (f32[64,512]{1,0:T(8,128)S(1)}, f32[64,512]{1,0:T(8,128)S(1)}, u32[]{:S(2)}, u32[]{:S(2)}) collective-permute-start(f32[64,512]{1,0:T(8,128)S(1)} %get-tuple-element.80.refs_4_), channel_id=1, source_target_pairs={{0,1},{1,0},{2,3},{3,2},{4,5},{5,4},{6,7},{7,6},{8,9},{9,8},{10,11... | collective-permute-start | bytes 393224 | tf_op jit(solution)/shard_map/ppermute | solution.py:522
  60.7 6.4 %collective-permute-start.12 = (f32[64,512]{1,0:T(8,128)S(1)}, f32[64,512]{1,0:T(8,128)S(1)}, u32[]{:S(2)}, u32[]{:S(2)}) collective-permute-start(f32[64,512]{1,0:T(8,128)S(1)} %collective-permute-done.11.refs_5_), channel_id=1, source_target_pairs={{0,1},{1,0},{2,3},{3,2},{4,5},{5,4},{6,7},{7,6},{8,9},{9,8},{10,11... | collective-permute-start | bytes 393224 | tf_op jit(solution)/shard_map/ppermute | solution.py:534
  62.9 9.0 %collective-permute-start.19 = (f32[64,256]{1,0:T(8,128)S(1)}, f32[64,256]{1,0:T(8,128)S(1)}, u32[]{:S(2)}, u32[]{:S(2)}) collective-permute-start(f32[64,256]{1,0:T(8,128)S(1)} %get-tuple-element.91), channel_id=1, source_target_pairs={{0,16},{4,20},{8,24},{12,28},{16,0},{20,4},{24,8},{28,12},{1,17},{... | collective-permute-start | bytes 196616 | tf_op jit(solution)/shard_map/ppermute | solution.py:498
  66.0 9.7 %collective-permute-start.20 = (f32[64,256]{1,0:T(8,128)S(1)}, f32[64,256]{1,0:T(8,128)S(1)}, u32[]{:S(2)}, u32[]{:S(2)}) collective-permute-start(f32[64,256]{1,0:T(8,128)S(1)} %get-tuple-element.92), channel_id=1, source_target_pairs={{0,20},{4,16},{8,28},{12,24},{16,4},{20,0},{24,12},{28,8},{1,21},{... | collective-permute-start | bytes 196616 | tf_op jit(solution)/shard_map/ppermute | solution.py:498
  67.1 10.6 %collective-permute-start.21 = (f32[64,256]{1,0:T(8,128)S(1)}, f32[64,256]{1,0:T(8,128)S(1)}, u32[]{:S(2)}, u32[]{:S(2)}) collective-permute-start(f32[64,256]{1,0:T(8,128)S(1)} %get-tuple-element.93), channel_id=1, source_target_pairs={{0,24},{4,28},{8,16},{12,20},{16,8},{20,12},{24,0},{28,4},{1,25},{... | collective-permute-start | bytes 196616 | tf_op jit(solution)/shard_map/ppermute | solution.py:498
  71.9 7.2 %collective-permute-start.22 = (f32[64,256]{1,0:T(8,128)S(1)}, f32[64,256]{1,0:T(8,128)S(1)}, u32[]{:S(2)}, u32[]{:S(2)}) collective-permute-start(f32[64,256]{1,0:T(8,128)S(1)} %get-tuple-element.94), channel_id=1, source_target_pairs={{0,28},{4,24},{8,20},{12,16},{16,12},{20,8},{24,4},{28,0},{1,29},{... | collective-permute-start | bytes 196616 | tf_op jit(solution)/shard_map/ppermute | solution.py:498
  71.9 7.3 %collective-permute-start.23 = (f32[64,256]{1,0:T(8,128)S(1)}, f32[64,256]{1,0:T(8,128)S(1)}, u32[]{:S(2)}, u32[]{:S(2)}) collective-permute-start(f32[64,256]{1,0:T(8,128)S(1)} %get-tuple-element.95), channel_id=1, source_target_pairs={{0,12},{4,8},{8,4},{12,0},{16,28},{20,24},{24,20},{28,16},{1,13},{... | collective-permute-start | bytes 196616 | tf_op jit(solution)/shard_map/ppermute | solution.py:498
  75.7 4.3 %collective-permute-start.24 = (f32[64,256]{1,0:T(8,128)S(1)}, f32[64,256]{1,0:T(8,128)S(1)}, u32[]{:S(2)}, u32[]{:S(2)}) collective-permute-start(f32[64,256]{1,0:T(8,128)S(1)} %get-tuple-element.96), channel_id=1, source_target_pairs={{0,8},{4,12},{8,0},{12,4},{16,24},{20,28},{24,16},{28,20},{1,9},{5... | collective-permute-start | bytes 196616 | tf_op jit(solution)/shard_map/ppermute | solution.py:498
  75.7 4.8 %collective-permute-start.25 = (f32[64,256]{1,0:T(8,128)S(1)}, f32[64,256]{1,0:T(8,128)S(1)}, u32[]{:S(2)}, u32[]{:S(2)}) collective-permute-start(f32[64,256]{1,0:T(8,128)S(1)} %get-tuple-element.97), channel_id=1, source_target_pairs={{0,4},{4,0},{8,12},{12,8},{16,20},{20,16},{24,28},{28,24},{1,5},{5... | collective-permute-start | bytes 196616 | tf_op jit(solution)/shard_map/ppermute | solution.py:498
  84.8 13.5 %collective-permute-start.30 = (f32[64,1792]{1,0:T(8,128)S(1)}, f32[64,1792]{1,0:T(8,128)S(1)}, u32[]{:S(2)}, u32[]{:S(2)}) collective-permute-start(f32[64,1792]{1,0:T(8,128)S(1)} %get-tuple-element.101.refs_3_), channel_id=1, source_target_pairs={{0,2},{1,3},{2,0},{3,1},{4,6},{5,7},{6,4},{7,5},{8,10},{9,11},{10,... | collective-permute-start | bytes 1376264 | tf_op jit(solution)/shard_map/ppermute | solution.py:521
  88.9 21.0 %collective-permute-start.36 = (f32[64,1280]{1,0:T(8,128)S(1)}, f32[64,1280]{1,0:T(8,128)S(1)}, u32[]{:S(2)}, u32[]{:S(2)}) collective-permute-start(f32[64,1280]{1,0:T(8,128)S(1)} %get-tuple-element.108.refs_4_), channel_id=1, source_target_pairs={{0,2},{1,3},{2,0},{3,1},{4,6},{5,7},{6,4},{7,5},{8,10},{9,11},{10,... | collective-permute-start | bytes 983048 | tf_op jit(solution)/shard_map/ppermute | solution.py:521
  89.5 17.6 %collective-permute-start.34 = (f32[64,512]{1,0:T(8,128)S(1)}, f32[64,512]{1,0:T(8,128)S(1)}, u32[]{:S(2)}, u32[]{:S(2)}) collective-permute-start(f32[64,512]{1,0:T(8,128)S(1)} %get-tuple-element.107.refs_3_), channel_id=1, source_target_pairs={{0,2},{1,3},{2,0},{3,1},{4,6},{5,7},{6,4},{7,5},{8,10},{9,11},{10,... | collective-permute-start | bytes 393224 | tf_op jit(solution)/shard_map/ppermute | solution.py:521
  91.0 17.4 %collective-permute-start.32 = (f32[64,512]{1,0:T(8,128)S(1)}, f32[64,512]{1,0:T(8,128)S(1)}, u32[]{:S(2)}, u32[]{:S(2)}) collective-permute-start(f32[64,512]{1,0:T(8,128)S(1)} %get-tuple-element.107.refs_3_), channel_id=1, source_target_pairs={{0,1},{1,0},{2,3},{3,2},{4,5},{5,4},{6,7},{7,6},{8,9},{9,8},{10,11... | collective-permute-start | bytes 393224 | tf_op jit(solution)/shard_map/ppermute | solution.py:522
  91.0 25.6 %collective-permute-start.26 = (f32[64,1792]{1,0:T(8,128)S(1)}, f32[64,1792]{1,0:T(8,128)S(1)}, u32[]{:S(2)}, u32[]{:S(2)}) collective-permute-start(f32[64,1792]{1,0:T(8,128)S(1)} %get-tuple-element.101.refs_3_), channel_id=1, source_target_pairs={{0,1},{1,0},{2,3},{3,2},{4,5},{5,4},{6,7},{7,6},{8,9},{9,8},{10,11... | collective-permute-start | bytes 1376264 | tf_op jit(solution)/shard_map/ppermute | solution.py:522
  98.3 19.2 %collective-permute-start.31 = (f32[64,1792]{1,0:T(8,128)S(1)}, f32[64,1792]{1,0:T(8,128)S(1)}, u32[]{:S(2)}, u32[]{:S(2)}) collective-permute-start(f32[64,1792]{1,0:T(8,128)S(1)} %collective-permute-done.30.refs_2_), channel_id=1, source_target_pairs={{0,1},{1,0},{2,3},{3,2},{4,5},{5,4},{6,7},{7,6},{8,9},{9,8},{10,11... | collective-permute-start | bytes 1376264 | tf_op jit(solution)/shard_map/ppermute | solution.py:534
  107.1 8.8 %collective-permute-start.33 = (f32[64,1280]{1,0:T(8,128)S(1)}, f32[64,1280]{1,0:T(8,128)S(1)}, u32[]{:S(2)}, u32[]{:S(2)}) collective-permute-start(f32[64,1280]{1,0:T(8,128)S(1)} %get-tuple-element.108.refs_4_), channel_id=1, source_target_pairs={{0,1},{1,0},{2,3},{3,2},{4,5},{5,4},{6,7},{7,6},{8,9},{9,8},{10,11... | collective-permute-start | bytes 983048 | tf_op jit(solution)/shard_map/ppermute | solution.py:522
  108.4 6.0 %collective-permute-start.28 = (f32[64,512]{1,0:T(8,128)S(1)}, f32[64,512]{1,0:T(8,128)S(1)}, u32[]{:S(2)}, u32[]{:S(2)}) collective-permute-start(f32[64,512]{1,0:T(8,128)S(1)} %get-tuple-element.102.refs_4_), channel_id=1, source_target_pairs={{0,2},{1,3},{2,0},{3,1},{4,6},{5,7},{6,4},{7,5},{8,10},{9,11},{10,... | collective-permute-start | bytes 393224 | tf_op jit(solution)/shard_map/ppermute | solution.py:521
  109.9 7.1 %collective-permute-start.37 = (f32[64,1280]{1,0:T(8,128)S(1)}, f32[64,1280]{1,0:T(8,128)S(1)}, u32[]{:S(2)}, u32[]{:S(2)}) collective-permute-start(f32[64,1280]{1,0:T(8,128)S(1)} %collective-permute-done.36.refs_5_), channel_id=1, source_target_pairs={{0,1},{1,0},{2,3},{3,2},{4,5},{5,4},{6,7},{7,6},{8,9},{9,8},{10,11... | collective-permute-start | bytes 983048 | tf_op jit(solution)/shard_map/ppermute | solution.py:534
  114.4 1.3 %collective-permute-start.27 = (f32[64,512]{1,0:T(8,128)S(1)}, f32[64,512]{1,0:T(8,128)S(1)}, u32[]{:S(2)}, u32[]{:S(2)}) collective-permute-start(f32[64,512]{1,0:T(8,128)S(1)} %get-tuple-element.102.refs_4_), channel_id=1, source_target_pairs={{0,1},{1,0},{2,3},{3,2},{4,5},{5,4},{6,7},{7,6},{8,9},{9,8},{10,11... | collective-permute-start | bytes 393224 | tf_op jit(solution)/shard_map/ppermute | solution.py:522
  115.7 1.3 %collective-permute-start.35 = (f32[64,512]{1,0:T(8,128)S(1)}, f32[64,512]{1,0:T(8,128)S(1)}, u32[]{:S(2)}, u32[]{:S(2)}) collective-permute-start(f32[64,512]{1,0:T(8,128)S(1)} %collective-permute-done.34.refs_2_), channel_id=1, source_target_pairs={{0,1},{1,0},{2,3},{3,2},{4,5},{5,4},{6,7},{7,6},{8,9},{9,8},{10,11... | collective-permute-start | bytes 393224 | tf_op jit(solution)/shard_map/ppermute | solution.py:534
  115.9 2.0 %collective-permute-start.29 = (f32[64,512]{1,0:T(8,128)S(1)}, f32[64,512]{1,0:T(8,128)S(1)}, u32[]{:S(2)}, u32[]{:S(2)}) collective-permute-start(f32[64,512]{1,0:T(8,128)S(1)} %collective-permute-done.28.refs_2_), channel_id=1, source_target_pairs={{0,1},{1,0},{2,3},{3,2},{4,5},{5,4},{6,7},{7,6},{8,9},{9,8},{10,11... | collective-permute-start | bytes 393224 | tf_op jit(solution)/shard_map/ppermute | solution.py:534
where the time goes:
time: 131 us
  waiting for transfers between devices  46.2 us (35%)
  starting transfers between devices  37.3 us (28%)
  Pallas kernels  36.4 us (28%)
  blocking collectives  10.7 us (8%)
    ppermute x8, waiting for transfers between devices, charges_of(): lax.ppermute(q, 'samp', [(i, (i + k) % groups) for i in range(groups)])  35.6 us
    pallas_call x22, Pallas kernels, kernel_call(): pl.pallas_call(kernel, in_specs=specs, out_specs=[scalars() if number els...  32.2 us
    ppermute x14, starting transfers between devices, exchange(): lax.ppermute(x, 'dom', [(i, i ^ k) for i in range(domains)])  24.2 us
    all_to_all x1, blocking collectives, body(): lax.all_to_all(sums, ('dom', 'samp'), split_axis=0, concat_axis=0, tiled=...  10.7 us
    ppermute x8, starting transfers between devices, charges_of(): lax.ppermute(q, 'samp', [(i, (i + k) % groups) for i in range(groups)])  10.3 us
    ppermute x14, waiting for transfers between devices, exchange(): lax.ppermute(x, 'dom', [(i, i ^ k) for i in range(domains)])  7.84 us
  transfers between devices with their start and end apart: 38, of which 14 were waited for; matrix products, arithmetic and copies ran while one was open for 0% of the time, Pallas kernels for 18%

commit v1 on v0

v1 whole, which is shorter than its diff:
```python
import functools

import jax
import jax.numpy as jnp
from jax import lax
from jax.experimental import pallas as pl
from jax.experimental.pallas import tpu as pltpu
from jax.sharding import PartitionSpec as P


LANES = 128
HALF = 64
GROUP = 4


LIMIT = 24 * 1024 * 1024


def whole():
    return pl.BlockSpec(memory_space=pltpu.VMEM)


def scalars():
    return pl.BlockSpec(memory_space=pltpu.SMEM)


def near_memory(x):
    return pltpu.with_memory_space_constraint(x, pltpu.VMEM)


def far_memory(x):
    return pltpu.with_memory_space_constraint(x, pltpu.HBM)


def kernel_call(kernel, inputs, outputs, aliases=None, table_copied=False):
    specs = []
    operands = []
    scratch = []
    for x in inputs:
        if x.dtype == jnp.int32 and table_copied:
            specs.append(pl.BlockSpec(memory_space=pl.ANY))
            operands.append(near_memory(x))
            scratch += [pltpu.SMEM(x.shape, x.dtype), pltpu.SemaphoreType.DMA]
        elif x.dtype == jnp.int32:
            specs.append(scalars())
            operands.append(x)
        else:
            specs.append(whole())
            operands.append(near_memory(x))
    integer = [dtype == jnp.int32 for _, dtype in outputs]
    out = [
        jax.ShapeDtypeStruct(shape, dtype) if number else pltpu.VMEM(shape, dtype)
        for (shape, dtype), number in zip(outputs, integer)
    ]
    return pl.pallas_call(
        kernel,
        in_specs=specs,
        out_specs=[scalars() if number else whole() for number in integer],
        out_shape=out,
        input_output_aliases=aliases or {},
        scratch_shapes=scratch,
        compiler_params=pltpu.CompilerParams(vmem_limit_bytes=LIMIT),
    )(*operands)


def split(x):
    high = x.astype(jnp.bfloat16)
    low = (x - high.astype(jnp.float32)).astype(jnp.bfloat16)
    return high, low


def spectral_rows(me, sources, samples, period):
    row = me * samples + lax.broadcasted_iota(jnp.int32, (samples, samples), 0)
    column = lax.broadcasted_iota(jnp.int32, (samples, samples), 1)
    blocks = []
    for source in sources:
        offset = row - (source * samples + column)
        sign = (1 - 2 * (offset & 1)).astype(jnp.float32)
        angle = jnp.pi / period * offset.astype(jnp.float32)
        nonzero = offset != 0
        safe = jnp.where(nonzero, angle, 0.5)
        value = sign * jnp.cos(safe) / jnp.sin(safe) / period
        blocks.append(jnp.where(nonzero, value, 0.0))
    high, low = split(jnp.concatenate(blocks, axis=1))
    return jnp.concatenate([high, low], axis=0)


def tables_kernel(groups, near_ref, far_ref):
    samples = near_ref.shape[1] // 2
    me = lax.axis_index("samp")
    partner = me + 1 - 2 * (me & 1)
    near_ref[...] = spectral_rows(me, [me, partner], samples, samples * groups)
    far = []
    for k in range(2, groups, 2):
        for source in (me - k, partner - k):
            far.append(jnp.where(source < 0, source + groups, source))
    far_ref[...] = spectral_rows(me, far, samples, samples * groups)


def prepare_kernel(first_row, last_row, perm_ref, stamps_ref, *refs):
    out_ref = refs[-1]
    width = stamps_ref.shape[2]

    def convert(row, carry):
        high, low = split(stamps_ref[perm_ref[row]])
        out_ref[row, :, :width] = high
        out_ref[row, :, width:] = low
        return carry

    lax.fori_loop(first_row, last_row, convert, 0, unroll=2)


def fetch_kernel(perm_ref, stamps_hbm, out_ref, buffer, sems):
    rows, _, width = buffer.shape
    copies = []
    for n in range(rows):
        copies.append(pltpu.make_async_copy(stamps_hbm.at[perm_ref[n]], buffer.at[n], sems.at[n]))
        copies[-1].start()
    for n, copy in enumerate(copies):
        copy.wait()
        high, low = split(buffer[n])
        out_ref[n, :, :width] = high
        out_ref[n, :, width:] = low


def fetch(perm, stamps, rows):
    total, depth, width = stamps.shape
    return pl.pallas_call(
        fetch_kernel,
        in_specs=[scalars(), pl.BlockSpec(memory_space=pl.ANY)],
        out_specs=whole(),
        out_shape=pltpu.VMEM((total, depth, 2 * width), jnp.bfloat16),
        scratch_shapes=[pltpu.VMEM((rows, depth, width), stamps.dtype), pltpu.SemaphoreType.DMA((rows,))],
        compiler_params=pltpu.CompilerParams(vmem_limit_bytes=LIMIT),
        name="prepare_0",
    )(perm, far_memory(stamps))


def pair_tile(ref, first, second):
    samples = ref.shape[0]
    lane = lax.broadcasted_iota(jnp.int32, (samples, LANES), 1)

    def placed(block, upper):
        start = pl.multiple_of((block // 2) * LANES, LANES)
        tile = ref[:, pl.ds(start, LANES)]
        turned = pltpu.roll(tile, HALF, 1)
        return jnp.where((block & 1) == upper, tile, turned)

    return jnp.where(lane < HALF, placed(first, 0), placed(second, 1))


def gather_blocks(targets, send_ref, field_ref, out_refs, inv_ref=None):
    slots = send_ref.shape[0]
    for d, out_ref in zip(targets, out_refs):
        for j in range(0, slots, 2):
            first, second = send_ref[j, d], send_ref[j + 1, d]
            if inv_ref is not None:
                first, second = inv_ref[first], inv_ref[second]
            out_ref[:, j * HALF : j * HALF + LANES] = pair_tile(field_ref, first, second)


def halo_offsets(domains):
    return sorted(range(1, domains), key=lambda k: (-(k >= domains // 2), k if k >= domains // 2 else -k))


def few(domains):
    return domains <= 8 and domains & (domains - 1) == 0


def gather_all(domains, send_ref, field_ref, out_refs, inv_ref=None):
    if few(domains):
        me = lax.axis_index("dom")
        gather_blocks([me ^ k for k in halo_offsets(domains)], send_ref, field_ref, out_refs, inv_ref)
    else:
        gather_blocks(range(domains), send_ref, field_ref, [out_refs[0].at[d] for d in range(domains)], inv_ref)


COPIES = 4


WORD = 32


def order_rows(domains, send_ref, perm_ref, inv_ref):
    rows = perm_ref.shape[0]
    masks = [jnp.int32(0)] * (rows // WORD)
    if few(domains):
        me = lax.axis_index("dom")
        for d in range(domains):
            for j in range(send_ref.shape[0]):
                block = send_ref[j, d]
                bit = jnp.where(d == me, 0, jnp.left_shift(jnp.int32(1), block & (WORD - 1)))
                masks = [m | jnp.where(block // WORD == n, bit, 0) for n, m in enumerate(masks)]
    flags = [lax.shift_right_logical(masks[row // WORD], jnp.int32(row % WORD)) & 1 for row in range(rows)]
    first = jnp.int32(0)
    later = sum(flags)
    for row, flag in enumerate(flags):
        position = jnp.where(flag == 1, first, later)
        inv_ref[row] = position
        perm_ref[position] = row
        first = first + flag
        later = later + 1 - flag


def gather_kernel(domains, send_hbm, field_hbm, field_ref, perm_ref, inv_ref, *refs):
    *out_refs, field_sem, send_ref, send_sem = refs
    table = pltpu.make_async_copy(send_hbm, send_ref, send_sem)
    table.start()
    width = field_ref.shape[1] // COPIES
    copies = []
    for n in range(COPIES):
        inside = pl.ds(n * width, width)
        copies.append(pltpu.make_async_copy(field_hbm.at[:, inside], field_ref.at[:, inside], field_sem.at[n]))
        copies[-1].start()
    table.wait()
    order_rows(domains, send_ref, perm_ref, inv_ref)
    for copy in copies:
        copy.wait()
    gather_all(domains, send_ref, field_ref, out_refs)


def gather(send, field, rows, domains, outputs):
    table = jax.ShapeDtypeStruct((rows,), jnp.int32)
    return pl.pallas_call(
        functools.partial(gather_kernel, domains),
        in_specs=[pl.BlockSpec(memory_space=pl.ANY)] * 2,
        out_specs=[whole(), scalars(), scalars()] + [whole()] * len(outputs),
        out_shape=[
            pltpu.VMEM(field.shape, field.dtype),
            table,
            table,
            *[pltpu.VMEM(shape, dtype) for shape, dtype in outputs],
        ],
        scratch_shapes=[
            pltpu.SemaphoreType.DMA((COPIES,)),
            pltpu.SMEM(send.shape, send.dtype),
            pltpu.SemaphoreType.DMA,
        ],
        compiler_params=pltpu.CompilerParams(vmem_limit_bytes=LIMIT),
        name="gather",
    )(far_memory(send), far_memory(field))


def store_tile(ext, index, x):
    high, low = split(x)
    ext[0, index] = jnp.concatenate([high, low], axis=0)
    high, low = split(pltpu.roll(x, HALF, 1))
    ext[1, index] = jnp.concatenate([high, low], axis=0)


def arrange_kernel(first_row, perm_ref, field_ref, g_ref, c_ref, g_out, c_out):
    samples = field_ref.shape[0]
    lane = lax.broadcasted_iota(jnp.int32, (samples, LANES), 1)

    def placed(block, upper):
        here = pl.ds(pl.multiple_of((block // 2) * LANES, LANES), LANES)
        own = field_ref[:, here]
        keep = (block & 1) == upper
        return [jnp.where(keep, x, pltpu.roll(x, HALF, 1)) for x in (g_ref[:, here] * own, c_ref[:, here] * own)]

    for i in range(g_out.shape[1] // LANES):
        inside = slice(i * LANES, (i + 1) * LANES)
        low = placed(perm_ref[first_row + 2 * i], 0)
        high = placed(perm_ref[first_row + 2 * i + 1], 1)
        g_out[:, inside] = jnp.where(lane < HALF, low[0], high[0])
        c_out[:, inside] = jnp.where(lane < HALF, low[1], high[1])


def restore_kernel(inv_ref, u_ref, out_ref, ext):
    for i in range(u_ref.shape[1] // LANES):
        tile = pair_tile(u_ref, inv_ref[2 * i], inv_ref[2 * i + 1])
        out_ref[:, i * LANES : (i + 1) * LANES] = tile
        store_tile(ext, i, tile)


def extend_kernel(field_ref, ext):
    for i in range(field_ref.shape[1] // LANES):
        store_tile(ext, i, field_ref[:, i * LANES : (i + 1) * LANES])


def extend_arrived(domains, own_tiles, inc_refs, ext):
    if few(domains):
        me = lax.axis_index("dom")
        arrived = [(me ^ k, ref) for k, ref in zip(halo_offsets(domains), inc_refs)]
    else:
        arrived = [(d, inc_refs[0].at[d]) for d in range(domains)]
    for source, ref in arrived:
        per_domain = ref.shape[1] // LANES
        for j in range(per_domain):
            store_tile(ext, own_tiles + source * per_domain + j, ref[:, j * LANES : (j + 1) * LANES])


def with_arrived(domains, product, own_tiles, cols_near, order_near, *refs):
    *inputs, out_ext, p_ref, q_ref, cols_ref, cols_sem, order_ref, order_sem = refs
    tables = [
        pltpu.make_async_copy(cols_near, cols_ref, cols_sem),
        pltpu.make_async_copy(order_near, order_ref, order_sem),
    ]
    for table in tables:
        table.start()
    offsets = domains - 1 if few(domains) else 1
    own_ext, *inputs = inputs
    extend_arrived(domains, own_tiles, inputs[len(inputs) - offsets :], out_ext)
    for table in tables:
        table.wait()
    product(cols_ref, order_ref, out_ext, *inputs[: len(inputs) - offsets], p_ref, q_ref)


def product_rows(first_row, permuted, cols_ref, order_ref, ext, w_ref, p_ref, q_ref, own_terms):
    samples = p_ref.shape[0]
    per_entry = cols_ref.shape[0]
    lane = lax.broadcasted_iota(jnp.int32, (2 * samples, LANES), 1)
    low_lane = lax.broadcasted_iota(jnp.int32, (samples, LANES), 1) < HALF

    def row_product(row):
        other = order_ref[row]
        source, place = (other, row) if permuted else (row, other)
        parts = []
        for k in range(0, per_entry, 2):
            first = cols_ref[k, source]
            second = cols_ref[k + 1, source]
            a = ext[first & 1, first // 2]
            b = ext[1 - (second & 1), second // 2]
            parts.append(jnp.where(lane < HALF, a, b))
        left = jnp.concatenate(parts, axis=1)
        full = jnp.dot(left, w_ref[place], preferred_element_type=jnp.float32)
        width = full.shape[1] // 2
        rows = full[:, :width] + full[:, width:]
        return rows[:samples] + rows[samples:]

    def block(step, carry):
        for pair in range(GROUP // 2):
            row = step * GROUP + 2 * pair
            first = row_product(first_row + row)
            second = row_product(first_row + row + 1)
            direct = jnp.where(low_lane, first, pltpu.roll(second, HALF, 1))
            charge = jnp.where(low_lane, pltpu.roll(first, HALF, 1), second)
            here = pl.ds(pl.multiple_of(row * HALF, LANES), LANES)
            g_term, c_term = own_terms(row)
            p_ref[:, here] = direct + g_term
            q_ref[:, here] = charge + c_term
        return carry

    lax.fori_loop(0, p_ref.shape[1] // (GROUP * HALF), block, 0)


def permuted_product(first_row, base_row, cols_ref, order_ref, ext, w_ref, g_ref, c_ref, p_ref, q_ref):
    def own_terms(row):
        there = pl.ds(pl.multiple_of((first_row - base_row + row) * HALF, LANES), LANES)
        return g_ref[:, there], c_ref[:, there]

    product_rows(first_row, True, cols_ref, order_ref, ext, w_ref, p_ref, q_ref, own_terms)


def plain_product(first_row, cols_ref, order_ref, ext, w_ref, field_ref, g_ref, c_ref, p_ref, q_ref):
    def own_terms(row):
        there = pl.ds(pl.multiple_of((first_row + row) * HALF, LANES), LANES)
        own = field_ref[:, there]
        return g_ref[:, there] * own, c_ref[:, there] * own

    product_rows(first_row, False, cols_ref, order_ref, ext, w_ref, p_ref, q_ref, own_terms)


def slope_columns(matrix, charges):
    samples = charges[0].shape[0]
    parts = [split(x) for x in charges]
    high = jnp.concatenate([h for h, _ in parts], axis=0)
    low = jnp.concatenate([l for _, l in parts], axis=0)
    first = jnp.dot(matrix, high, preferred_element_type=jnp.float32)
    second = jnp.dot(matrix[:samples], low, preferred_element_type=jnp.float32)
    return first[:samples] + first[samples:] + second


CHUNK = 256


def near_kernel(chunks, *refs):
    matrix = refs[0][...]
    p_refs, q_refs, mate_refs, out_refs = [refs[1 + n * chunks : 1 + (n + 1) * chunks] for n in range(4)]
    for p_ref, q_ref, mate_ref, out_ref in zip(p_refs, q_refs, mate_refs, out_refs):
        for start in range(0, p_ref.shape[1], CHUNK):
            inside = slice(start, start + CHUNK)
            out_ref[:, inside] = p_ref[:, inside] + slope_columns(matrix, [q_ref[:, inside], mate_ref[:, inside]])


def far_columns(matrix, p_ref, charge_refs):
    for start in range(0, p_ref.shape[1], CHUNK):
        inside = slice(start, start + CHUNK)
        yield start, p_ref[:, inside] + slope_columns(matrix, [c[:, inside] for c in charge_refs])


def far_kernel(count, base, chunks, *refs):
    matrix = refs[0][...]
    out_ref = refs[-1]
    size = 1 + count
    for n in range(chunks):
        p_ref, *charge_refs = refs[1 + n * size : 1 + (n + 1) * size]
        for start, value in far_columns(matrix, p_ref, charge_refs):
            out_ref[:, base + start : base + start + CHUNK] = value
        base += p_ref.shape[1]


def far_send_kernel(count, chunks, domains, send_near, inv_near, *refs):
    size = 1 + count
    u_ref, *out_refs, send_ref, send_sem, inv_ref, inv_sem = refs[1 + chunks * size :]
    tables = [
        pltpu.make_async_copy(send_near, send_ref, send_sem),
        pltpu.make_async_copy(inv_near, inv_ref, inv_sem),
    ]
    for table in tables:
        table.start()
    far_kernel(count, 0, chunks, *refs[: 1 + chunks * size], u_ref)
    for table in tables:
        table.wait()
    gather_all(domains, send_ref, u_ref, out_refs, inv_ref)


def dot_totals(totals, r_ref, u_ref, base, v):
    for i in range(0, v.shape[1], LANES):
        vv = v[:, i : i + LANES]
        rr = r_ref[:, base + i : base + i + LANES]
        uu = u_ref[:, base + i : base + i + LANES]
        for n, (a, b) in enumerate(((uu, uu), (uu, vv), (vv, vv), (rr, uu), (rr, vv))):
            totals[n] = totals[n] + a * b


def far_dots_kernel(count, base, chunks, *refs):
    matrix = refs[0][...]
    out_ref = refs[-1]
    size = 1 + count
    r_ref, u_ref, *before = refs[1 + chunks * size : -1]
    samples = r_ref.shape[0]
    totals = [before[0][n] if before else jnp.zeros((samples, LANES), jnp.float32) for n in range(5)]
    for n in range(chunks):
        p_ref, *charge_refs = refs[1 + n * size : 1 + (n + 1) * size]
        for start, value in far_columns(matrix, p_ref, charge_refs):
            dot_totals(totals, r_ref, u_ref, base + start, value)
        base += p_ref.shape[1]
    if base < u_ref.shape[1]:
        for n in range(5):
            out_ref[n] = totals[n]
        return
    lane = lax.broadcasted_iota(jnp.int32, (1, LANES), 1)
    packed = jnp.zeros((1, LANES), jnp.float32)
    for n, total in enumerate(totals):
        packed = jnp.where(lane == n, jnp.sum(total), packed)
    for d in range(out_ref.shape[0]):
        out_ref[d] = packed


def update_kernel(sums_ref, r_ref, u_ref, out_hbm, out_ref, sems):
    total = jnp.sum(sums_ref[...], axis=0)
    lane = lax.broadcasted_iota(jnp.int32, total.shape, 1)
    uu, uv, vv, ru, rv = [jnp.sum(jnp.where(lane == n, total, 0.0), axis=1, keepdims=True) for n in range(5)]
    length_u = jnp.sqrt(uu)
    length_v = jnp.sqrt(vv)
    cross = uv / length_u / length_v
    target_u = ru / length_u
    target_v = rv / length_v
    determinant = 1.0 - cross * cross
    weight_r = (target_u - cross * target_v) / determinant / length_u
    weight_u = (target_v - cross * target_u) / determinant / length_v
    part = r_ref.shape[0] // COPIES
    copies = []
    for n in range(COPIES):
        rows = slice(n * part, (n + 1) * part)
        for start in range(0, r_ref.shape[1], LANES):
            inside = slice(start, start + LANES)
            out_ref[rows, inside] = weight_r * r_ref[rows, inside] + weight_u * u_ref[rows, inside]
        copies.append(pltpu.make_async_copy(out_ref.at[rows], out_hbm.at[rows], sems.at[n]))
        copies[-1].start()
    for copy in copies:
        copy.wait()


def update(sums, r, u):
    return pl.pallas_call(
        update_kernel,
        in_specs=[whole()] * 3,
        out_specs=pl.BlockSpec(memory_space=pl.ANY),
        out_shape=jax.ShapeDtypeStruct(r.shape, r.dtype),
        scratch_shapes=[pltpu.VMEM(r.shape, r.dtype), pltpu.SemaphoreType.DMA((COPIES,))],
        compiler_params=pltpu.CompilerParams(vmem_limit_bytes=LIMIT),
        name="update",
    )(near_memory(sums), near_memory(r), near_memory(u))


def chunk_sizes(rows, domains, slots):
    unit = rows // 8
    early = (domains - 1) * slots if few(domains) else 3 * unit
    return [unit, early - unit, rows - early], [unit, 2 * unit, 4 * unit, unit]


def body(residual, conductance, capacitance, stamps, block_cols, send_blocks):
    samples, unknowns = residual.shape
    rows, per_entry = block_cols.shape
    width = stamps.shape[2]
    slots = send_blocks.shape[2]
    domains = lax.axis_size("dom")
    groups = lax.axis_size("samp")
    pairs = [(i, i ^ 1) for i in range(groups)]
    shifts = range(2, groups, 2)
    count = 2 * len(shifts)
    sizes_one, sizes_two = chunk_sizes(rows, domains, slots)
    early = sizes_one[0] + sizes_one[1]
    f32 = jnp.float32
    if few(domains):
        outgoing_shapes = [((samples, slots * width), f32)] * (domains - 1)
    else:
        outgoing_shapes = [((domains, samples, slots * width), f32)]
    field_shape = ((samples, unknowns), f32)
    own_tiles = unknowns // LANES
    tiles = own_tiles + domains * slots * width // LANES
    ext_shape = ((2, tiles, 2 * samples, LANES), jnp.bfloat16)
    weight_shape = ((rows, per_entry * width, 4 * width), jnp.bfloat16)
    cols = block_cols.T
    send = send_blocks[0].T

    def exchange(outgoing):
        if not few(domains):
            return [lax.all_to_all(outgoing[0], "dom", split_axis=0, concat_axis=0, tiled=True)]
        incoming = []
        for k, x in zip(halo_offsets(domains), outgoing):
            incoming.append(lax.ppermute(x, "dom", [(i, i ^ k) for i in range(domains)]))
        return incoming

    def product_call(n, size, product, operands, incoming):
        shape = ((samples, size * width), f32)
        if n:
            p, q = kernel_call(product, operands, [shape, shape])
            return operands[2], p, q
        return kernel_call(
            functools.partial(with_arrived, domains, product, own_tiles),
            (*operands, *incoming),
            [ext_shape, shape, shape],
            aliases={2: 0},
            table_copied=True,
        )

    def spread(q):
        far = [lax.ppermute(q, "samp", [(i, (i + k) % groups) for i in range(groups)]) for k in shifts]
        return far, lax.ppermute(q, "samp", pairs)

    def near_call(chunks):
        return kernel_call(
            functools.partial(near_kernel, len(chunks)),
            (near_matrix, *[p for p, _, _, _ in chunks], *[q for _, q, _, _ in chunks], *[m for _, _, _, m in chunks]),
            [(p.shape, f32) for p, _, _, _ in chunks],
        )

    def forward(half, far):
        charges = []
        for x in far:
            charges += [x, lax.ppermute(x, "samp", pairs)]
        return [half, *charges]

    field, perm, inv, *outgoing = gather(send, residual, rows, domains, outgoing_shapes)
    incoming = exchange(outgoing)
    near_matrix, far_matrix = kernel_call(
        functools.partial(tables_kernel, groups),
        (),
        [((2 * samples, 2 * samples), jnp.bfloat16), ((2 * samples, count * samples), jnp.bfloat16)],
    )
    blocks = stamps.reshape(rows, per_entry * width, 2 * width)
    (ext,) = kernel_call(extend_kernel, (field,), [ext_shape])
    weights = None
    own = []
    for n, (low, high) in enumerate(((0, early), (early, rows))):
        if n == 0:
            weights = fetch(perm, blocks, early)
        else:
            (weights,) = kernel_call(
                functools.partial(prepare_kernel, low, high), (perm, blocks, weights), [weight_shape], aliases={2: 0}
            )
        terms = kernel_call(
            functools.partial(arrange_kernel, low),
            (perm, field, conductance, capacitance),
            [((samples, (high - low) * width), f32)] * 2,
        )
        own.append((low, weights, terms))
    chunks = []
    first = 0
    for n, size in enumerate(sizes_one):
        base, w, terms = own[first >= early]
        ext, p, q = product_call(
            n, size, functools.partial(permuted_product, first, base), (cols, perm, ext, w, *terms), incoming
        )
        chunks.append((p, q, *spread(q)))
        first += size
    half = near_call(chunks[:2]) + near_call(chunks[2:])
    pieces = [forward(half[n], chunk[2]) for n, chunk in enumerate(chunks)]
    ready = 2 if few(domains) else len(chunks)
    u, *outgoing = kernel_call(
        functools.partial(far_send_kernel, count, ready, domains),
        (send, inv, far_matrix, *[x for piece in pieces[:ready] for x in piece]),
        [field_shape, *outgoing_shapes],
        table_copied=True,
    )
    incoming = exchange(outgoing)
    if ready < len(chunks):
        operands = [far_matrix, *[x for piece in pieces[ready:] for x in piece]]
        (u,) = kernel_call(
            functools.partial(far_kernel, count, early * width, len(chunks) - ready),
            operands + [u],
            [field_shape],
            aliases={len(operands): 0},
        )
    u, ext = kernel_call(restore_kernel, (inv, u), [field_shape, ext_shape])
    chunks = []
    first = 0
    for n, size in enumerate(sizes_two):
        operands = (cols, inv, ext, weights, u, conductance, capacitance)
        ext, p, q = product_call(n, size, functools.partial(plain_product, first), operands, incoming)
        chunks.append((p, q, *spread(q)))
        first += size
    half = near_call(chunks)
    pieces = [forward(half[n], chunk[2]) for n, chunk in enumerate(chunks)]
    sums = None
    last = len(chunks) - 1
    for n, (low, high) in enumerate(((0, last - 1), (last - 1, last), (last, last + 1))):
        final = high > last
        (sums,) = kernel_call(
            functools.partial(far_dots_kernel, count, sum(sizes_two[:low]) * width, high - low),
            [far_matrix, *[x for piece in pieces[low:high] for x in piece], field, u] + [sums] * (n > 0),
            [((domains * groups, 1, LANES) if final else (5, samples, LANES), f32)],
        )
    sums = lax.all_to_all(sums, ("dom", "samp"), split_axis=0, concat_axis=0, tiled=True)
    return update(sums, field, u)


def solution(mesh):
    in_specs = (
        P("samp", "dom"),
        P("samp", "dom"),
        P("samp", "dom"),
        P("dom", None, None, None),
        P("dom", None),
        P("dom", None, None),
    )
    out_specs = P("samp", "dom")
    return jax.shard_map(body, mesh=mesh, in_specs=in_specs, out_specs=out_specs, check_vma=False)
```

time: 131 us -> 126 us (0.962)
  Pallas kernels: 36.4 us -> 33.9 us
  starting transfers between devices: 37.3 us -> 35.1 us
    pallas_call x22 -> x21, Pallas kernels: 32.2 us -> 27.4 us  [kernel_call(): pl.pallas_call(kernel, in_specs=specs, out_specs=[scalars() if number els...]
    ppermute x14, waiting for transfers between devices: 7.84 us -> 5.12 us  [exchange(): lax.ppermute(x, 'dom', [(i, i ^ k) for i in range(domains)])]
    pallas_call x1 -> x2, Pallas kernels: 1.95 us -> 4.31 us  [the longest x1 3.14 us: fetch(): pl.pallas_call(fetch_kernel, in_specs=[scalars(), pl.BlockSpec(memory_spa...]
    ppermute x24 -> x21, starting transfers between devices: 13.1 us -> 10.9 us  [the longest x7 8.72 us: spread(): lax.ppermute(q, 'samp', [(i, (i + k) % groups) for i in range(groups)])]
    ppermute x24 -> x21, waiting for transfers between devices: 38.4 us -> 39.8 us  [the longest x7 39 us: spread(): lax.ppermute(q, 'samp', [(i, (i + k) % groups) for i in range(groups)])]
  transfers between devices with their start and end apart: 38 -> 35, of which waited for: 14 -> 11; matrix products, arithmetic and copies ran while one was open for 0% -> 0% of each run, Pallas kernels for 18% -> 13%
where the time goes in v1:
time: 126 us
  waiting for transfers between devices  44.9 us (36%)
  starting transfers between devices  35.1 us (28%)
  Pallas kernels  33.9 us (27%)
  blocking collectives  11.3 us (9%)
    ppermute x7, waiting for transfers between devices, spread(): lax.ppermute(q, 'samp', [(i, (i + k) % groups) for i in range(groups)])  39 us
    pallas_call x21, Pallas kernels, kernel_call(): pl.pallas_call(kernel, in_specs=specs, out_specs=[scalars() if number els...  27.4 us
    ppermute x14, starting transfers between devices, exchange(): lax.ppermute(x, 'dom', [(i, i ^ k) for i in range(domains)])  24.2 us
    all_to_all x1, blocking collectives, body(): lax.all_to_all(sums, ('dom', 'samp'), split_axis=0, concat_axis=0, tiled=...  11.3 us
    ppermute x7, starting transfers between devices, spread(): lax.ppermute(q, 'samp', [(i, (i + k) % groups) for i in range(groups)])  8.72 us
    ppermute x14, waiting for transfers between devices, exchange(): lax.ppermute(x, 'dom', [(i, i ^ k) for i in range(domains)])  5.12 us
    pallas_call x1, Pallas kernels, fetch(): pl.pallas_call(fetch_kernel, in_specs=[scalars(), pl.BlockSpec(memory_spa...  3.14 us
  transfers between devices with their start and end apart: 35, of which 11 were waited for; matrix products, arithmetic and copies ran while one was open for 0% of the time, Pallas kernels for 13%

profile of v1, /device:TPU:0, one launch (start us, length us, event | category | flops | bytes accessed | tf_op | source)
XLA Modules:
  0.0 125.8 jit_solution(2860068735613988630)
XLA Ops:
  0.0 2.2 %gather.1 = (f32[64,4096]{1,0:T(8,128)S(1)}, s32[64]{0:T(128)S(1)}, s32[64]{0:T(128)S(1)}, f32[64,256]{1,0:T(8,128)S(1)}, f32[64,256]{1,0:T(8,128)S(1)}, /*index...) custom-call(s32[4,8]{1,0:T(4,128)} %bitcast.16, ...), custom_call_target="tpu_custom_call" | custom-call | tf_op jit(solution)/shard_map/gather/pallas_call | solution.py:224
  2.2 4.1 %collective-permute-start = (f32[64,256]{1,0:T(8,128)S(1)}, f32[64,256]{1,0:T(8,128)S(1)}, u32[]{:S(2)}, u32[]{:S(2)}) collective-permute-start(f32[64,256]{1,0:T(8,128)S(1)} %get-tuple-element.60), channel_id=1, source_target_pairs={{0,16},{4,20},{8,24},{12,28},{16,0},{20,4},{24,8},{28,12},{1,17},{... | collective-permute-start | bytes 196616 | tf_op jit(solution)/shard_map/ppermute | solution.py:524
  6.4 1.3 %collective-permute-start.1 = (f32[64,256]{1,0:T(8,128)S(1)}, f32[64,256]{1,0:T(8,128)S(1)}, u32[]{:S(2)}, u32[]{:S(2)}) collective-permute-start(f32[64,256]{1,0:T(8,128)S(1)} %get-tuple-element.61), channel_id=1, source_target_pairs={{0,20},{4,16},{8,28},{12,24},{16,4},{20,0},{24,12},{28,8},{1,21},{... | collective-permute-start | bytes 196616 | tf_op jit(solution)/shard_map/ppermute | solution.py:524
  7.7 3.6 %collective-permute-start.2 = (f32[64,256]{1,0:T(8,128)S(1)}, f32[64,256]{1,0:T(8,128)S(1)}, u32[]{:S(2)}, u32[]{:S(2)}) collective-permute-start(f32[64,256]{1,0:T(8,128)S(1)} %get-tuple-element.62), channel_id=1, source_target_pairs={{0,24},{4,28},{8,16},{12,20},{16,8},{20,12},{24,0},{28,4},{1,25},{... | collective-permute-start | bytes 196616 | tf_op jit(solution)/shard_map/ppermute | solution.py:524
  11.3 0.9 collective-permute-start.4
  12.2 2.2 %collective-permute-start.5 = (f32[64,256]{1,0:T(8,128)S(1)}, f32[64,256]{1,0:T(8,128)S(1)}, u32[]{:S(2)}, u32[]{:S(2)}) collective-permute-start(f32[64,256]{1,0:T(8,128)S(1)} %get-tuple-element.65), channel_id=1, source_target_pairs={{0,8},{4,12},{8,0},{12,4},{16,24},{20,28},{24,16},{28,20},{1,9},{5... | collective-permute-start | bytes 196616 | tf_op jit(solution)/shard_map/ppermute | solution.py:524
  14.4 2.0 %collective-permute-done.1.refs_5_ = f32[64,256]{1,0:T(8,128)S(1)} collective-permute-done((f32[64,256]{1,0:T(8,128)S(1)}, f32[64,256]{1,0:T(8,128)S(1)}, u32[]{:S(2)}, u32[]{:S(2)}) %collective-permute-start.1) | collective-permute-done | bytes 65568 | tf_op jit(solution)/shard_map/ppermute | solution.py:524
  16.4 1.5 %collective-permute-start.6 = (f32[64,256]{1,0:T(8,128)S(1)}, f32[64,256]{1,0:T(8,128)S(1)}, u32[]{:S(2)}, u32[]{:S(2)}) collective-permute-start(f32[64,256]{1,0:T(8,128)S(1)} %get-tuple-element.66), channel_id=1, source_target_pairs={{0,4},{4,0},{8,12},{12,8},{16,20},{20,16},{24,28},{28,24},{1,5},{5... | collective-permute-start | bytes 196616 | tf_op jit(solution)/shard_map/ppermute | solution.py:524
  17.9 0.3 shard_map.65.refs_0_
  18.2 1.1 shard_map.66
  19.3 1.2 shard_map.69
  20.6 0.0 copy-start.2
  20.6 0.0 slice-start
  20.6 3.1 %prepare_0.1.refs_1_.refs_0_.w_ref = bf16[64,256,256]{2,1,0:T(8,128)(2,1)S(1)} custom-call(s32[64]{0:T(128)S(1)} %get-tuple-element.56.perm_ref.order_near.order_ref, f32[64,256,128]{2,1,0:T(8,128)} %bitcast.5), custom_call_target="tpu_custom_call" | custom-call | tf_op jit(solution)/shard_map/prepare_0/pallas_call | solution.py:128
  23.8 0.0 slice-start.1
  23.8 1.6 %shard_map.67 = (bf16[2,48,128,128]{3,2,1,0:T(8,128)(2,1)S(1)}, f32[64,512]{1,0:T(8,128)S(1)}, f32[64,512]{1,0:T(8,128)S(1)}) custom-call(s32[4,64]{1,0:T(4,128)S(1)} %bitcast.9, s32[64]{0:T(128)S(1)} %get-tuple-element.56.perm_ref.order_near.order_ref, bf16[2,48,128,128]{3,2,1,0:T(8,128)(2,1)S(1)} %shard_map.65.refs_0_, ...), custom_call_target="tpu_custom_call", output_to_operand_aliasing={{0}: (2, {})} | custom-call | tf_op jit(solution)/shard_map/pallas_call | solution.py:55
  25.4 2.4 %shard_map.72 = (f32[64,1280]{1,0:T(8,128)S(1)}, f32[64,1280]{1,0:T(8,128)S(1)}) custom-call(s32[4,64]{1,0:T(4,128)S(1)} %bitcast.10, s32[64]{0:T(128)S(1)} %get-tuple-element.56.perm_ref.order_near.order_ref, bf16[2,48,128,128]{3,2,1,0:T(8,128)(2,1)S(1)} %get-tuple-element.67.ext, bf16[64,256,256]{2,1,0:T(8,128)(2,1)S(1)} %prepare_0.1.refs_1_.refs_0_.w_ref, ...), custom_call_target="tpu_custom_call" | custom-call | tf_op jit(solution)/shard_map/pallas_call | solution.py:55
  27.8 1.4 %shard_map.68.w_ref.refs_1_ = bf16[64,256,256]{2,1,0:T(8,128)(2,1)S(1)} custom-call(s32[64]{0:T(128)S(1)} %get-tuple-element.56.perm_ref.order_near.order_ref, f32[64,256,128]{2,1,0:T(8,128)S(1)} %bitcast.8, bf16[64,256,256]{2,1,0:T(8,128)(2,1)S(1)} %prepare_0.1.refs_1_.refs_0_.w_ref), custom_call_target="tpu_custom_call", output_to_operand_aliasing={{}: (2, {})} | custom-call | tf_op jit(solution)/shard_map/pallas_call | solution.py:55
  29.2 0.0 copy-start.3
  29.2 3.8 %shard_map.70 = (f32[64,2304]{1,0:T(8,128)S(1)}, f32[64,2304]{1,0:T(8,128)S(1)}) custom-call(s32[4,64]{1,0:T(4,128)S(1)} %bitcast.11, s32[64]{0:T(128)S(1)} %get-tuple-element.56.perm_ref.order_near.order_ref, bf16[2,48,128,128]{3,2,1,0:T(8,128)(2,1)S(1)} %get-tuple-element.67.ext, bf16[64,256,256]{2,1,0:T(8,128)(2,1)S(1)} %shard_map.68.w_ref.refs_1_, ...), custom_call_target="tpu_custom_call" | custom-call | tf_op jit(solution)/shard_map/pallas_call | solution.py:55
  33.0 1.6 %collective-permute-start.8 = (f32[64,2304]{1,0:T(8,128)S(1)}, f32[64,2304]{1,0:T(8,128)S(1)}, u32[]{:S(2)}, u32[]{:S(2)}) collective-permute-start(f32[64,2304]{1,0:T(8,128)S(1)} %get-tuple-element.71.refs_2_), channel_id=1, source_target_pairs={{0,2},{1,3},{2,0},{3,1},{4,6},{5,7},{6,4},{7,5},{8,10},{9,11},{10,... | collective-permute-start | bytes 1769480 | tf_op jit(solution)/shard_map/ppermute | solution.py:541
  34.6 0.5 collective-permute-start.14
  35.1 14.1 %collective-permute-done.8.refs_2_ = f32[64,2304]{1,0:T(8,128)S(1)} collective-permute-done((f32[64,2304]{1,0:T(8,128)S(1)}, f32[64,2304]{1,0:T(8,128)S(1)}, u32[]{:S(2)}, u32[]{:S(2)}) %collective-permute-start.8) | collective-permute-done | bytes 589856 | tf_op jit(solution)/shard_map/ppermute | solution.py:541
  49.2 0.5 collective-permute-start.10
  49.7 0.0 collective-permute-start.11
  49.7 3.0 %collective-permute-done.14.refs_5_ = f32[64,1280]{1,0:T(8,128)S(1)} collective-permute-done((f32[64,1280]{1,0:T(8,128)S(1)}, f32[64,1280]{1,0:T(8,128)S(1)}, u32[]{:S(2)}, u32[]{:S(2)}) %collective-permute-start.14) | collective-permute-done | bytes 327712 | tf_op jit(solution)/shard_map/ppermute | solution.py:541
  52.7 1.5 %collective-permute-start.12 = (f32[64,512]{1,0:T(8,128)S(1)}, f32[64,512]{1,0:T(8,128)S(1)}, u32[]{:S(2)}, u32[]{:S(2)}) collective-permute-start(f32[64,512]{1,0:T(8,128)S(1)} %get-tuple-element.74.refs_3_), channel_id=1, source_target_pairs={{0,2},{1,3},{2,0},{3,1},{4,6},{5,7},{6,4},{7,5},{8,10},{9,11},{10,... | collective-permute-start | bytes 393224 | tf_op jit(solution)/shard_map/ppermute | solution.py:541
  54.2 4.4 %collective-permute-done.12.refs_2_ = f32[64,512]{1,0:T(8,128)S(1)} collective-permute-done((f32[64,512]{1,0:T(8,128)S(1)}, f32[64,512]{1,0:T(8,128)S(1)}, u32[]{:S(2)}, u32[]{:S(2)}) %collective-permute-start.12) | collective-permute-done | bytes 131104 | tf_op jit(solution)/shard_map/ppermute | solution.py:541
  58.6 0.5 shard_map.64
  59.2 0.4 shard_map.73
  59.6 0.4 collective-permute-done.13.refs_3_
  60.0 1.1 shard_map.74
  61.1 3.1 %collective-permute-start.16 = (f32[64,256]{1,0:T(8,128)S(1)}, f32[64,256]{1,0:T(8,128)S(1)}, u32[]{:S(2)}, u32[]{:S(2)}) collective-permute-start(f32[64,256]{1,0:T(8,128)S(1)} %get-tuple-element.81), channel_id=1, source_target_pairs={{0,16},{4,20},{8,24},{12,28},{16,0},{20,4},{24,8},{28,12},{1,17},{... | collective-permute-start | bytes 196616 | tf_op jit(solution)/shard_map/ppermute | solution.py:524
  64.2 1.1 collective-permute-start.17
  65.3 4.8 %collective-permute-start.18 = (f32[64,256]{1,0:T(8,128)S(1)}, f32[64,256]{1,0:T(8,128)S(1)}, u32[]{:S(2)}, u32[]{:S(2)}) collective-permute-start(f32[64,256]{1,0:T(8,128)S(1)} %get-tuple-element.83), channel_id=1, source_target_pairs={{0,24},{4,28},{8,16},{12,20},{16,8},{20,12},{24,0},{28,4},{1,25},{... | collective-permute-start | bytes 196616 | tf_op jit(solution)/shard_map/ppermute | solution.py:524
  70.1 0.6 collective-permute-start.20
  70.7 3.1 %collective-permute-done.17.refs_6_ = f32[64,256]{1,0:T(8,128)S(1)} collective-permute-done((f32[64,256]{1,0:T(8,128)S(1)}, f32[64,256]{1,0:T(8,128)S(1)}, u32[]{:S(2)}, u32[]{:S(2)}) %collective-permute-start.17) | collective-permute-done | bytes 65568 | tf_op jit(solution)/shard_map/ppermute | solution.py:524
  73.9 0.9 collective-permute-start.22
  74.7 0.4 shard_map.71.refs_1_
  75.2 0.4 shard_map.75.u_ref
  75.6 3.1 %shard_map.76 = (f32[64,4096]{1,0:T(8,128)S(1)}, bf16[2,48,128,128]{3,2,1,0:T(8,128)(2,1)S(1)}) custom-call(s32[64]{0:T(128)S(1)} %get-tuple-element.55.inv_near.inv_ref.order_near.order_ref, f32[64,4096]{1,0:T(8,128)S(1)} %shard_map.75.u_ref), custom_call_target="tpu_custom_call" | custom-call | tf_op jit(solution)/shard_map/pallas_call | solution.py:55
  78.7 1.4 %shard_map.77 = (bf16[2,48,128,128]{3,2,1,0:T(8,128)(2,1)S(1)}, f32[64,512]{1,0:T(8,128)S(1)}, f32[64,512]{1,0:T(8,128)S(1)}) custom-call(s32[4,64]{1,0:T(4,128)S(1)} %bitcast.12, s32[64]{0:T(128)S(1)} %get-tuple-element.55.inv_near.inv_ref.order_near.order_ref, ...), custom_call_target="tpu_custom_call", output_to_operand_aliasing={{0}: (2, {})} | custom-call | tf_op jit(solution)/shard_map/pallas_call | solution.py:55
  80.1 3.4 %shard_map.79 = (f32[64,2048]{1,0:T(8,128)S(1)}, f32[64,2048]{1,0:T(8,128)S(1)}) custom-call(s32[4,64]{1,0:T(4,128)S(1)} %bitcast.13, s32[64]{0:T(128)S(1)} %get-tuple-element.55.inv_near.inv_ref.order_near.order_ref, bf16[2,48,128,128]{3,2,1,0:T(8,128)(2,1)S(1)} %get-tuple-element.89.ext, bf16[64,256,256]{2,1,0:T(8,128)(2,1)S(1)} %shard_map.68.w_ref.refs_1_, ...), custom_call_target="tpu_custom_call" | custom-call | tf_op jit(solution)/shard_map/pallas_call | solution.py:55
  83.5 1.6 %collective-permute-start.29 = (f32[64,2048]{1,0:T(8,128)S(1)}, f32[64,2048]{1,0:T(8,128)S(1)}, u32[]{:S(2)}, u32[]{:S(2)}) collective-permute-start(f32[64,2048]{1,0:T(8,128)S(1)} %get-tuple-element.95.refs_7_), channel_id=1, source_target_pairs={{0,2},{1,3},{2,0},{3,1},{4,6},{5,7},{6,4},{7,5},{8,10},{9,11},{10,... | collective-permute-start | bytes 1572872 | tf_op jit(solution)/shard_map/ppermute | solution.py:541
  85.0 0.5 collective-permute-start.23
  85.5 2.0 %shard_map.78 = (f32[64,1024]{1,0:T(8,128)S(1)}, f32[64,1024]{1,0:T(8,128)S(1)}) custom-call(s32[4,64]{1,0:T(4,128)S(1)} %bitcast.14, s32[64]{0:T(128)S(1)} %get-tuple-element.55.inv_near.inv_ref.order_near.order_ref, bf16[2,48,128,128]{3,2,1,0:T(8,128)(2,1)S(1)} %get-tuple-element.89.ext, bf16[64,256,256]{2,1,0:T(8,128)(2,1)S(1)} %shard_map.68.w_ref.refs_1_, ...), custom_call_target="tpu_custom_call" | custom-call | tf_op jit(solution)/shard_map/pallas_call | solution.py:55
  87.5 0.6 collective-permute-start.33
  88.1 1.3 %shard_map.80 = (f32[64,512]{1,0:T(8,128)S(1)}, f32[64,512]{1,0:T(8,128)S(1)}) custom-call(s32[4,64]{1,0:T(4,128)S(1)} %bitcast.15, s32[64]{0:T(128)S(1)} %get-tuple-element.55.inv_near.inv_ref.order_near.order_ref, bf16[2,48,128,128]{3,2,1,0:T(8,128)(2,1)S(1)} %get-tuple-element.89.ext, bf16[64,256,256]{2,1,0:T(8,128)(2,1)S(1)} %shard_map.68.w_ref.refs_1_, ...), custom_call_target="tpu_custom_call" | custom-call | tf_op jit(solution)/shard_map/pallas_call | solution.py:55
  89.4 8.9 %collective-permute-done.29.refs_2_ = f32[64,2048]{1,0:T(8,128)S(1)} collective-permute-done((f32[64,2048]{1,0:T(8,128)S(1)}, f32[64,2048]{1,0:T(8,128)S(1)}, u32[]{:S(2)}, u32[]{:S(2)}) %collective-permute-start.29) | collective-permute-done | bytes 524320 | tf_op jit(solution)/shard_map/ppermute | solution.py:541
  98.3 0.5 collective-permute-start.26
  98.8 1.5 %collective-permute-start.27 = (f32[64,512]{1,0:T(8,128)S(1)}, f32[64,512]{1,0:T(8,128)S(1)}, u32[]{:S(2)}, u32[]{:S(2)}) collective-permute-start(f32[64,512]{1,0:T(8,128)S(1)} %get-tuple-element.96.refs_8_), channel_id=1, source_target_pairs={{0,2},{1,3},{2,0},{3,1},{4,6},{5,7},{6,4},{7,5},{8,10},{9,11},{10,... | collective-permute-start | bytes 393224 | tf_op jit(solution)/shard_map/ppermute | solution.py:541
  100.3 0.1 collective-permute-done.26.refs_12_
  100.4 0.1 collective-permute-start.24
  100.6 5.1 %collective-permute-done.27.refs_2_ = f32[64,512]{1,0:T(8,128)S(1)} collective-permute-done((f32[64,512]{1,0:T(8,128)S(1)}, f32[64,512]{1,0:T(8,128)S(1)}, u32[]{:S(2)}, u32[]{:S(2)}) %collective-permute-start.27) | collective-permute-done | bytes 131104 | tf_op jit(solution)/shard_map/ppermute | solution.py:541
  105.7 1.5 %collective-permute-start.31 = (f32[64,512]{1,0:T(8,128)S(1)}, f32[64,512]{1,0:T(8,128)S(1)}, u32[]{:S(2)}, u32[]{:S(2)}) collective-permute-start(f32[64,512]{1,0:T(8,128)S(1)} %get-tuple-element.93.refs_5_), channel_id=1, source_target_pairs={{0,2},{1,3},{2,0},{3,1},{4,6},{5,7},{6,4},{7,5},{8,10},{9,11},{10,... | collective-permute-start | bytes 393224 | tf_op jit(solution)/shard_map/ppermute | solution.py:541
  107.2 3.5 %collective-permute-done.31.refs_2_ = f32[64,512]{1,0:T(8,128)S(1)} collective-permute-done((f32[64,512]{1,0:T(8,128)S(1)}, f32[64,512]{1,0:T(8,128)S(1)}, u32[]{:S(2)}, u32[]{:S(2)}) %collective-permute-start.31) | collective-permute-done | bytes 131104 | tf_op jit(solution)/shard_map/ppermute | solution.py:541
  110.6 0.5 collective-permute-start.28
  111.2 0.6 shard_map.81
  111.8 0.2 collective-permute-done.32.refs_3_
  112.0 0.3 shard_map.82.refs_6_
  112.3 0.4 shard_map.83.refs_6_
  112.8 0.4 shard_map.84
  113.2 11.3 %all_to_all.5.sums_ref = f32[32,1,128]{2,1,0:T(1,128)S(1)} all-to-all(f32[32,1,128]{2,1,0:T(1,128)S(1)} %shard_map.84), channel_id=1, replica_groups=mesh['dom'=8,'samp'=4] {'dom','samp'}, dimensions={0} | all-to-all | bytes 32768 | tf_op jit(solution)/shard_map/all_to_all | solution.py:627
  124.5 1.2 update.1
  (44 shorter events, 0.1 us)
Async XLA Ops:
  0.0 18.2 %copy-start = (f32[64,4096]{1,0:T(8,128)S(1)}, f32[64,4096]{1,0:T(8,128)}, u32[]{:S(2)}) copy-start(f32[64,4096]{1,0:T(8,128)} %g_ref.9) | copy-start | bytes 3145732
  0.0 18.2 %copy-start.1 = (f32[64,4096]{1,0:T(8,128)S(1)}, f32[64,4096]{1,0:T(8,128)}, u32[]{:S(2)}) copy-start(f32[64,4096]{1,0:T(8,128)} %c_ref.9) | copy-start | bytes 3145732
  2.2 9.9 %collective-permute-start = (f32[64,256]{1,0:T(8,128)S(1)}, f32[64,256]{1,0:T(8,128)S(1)}, u32[]{:S(2)}, u32[]{:S(2)}) collective-permute-start(f32[64,256]{1,0:T(8,128)S(1)} %get-tuple-element.60), channel_id=1, source_target_pairs={{0,16},{4,20},{8,24},{12,28},{16,0},{20,4},{24,8},{28,12},{1,17},{... | collective-permute-start | bytes 196616 | tf_op jit(solution)/shard_map/ppermute | solution.py:524
  6.4 10.0 %collective-permute-start.1 = (f32[64,256]{1,0:T(8,128)S(1)}, f32[64,256]{1,0:T(8,128)S(1)}, u32[]{:S(2)}, u32[]{:S(2)}) collective-permute-start(f32[64,256]{1,0:T(8,128)S(1)} %get-tuple-element.61), channel_id=1, source_target_pairs={{0,20},{4,16},{8,28},{12,24},{16,4},{20,0},{24,12},{28,8},{1,21},{... | collective-permute-start | bytes 196616 | tf_op jit(solution)/shard_map/ppermute | solution.py:524
  7.7 16.1 %collective-permute-start.2 = (f32[64,256]{1,0:T(8,128)S(1)}, f32[64,256]{1,0:T(8,128)S(1)}, u32[]{:S(2)}, u32[]{:S(2)}) collective-permute-start(f32[64,256]{1,0:T(8,128)S(1)} %get-tuple-element.62), channel_id=1, source_target_pairs={{0,24},{4,28},{8,16},{12,20},{16,8},{20,12},{24,0},{28,4},{1,25},{... | collective-permute-start | bytes 196616 | tf_op jit(solution)/shard_map/ppermute | solution.py:524
  11.3 12.5 %collective-permute-start.3 = (f32[64,256]{1,0:T(8,128)S(1)}, f32[64,256]{1,0:T(8,128)S(1)}, u32[]{:S(2)}, u32[]{:S(2)}) collective-permute-start(f32[64,256]{1,0:T(8,128)S(1)} %get-tuple-element.63), channel_id=1, source_target_pairs={{0,28},{4,24},{8,20},{12,16},{16,12},{20,8},{24,4},{28,0},{1,29},{... | collective-permute-start | bytes 196616 | tf_op jit(solution)/shard_map/ppermute | solution.py:524
  11.3 12.5 %collective-permute-start.4 = (f32[64,256]{1,0:T(8,128)S(1)}, f32[64,256]{1,0:T(8,128)S(1)}, u32[]{:S(2)}, u32[]{:S(2)}) collective-permute-start(f32[64,256]{1,0:T(8,128)S(1)} %get-tuple-element.64), channel_id=1, source_target_pairs={{0,12},{4,8},{8,4},{12,0},{16,28},{20,24},{24,20},{28,16},{1,13},{... | collective-permute-start | bytes 196616 | tf_op jit(solution)/shard_map/ppermute | solution.py:524
  12.2 11.6 %collective-permute-start.5 = (f32[64,256]{1,0:T(8,128)S(1)}, f32[64,256]{1,0:T(8,128)S(1)}, u32[]{:S(2)}, u32[]{:S(2)}) collective-permute-start(f32[64,256]{1,0:T(8,128)S(1)} %get-tuple-element.65), channel_id=1, source_target_pairs={{0,8},{4,12},{8,0},{12,4},{16,24},{20,28},{24,16},{28,20},{1,9},{5... | collective-permute-start | bytes 196616 | tf_op jit(solution)/shard_map/ppermute | solution.py:524
  16.4 7.4 %collective-permute-start.6 = (f32[64,256]{1,0:T(8,128)S(1)}, f32[64,256]{1,0:T(8,128)S(1)}, u32[]{:S(2)}, u32[]{:S(2)}) collective-permute-start(f32[64,256]{1,0:T(8,128)S(1)} %get-tuple-element.66), channel_id=1, source_target_pairs={{0,4},{4,0},{8,12},{12,8},{16,20},{20,16},{24,28},{28,24},{1,5},{5... | collective-permute-start | bytes 196616 | tf_op jit(solution)/shard_map/ppermute | solution.py:524
  20.6 3.2 %copy-start.2 = (s32[64,4]{0,1:T(4,128)S(1)}, s32[64,4]{0,1:T(4,128)}, u32[]{:S(2)}) copy-start(s32[64,4]{0,1:T(4,128)} %param.10) | copy-start | bytes 3076
  20.6 7.2 %slice-start = ((s8[8388608]{0:T(1024)(128)(4,1)}), s8[4194304]{0:T(1024)(128)(4,1)S(1)}, s32[]{:S(2)}) async-start(s8[8388608]{0:T(1024)(128)(4,1)} %bitcast.6), calls=%async_computation.1 | async-start | bytes 8388608
  23.8 4.0 %slice-start.1 = ((s8[8388608]{0:T(1024)(128)(4,1)}), s8[4194304]{0:T(1024)(128)(4,1)S(1)}, s32[]{:S(2)}) async-start(s8[8388608]{0:T(1024)(128)(4,1)} %bitcast.6), calls=%async_computation.2 | async-start | bytes 8388608
  29.2 30.8 %copy-start.3 = (s32[1,8,4]{1,2,0:T(4,128)S(1)}, s32[1,8,4]{1,2,0:T(4,128)}, u32[]{:S(2)}) copy-start(s32[1,8,4]{1,2,0:T(4,128)} %param.11) | copy-start | bytes 388
  33.0 16.2 %collective-permute-start.8 = (f32[64,2304]{1,0:T(8,128)S(1)}, f32[64,2304]{1,0:T(8,128)S(1)}, u32[]{:S(2)}, u32[]{:S(2)}) collective-permute-start(f32[64,2304]{1,0:T(8,128)S(1)} %get-tuple-element.71.refs_2_), channel_id=1, source_target_pairs={{0,2},{1,3},{2,0},{3,1},{4,6},{5,7},{6,4},{7,5},{8,10},{9,11},{10,... | collective-permute-start | bytes 1769480 | tf_op jit(solution)/shard_map/ppermute | solution.py:541
  34.6 18.2 %collective-permute-start.14 = (f32[64,1280]{1,0:T(8,128)S(1)}, f32[64,1280]{1,0:T(8,128)S(1)}, u32[]{:S(2)}, u32[]{:S(2)}) collective-permute-start(f32[64,1280]{1,0:T(8,128)S(1)} %get-tuple-element.75.refs_4_), channel_id=1, source_target_pairs={{0,2},{1,3},{2,0},{3,1},{4,6},{5,7},{6,4},{7,5},{8,10},{9,11},{10,... | collective-permute-start | bytes 983048 | tf_op jit(solution)/shard_map/ppermute | solution.py:541
  35.1 35.0 %collective-permute-start.7 = (f32[64,2304]{1,0:T(8,128)S(1)}, f32[64,2304]{1,0:T(8,128)S(1)}, u32[]{:S(2)}, u32[]{:S(2)}) collective-permute-start(f32[64,2304]{1,0:T(8,128)S(1)} %get-tuple-element.71.refs_2_), channel_id=1, source_target_pairs={{0,1},{1,0},{2,3},{3,2},{4,5},{5,4},{6,7},{7,6},{8,9},{9,8},{10,11... | collective-permute-start | bytes 1769480 | tf_op jit(solution)/shard_map/ppermute | solution.py:542
  49.2 24.6 %collective-permute-start.9 = (f32[64,2304]{1,0:T(8,128)S(1)}, f32[64,2304]{1,0:T(8,128)S(1)}, u32[]{:S(2)}, u32[]{:S(2)}) collective-permute-start(f32[64,2304]{1,0:T(8,128)S(1)} %collective-permute-done.8.refs_2_), channel_id=1, source_target_pairs={{0,1},{1,0},{2,3},{3,2},{4,5},{5,4},{6,7},{7,6},{8,9},{9,8},{10,11... | collective-permute-start | bytes 1769480 | tf_op jit(solution)/shard_map/ppermute | solution.py:554
  49.2 3.5 %collective-permute-start.10 = (f32[64,512]{1,0:T(8,128)S(1)}, f32[64,512]{1,0:T(8,128)S(1)}, u32[]{:S(2)}, u32[]{:S(2)}) collective-permute-start(f32[64,512]{1,0:T(8,128)S(1)} %get-tuple-element.74.refs_3_), channel_id=1, source_target_pairs={{0,1},{1,0},{2,3},{3,2},{4,5},{5,4},{6,7},{7,6},{8,9},{9,8},{10,11... | collective-permute-start | bytes 393224 | tf_op jit(solution)/shard_map/ppermute | solution.py:542
  49.7 9.5 %collective-permute-start.11 = (f32[64,1280]{1,0:T(8,128)S(1)}, f32[64,1280]{1,0:T(8,128)S(1)}, u32[]{:S(2)}, u32[]{:S(2)}) collective-permute-start(f32[64,1280]{1,0:T(8,128)S(1)} %get-tuple-element.75.refs_4_), channel_id=1, source_target_pairs={{0,1},{1,0},{2,3},{3,2},{4,5},{5,4},{6,7},{7,6},{8,9},{9,8},{10,11... | collective-permute-start | bytes 983048 | tf_op jit(solution)/shard_map/ppermute | solution.py:542
  52.7 7.3 %collective-permute-start.15 = (f32[64,1280]{1,0:T(8,128)S(1)}, f32[64,1280]{1,0:T(8,128)S(1)}, u32[]{:S(2)}, u32[]{:S(2)}) collective-permute-start(f32[64,1280]{1,0:T(8,128)S(1)} %collective-permute-done.14.refs_5_), channel_id=1, source_target_pairs={{0,1},{1,0},{2,3},{3,2},{4,5},{5,4},{6,7},{7,6},{8,9},{9,8},{10,11... | collective-permute-start | bytes 983048 | tf_op jit(solution)/shard_map/ppermute | solution.py:554
  52.7 5.9 %collective-permute-start.12 = (f32[64,512]{1,0:T(8,128)S(1)}, f32[64,512]{1,0:T(8,128)S(1)}, u32[]{:S(2)}, u32[]{:S(2)}) collective-permute-start(f32[64,512]{1,0:T(8,128)S(1)} %get-tuple-element.74.refs_3_), channel_id=1, source_target_pairs={{0,2},{1,3},{2,0},{3,1},{4,6},{5,7},{6,4},{7,5},{8,10},{9,11},{10,... | collective-permute-start | bytes 393224 | tf_op jit(solution)/shard_map/ppermute | solution.py:541
  58.6 1.3 %collective-permute-start.13 = (f32[64,512]{1,0:T(8,128)S(1)}, f32[64,512]{1,0:T(8,128)S(1)}, u32[]{:S(2)}, u32[]{:S(2)}) collective-permute-start(f32[64,512]{1,0:T(8,128)S(1)} %collective-permute-done.12.refs_2_), channel_id=1, source_target_pairs={{0,1},{1,0},{2,3},{3,2},{4,5},{5,4},{6,7},{7,6},{8,9},{9,8},{10,11... | collective-permute-start | bytes 393224 | tf_op jit(solution)/shard_map/ppermute | solution.py:554
  61.1 9.0 %collective-permute-start.16 = (f32[64,256]{1,0:T(8,128)S(1)}, f32[64,256]{1,0:T(8,128)S(1)}, u32[]{:S(2)}, u32[]{:S(2)}) collective-permute-start(f32[64,256]{1,0:T(8,128)S(1)} %get-tuple-element.81), channel_id=1, source_target_pairs={{0,16},{4,20},{8,24},{12,28},{16,0},{20,4},{24,8},{28,12},{1,17},{... | collective-permute-start | bytes 196616 | tf_op jit(solution)/shard_map/ppermute | solution.py:524
  64.2 9.7 %collective-permute-start.17 = (f32[64,256]{1,0:T(8,128)S(1)}, f32[64,256]{1,0:T(8,128)S(1)}, u32[]{:S(2)}, u32[]{:S(2)}) collective-permute-start(f32[64,256]{1,0:T(8,128)S(1)} %get-tuple-element.82), channel_id=1, source_target_pairs={{0,20},{4,16},{8,28},{12,24},{16,4},{20,0},{24,12},{28,8},{1,21},{... | collective-permute-start | bytes 196616 | tf_op jit(solution)/shard_map/ppermute | solution.py:524
  65.3 13.4 %collective-permute-start.18 = (f32[64,256]{1,0:T(8,128)S(1)}, f32[64,256]{1,0:T(8,128)S(1)}, u32[]{:S(2)}, u32[]{:S(2)}) collective-permute-start(f32[64,256]{1,0:T(8,128)S(1)} %get-tuple-element.83), channel_id=1, source_target_pairs={{0,24},{4,28},{8,16},{12,20},{16,8},{20,12},{24,0},{28,4},{1,25},{... | collective-permute-start | bytes 196616 | tf_op jit(solution)/shard_map/ppermute | solution.py:524
  70.1 8.6 %collective-permute-start.19 = (f32[64,256]{1,0:T(8,128)S(1)}, f32[64,256]{1,0:T(8,128)S(1)}, u32[]{:S(2)}, u32[]{:S(2)}) collective-permute-start(f32[64,256]{1,0:T(8,128)S(1)} %get-tuple-element.84), channel_id=1, source_target_pairs={{0,28},{4,24},{8,20},{12,16},{16,12},{20,8},{24,4},{28,0},{1,29},{... | collective-permute-start | bytes 196616 | tf_op jit(solution)/shard_map/ppermute | solution.py:524
  70.1 8.6 %collective-permute-start.20 = (f32[64,256]{1,0:T(8,128)S(1)}, f32[64,256]{1,0:T(8,128)S(1)}, u32[]{:S(2)}, u32[]{:S(2)}) collective-permute-start(f32[64,256]{1,0:T(8,128)S(1)} %get-tuple-element.85), channel_id=1, source_target_pairs={{0,12},{4,8},{8,4},{12,0},{16,28},{20,24},{24,20},{28,16},{1,13},{... | collective-permute-start | bytes 196616 | tf_op jit(solution)/shard_map/ppermute | solution.py:524
  73.9 4.8 %collective-permute-start.21 = (f32[64,256]{1,0:T(8,128)S(1)}, f32[64,256]{1,0:T(8,128)S(1)}, u32[]{:S(2)}, u32[]{:S(2)}) collective-permute-start(f32[64,256]{1,0:T(8,128)S(1)} %get-tuple-element.86), channel_id=1, source_target_pairs={{0,8},{4,12},{8,0},{12,4},{16,24},{20,28},{24,16},{28,20},{1,9},{5... | collective-permute-start | bytes 196616 | tf_op jit(solution)/shard_map/ppermute | solution.py:524
  73.9 4.8 %collective-permute-start.22 = (f32[64,256]{1,0:T(8,128)S(1)}, f32[64,256]{1,0:T(8,128)S(1)}, u32[]{:S(2)}, u32[]{:S(2)}) collective-permute-start(f32[64,256]{1,0:T(8,128)S(1)} %get-tuple-element.87), channel_id=1, source_target_pairs={{0,4},{4,0},{8,12},{12,8},{16,20},{20,16},{24,28},{28,24},{1,5},{5... | collective-permute-start | bytes 196616 | tf_op jit(solution)/shard_map/ppermute | solution.py:524
  83.5 14.9 %collective-permute-start.29 = (f32[64,2048]{1,0:T(8,128)S(1)}, f32[64,2048]{1,0:T(8,128)S(1)}, u32[]{:S(2)}, u32[]{:S(2)}) collective-permute-start(f32[64,2048]{1,0:T(8,128)S(1)} %get-tuple-element.95.refs_7_), channel_id=1, source_target_pairs={{0,2},{1,3},{2,0},{3,1},{4,6},{5,7},{6,4},{7,5},{8,10},{9,11},{10,... | collective-permute-start | bytes 1572872 | tf_op jit(solution)/shard_map/ppermute | solution.py:541
  85.0 26.1 %collective-permute-start.25 = (f32[64,2048]{1,0:T(8,128)S(1)}, f32[64,2048]{1,0:T(8,128)S(1)}, u32[]{:S(2)}, u32[]{:S(2)}) collective-permute-start(f32[64,2048]{1,0:T(8,128)S(1)} %get-tuple-element.95.refs_7_), channel_id=1, source_target_pairs={{0,1},{1,0},{2,3},{3,2},{4,5},{5,4},{6,7},{7,6},{8,9},{9,8},{10,11... | collective-permute-start | bytes 1572872 | tf_op jit(solution)/shard_map/ppermute | solution.py:542
  85.0 13.8 %collective-permute-start.23 = (f32[64,512]{1,0:T(8,128)S(1)}, f32[64,512]{1,0:T(8,128)S(1)}, u32[]{:S(2)}, u32[]{:S(2)}) collective-permute-start(f32[64,512]{1,0:T(8,128)S(1)} %get-tuple-element.93.refs_5_), channel_id=1, source_target_pairs={{0,1},{1,0},{2,3},{3,2},{4,5},{5,4},{6,7},{7,6},{8,9},{9,8},{10,11... | collective-permute-start | bytes 393224 | tf_op jit(solution)/shard_map/ppermute | solution.py:542
  87.5 19.6 %collective-permute-start.33 = (f32[64,1024]{1,0:T(8,128)S(1)}, f32[64,1024]{1,0:T(8,128)S(1)}, u32[]{:S(2)}, u32[]{:S(2)}) collective-permute-start(f32[64,1024]{1,0:T(8,128)S(1)} %get-tuple-element.94.refs_6_), channel_id=1, source_target_pairs={{0,2},{1,3},{2,0},{3,1},{4,6},{5,7},{6,4},{7,5},{8,10},{9,11},{10,... | collective-permute-start | bytes 786440 | tf_op jit(solution)/shard_map/ppermute | solution.py:541
  98.3 14.0 %collective-permute-start.30 = (f32[64,2048]{1,0:T(8,128)S(1)}, f32[64,2048]{1,0:T(8,128)S(1)}, u32[]{:S(2)}, u32[]{:S(2)}) collective-permute-start(f32[64,2048]{1,0:T(8,128)S(1)} %collective-permute-done.29.refs_2_), channel_id=1, source_target_pairs={{0,1},{1,0},{2,3},{3,2},{4,5},{5,4},{6,7},{7,6},{8,9},{9,8},{10,11... | collective-permute-start | bytes 1572872 | tf_op jit(solution)/shard_map/ppermute | solution.py:554
  98.3 2.1 %collective-permute-start.26 = (f32[64,512]{1,0:T(8,128)S(1)}, f32[64,512]{1,0:T(8,128)S(1)}, u32[]{:S(2)}, u32[]{:S(2)}) collective-permute-start(f32[64,512]{1,0:T(8,128)S(1)} %get-tuple-element.96.refs_8_), channel_id=1, source_target_pairs={{0,1},{1,0},{2,3},{3,2},{4,5},{5,4},{6,7},{7,6},{8,9},{9,8},{10,11... | collective-permute-start | bytes 393224 | tf_op jit(solution)/shard_map/ppermute | solution.py:542
  98.8 6.8 %collective-permute-start.27 = (f32[64,512]{1,0:T(8,128)S(1)}, f32[64,512]{1,0:T(8,128)S(1)}, u32[]{:S(2)}, u32[]{:S(2)}) collective-permute-start(f32[64,512]{1,0:T(8,128)S(1)} %get-tuple-element.96.refs_8_), channel_id=1, source_target_pairs={{0,2},{1,3},{2,0},{3,1},{4,6},{5,7},{6,4},{7,5},{8,10},{9,11},{10,... | collective-permute-start | bytes 393224 | tf_op jit(solution)/shard_map/ppermute | solution.py:541
  100.4 10.2 %collective-permute-start.24 = (f32[64,1024]{1,0:T(8,128)S(1)}, f32[64,1024]{1,0:T(8,128)S(1)}, u32[]{:S(2)}, u32[]{:S(2)}) collective-permute-start(f32[64,1024]{1,0:T(8,128)S(1)} %get-tuple-element.94.refs_6_), channel_id=1, source_target_pairs={{0,1},{1,0},{2,3},{3,2},{4,5},{5,4},{6,7},{7,6},{8,9},{9,8},{10,11... | collective-permute-start | bytes 786440 | tf_op jit(solution)/shard_map/ppermute | solution.py:542
  105.7 5.0 %collective-permute-start.31 = (f32[64,512]{1,0:T(8,128)S(1)}, f32[64,512]{1,0:T(8,128)S(1)}, u32[]{:S(2)}, u32[]{:S(2)}) collective-permute-start(f32[64,512]{1,0:T(8,128)S(1)} %get-tuple-element.93.refs_5_), channel_id=1, source_target_pairs={{0,2},{1,3},{2,0},{3,1},{4,6},{5,7},{6,4},{7,5},{8,10},{9,11},{10,... | collective-permute-start | bytes 393224 | tf_op jit(solution)/shard_map/ppermute | solution.py:541
  107.2 4.8 %collective-permute-start.34 = (f32[64,1024]{1,0:T(8,128)S(1)}, f32[64,1024]{1,0:T(8,128)S(1)}, u32[]{:S(2)}, u32[]{:S(2)}) collective-permute-start(f32[64,1024]{1,0:T(8,128)S(1)} %collective-permute-done.33.refs_5_), channel_id=1, source_target_pairs={{0,1},{1,0},{2,3},{3,2},{4,5},{5,4},{6,7},{7,6},{8,9},{9,8},{10,11... | collective-permute-start | bytes 786440 | tf_op jit(solution)/shard_map/ppermute | solution.py:554
  110.6 1.3 %collective-permute-start.32 = (f32[64,512]{1,0:T(8,128)S(1)}, f32[64,512]{1,0:T(8,128)S(1)}, u32[]{:S(2)}, u32[]{:S(2)}) collective-permute-start(f32[64,512]{1,0:T(8,128)S(1)} %collective-permute-done.31.refs_2_), channel_id=1, source_target_pairs={{0,1},{1,0},{2,3},{3,2},{4,5},{5,4},{6,7},{7,6},{8,9},{9,8},{10,11... | collective-permute-start | bytes 393224 | tf_op jit(solution)/shard_map/ppermute | solution.py:554
  110.6 2.1 %collective-permute-start.28 = (f32[64,512]{1,0:T(8,128)S(1)}, f32[64,512]{1,0:T(8,128)S(1)}, u32[]{:S(2)}, u32[]{:S(2)}) collective-permute-start(f32[64,512]{1,0:T(8,128)S(1)} %collective-permute-done.27.refs_2_), channel_id=1, source_target_pairs={{0,1},{1,0},{2,3},{3,2},{4,5},{5,4},{6,7},{7,6},{8,9},{9,8},{10,11... | collective-permute-start | bytes 393224 | tf_op jit(solution)/shard_map/ppermute | solution.py:554

commit v2 on v1

--- a/solution.py
+++ b/solution.py
@@ -97,12 +97,12 @@
     far_ref[...] = spectral_rows(me, far, samples, samples * groups)
 
 
-def prepare_kernel(first_row, last_row, perm_ref, stamps_ref, *refs):
+def prepare_kernel(first_row, last_row, order_ref, stamps_ref, *refs):
     out_ref = refs[-1]
     width = stamps_ref.shape[2]
 
     def convert(row, carry):
-        high, low = split(stamps_ref[perm_ref[row]])
+        high, low = split(stamps_ref[order_ref[0, row]])
         out_ref[row, :, :width] = high
         out_ref[row, :, width:] = low
         return carry
@@ -110,11 +110,11 @@
     lax.fori_loop(first_row, last_row, convert, 0, unroll=2)
 
 
-def fetch_kernel(perm_ref, stamps_hbm, out_ref, buffer, sems):
+def fetch_kernel(order_ref, stamps_hbm, out_ref, buffer, sems):
     rows, _, width = buffer.shape
     copies = []
     for n in range(rows):
-        copies.append(pltpu.make_async_copy(stamps_hbm.at[perm_ref[n]], buffer.at[n], sems.at[n]))
+        copies.append(pltpu.make_async_copy(stamps_hbm.at[order_ref[0, n]], buffer.at[n], sems.at[n]))
         copies[-1].start()
     for n, copy in enumerate(copies):
         copy.wait()
@@ -123,7 +123,7 @@
         out_ref[n, :, width:] = low
 
 
-def fetch(perm, stamps, rows):
+def fetch(order, stamps, rows):
     total, depth, width = stamps.shape
     return pl.pallas_call(
         fetch_kernel,
@@ -133,7 +133,7 @@
         scratch_shapes=[pltpu.VMEM((rows, depth, width), stamps.dtype), pltpu.SemaphoreType.DMA((rows,))],
         compiler_params=pltpu.CompilerParams(vmem_limit_bytes=LIMIT),
         name="prepare_0",
-    )(perm, far_memory(stamps))
+    )(order, far_memory(stamps))
 
 
 def pair_tile(ref, first, second):
@@ -149,13 +149,13 @@
     return jnp.where(lane < HALF, placed(first, 0), placed(second, 1))
 
 
-def gather_blocks(targets, send_ref, field_ref, out_refs, inv_ref=None):
+def gather_blocks(targets, send_ref, field_ref, out_refs, order_ref=None):
     slots = send_ref.shape[0]
     for d, out_ref in zip(targets, out_refs):
         for j in range(0, slots, 2):
             first, second = send_ref[j, d], send_ref[j + 1, d]
-            if inv_ref is not None:
-                first, second = inv_ref[first], inv_ref[second]
+            if order_ref is not None:
+                first, second = order_ref[1, first], order_ref[1, second]
             out_ref[:, j * HALF : j * HALF + LANES] = pair_tile(field_ref, first, second)
 
 
@@ -167,12 +167,12 @@
     return domains <= 8 and domains & (domains - 1) == 0
 
 
-def gather_all(domains, send_ref, field_ref, out_refs, inv_ref=None):
+def gather_all(domains, send_ref, field_ref, out_refs, order_ref=None):
     if few(domains):
         me = lax.axis_index("dom")
-        gather_blocks([me ^ k for k in halo_offsets(domains)], send_ref, field_ref, out_refs, inv_ref)
+        gather_blocks([me ^ k for k in halo_offsets(domains)], send_ref, field_ref, out_refs, order_ref)
     else:
-        gather_blocks(range(domains), send_ref, field_ref, [out_refs[0].at[d] for d in range(domains)], inv_ref)
+        gather_blocks(range(domains), send_ref, field_ref, [out_refs[0].at[d] for d in range(domains)], order_ref)
 
 
 COPIES = 4
@@ -181,8 +181,8 @@
 WORD = 32
 
 
-def order_rows(domains, send_ref, perm_ref, inv_ref):
-    rows = perm_ref.shape[0]
+def order_rows(domains, send_ref, order_ref):
+    rows = order_ref.shape[1]
     masks = [jnp.int32(0)] * (rows // WORD)
     if few(domains):
         me = lax.axis_index("dom")
@@ -196,13 +196,13 @@
     later = sum(flags)
     for row, flag in enumerate(flags):
         position = jnp.where(flag == 1, first, later)
-        inv_ref[row] = position
-        perm_ref[position] = row
+        order_ref[0, position] = row
+        order_ref[1, row] = position
         first = first + flag
         later = later + 1 - flag
 
 
-def gather_kernel(domains, send_hbm, field_hbm, field_ref, perm_ref, inv_ref, *refs):
+def gather_kernel(domains, send_hbm, field_hbm, field_ref, order_ref, *refs):
     *out_refs, field_sem, send_ref, send_sem = refs
     table = pltpu.make_async_copy(send_hbm, send_ref, send_sem)
     table.start()
@@ -213,21 +213,20 @@
         copies.append(pltpu.make_async_copy(field_hbm.at[:, inside], field_ref.at[:, inside], field_sem.at[n]))
         copies[-1].start()
     table.wait()
-    order_rows(domains, send_ref, perm_ref, inv_ref)
+    order_rows(domains, send_ref, order_ref)
     for copy in copies:
         copy.wait()
     gather_all(domains, send_ref, field_ref, out_refs)
 
 
 def gather(send, field, rows, domains, outputs):
-    table = jax.ShapeDtypeStruct((rows,), jnp.int32)
+    table = jax.ShapeDtypeStruct((2, rows), jnp.int32)
     return pl.pallas_call(
         functools.partial(gather_kernel, domains),
         in_specs=[pl.BlockSpec(memory_space=pl.ANY)] * 2,
-        out_specs=[whole(), scalars(), scalars()] + [whole()] * len(outputs),
+        out_specs=[whole(), scalars()] + [whole()] * len(outputs),
         out_shape=[
             pltpu.VMEM(field.shape, field.dtype),
-            table,
             table,
             *[pltpu.VMEM(shape, dtype) for shape, dtype in outputs],
         ],
@@ -248,7 +247,7 @@
     ext[1, index] = jnp.concatenate([high, low], axis=0)
 
 
-def arrange_kernel(first_row, perm_ref, field_ref, g_ref, c_ref, g_out, c_out):
+def arrange_kernel(first_row, order_ref, field_ref, g_ref, c_ref, g_out, c_out):
     samples = field_ref.shape[0]
     lane = lax.broadcasted_iota(jnp.int32, (samples, LANES), 1)
 
@@ -260,17 +259,16 @@
 
     for i in range(g_out.shape[1] // LANES):
         inside = slice(i * LANES, (i + 1) * LANES)
-        low = placed(perm_ref[first_row + 2 * i], 0)
-        high = placed(perm_ref[first_row + 2 * i + 1], 1)
+        low = placed(order_ref[0, first_row + 2 * i], 0)
+        high = placed(order_ref[0, first_row + 2 * i + 1], 1)
         g_out[:, inside] = jnp.where(lane < HALF, low[0], high[0])
         c_out[:, inside] = jnp.where(lane < HALF, low[1], high[1])
 
 
-def restore_kernel(inv_ref, u_ref, out_ref, ext):
+def restore_kernel(order_ref, u_ref, out_ref):
     for i in range(u_ref.shape[1] // LANES):
-        tile = pair_tile(u_ref, inv_ref[2 * i], inv_ref[2 * i + 1])
-        out_ref[:, i * LANES : (i + 1) * LANES] = tile
-        store_tile(ext, i, tile)
+        inside = slice(i * LANES, (i + 1) * LANES)
+        out_ref[:, inside] = pair_tile(u_ref, order_ref[1, 2 * i], order_ref[1, 2 * i + 1])
 
 
 def extend_kernel(field_ref, ext):
@@ -312,21 +310,28 @@
     lane = lax.broadcasted_iota(jnp.int32, (2 * samples, LANES), 1)
     low_lane = lax.broadcasted_iota(jnp.int32, (samples, LANES), 1) < HALF
 
+    rows = cols_ref.shape[1]
+
+    def entry_of(k, row):
+        entry = cols_ref[k, row]
+        if permuted:
+            return entry
+        return jnp.where(entry < rows, order_ref[1, jnp.minimum(entry, rows - 1)], entry)
+
     def row_product(row):
-        other = order_ref[row]
-        source, place = (other, row) if permuted else (row, other)
+        source, place = (order_ref[0, row], row) if permuted else (row, order_ref[1, row])
         parts = []
         for k in range(0, per_entry, 2):
-            first = cols_ref[k, source]
-            second = cols_ref[k + 1, source]
+            first = entry_of(k, source)
+            second = entry_of(k + 1, source)
             a = ext[first & 1, first // 2]
             b = ext[1 - (second & 1), second // 2]
             parts.append(jnp.where(lane < HALF, a, b))
         left = jnp.concatenate(parts, axis=1)
         full = jnp.dot(left, w_ref[place], preferred_element_type=jnp.float32)
         width = full.shape[1] // 2
-        rows = full[:, :width] + full[:, width:]
-        return rows[:samples] + rows[samples:]
+        both = full[:, :width] + full[:, width:]
+        return both[:samples] + both[samples:]
 
     def block(step, carry):
         for pair in range(GROUP // 2):
@@ -355,7 +360,7 @@
 def plain_product(first_row, cols_ref, order_ref, ext, w_ref, field_ref, g_ref, c_ref, p_ref, q_ref):
     def own_terms(row):
         there = pl.ds(pl.multiple_of((first_row + row) * HALF, LANES), LANES)
-        own = field_ref[:, there]
+        own = pair_tile(field_ref, order_ref[1, first_row + row], order_ref[1, first_row + row + 1])
         return g_ref[:, there] * own, c_ref[:, there] * own
 
     product_rows(first_row, False, cols_ref, order_ref, ext, w_ref, p_ref, q_ref, own_terms)
@@ -400,19 +405,19 @@
         base += p_ref.shape[1]
 
 
-def far_send_kernel(count, chunks, domains, send_near, inv_near, *refs):
+def far_send_kernel(count, chunks, domains, send_near, order_near, *refs):
     size = 1 + count
-    u_ref, *out_refs, send_ref, send_sem, inv_ref, inv_sem = refs[1 + chunks * size :]
+    u_ref, *out_refs, send_ref, send_sem, order_ref, order_sem = refs[1 + chunks * size :]
     tables = [
         pltpu.make_async_copy(send_near, send_ref, send_sem),
-        pltpu.make_async_copy(inv_near, inv_ref, inv_sem),
+        pltpu.make_async_copy(order_near, order_ref, order_sem),
     ]
     for table in tables:
         table.start()
     far_kernel(count, 0, chunks, *refs[: 1 + chunks * size], u_ref)
     for table in tables:
         table.wait()
-    gather_all(domains, send_ref, u_ref, out_refs, inv_ref)
+    gather_all(domains, send_ref, u_ref, out_refs, order_ref)
 
 
 def dot_totals(totals, r_ref, u_ref, base, v):
@@ -554,7 +559,7 @@
             charges += [x, lax.ppermute(x, "samp", pairs)]
         return [half, *charges]
 
-    field, perm, inv, *outgoing = gather(send, residual, rows, domains, outgoing_shapes)
+    field, order, *outgoing = gather(send, residual, rows, domains, outgoing_shapes)
     incoming = exchange(outgoing)
     near_matrix, far_matrix = kernel_call(
         functools.partial(tables_kernel, groups),
@@ -567,14 +572,14 @@
     own = []
     for n, (low, high) in enumerate(((0, early), (early, rows))):
         if n == 0:
-            weights = fetch(perm, blocks, early)
+            weights = fetch(order, blocks, early)
         else:
             (weights,) = kernel_call(
-                functools.partial(prepare_kernel, low, high), (perm, blocks, weights), [weight_shape], aliases={2: 0}
+                functools.partial(prepare_kernel, low, high), (order, blocks, weights), [weight_shape], aliases={2: 0}
             )
         terms = kernel_call(
             functools.partial(arrange_kernel, low),
-            (perm, field, conductance, capacitance),
+            (order, field, conductance, capacitance),
             [((samples, (high - low) * width), f32)] * 2,
         )
         own.append((low, weights, terms))
@@ -583,7 +588,7 @@
     for n, size in enumerate(sizes_one):
         base, w, terms = own[first >= early]
         ext, p, q = product_call(
-            n, size, functools.partial(permuted_product, first, base), (cols, perm, ext, w, *terms), incoming
+            n, size, functools.partial(permuted_product, first, base), (cols, order, ext, w, *terms), incoming
         )
         chunks.append((p, q, *spread(q)))
         first += size
@@ -592,7 +597,7 @@
     ready = 2 if few(domains) else len(chunks)
     u, *outgoing = kernel_call(
         functools.partial(far_send_kernel, count, ready, domains),
-        (send, inv, far_matrix, *[x for piece in pieces[:ready] for x in piece]),
+        (send, order, far_matrix, *[x for piece in pieces[:ready] for x in piece]),
         [field_shape, *outgoing_shapes],
         table_copied=True,
     )
@@ -605,14 +610,15 @@
             [field_shape],
             aliases={len(operands): 0},
         )
-    u, ext = kernel_call(restore_kernel, (inv, u), [field_shape, ext_shape])
+    (ext,) = kernel_call(extend_kernel, (u,), [ext_shape])
     chunks = []
     first = 0
     for n, size in enumerate(sizes_two):
-        operands = (cols, inv, ext, weights, u, conductance, capacitance)
+        operands = (cols, order, ext, weights, u, conductance, capacitance)
         ext, p, q = product_call(n, size, functools.partial(plain_product, first), operands, incoming)
         chunks.append((p, q, *spread(q)))
         first += size
+    (u,) = kernel_call(restore_kernel, (order, u), [field_shape])
     half = near_call(chunks)
     pieces = [forward(half[n], chunk[2]) for n, chunk in enumerate(chunks)]
     sums = None

time: 126 us -> 127 us (level)
  waiting for transfers between devices: 44.9 us -> 47.1 us
    ppermute x14, waiting for transfers between devices: 5.12 us -> 7.85 us  [exchange(): lax.ppermute(x, 'dom', [(i, i ^ k) for i in range(domains)])]
    pallas_call x21 -> x22, Pallas kernels: 27.4 us -> 26.7 us  [kernel_call(): pl.pallas_call(kernel, in_specs=specs, out_specs=[scalars() if number els...]
  transfers between devices with their start and end apart: 35 -> 35, of which waited for: 11 -> 14; matrix products, arithmetic and copies ran while one was open for 0% -> 0% of each run, Pallas kernels for 13% -> 12%
where the time goes in v2:
time: 127 us
  waiting for transfers between devices  47.1 us (37%)
  starting transfers between devices  35.1 us (28%)
  Pallas kernels  33.3 us (26%)
  blocking collectives  10.7 us (8%)
    ppermute x7, waiting for transfers between devices, spread(): lax.ppermute(q, 'samp', [(i, (i + k) % groups) for i in range(groups)])  38.7 us
    pallas_call x22, Pallas kernels, kernel_call(): pl.pallas_call(kernel, in_specs=specs, out_specs=[scalars() if number els...  26.7 us
    ppermute x14, starting transfers between devices, exchange(): lax.ppermute(x, 'dom', [(i, i ^ k) for i in range(domains)])  24.2 us
    all_to_all x1, blocking collectives, body(): lax.all_to_all(sums, ('dom', 'samp'), split_axis=0, concat_axis=0, tiled=...  10.7 us
    ppermute x7, starting transfers between devices, spread(): lax.ppermute(q, 'samp', [(i, (i + k) % groups) for i in range(groups)])  8.73 us
    ppermute x14, waiting for transfers between devices, exchange(): lax.ppermute(x, 'dom', [(i, i ^ k) for i in range(domains)])  7.85 us
    pallas_call x1, Pallas kernels, fetch(): pl.pallas_call(fetch_kernel, in_specs=[scalars(), pl.BlockSpec(memory_spa...  3.15 us
  transfers between devices with their start and end apart: 35, of which 14 were waited for; matrix products, arithmetic and copies ran while one was open for 0% of the time, Pallas kernels for 12%

profile of v2, /device:TPU:0, one launch (start us, length us, event | category | flops | bytes accessed | tf_op | source)
XLA Modules:
  0.0 126.8 jit_solution(3547056313742332637)
XLA Ops:
  0.0 2.2 %gather.1 = (f32[64,4096]{1,0:T(8,128)S(1)}, s32[2,64]{1,0:T(2,128)S(1)}, f32[64,256]{1,0:T(8,128)S(1)}, f32[64,256]{1,0:T(8,128)S(1)}, f32[64,256]{1,0:T(8,128)...) custom-call(s32[4,8]{1,0:T(4,128)} %bitcast.16, ...), custom_call_target="tpu_custom_call" | custom-call | tf_op jit(solution)/shard_map/gather/pallas_call | solution.py:224
  2.2 4.1 %collective-permute-start = (f32[64,256]{1,0:T(8,128)S(1)}, f32[64,256]{1,0:T(8,128)S(1)}, u32[]{:S(2)}, u32[]{:S(2)}) collective-permute-start(f32[64,256]{1,0:T(8,128)S(1)} %get-tuple-element.56), channel_id=1, source_target_pairs={{0,16},{4,20},{8,24},{12,28},{16,0},{20,4},{24,8},{28,12},{1,17},{... | collective-permute-start | bytes 196616 | tf_op jit(solution)/shard_map/ppermute | solution.py:529
  6.4 1.3 %collective-permute-start.1 = (f32[64,256]{1,0:T(8,128)S(1)}, f32[64,256]{1,0:T(8,128)S(1)}, u32[]{:S(2)}, u32[]{:S(2)}) collective-permute-start(f32[64,256]{1,0:T(8,128)S(1)} %get-tuple-element.57), channel_id=1, source_target_pairs={{0,20},{4,16},{8,28},{12,24},{16,4},{20,0},{24,12},{28,8},{1,21},{... | collective-permute-start | bytes 196616 | tf_op jit(solution)/shard_map/ppermute | solution.py:529
  7.7 3.6 %collective-permute-start.2 = (f32[64,256]{1,0:T(8,128)S(1)}, f32[64,256]{1,0:T(8,128)S(1)}, u32[]{:S(2)}, u32[]{:S(2)}) collective-permute-start(f32[64,256]{1,0:T(8,128)S(1)} %get-tuple-element.58), channel_id=1, source_target_pairs={{0,24},{4,28},{8,16},{12,20},{16,8},{20,12},{24,0},{28,4},{1,25},{... | collective-permute-start | bytes 196616 | tf_op jit(solution)/shard_map/ppermute | solution.py:529
  11.3 0.9 collective-permute-start.4
  12.2 2.2 %collective-permute-start.5 = (f32[64,256]{1,0:T(8,128)S(1)}, f32[64,256]{1,0:T(8,128)S(1)}, u32[]{:S(2)}, u32[]{:S(2)}) collective-permute-start(f32[64,256]{1,0:T(8,128)S(1)} %get-tuple-element.61), channel_id=1, source_target_pairs={{0,8},{4,12},{8,0},{12,4},{16,24},{20,28},{24,16},{28,20},{1,9},{5... | collective-permute-start | bytes 196616 | tf_op jit(solution)/shard_map/ppermute | solution.py:529
  14.4 2.0 %collective-permute-done.1.refs_5_ = f32[64,256]{1,0:T(8,128)S(1)} collective-permute-done((f32[64,256]{1,0:T(8,128)S(1)}, f32[64,256]{1,0:T(8,128)S(1)}, u32[]{:S(2)}, u32[]{:S(2)}) %collective-permute-start.1) | collective-permute-done | bytes 65568 | tf_op jit(solution)/shard_map/ppermute | solution.py:529
  16.4 1.5 %collective-permute-start.6 = (f32[64,256]{1,0:T(8,128)S(1)}, f32[64,256]{1,0:T(8,128)S(1)}, u32[]{:S(2)}, u32[]{:S(2)}) collective-permute-start(f32[64,256]{1,0:T(8,128)S(1)} %get-tuple-element.62), channel_id=1, source_target_pairs={{0,4},{4,0},{8,12},{12,8},{16,20},{20,16},{24,28},{28,24},{1,5},{5... | collective-permute-start | bytes 196616 | tf_op jit(solution)/shard_map/ppermute | solution.py:529
  17.9 0.3 shard_map.65.refs_0_
  18.2 1.1 shard_map.66
  19.3 1.3 shard_map.69
  20.6 3.2 %prepare_0.1.refs_1_.refs_0_.w_ref = bf16[64,256,256]{2,1,0:T(8,128)(2,1)S(1)} custom-call(s32[2,64]{1,0:T(2,128)S(1)} %get-tuple-element.52.order_ref.order_near, f32[64,256,128]{2,1,0:T(8,128)} %bitcast.5), custom_call_target="tpu_custom_call" | custom-call | tf_op jit(solution)/shard_map/prepare_0/pallas_call | solution.py:128
  23.9 0.0 slice-start.1
  23.9 1.6 %shard_map.67 = (bf16[2,48,128,128]{3,2,1,0:T(8,128)(2,1)S(1)}, f32[64,512]{1,0:T(8,128)S(1)}, f32[64,512]{1,0:T(8,128)S(1)}) custom-call(s32[4,64]{1,0:T(4,128)S(1)} %bitcast.9, s32[2,64]{1,0:T(2,128)S(1)} %get-tuple-element.52.order_ref.order_near, bf16[2,48,128,128]{3,2,1,0:T(8,128)(2,1)S(1)} %shard_map.65.refs_0_, ...), custom_call_target="tpu_custom_call", output_to_operand_aliasing={{0}: (2, {})} | custom-call | tf_op jit(solution)/shard_map/pallas_call | solution.py:55
  25.5 2.4 %shard_map.72 = (f32[64,1280]{1,0:T(8,128)S(1)}, f32[64,1280]{1,0:T(8,128)S(1)}) custom-call(s32[4,64]{1,0:T(4,128)S(1)} %bitcast.10, s32[2,64]{1,0:T(2,128)S(1)} %get-tuple-element.52.order_ref.order_near, bf16[2,48,128,128]{3,2,1,0:T(8,128)(2,1)S(1)} %get-tuple-element.63.ext, bf16[64,256,256]{2,1,0:T(8,128)(2,1)S(1)} %prepare_0.1.refs_1_.refs_0_.w_ref, ...), custom_call_target="tpu_custom_call" | custom-call | tf_op jit(solution)/shard_map/pallas_call | solution.py:55
  27.9 1.4 %shard_map.68.w_ref.refs_1_ = bf16[64,256,256]{2,1,0:T(8,128)(2,1)S(1)} custom-call(s32[2,64]{1,0:T(2,128)S(1)} %get-tuple-element.52.order_ref.order_near, f32[64,256,128]{2,1,0:T(8,128)S(1)} %bitcast.8, bf16[64,256,256]{2,1,0:T(8,128)(2,1)S(1)} %prepare_0.1.refs_1_.refs_0_.w_ref), custom_call_target="tpu_custom_call", output_to_operand_aliasing={{}: (2, {})} | custom-call | tf_op jit(solution)/shard_map/pallas_call | solution.py:55
  29.3 3.8 %shard_map.70 = (f32[64,2304]{1,0:T(8,128)S(1)}, f32[64,2304]{1,0:T(8,128)S(1)}) custom-call(s32[4,64]{1,0:T(4,128)S(1)} %bitcast.11, s32[2,64]{1,0:T(2,128)S(1)} %get-tuple-element.52.order_ref.order_near, bf16[2,48,128,128]{3,2,1,0:T(8,128)(2,1)S(1)} %get-tuple-element.63.ext, bf16[64,256,256]{2,1,0:T(8,128)(2,1)S(1)} %shard_map.68.w_ref.refs_1_, ...), custom_call_target="tpu_custom_call" | custom-call | tf_op jit(solution)/shard_map/pallas_call | solution.py:55
  33.1 1.6 %collective-permute-start.8 = (f32[64,2304]{1,0:T(8,128)S(1)}, f32[64,2304]{1,0:T(8,128)S(1)}, u32[]{:S(2)}, u32[]{:S(2)}) collective-permute-start(f32[64,2304]{1,0:T(8,128)S(1)} %get-tuple-element.67.refs_2_), channel_id=1, source_target_pairs={{0,2},{1,3},{2,0},{3,1},{4,6},{5,7},{6,4},{7,5},{8,10},{9,11},{10,... | collective-permute-start | bytes 1769480 | tf_op jit(solution)/shard_map/ppermute | solution.py:546
  34.6 0.5 collective-permute-start.14
  35.2 14.1 %collective-permute-done.8.refs_2_ = f32[64,2304]{1,0:T(8,128)S(1)} collective-permute-done((f32[64,2304]{1,0:T(8,128)S(1)}, f32[64,2304]{1,0:T(8,128)S(1)}, u32[]{:S(2)}, u32[]{:S(2)}) %collective-permute-start.8) | collective-permute-done | bytes 589856 | tf_op jit(solution)/shard_map/ppermute | solution.py:546
  49.3 0.5 collective-permute-start.10
  49.8 3.0 %collective-permute-done.14.refs_5_ = f32[64,1280]{1,0:T(8,128)S(1)} collective-permute-done((f32[64,1280]{1,0:T(8,128)S(1)}, f32[64,1280]{1,0:T(8,128)S(1)}, u32[]{:S(2)}, u32[]{:S(2)}) %collective-permute-start.14) | collective-permute-done | bytes 327712 | tf_op jit(solution)/shard_map/ppermute | solution.py:546
  52.8 1.5 %collective-permute-start.12 = (f32[64,512]{1,0:T(8,128)S(1)}, f32[64,512]{1,0:T(8,128)S(1)}, u32[]{:S(2)}, u32[]{:S(2)}) collective-permute-start(f32[64,512]{1,0:T(8,128)S(1)} %get-tuple-element.70.refs_3_), channel_id=1, source_target_pairs={{0,2},{1,3},{2,0},{3,1},{4,6},{5,7},{6,4},{7,5},{8,10},{9,11},{10,... | collective-permute-start | bytes 393224 | tf_op jit(solution)/shard_map/ppermute | solution.py:546
  54.3 4.4 %collective-permute-done.12.refs_2_ = f32[64,512]{1,0:T(8,128)S(1)} collective-permute-done((f32[64,512]{1,0:T(8,128)S(1)}, f32[64,512]{1,0:T(8,128)S(1)}, u32[]{:S(2)}, u32[]{:S(2)}) %collective-permute-start.12) | collective-permute-done | bytes 131104 | tf_op jit(solution)/shard_map/ppermute | solution.py:546
  58.7 0.5 shard_map.64
  59.3 0.4 shard_map.73
  59.6 0.4 collective-permute-done.13.refs_3_
  60.1 1.1 shard_map.74
  61.2 3.1 %collective-permute-start.16 = (f32[64,256]{1,0:T(8,128)S(1)}, f32[64,256]{1,0:T(8,128)S(1)}, u32[]{:S(2)}, u32[]{:S(2)}) collective-permute-start(f32[64,256]{1,0:T(8,128)S(1)} %get-tuple-element.75), channel_id=1, source_target_pairs={{0,16},{4,20},{8,24},{12,28},{16,0},{20,4},{24,8},{28,12},{1,17},{... | collective-permute-start | bytes 196616 | tf_op jit(solution)/shard_map/ppermute | solution.py:529
  64.2 1.1 collective-permute-start.17
  65.3 4.8 %collective-permute-start.18 = (f32[64,256]{1,0:T(8,128)S(1)}, f32[64,256]{1,0:T(8,128)S(1)}, u32[]{:S(2)}, u32[]{:S(2)}) collective-permute-start(f32[64,256]{1,0:T(8,128)S(1)} %get-tuple-element.77), channel_id=1, source_target_pairs={{0,24},{4,28},{8,16},{12,20},{16,8},{20,12},{24,0},{28,4},{1,25},{... | collective-permute-start | bytes 196616 | tf_op jit(solution)/shard_map/ppermute | solution.py:529
  70.1 0.6 collective-permute-start.20
  70.8 3.1 %collective-permute-done.17.refs_6_ = f32[64,256]{1,0:T(8,128)S(1)} collective-permute-done((f32[64,256]{1,0:T(8,128)S(1)}, f32[64,256]{1,0:T(8,128)S(1)}, u32[]{:S(2)}, u32[]{:S(2)}) %collective-permute-start.17) | collective-permute-done | bytes 65568 | tf_op jit(solution)/shard_map/ppermute | solution.py:529
  73.9 0.9 collective-permute-start.22
  74.8 0.4 shard_map.71.refs_1_
  75.2 0.4 shard_map.75.field_ref.refs_2_.u_ref
  75.6 0.3 shard_map.76.refs_0_
  76.0 1.3 %collective-permute-done.19.refs_8_ = f32[64,256]{1,0:T(8,128)S(1)} collective-permute-done((f32[64,256]{1,0:T(8,128)S(1)}, f32[64,256]{1,0:T(8,128)S(1)}, u32[]{:S(2)}, u32[]{:S(2)}) %collective-permute-start.19) | collective-permute-done | bytes 65568 | tf_op jit(solution)/shard_map/ppermute | solution.py:529
  77.3 0.1 collective-permute-done.20.refs_9_
  77.4 0.7 collective-permute-done.21.refs_10_
  78.2 0.5 collective-permute-done.22.refs_11_
  78.7 1.5 %shard_map.77 = (bf16[2,48,128,128]{3,2,1,0:T(8,128)(2,1)S(1)}, f32[64,512]{1,0:T(8,128)S(1)}, f32[64,512]{1,0:T(8,128)S(1)}) custom-call(s32[4,64]{1,0:T(4,128)S(1)} %bitcast.12, s32[2,64]{1,0:T(2,128)S(1)} %get-tuple-element.52.order_ref.order_near, bf16[2,48,128,128]{3,2,1,0:T(8,128)(2,1)S(1)} %shard_map.76.refs_0_, ...), custom_call_target="tpu_custom_call", output_to_operand_aliasing={{0}: (2, {})} | custom-call | tf_op jit(solution)/shard_map/pallas_call | solution.py:55
  80.2 3.8 %shard_map.79 = (f32[64,2048]{1,0:T(8,128)S(1)}, f32[64,2048]{1,0:T(8,128)S(1)}) custom-call(s32[4,64]{1,0:T(4,128)S(1)} %bitcast.13, s32[2,64]{1,0:T(2,128)S(1)} %get-tuple-element.52.order_ref.order_near, bf16[2,48,128,128]{3,2,1,0:T(8,128)(2,1)S(1)} %get-tuple-element.83.ext, bf16[64,256,256]{2,1,0:T(8,128)(2,1)S(1)} %shard_map.68.w_ref.refs_1_, ...), custom_call_target="tpu_custom_call" | custom-call | tf_op jit(solution)/shard_map/pallas_call | solution.py:55
  84.0 1.6 %collective-permute-start.29 = (f32[64,2048]{1,0:T(8,128)S(1)}, f32[64,2048]{1,0:T(8,128)S(1)}, u32[]{:S(2)}, u32[]{:S(2)}) collective-permute-start(f32[64,2048]{1,0:T(8,128)S(1)} %get-tuple-element.89.refs_7_), channel_id=1, source_target_pairs={{0,2},{1,3},{2,0},{3,1},{4,6},{5,7},{6,4},{7,5},{8,10},{9,11},{10,... | collective-permute-start | bytes 1572872 | tf_op jit(solution)/shard_map/ppermute | solution.py:546
  85.6 0.5 collective-permute-start.23
  86.1 2.2 %shard_map.78 = (f32[64,1024]{1,0:T(8,128)S(1)}, f32[64,1024]{1,0:T(8,128)S(1)}) custom-call(s32[4,64]{1,0:T(4,128)S(1)} %bitcast.14, s32[2,64]{1,0:T(2,128)S(1)} %get-tuple-element.52.order_ref.order_near, bf16[2,48,128,128]{3,2,1,0:T(8,128)(2,1)S(1)} %get-tuple-element.83.ext, bf16[64,256,256]{2,1,0:T(8,128)(2,1)S(1)} %shard_map.68.w_ref.refs_1_, ...), custom_call_target="tpu_custom_call" | custom-call | tf_op jit(solution)/shard_map/pallas_call | solution.py:55
  88.3 0.6 collective-permute-start.33
  88.9 1.4 %shard_map.80 = (f32[64,512]{1,0:T(8,128)S(1)}, f32[64,512]{1,0:T(8,128)S(1)}) custom-call(s32[4,64]{1,0:T(4,128)S(1)} %bitcast.15, s32[2,64]{1,0:T(2,128)S(1)} %get-tuple-element.52.order_ref.order_near, bf16[2,48,128,128]{3,2,1,0:T(8,128)(2,1)S(1)} %get-tuple-element.83.ext, bf16[64,256,256]{2,1,0:T(8,128)(2,1)S(1)} %shard_map.68.w_ref.refs_1_, ...), custom_call_target="tpu_custom_call" | custom-call | tf_op jit(solution)/shard_map/pallas_call | solution.py:55
  90.2 8.6 %collective-permute-done.29.refs_2_ = f32[64,2048]{1,0:T(8,128)S(1)} collective-permute-done((f32[64,2048]{1,0:T(8,128)S(1)}, f32[64,2048]{1,0:T(8,128)S(1)}, u32[]{:S(2)}, u32[]{:S(2)}) %collective-permute-start.29) | collective-permute-done | bytes 524320 | tf_op jit(solution)/shard_map/ppermute | solution.py:546
  98.9 0.5 collective-permute-start.26
  99.4 1.5 %collective-permute-start.27 = (f32[64,512]{1,0:T(8,128)S(1)}, f32[64,512]{1,0:T(8,128)S(1)}, u32[]{:S(2)}, u32[]{:S(2)}) collective-permute-start(f32[64,512]{1,0:T(8,128)S(1)} %get-tuple-element.90.refs_8_), channel_id=1, source_target_pairs={{0,2},{1,3},{2,0},{3,1},{4,6},{5,7},{6,4},{7,5},{8,10},{9,11},{10,... | collective-permute-start | bytes 393224 | tf_op jit(solution)/shard_map/ppermute | solution.py:546
  100.9 0.1 collective-permute-done.26.refs_12_
  101.0 0.1 collective-permute-start.24
  101.1 5.2 %collective-permute-done.27.refs_2_ = f32[64,512]{1,0:T(8,128)S(1)} collective-permute-done((f32[64,512]{1,0:T(8,128)S(1)}, f32[64,512]{1,0:T(8,128)S(1)}, u32[]{:S(2)}, u32[]{:S(2)}) %collective-permute-start.27) | collective-permute-done | bytes 131104 | tf_op jit(solution)/shard_map/ppermute | solution.py:546
  106.3 1.5 %collective-permute-start.31 = (f32[64,512]{1,0:T(8,128)S(1)}, f32[64,512]{1,0:T(8,128)S(1)}, u32[]{:S(2)}, u32[]{:S(2)}) collective-permute-start(f32[64,512]{1,0:T(8,128)S(1)} %get-tuple-element.87.refs_5_), channel_id=1, source_target_pairs={{0,2},{1,3},{2,0},{3,1},{4,6},{5,7},{6,4},{7,5},{8,10},{9,11},{10,... | collective-permute-start | bytes 393224 | tf_op jit(solution)/shard_map/ppermute | solution.py:546
  107.8 3.5 %collective-permute-done.31.refs_2_ = f32[64,512]{1,0:T(8,128)S(1)} collective-permute-done((f32[64,512]{1,0:T(8,128)S(1)}, f32[64,512]{1,0:T(8,128)S(1)}, u32[]{:S(2)}, u32[]{:S(2)}) %collective-permute-start.31) | collective-permute-done | bytes 131104 | tf_op jit(solution)/shard_map/ppermute | solution.py:546
  111.2 0.5 collective-permute-start.28
  111.7 1.2 shard_map.82.refs_8_.refs_5_.u_ref
  112.9 0.6 shard_map.81
  113.6 0.3 shard_map.83.refs_6_
  113.9 0.5 shard_map.84.refs_6_
  114.4 0.4 shard_map.85
  114.7 10.7 %all_to_all.5.sums_ref = f32[32,1,128]{2,1,0:T(1,128)S(1)} all-to-all(f32[32,1,128]{2,1,0:T(1,128)S(1)} %shard_map.85), channel_id=1, replica_groups=mesh['dom'=8,'samp'=4] {'dom','samp'}, dimensions={0} | all-to-all | bytes 32768 | tf_op jit(solution)/shard_map/all_to_all | solution.py:633
  125.5 1.2 update.1
  (45 shorter events, 0.1 us)
Async XLA Ops:
  0.0 18.2 %copy-start = (f32[64,4096]{1,0:T(8,128)S(1)}, f32[64,4096]{1,0:T(8,128)}, u32[]{:S(2)}) copy-start(f32[64,4096]{1,0:T(8,128)} %g_ref.9) | copy-start | bytes 3145732
  0.0 18.2 %copy-start.1 = (f32[64,4096]{1,0:T(8,128)S(1)}, f32[64,4096]{1,0:T(8,128)}, u32[]{:S(2)}) copy-start(f32[64,4096]{1,0:T(8,128)} %c_ref.9) | copy-start | bytes 3145732
  2.2 9.9 %collective-permute-start = (f32[64,256]{1,0:T(8,128)S(1)}, f32[64,256]{1,0:T(8,128)S(1)}, u32[]{:S(2)}, u32[]{:S(2)}) collective-permute-start(f32[64,256]{1,0:T(8,128)S(1)} %get-tuple-element.56), channel_id=1, source_target_pairs={{0,16},{4,20},{8,24},{12,28},{16,0},{20,4},{24,8},{28,12},{1,17},{... | collective-permute-start | bytes 196616 | tf_op jit(solution)/shard_map/ppermute | solution.py:529
  6.4 10.0 %collective-permute-start.1 = (f32[64,256]{1,0:T(8,128)S(1)}, f32[64,256]{1,0:T(8,128)S(1)}, u32[]{:S(2)}, u32[]{:S(2)}) collective-permute-start(f32[64,256]{1,0:T(8,128)S(1)} %get-tuple-element.57), channel_id=1, source_target_pairs={{0,20},{4,16},{8,28},{12,24},{16,4},{20,0},{24,12},{28,8},{1,21},{... | collective-permute-start | bytes 196616 | tf_op jit(solution)/shard_map/ppermute | solution.py:529
  7.7 16.1 %collective-permute-start.2 = (f32[64,256]{1,0:T(8,128)S(1)}, f32[64,256]{1,0:T(8,128)S(1)}, u32[]{:S(2)}, u32[]{:S(2)}) collective-permute-start(f32[64,256]{1,0:T(8,128)S(1)} %get-tuple-element.58), channel_id=1, source_target_pairs={{0,24},{4,28},{8,16},{12,20},{16,8},{20,12},{24,0},{28,4},{1,25},{... | collective-permute-start | bytes 196616 | tf_op jit(solution)/shard_map/ppermute | solution.py:529
  11.3 12.5 %collective-permute-start.3 = (f32[64,256]{1,0:T(8,128)S(1)}, f32[64,256]{1,0:T(8,128)S(1)}, u32[]{:S(2)}, u32[]{:S(2)}) collective-permute-start(f32[64,256]{1,0:T(8,128)S(1)} %get-tuple-element.59), channel_id=1, source_target_pairs={{0,28},{4,24},{8,20},{12,16},{16,12},{20,8},{24,4},{28,0},{1,29},{... | collective-permute-start | bytes 196616 | tf_op jit(solution)/shard_map/ppermute | solution.py:529
  11.3 12.6 %collective-permute-start.4 = (f32[64,256]{1,0:T(8,128)S(1)}, f32[64,256]{1,0:T(8,128)S(1)}, u32[]{:S(2)}, u32[]{:S(2)}) collective-permute-start(f32[64,256]{1,0:T(8,128)S(1)} %get-tuple-element.60), channel_id=1, source_target_pairs={{0,12},{4,8},{8,4},{12,0},{16,28},{20,24},{24,20},{28,16},{1,13},{... | collective-permute-start | bytes 196616 | tf_op jit(solution)/shard_map/ppermute | solution.py:529
  12.2 11.7 %collective-permute-start.5 = (f32[64,256]{1,0:T(8,128)S(1)}, f32[64,256]{1,0:T(8,128)S(1)}, u32[]{:S(2)}, u32[]{:S(2)}) collective-permute-start(f32[64,256]{1,0:T(8,128)S(1)} %get-tuple-element.61), channel_id=1, source_target_pairs={{0,8},{4,12},{8,0},{12,4},{16,24},{20,28},{24,16},{28,20},{1,9},{5... | collective-permute-start | bytes 196616 | tf_op jit(solution)/shard_map/ppermute | solution.py:529
  16.4 7.5 %collective-permute-start.6 = (f32[64,256]{1,0:T(8,128)S(1)}, f32[64,256]{1,0:T(8,128)S(1)}, u32[]{:S(2)}, u32[]{:S(2)}) collective-permute-start(f32[64,256]{1,0:T(8,128)S(1)} %get-tuple-element.62), channel_id=1, source_target_pairs={{0,4},{4,0},{8,12},{12,8},{16,20},{20,16},{24,28},{28,24},{1,5},{5... | collective-permute-start | bytes 196616 | tf_op jit(solution)/shard_map/ppermute | solution.py:529
  20.6 3.2 %copy-start.2 = (s32[64,4]{0,1:T(4,128)S(1)}, s32[64,4]{0,1:T(4,128)}, u32[]{:S(2)}) copy-start(s32[64,4]{0,1:T(4,128)} %param.10) | copy-start | bytes 3076
  20.6 7.2 %slice-start = ((s8[8388608]{0:T(1024)(128)(4,1)}), s8[4194304]{0:T(1024)(128)(4,1)S(1)}, s32[]{:S(2)}) async-start(s8[8388608]{0:T(1024)(128)(4,1)} %bitcast.6), calls=%async_computation.1 | async-start | bytes 8388608
  23.9 4.0 %slice-start.1 = ((s8[8388608]{0:T(1024)(128)(4,1)}), s8[4194304]{0:T(1024)(128)(4,1)S(1)}, s32[]{:S(2)}) async-start(s8[8388608]{0:T(1024)(128)(4,1)} %bitcast.6), calls=%async_computation.2 | async-start | bytes 8388608
  29.3 30.8 %copy-start.3 = (s32[1,8,4]{1,2,0:T(4,128)S(1)}, s32[1,8,4]{1,2,0:T(4,128)}, u32[]{:S(2)}) copy-start(s32[1,8,4]{1,2,0:T(4,128)} %param.11) | copy-start | bytes 388
  33.1 16.2 %collective-permute-start.8 = (f32[64,2304]{1,0:T(8,128)S(1)}, f32[64,2304]{1,0:T(8,128)S(1)}, u32[]{:S(2)}, u32[]{:S(2)}) collective-permute-start(f32[64,2304]{1,0:T(8,128)S(1)} %get-tuple-element.67.refs_2_), channel_id=1, source_target_pairs={{0,2},{1,3},{2,0},{3,1},{4,6},{5,7},{6,4},{7,5},{8,10},{9,11},{10,... | collective-permute-start | bytes 1769480 | tf_op jit(solution)/shard_map/ppermute | solution.py:546
  34.6 18.1 %collective-permute-start.14 = (f32[64,1280]{1,0:T(8,128)S(1)}, f32[64,1280]{1,0:T(8,128)S(1)}, u32[]{:S(2)}, u32[]{:S(2)}) collective-permute-start(f32[64,1280]{1,0:T(8,128)S(1)} %get-tuple-element.71.refs_4_), channel_id=1, source_target_pairs={{0,2},{1,3},{2,0},{3,1},{4,6},{5,7},{6,4},{7,5},{8,10},{9,11},{10,... | collective-permute-start | bytes 983048 | tf_op jit(solution)/shard_map/ppermute | solution.py:546
  35.2 35.0 %collective-permute-start.7 = (f32[64,2304]{1,0:T(8,128)S(1)}, f32[64,2304]{1,0:T(8,128)S(1)}, u32[]{:S(2)}, u32[]{:S(2)}) collective-permute-start(f32[64,2304]{1,0:T(8,128)S(1)} %get-tuple-element.67.refs_2_), channel_id=1, source_target_pairs={{0,1},{1,0},{2,3},{3,2},{4,5},{5,4},{6,7},{7,6},{8,9},{9,8},{10,11... | collective-permute-start | bytes 1769480 | tf_op jit(solution)/shard_map/ppermute | solution.py:547
  49.3 24.6 %collective-permute-start.9 = (f32[64,2304]{1,0:T(8,128)S(1)}, f32[64,2304]{1,0:T(8,128)S(1)}, u32[]{:S(2)}, u32[]{:S(2)}) collective-permute-start(f32[64,2304]{1,0:T(8,128)S(1)} %collective-permute-done.8.refs_2_), channel_id=1, source_target_pairs={{0,1},{1,0},{2,3},{3,2},{4,5},{5,4},{6,7},{7,6},{8,9},{9,8},{10,11... | collective-permute-start | bytes 1769480 | tf_op jit(solution)/shard_map/ppermute | solution.py:559
  49.3 3.5 %collective-permute-start.10 = (f32[64,512]{1,0:T(8,128)S(1)}, f32[64,512]{1,0:T(8,128)S(1)}, u32[]{:S(2)}, u32[]{:S(2)}) collective-permute-start(f32[64,512]{1,0:T(8,128)S(1)} %get-tuple-element.70.refs_3_), channel_id=1, source_target_pairs={{0,1},{1,0},{2,3},{3,2},{4,5},{5,4},{6,7},{7,6},{8,9},{9,8},{10,11... | collective-permute-start | bytes 393224 | tf_op jit(solution)/shard_map/ppermute | solution.py:547
  49.8 9.5 %collective-permute-start.11 = (f32[64,1280]{1,0:T(8,128)S(1)}, f32[64,1280]{1,0:T(8,128)S(1)}, u32[]{:S(2)}, u32[]{:S(2)}) collective-permute-start(f32[64,1280]{1,0:T(8,128)S(1)} %get-tuple-element.71.refs_4_), channel_id=1, source_target_pairs={{0,1},{1,0},{2,3},{3,2},{4,5},{5,4},{6,7},{7,6},{8,9},{9,8},{10,11... | collective-permute-start | bytes 983048 | tf_op jit(solution)/shard_map/ppermute | solution.py:547
  52.8 7.3 %collective-permute-start.15 = (f32[64,1280]{1,0:T(8,128)S(1)}, f32[64,1280]{1,0:T(8,128)S(1)}, u32[]{:S(2)}, u32[]{:S(2)}) collective-permute-start(f32[64,1280]{1,0:T(8,128)S(1)} %collective-permute-done.14.refs_5_), channel_id=1, source_target_pairs={{0,1},{1,0},{2,3},{3,2},{4,5},{5,4},{6,7},{7,6},{8,9},{9,8},{10,11... | collective-permute-start | bytes 983048 | tf_op jit(solution)/shard_map/ppermute | solution.py:559
  52.8 5.9 %collective-permute-start.12 = (f32[64,512]{1,0:T(8,128)S(1)}, f32[64,512]{1,0:T(8,128)S(1)}, u32[]{:S(2)}, u32[]{:S(2)}) collective-permute-start(f32[64,512]{1,0:T(8,128)S(1)} %get-tuple-element.70.refs_3_), channel_id=1, source_target_pairs={{0,2},{1,3},{2,0},{3,1},{4,6},{5,7},{6,4},{7,5},{8,10},{9,11},{10,... | collective-permute-start | bytes 393224 | tf_op jit(solution)/shard_map/ppermute | solution.py:546
  58.7 1.3 %collective-permute-start.13 = (f32[64,512]{1,0:T(8,128)S(1)}, f32[64,512]{1,0:T(8,128)S(1)}, u32[]{:S(2)}, u32[]{:S(2)}) collective-permute-start(f32[64,512]{1,0:T(8,128)S(1)} %collective-permute-done.12.refs_2_), channel_id=1, source_target_pairs={{0,1},{1,0},{2,3},{3,2},{4,5},{5,4},{6,7},{7,6},{8,9},{9,8},{10,11... | collective-permute-start | bytes 393224 | tf_op jit(solution)/shard_map/ppermute | solution.py:559
  61.2 9.0 %collective-permute-start.16 = (f32[64,256]{1,0:T(8,128)S(1)}, f32[64,256]{1,0:T(8,128)S(1)}, u32[]{:S(2)}, u32[]{:S(2)}) collective-permute-start(f32[64,256]{1,0:T(8,128)S(1)} %get-tuple-element.75), channel_id=1, source_target_pairs={{0,16},{4,20},{8,24},{12,28},{16,0},{20,4},{24,8},{28,12},{1,17},{... | collective-permute-start | bytes 196616 | tf_op jit(solution)/shard_map/ppermute | solution.py:529
  64.2 9.7 %collective-permute-start.17 = (f32[64,256]{1,0:T(8,128)S(1)}, f32[64,256]{1,0:T(8,128)S(1)}, u32[]{:S(2)}, u32[]{:S(2)}) collective-permute-start(f32[64,256]{1,0:T(8,128)S(1)} %get-tuple-element.76), channel_id=1, source_target_pairs={{0,20},{4,16},{8,28},{12,24},{16,4},{20,0},{24,12},{28,8},{1,21},{... | collective-permute-start | bytes 196616 | tf_op jit(solution)/shard_map/ppermute | solution.py:529
  65.3 10.6 %collective-permute-start.18 = (f32[64,256]{1,0:T(8,128)S(1)}, f32[64,256]{1,0:T(8,128)S(1)}, u32[]{:S(2)}, u32[]{:S(2)}) collective-permute-start(f32[64,256]{1,0:T(8,128)S(1)} %get-tuple-element.77), channel_id=1, source_target_pairs={{0,24},{4,28},{8,16},{12,20},{16,8},{20,12},{24,0},{28,4},{1,25},{... | collective-permute-start | bytes 196616 | tf_op jit(solution)/shard_map/ppermute | solution.py:529
  70.1 7.2 %collective-permute-start.19 = (f32[64,256]{1,0:T(8,128)S(1)}, f32[64,256]{1,0:T(8,128)S(1)}, u32[]{:S(2)}, u32[]{:S(2)}) collective-permute-start(f32[64,256]{1,0:T(8,128)S(1)} %get-tuple-element.78), channel_id=1, source_target_pairs={{0,28},{4,24},{8,20},{12,16},{16,12},{20,8},{24,4},{28,0},{1,29},{... | collective-permute-start | bytes 196616 | tf_op jit(solution)/shard_map/ppermute | solution.py:529
  70.1 7.3 %collective-permute-start.20 = (f32[64,256]{1,0:T(8,128)S(1)}, f32[64,256]{1,0:T(8,128)S(1)}, u32[]{:S(2)}, u32[]{:S(2)}) collective-permute-start(f32[64,256]{1,0:T(8,128)S(1)} %get-tuple-element.79), channel_id=1, source_target_pairs={{0,12},{4,8},{8,4},{12,0},{16,28},{20,24},{24,20},{28,16},{1,13},{... | collective-permute-start | bytes 196616 | tf_op jit(solution)/shard_map/ppermute | solution.py:529
  73.9 4.3 %collective-permute-start.21 = (f32[64,256]{1,0:T(8,128)S(1)}, f32[64,256]{1,0:T(8,128)S(1)}, u32[]{:S(2)}, u32[]{:S(2)}) collective-permute-start(f32[64,256]{1,0:T(8,128)S(1)} %get-tuple-element.80), channel_id=1, source_target_pairs={{0,8},{4,12},{8,0},{12,4},{16,24},{20,28},{24,16},{28,20},{1,9},{5... | collective-permute-start | bytes 196616 | tf_op jit(solution)/shard_map/ppermute | solution.py:529
  73.9 4.8 %collective-permute-start.22 = (f32[64,256]{1,0:T(8,128)S(1)}, f32[64,256]{1,0:T(8,128)S(1)}, u32[]{:S(2)}, u32[]{:S(2)}) collective-permute-start(f32[64,256]{1,0:T(8,128)S(1)} %get-tuple-element.81), channel_id=1, source_target_pairs={{0,4},{4,0},{8,12},{12,8},{16,20},{20,16},{24,28},{28,24},{1,5},{5... | collective-permute-start | bytes 196616 | tf_op jit(solution)/shard_map/ppermute | solution.py:529
  84.0 14.9 %collective-permute-start.29 = (f32[64,2048]{1,0:T(8,128)S(1)}, f32[64,2048]{1,0:T(8,128)S(1)}, u32[]{:S(2)}, u32[]{:S(2)}) collective-permute-start(f32[64,2048]{1,0:T(8,128)S(1)} %get-tuple-element.89.refs_7_), channel_id=1, source_target_pairs={{0,2},{1,3},{2,0},{3,1},{4,6},{5,7},{6,4},{7,5},{8,10},{9,11},{10,... | collective-permute-start | bytes 1572872 | tf_op jit(solution)/shard_map/ppermute | solution.py:546
  85.6 27.3 %collective-permute-start.25 = (f32[64,2048]{1,0:T(8,128)S(1)}, f32[64,2048]{1,0:T(8,128)S(1)}, u32[]{:S(2)}, u32[]{:S(2)}) collective-permute-start(f32[64,2048]{1,0:T(8,128)S(1)} %get-tuple-element.89.refs_7_), channel_id=1, source_target_pairs={{0,1},{1,0},{2,3},{3,2},{4,5},{5,4},{6,7},{7,6},{8,9},{9,8},{10,11... | collective-permute-start | bytes 1572872 | tf_op jit(solution)/shard_map/ppermute | solution.py:547
  85.6 13.8 %collective-permute-start.23 = (f32[64,512]{1,0:T(8,128)S(1)}, f32[64,512]{1,0:T(8,128)S(1)}, u32[]{:S(2)}, u32[]{:S(2)}) collective-permute-start(f32[64,512]{1,0:T(8,128)S(1)} %get-tuple-element.87.refs_5_), channel_id=1, source_target_pairs={{0,1},{1,0},{2,3},{3,2},{4,5},{5,4},{6,7},{7,6},{8,9},{9,8},{10,11... | collective-permute-start | bytes 393224 | tf_op jit(solution)/shard_map/ppermute | solution.py:547
  88.3 19.5 %collective-permute-start.33 = (f32[64,1024]{1,0:T(8,128)S(1)}, f32[64,1024]{1,0:T(8,128)S(1)}, u32[]{:S(2)}, u32[]{:S(2)}) collective-permute-start(f32[64,1024]{1,0:T(8,128)S(1)} %get-tuple-element.88.refs_6_), channel_id=1, source_target_pairs={{0,2},{1,3},{2,0},{3,1},{4,6},{5,7},{6,4},{7,5},{8,10},{9,11},{10,... | collective-permute-start | bytes 786440 | tf_op jit(solution)/shard_map/ppermute | solution.py:546
  98.9 15.0 %collective-permute-start.30 = (f32[64,2048]{1,0:T(8,128)S(1)}, f32[64,2048]{1,0:T(8,128)S(1)}, u32[]{:S(2)}, u32[]{:S(2)}) collective-permute-start(f32[64,2048]{1,0:T(8,128)S(1)} %collective-permute-done.29.refs_2_), channel_id=1, source_target_pairs={{0,1},{1,0},{2,3},{3,2},{4,5},{5,4},{6,7},{7,6},{8,9},{9,8},{10,11... | collective-permute-start | bytes 1572872 | tf_op jit(solution)/shard_map/ppermute | solution.py:559
  98.9 2.1 %collective-permute-start.26 = (f32[64,512]{1,0:T(8,128)S(1)}, f32[64,512]{1,0:T(8,128)S(1)}, u32[]{:S(2)}, u32[]{:S(2)}) collective-permute-start(f32[64,512]{1,0:T(8,128)S(1)} %get-tuple-element.90.refs_8_), channel_id=1, source_target_pairs={{0,1},{1,0},{2,3},{3,2},{4,5},{5,4},{6,7},{7,6},{8,9},{9,8},{10,11... | collective-permute-start | bytes 393224 | tf_op jit(solution)/shard_map/ppermute | solution.py:547
  99.4 6.9 %collective-permute-start.27 = (f32[64,512]{1,0:T(8,128)S(1)}, f32[64,512]{1,0:T(8,128)S(1)}, u32[]{:S(2)}, u32[]{:S(2)}) collective-permute-start(f32[64,512]{1,0:T(8,128)S(1)} %get-tuple-element.90.refs_8_), channel_id=1, source_target_pairs={{0,2},{1,3},{2,0},{3,1},{4,6},{5,7},{6,4},{7,5},{8,10},{9,11},{10,... | collective-permute-start | bytes 393224 | tf_op jit(solution)/shard_map/ppermute | solution.py:546
  101.0 10.3 %collective-permute-start.24 = (f32[64,1024]{1,0:T(8,128)S(1)}, f32[64,1024]{1,0:T(8,128)S(1)}, u32[]{:S(2)}, u32[]{:S(2)}) collective-permute-start(f32[64,1024]{1,0:T(8,128)S(1)} %get-tuple-element.88.refs_6_), channel_id=1, source_target_pairs={{0,1},{1,0},{2,3},{3,2},{4,5},{5,4},{6,7},{7,6},{8,9},{9,8},{10,11... | collective-permute-start | bytes 786440 | tf_op jit(solution)/shard_map/ppermute | solution.py:547
  106.3 5.0 %collective-permute-start.31 = (f32[64,512]{1,0:T(8,128)S(1)}, f32[64,512]{1,0:T(8,128)S(1)}, u32[]{:S(2)}, u32[]{:S(2)}) collective-permute-start(f32[64,512]{1,0:T(8,128)S(1)} %get-tuple-element.87.refs_5_), channel_id=1, source_target_pairs={{0,2},{1,3},{2,0},{3,1},{4,6},{5,7},{6,4},{7,5},{8,10},{9,11},{10,... | collective-permute-start | bytes 393224 | tf_op jit(solution)/shard_map/ppermute | solution.py:546
  107.8 5.8 %collective-permute-start.34 = (f32[64,1024]{1,0:T(8,128)S(1)}, f32[64,1024]{1,0:T(8,128)S(1)}, u32[]{:S(2)}, u32[]{:S(2)}) collective-permute-start(f32[64,1024]{1,0:T(8,128)S(1)} %collective-permute-done.33.refs_5_), channel_id=1, source_target_pairs={{0,1},{1,0},{2,3},{3,2},{4,5},{5,4},{6,7},{7,6},{8,9},{9,8},{10,11... | collective-permute-start | bytes 786440 | tf_op jit(solution)/shard_map/ppermute | solution.py:559
  111.2 2.3 %collective-permute-start.32 = (f32[64,512]{1,0:T(8,128)S(1)}, f32[64,512]{1,0:T(8,128)S(1)}, u32[]{:S(2)}, u32[]{:S(2)}) collective-permute-start(f32[64,512]{1,0:T(8,128)S(1)} %collective-permute-done.31.refs_2_), channel_id=1, source_target_pairs={{0,1},{1,0},{2,3},{3,2},{4,5},{5,4},{6,7},{7,6},{8,9},{9,8},{10,11... | collective-permute-start | bytes 393224 | tf_op jit(solution)/shard_map/ppermute | solution.py:559
  111.2 3.1 %collective-permute-start.28 = (f32[64,512]{1,0:T(8,128)S(1)}, f32[64,512]{1,0:T(8,128)S(1)}, u32[]{:S(2)}, u32[]{:S(2)}) collective-permute-start(f32[64,512]{1,0:T(8,128)S(1)} %collective-permute-done.27.refs_2_), channel_id=1, source_target_pairs={{0,1},{1,0},{2,3},{3,2},{4,5},{5,4},{6,7},{7,6},{8,9},{9,8},{10,11... | collective-permute-start | bytes 393224 | tf_op jit(solution)/shard_map/ppermute | solution.py:559

commit v3 on v2

--- a/solution.py
+++ b/solution.py
@@ -10,7 +10,7 @@
 
 LANES = 128
 HALF = 64
-GROUP = 4
+GROUP = 12
 
 
 LIMIT = 24 * 1024 * 1024
@@ -213,10 +213,10 @@
         copies.append(pltpu.make_async_copy(field_hbm.at[:, inside], field_ref.at[:, inside], field_sem.at[n]))
         copies[-1].start()
     table.wait()
-    order_rows(domains, send_ref, order_ref)
     for copy in copies:
         copy.wait()
     gather_all(domains, send_ref, field_ref, out_refs)
+    order_rows(domains, send_ref, order_ref)
 
 
 def gather(send, field, rows, domains, outputs):
@@ -271,6 +271,11 @@
         out_ref[:, inside] = pair_tile(u_ref, order_ref[1, 2 * i], order_ref[1, 2 * i + 1])
 
 
+def first_extend_kernel(groups, field_ref, ext, near_ref, far_ref):
+    extend_kernel(field_ref, ext)
+    tables_kernel(groups, near_ref, far_ref)
+
+
 def extend_kernel(field_ref, ext):
     for i in range(field_ref.shape[1] // LANES):
         store_tile(ext, i, field_ref[:, i * LANES : (i + 1) * LANES])
@@ -333,9 +338,12 @@
         both = full[:, :width] + full[:, width:]
         return both[:samples] + both[samples:]
 
+    count = p_ref.shape[1] // HALF
+    group = max(n for n in range(2, GROUP + 1, 2) if count % n == 0)
+
     def block(step, carry):
-        for pair in range(GROUP // 2):
-            row = step * GROUP + 2 * pair
+        for pair in range(group // 2):
+            row = step * group + 2 * pair
             first = row_product(first_row + row)
             second = row_product(first_row + row + 1)
             direct = jnp.where(low_lane, first, pltpu.roll(second, HALF, 1))
@@ -346,7 +354,7 @@
             q_ref[:, here] = charge + c_term
         return carry
 
-    lax.fori_loop(0, p_ref.shape[1] // (GROUP * HALF), block, 0)
+    lax.fori_loop(0, count // group, block, 0)
 
 
 def permuted_product(first_row, base_row, cols_ref, order_ref, ext, w_ref, g_ref, c_ref, p_ref, q_ref):
@@ -493,7 +501,7 @@
 def chunk_sizes(rows, domains, slots):
     unit = rows // 8
     early = (domains - 1) * slots if few(domains) else 3 * unit
-    return [unit, early - unit, rows - early], [unit, 2 * unit, 4 * unit, unit]
+    return [unit, early - unit, rows - early], [unit, rows // 16 * 3, 2 * unit, rows // 16 * 5, unit]
 
 
 def body(residual, conductance, capacitance, stamps, block_cols, send_blocks):
@@ -561,13 +569,16 @@
 
     field, order, *outgoing = gather(send, residual, rows, domains, outgoing_shapes)
     incoming = exchange(outgoing)
-    near_matrix, far_matrix = kernel_call(
-        functools.partial(tables_kernel, groups),
-        (),
-        [((2 * samples, 2 * samples), jnp.bfloat16), ((2 * samples, count * samples), jnp.bfloat16)],
+    blocks = stamps.reshape(rows, per_entry * width, 2 * width)
+    ext, near_matrix, far_matrix = kernel_call(
+        functools.partial(first_extend_kernel, groups),
+        (field,),
+        [
+            ext_shape,
+            ((2 * samples, 2 * samples), jnp.bfloat16),
+            ((2 * samples, count * samples), jnp.bfloat16),
+        ],
     )
-    blocks = stamps.reshape(rows, per_entry * width, 2 * width)
-    (ext,) = kernel_call(extend_kernel, (field,), [ext_shape])
     weights = None
     own = []
     for n, (low, high) in enumerate(((0, early), (early, rows))):

time: 127 us -> 127 us (level)
  Pallas kernels: 33.3 us -> 30.1 us
  local copies, waits for them, and re-layouts: 0.04 us -> 2.49 us
    pallas_call x22, Pallas kernels: 26.7 us -> 23.3 us  [kernel_call(): pl.pallas_call(kernel, in_specs=specs, out_specs=[scalars() if number els...]
    unnamed x12 -> x16, local copies, waits for them, and re-layouts: 0.04 us -> 2.49 us
    ppermute x7 -> x8, waiting for transfers between devices: 38.7 us -> 37.4 us  [spread(): lax.ppermute(q, 'samp', [(i, (i + k) % groups) for i in range(groups)])]
    ppermute x7 -> x8, starting transfers between devices: 8.73 us -> 9.32 us  [spread(): lax.ppermute(q, 'samp', [(i, (i + k) % groups) for i in range(groups)])]
  transfers between devices with their start and end apart: 35 -> 38, of which waited for: 14 -> 14; matrix products, arithmetic and copies ran while one was open for 0% -> 0% of each run, Pallas kernels for 12% -> 14%
where the time goes in v3:
time: 127 us
  waiting for transfers between devices  46.2 us (36%)
  starting transfers between devices  35.5 us (28%)
  Pallas kernels  30.1 us (24%)
  blocking collectives  11.8 us (9%)
  local copies, waits for them, and re-layouts  2.49 us (2%)
    ppermute x8, waiting for transfers between devices, spread(): lax.ppermute(q, 'samp', [(i, (i + k) % groups) for i in range(groups)])  37.4 us
    ppermute x14, starting transfers between devices, exchange(): lax.ppermute(x, 'dom', [(i, i ^ k) for i in range(domains)])  24.1 us
    pallas_call x22, Pallas kernels, kernel_call(): pl.pallas_call(kernel, in_specs=specs, out_specs=[scalars() if number els...  23.3 us
    all_to_all x1, blocking collectives, body(): lax.all_to_all(sums, ('dom', 'samp'), split_axis=0, concat_axis=0, tiled=...  11.8 us
    ppermute x8, starting transfers between devices, spread(): lax.ppermute(q, 'samp', [(i, (i + k) % groups) for i in range(groups)])  9.32 us
    ppermute x14, waiting for transfers between devices, exchange(): lax.ppermute(x, 'dom', [(i, i ^ k) for i in range(domains)])  7.82 us
    pallas_call x1, Pallas kernels, fetch(): pl.pallas_call(fetch_kernel, in_specs=[scalars(), pl.BlockSpec(memory_spa...  3.15 us
  transfers between devices with their start and end apart: 38, of which 14 were waited for; matrix products, arithmetic and copies ran while one was open for 0% of the time, Pallas kernels for 14%

profile of v3, /device:TPU:0, one launch (start us, length us, event | category | flops | bytes accessed | tf_op | source)
XLA Modules:
  0.0 126.7 jit_solution(901507201390797834)
XLA Ops:
  0.0 2.4 %gather.1 = (f32[64,4096]{1,0:T(8,128)S(1)}, s32[2,64]{1,0:T(2,128)S(1)}, f32[64,256]{1,0:T(8,128)S(1)}, f32[64,256]{1,0:T(8,128)S(1)}, f32[64,256]{1,0:T(8,128)...) custom-call(s32[4,8]{1,0:T(4,128)} %bitcast.17, ...), custom_call_target="tpu_custom_call" | custom-call | tf_op jit(solution)/shard_map/gather/pallas_call | solution.py:224
  2.4 4.1 %collective-permute-start = (f32[64,256]{1,0:T(8,128)S(1)}, f32[64,256]{1,0:T(8,128)S(1)}, u32[]{:S(2)}, u32[]{:S(2)}) collective-permute-start(f32[64,256]{1,0:T(8,128)S(1)} %get-tuple-element.61), channel_id=1, source_target_pairs={{0,16},{4,20},{8,24},{12,28},{16,0},{20,4},{24,8},{28,12},{1,17},{... | collective-permute-start | bytes 196616 | tf_op jit(solution)/shard_map/ppermute | solution.py:537
  6.6 1.3 %collective-permute-start.1 = (f32[64,256]{1,0:T(8,128)S(1)}, f32[64,256]{1,0:T(8,128)S(1)}, u32[]{:S(2)}, u32[]{:S(2)}) collective-permute-start(f32[64,256]{1,0:T(8,128)S(1)} %get-tuple-element.62), channel_id=1, source_target_pairs={{0,20},{4,16},{8,28},{12,24},{16,4},{20,0},{24,12},{28,8},{1,21},{... | collective-permute-start | bytes 196616 | tf_op jit(solution)/shard_map/ppermute | solution.py:537
  7.9 3.6 %collective-permute-start.2 = (f32[64,256]{1,0:T(8,128)S(1)}, f32[64,256]{1,0:T(8,128)S(1)}, u32[]{:S(2)}, u32[]{:S(2)}) collective-permute-start(f32[64,256]{1,0:T(8,128)S(1)} %get-tuple-element.63), channel_id=1, source_target_pairs={{0,24},{4,28},{8,16},{12,20},{16,8},{20,12},{24,0},{28,4},{1,25},{... | collective-permute-start | bytes 196616 | tf_op jit(solution)/shard_map/ppermute | solution.py:537
  11.5 0.9 collective-permute-start.4
  12.4 2.2 %collective-permute-start.5 = (f32[64,256]{1,0:T(8,128)S(1)}, f32[64,256]{1,0:T(8,128)S(1)}, u32[]{:S(2)}, u32[]{:S(2)}) collective-permute-start(f32[64,256]{1,0:T(8,128)S(1)} %get-tuple-element.66), channel_id=1, source_target_pairs={{0,8},{4,12},{8,0},{12,4},{16,24},{20,28},{24,16},{28,20},{1,9},{5... | collective-permute-start | bytes 196616 | tf_op jit(solution)/shard_map/ppermute | solution.py:537
  14.6 2.0 %collective-permute-done.1.refs_5_ = f32[64,256]{1,0:T(8,128)S(1)} collective-permute-done((f32[64,256]{1,0:T(8,128)S(1)}, f32[64,256]{1,0:T(8,128)S(1)}, u32[]{:S(2)}, u32[]{:S(2)}) %collective-permute-start.1) | collective-permute-done | bytes 65568 | tf_op jit(solution)/shard_map/ppermute | solution.py:537
  16.6 1.5 %collective-permute-start.6 = (f32[64,256]{1,0:T(8,128)S(1)}, f32[64,256]{1,0:T(8,128)S(1)}, u32[]{:S(2)}, u32[]{:S(2)}) collective-permute-start(f32[64,256]{1,0:T(8,128)S(1)} %get-tuple-element.67), channel_id=1, source_target_pairs={{0,4},{4,0},{8,12},{12,8},{16,20},{20,16},{24,28},{28,24},{1,5},{5... | collective-permute-start | bytes 196616 | tf_op jit(solution)/shard_map/ppermute | solution.py:537
  18.1 0.8 shard_map.64
  18.9 1.2 copy-done
  20.1 1.2 copy-done.2
  21.3 1.1 shard_map.65
  22.4 1.3 shard_map.68
  23.7 3.2 %prepare_0.1.refs_1_.refs_0_.w_ref = bf16[64,256,256]{2,1,0:T(8,128)(2,1)S(1)} custom-call(s32[2,64]{1,0:T(2,128)S(1)} %get-tuple-element.57.order_ref.order_near, f32[64,256,128]{2,1,0:T(8,128)} %bitcast.5), custom_call_target="tpu_custom_call" | custom-call | tf_op jit(solution)/shard_map/prepare_0/pallas_call | solution.py:128
  27.0 1.2 shard_map.66
  28.1 1.9 %shard_map.71 = (f32[64,1280]{1,0:T(8,128)S(1)}, f32[64,1280]{1,0:T(8,128)S(1)}) custom-call(s32[4,64]{1,0:T(4,128)S(1)} %bitcast.10, s32[2,64]{1,0:T(2,128)S(1)} %get-tuple-element.57.order_ref.order_near, bf16[2,48,128,128]{3,2,1,0:T(8,128)(2,1)S(1)} %get-tuple-element.68.ext, bf16[64,256,256]{2,1,0:T(8,128)(2,1)S(1)} %prepare_0.1.refs_1_.refs_0_.w_ref, ...), custom_call_target="tpu_custom_call" | custom-call | tf_op jit(solution)/shard_map/pallas_call | solution.py:55
  30.1 1.4 %shard_map.67.w_ref.refs_1_ = bf16[64,256,256]{2,1,0:T(8,128)(2,1)S(1)} custom-call(s32[2,64]{1,0:T(2,128)S(1)} %get-tuple-element.57.order_ref.order_near, f32[64,256,128]{2,1,0:T(8,128)S(1)} %bitcast.8, bf16[64,256,256]{2,1,0:T(8,128)(2,1)S(1)} %prepare_0.1.refs_1_.refs_0_.w_ref), custom_call_target="tpu_custom_call", output_to_operand_aliasing={{}: (2, {})} | custom-call | tf_op jit(solution)/shard_map/pallas_call | solution.py:55
  31.5 2.5 %shard_map.69 = (f32[64,2304]{1,0:T(8,128)S(1)}, f32[64,2304]{1,0:T(8,128)S(1)}) custom-call(s32[4,64]{1,0:T(4,128)S(1)} %bitcast.11, s32[2,64]{1,0:T(2,128)S(1)} %get-tuple-element.57.order_ref.order_near, bf16[2,48,128,128]{3,2,1,0:T(8,128)(2,1)S(1)} %get-tuple-element.68.ext, bf16[64,256,256]{2,1,0:T(8,128)(2,1)S(1)} %shard_map.67.w_ref.refs_1_, ...), custom_call_target="tpu_custom_call" | custom-call | tf_op jit(solution)/shard_map/pallas_call | solution.py:55
  34.0 1.6 %collective-permute-start.8 = (f32[64,2304]{1,0:T(8,128)S(1)}, f32[64,2304]{1,0:T(8,128)S(1)}, u32[]{:S(2)}, u32[]{:S(2)}) collective-permute-start(f32[64,2304]{1,0:T(8,128)S(1)} %get-tuple-element.72.refs_2_), channel_id=1, source_target_pairs={{0,2},{1,3},{2,0},{3,1},{4,6},{5,7},{6,4},{7,5},{8,10},{9,11},{10,... | collective-permute-start | bytes 1769480 | tf_op jit(solution)/shard_map/ppermute | solution.py:554
  35.5 0.5 collective-permute-start.14
  36.1 14.1 %collective-permute-done.8.refs_2_ = f32[64,2304]{1,0:T(8,128)S(1)} collective-permute-done((f32[64,2304]{1,0:T(8,128)S(1)}, f32[64,2304]{1,0:T(8,128)S(1)}, u32[]{:S(2)}, u32[]{:S(2)}) %collective-permute-start.8) | collective-permute-done | bytes 589856 | tf_op jit(solution)/shard_map/ppermute | solution.py:554
  50.2 0.5 collective-permute-start.10
  50.7 3.0 %collective-permute-done.14.refs_5_ = f32[64,1280]{1,0:T(8,128)S(1)} collective-permute-done((f32[64,1280]{1,0:T(8,128)S(1)}, f32[64,1280]{1,0:T(8,128)S(1)}, u32[]{:S(2)}, u32[]{:S(2)}) %collective-permute-start.14) | collective-permute-done | bytes 327712 | tf_op jit(solution)/shard_map/ppermute | solution.py:554
  53.7 1.5 %collective-permute-start.12 = (f32[64,512]{1,0:T(8,128)S(1)}, f32[64,512]{1,0:T(8,128)S(1)}, u32[]{:S(2)}, u32[]{:S(2)}) collective-permute-start(f32[64,512]{1,0:T(8,128)S(1)} %get-tuple-element.75.refs_3_), channel_id=1, source_target_pairs={{0,2},{1,3},{2,0},{3,1},{4,6},{5,7},{6,4},{7,5},{8,10},{9,11},{10,... | collective-permute-start | bytes 393224 | tf_op jit(solution)/shard_map/ppermute | solution.py:554
  55.2 4.4 %collective-permute-done.12.refs_2_ = f32[64,512]{1,0:T(8,128)S(1)} collective-permute-done((f32[64,512]{1,0:T(8,128)S(1)}, f32[64,512]{1,0:T(8,128)S(1)}, u32[]{:S(2)}, u32[]{:S(2)}) %collective-permute-start.12) | collective-permute-done | bytes 131104 | tf_op jit(solution)/shard_map/ppermute | solution.py:554
  59.6 0.3 shard_map.72
  59.9 1.0 collective-permute-done.13.refs_3_
  60.9 1.1 shard_map.73
  62.0 3.1 %collective-permute-start.16 = (f32[64,256]{1,0:T(8,128)S(1)}, f32[64,256]{1,0:T(8,128)S(1)}, u32[]{:S(2)}, u32[]{:S(2)}) collective-permute-start(f32[64,256]{1,0:T(8,128)S(1)} %get-tuple-element.80), channel_id=1, source_target_pairs={{0,16},{4,20},{8,24},{12,28},{16,0},{20,4},{24,8},{28,12},{1,17},{... | collective-permute-start | bytes 196616 | tf_op jit(solution)/shard_map/ppermute | solution.py:537
  65.1 1.1 collective-permute-start.17
  66.2 4.8 %collective-permute-start.18 = (f32[64,256]{1,0:T(8,128)S(1)}, f32[64,256]{1,0:T(8,128)S(1)}, u32[]{:S(2)}, u32[]{:S(2)}) collective-permute-start(f32[64,256]{1,0:T(8,128)S(1)} %get-tuple-element.82), channel_id=1, source_target_pairs={{0,24},{4,28},{8,16},{12,20},{16,8},{20,12},{24,0},{28,4},{1,25},{... | collective-permute-start | bytes 196616 | tf_op jit(solution)/shard_map/ppermute | solution.py:537
  71.0 0.6 collective-permute-start.20
  71.7 3.1 %collective-permute-done.17.refs_6_ = f32[64,256]{1,0:T(8,128)S(1)} collective-permute-done((f32[64,256]{1,0:T(8,128)S(1)}, f32[64,256]{1,0:T(8,128)S(1)}, u32[]{:S(2)}, u32[]{:S(2)}) %collective-permute-start.17) | collective-permute-done | bytes 65568 | tf_op jit(solution)/shard_map/ppermute | solution.py:537
  74.8 0.9 collective-permute-start.22
  75.7 0.4 shard_map.70.refs_1_
  76.1 0.4 shard_map.74.field_ref.refs_2_.u_ref
  76.5 0.3 shard_map.75.refs_0_
  76.9 1.3 %collective-permute-done.19.refs_8_ = f32[64,256]{1,0:T(8,128)S(1)} collective-permute-done((f32[64,256]{1,0:T(8,128)S(1)}, f32[64,256]{1,0:T(8,128)S(1)}, u32[]{:S(2)}, u32[]{:S(2)}) %collective-permute-start.19) | collective-permute-done | bytes 65568 | tf_op jit(solution)/shard_map/ppermute | solution.py:537
  78.3 0.7 collective-permute-done.21.refs_10_
  79.1 0.5 collective-permute-done.22.refs_11_
  79.6 1.2 shard_map.76
  80.9 1.2 shard_map.80
  82.1 0.6 collective-permute-start.27
  82.6 2.1 %shard_map.79 = (f32[64,1280]{1,0:T(8,128)S(1)}, f32[64,1280]{1,0:T(8,128)S(1)}) custom-call(s32[4,64]{1,0:T(4,128)S(1)} %bitcast.14, s32[2,64]{1,0:T(2,128)S(1)} %get-tuple-element.57.order_ref.order_near, bf16[2,48,128,128]{3,2,1,0:T(8,128)(2,1)S(1)} %get-tuple-element.88.ext, bf16[64,256,256]{2,1,0:T(8,128)(2,1)S(1)} %shard_map.67.w_ref.refs_1_, ...), custom_call_target="tpu_custom_call" | custom-call | tf_op jit(solution)/shard_map/pallas_call | solution.py:55
  84.7 1.6 %collective-permute-start.30 = (f32[64,1280]{1,0:T(8,128)S(1)}, f32[64,1280]{1,0:T(8,128)S(1)}, u32[]{:S(2)}, u32[]{:S(2)}) collective-permute-start(f32[64,1280]{1,0:T(8,128)S(1)} %get-tuple-element.96.refs_9_), channel_id=1, source_target_pairs={{0,2},{1,3},{2,0},{3,1},{4,6},{5,7},{6,4},{7,5},{8,10},{9,11},{10,... | collective-permute-start | bytes 983048 | tf_op jit(solution)/shard_map/ppermute | solution.py:554
  86.3 1.4 %shard_map.77 = (f32[64,768]{1,0:T(8,128)S(1)}, f32[64,768]{1,0:T(8,128)S(1)}) custom-call(s32[4,64]{1,0:T(4,128)S(1)} %bitcast.15, s32[2,64]{1,0:T(2,128)S(1)} %get-tuple-element.57.order_ref.order_near, bf16[2,48,128,128]{3,2,1,0:T(8,128)(2,1)S(1)} %get-tuple-element.88.ext, bf16[64,256,256]{2,1,0:T(8,128)(2,1)S(1)} %shard_map.67.w_ref.refs_1_, ...), custom_call_target="tpu_custom_call" | custom-call | tf_op jit(solution)/shard_map/pallas_call | solution.py:55
  87.7 0.6 collective-permute-start.28
  88.3 1.5 %collective-permute-start.32 = (f32[64,512]{1,0:T(8,128)S(1)}, f32[64,512]{1,0:T(8,128)S(1)}, u32[]{:S(2)}, u32[]{:S(2)}) collective-permute-start(f32[64,512]{1,0:T(8,128)S(1)} %get-tuple-element.93.refs_6_), channel_id=1, source_target_pairs={{0,2},{1,3},{2,0},{3,1},{4,6},{5,7},{6,4},{7,5},{8,10},{9,11},{10,... | collective-permute-start | bytes 393224 | tf_op jit(solution)/shard_map/ppermute | solution.py:554
  89.8 1.8 %shard_map.78 = (f32[64,1024]{1,0:T(8,128)S(1)}, f32[64,1024]{1,0:T(8,128)S(1)}) custom-call(s32[4,64]{1,0:T(4,128)S(1)} %bitcast.16, s32[2,64]{1,0:T(2,128)S(1)} %get-tuple-element.57.order_ref.order_near, bf16[2,48,128,128]{3,2,1,0:T(8,128)(2,1)S(1)} %get-tuple-element.88.ext, bf16[64,256,256]{2,1,0:T(8,128)(2,1)S(1)} %shard_map.67.w_ref.refs_1_, ...), custom_call_target="tpu_custom_call" | custom-call | tf_op jit(solution)/shard_map/pallas_call | solution.py:55
  91.6 0.6 collective-permute-start.36
  92.2 5.9 %collective-permute-done.28.refs_2_ = f32[64,512]{1,0:T(8,128)S(1)} collective-permute-done((f32[64,512]{1,0:T(8,128)S(1)}, f32[64,512]{1,0:T(8,128)S(1)}, u32[]{:S(2)}, u32[]{:S(2)}) %collective-permute-start.28) | collective-permute-done | bytes 131104 | tf_op jit(solution)/shard_map/ppermute | solution.py:554
  98.2 2.8 %collective-permute-done.32.refs_2_ = f32[64,512]{1,0:T(8,128)S(1)} collective-permute-done((f32[64,512]{1,0:T(8,128)S(1)}, f32[64,512]{1,0:T(8,128)S(1)}, u32[]{:S(2)}, u32[]{:S(2)}) %collective-permute-start.32) | collective-permute-done | bytes 131104 | tf_op jit(solution)/shard_map/ppermute | solution.py:554
  101.0 1.5 %collective-permute-start.34 = (f32[64,768]{1,0:T(8,128)S(1)}, f32[64,768]{1,0:T(8,128)S(1)}, u32[]{:S(2)}, u32[]{:S(2)}) collective-permute-start(f32[64,768]{1,0:T(8,128)S(1)} %get-tuple-element.94.refs_7_), channel_id=1, source_target_pairs={{0,2},{1,3},{2,0},{3,1},{4,6},{5,7},{6,4},{7,5},{8,10},{9,11},{10,... | collective-permute-start | bytes 589832 | tf_op jit(solution)/shard_map/ppermute | solution.py:554
  102.5 0.2 collective-permute-start.31
  102.7 3.9 %collective-permute-done.36.refs_8_ = f32[64,1024]{1,0:T(8,128)S(1)} collective-permute-done((f32[64,1024]{1,0:T(8,128)S(1)}, f32[64,1024]{1,0:T(8,128)S(1)}, u32[]{:S(2)}, u32[]{:S(2)}) %collective-permute-start.36) | collective-permute-done | bytes 262176 | tf_op jit(solution)/shard_map/ppermute | solution.py:554
  106.6 3.3 %collective-permute-done.34.refs_5_ = f32[64,768]{1,0:T(8,128)S(1)} collective-permute-done((f32[64,768]{1,0:T(8,128)S(1)}, f32[64,768]{1,0:T(8,128)S(1)}, u32[]{:S(2)}, u32[]{:S(2)}) %collective-permute-start.34) | collective-permute-done | bytes 196640 | tf_op jit(solution)/shard_map/ppermute | solution.py:554
  109.9 0.5 collective-permute-start.33
  110.4 1.2 shard_map.82.refs_11_.refs_5_.u_ref
  111.6 0.6 shard_map.81
  112.2 0.6 shard_map.83.refs_6_
  112.8 0.3 shard_map.84.refs_6_
  113.2 0.4 shard_map.85
  113.5 11.8 %all_to_all.5.sums_ref = f32[32,1,128]{2,1,0:T(1,128)S(1)} all-to-all(f32[32,1,128]{2,1,0:T(1,128)S(1)} %shard_map.85), channel_id=1, replica_groups=mesh['dom'=8,'samp'=4] {'dom','samp'}, dimensions={0} | all-to-all | bytes 32768 | tf_op jit(solution)/shard_map/all_to_all | solution.py:644
  125.4 1.2 update.1
  (55 shorter events, 0.5 us)
Async XLA Ops:
  2.4 9.9 %collective-permute-start = (f32[64,256]{1,0:T(8,128)S(1)}, f32[64,256]{1,0:T(8,128)S(1)}, u32[]{:S(2)}, u32[]{:S(2)}) collective-permute-start(f32[64,256]{1,0:T(8,128)S(1)} %get-tuple-element.61), channel_id=1, source_target_pairs={{0,16},{4,20},{8,24},{12,28},{16,0},{20,4},{24,8},{28,12},{1,17},{... | collective-permute-start | bytes 196616 | tf_op jit(solution)/shard_map/ppermute | solution.py:537
  6.6 10.0 %collective-permute-start.1 = (f32[64,256]{1,0:T(8,128)S(1)}, f32[64,256]{1,0:T(8,128)S(1)}, u32[]{:S(2)}, u32[]{:S(2)}) collective-permute-start(f32[64,256]{1,0:T(8,128)S(1)} %get-tuple-element.62), channel_id=1, source_target_pairs={{0,20},{4,16},{8,28},{12,24},{16,4},{20,0},{24,12},{28,8},{1,21},{... | collective-permute-start | bytes 196616 | tf_op jit(solution)/shard_map/ppermute | solution.py:537
  7.9 19.0 %collective-permute-start.2 = (f32[64,256]{1,0:T(8,128)S(1)}, f32[64,256]{1,0:T(8,128)S(1)}, u32[]{:S(2)}, u32[]{:S(2)}) collective-permute-start(f32[64,256]{1,0:T(8,128)S(1)} %get-tuple-element.63), channel_id=1, source_target_pairs={{0,24},{4,28},{8,16},{12,20},{16,8},{20,12},{24,0},{28,4},{1,25},{... | collective-permute-start | bytes 196616 | tf_op jit(solution)/shard_map/ppermute | solution.py:537
  11.5 15.4 %collective-permute-start.3 = (f32[64,256]{1,0:T(8,128)S(1)}, f32[64,256]{1,0:T(8,128)S(1)}, u32[]{:S(2)}, u32[]{:S(2)}) collective-permute-start(f32[64,256]{1,0:T(8,128)S(1)} %get-tuple-element.64), channel_id=1, source_target_pairs={{0,28},{4,24},{8,20},{12,16},{16,12},{20,8},{24,4},{28,0},{1,29},{... | collective-permute-start | bytes 196616 | tf_op jit(solution)/shard_map/ppermute | solution.py:537
  11.5 15.4 %collective-permute-start.4 = (f32[64,256]{1,0:T(8,128)S(1)}, f32[64,256]{1,0:T(8,128)S(1)}, u32[]{:S(2)}, u32[]{:S(2)}) collective-permute-start(f32[64,256]{1,0:T(8,128)S(1)} %get-tuple-element.65), channel_id=1, source_target_pairs={{0,12},{4,8},{8,4},{12,0},{16,28},{20,24},{24,20},{28,16},{1,13},{... | collective-permute-start | bytes 196616 | tf_op jit(solution)/shard_map/ppermute | solution.py:537
  12.4 14.5 %collective-permute-start.5 = (f32[64,256]{1,0:T(8,128)S(1)}, f32[64,256]{1,0:T(8,128)S(1)}, u32[]{:S(2)}, u32[]{:S(2)}) collective-permute-start(f32[64,256]{1,0:T(8,128)S(1)} %get-tuple-element.66), channel_id=1, source_target_pairs={{0,8},{4,12},{8,0},{12,4},{16,24},{20,28},{24,16},{28,20},{1,9},{5... | collective-permute-start | bytes 196616 | tf_op jit(solution)/shard_map/ppermute | solution.py:537
  16.6 10.4 %collective-permute-start.6 = (f32[64,256]{1,0:T(8,128)S(1)}, f32[64,256]{1,0:T(8,128)S(1)}, u32[]{:S(2)}, u32[]{:S(2)}) collective-permute-start(f32[64,256]{1,0:T(8,128)S(1)} %get-tuple-element.67), channel_id=1, source_target_pairs={{0,4},{4,0},{8,12},{12,8},{16,20},{20,16},{24,28},{28,24},{1,5},{5... | collective-permute-start | bytes 196616 | tf_op jit(solution)/shard_map/ppermute | solution.py:537
  18.9 1.2 copy-start
  20.1 1.2 copy-start.2
  23.7 3.2 %copy-start.4 = (s32[64,4]{0,1:T(4,128)S(1)}, s32[64,4]{0,1:T(4,128)}, u32[]{:S(2)}) copy-start(s32[64,4]{0,1:T(4,128)} %param.10) | copy-start | bytes 3076
  23.7 6.3 %slice-start = ((s8[8388608]{0:T(1024)(128)(4,1)}), s8[4194304]{0:T(1024)(128)(4,1)S(1)}, s32[]{:S(2)}) async-start(s8[8388608]{0:T(1024)(128)(4,1)} %bitcast.6), calls=%async_computation.1 | async-start | bytes 8388608
  26.9 3.1 %slice-start.1 = ((s8[8388608]{0:T(1024)(128)(4,1)}), s8[4194304]{0:T(1024)(128)(4,1)S(1)}, s32[]{:S(2)}) async-start(s8[8388608]{0:T(1024)(128)(4,1)} %bitcast.6), calls=%async_computation.2 | async-start | bytes 8388608
  31.5 29.4 %copy-start.5 = (s32[1,8,4]{1,2,0:T(4,128)S(1)}, s32[1,8,4]{1,2,0:T(4,128)}, u32[]{:S(2)}) copy-start(s32[1,8,4]{1,2,0:T(4,128)} %param.11) | copy-start | bytes 388
  34.0 16.2 %collective-permute-start.8 = (f32[64,2304]{1,0:T(8,128)S(1)}, f32[64,2304]{1,0:T(8,128)S(1)}, u32[]{:S(2)}, u32[]{:S(2)}) collective-permute-start(f32[64,2304]{1,0:T(8,128)S(1)} %get-tuple-element.72.refs_2_), channel_id=1, source_target_pairs={{0,2},{1,3},{2,0},{3,1},{4,6},{5,7},{6,4},{7,5},{8,10},{9,11},{10,... | collective-permute-start | bytes 1769480 | tf_op jit(solution)/shard_map/ppermute | solution.py:554
  35.5 18.1 %collective-permute-start.14 = (f32[64,1280]{1,0:T(8,128)S(1)}, f32[64,1280]{1,0:T(8,128)S(1)}, u32[]{:S(2)}, u32[]{:S(2)}) collective-permute-start(f32[64,1280]{1,0:T(8,128)S(1)} %get-tuple-element.76.refs_4_), channel_id=1, source_target_pairs={{0,2},{1,3},{2,0},{3,1},{4,6},{5,7},{6,4},{7,5},{8,10},{9,11},{10,... | collective-permute-start | bytes 983048 | tf_op jit(solution)/shard_map/ppermute | solution.py:554
  36.1 35.0 %collective-permute-start.7 = (f32[64,2304]{1,0:T(8,128)S(1)}, f32[64,2304]{1,0:T(8,128)S(1)}, u32[]{:S(2)}, u32[]{:S(2)}) collective-permute-start(f32[64,2304]{1,0:T(8,128)S(1)} %get-tuple-element.72.refs_2_), channel_id=1, source_target_pairs={{0,1},{1,0},{2,3},{3,2},{4,5},{5,4},{6,7},{7,6},{8,9},{9,8},{10,11... | collective-permute-start | bytes 1769480 | tf_op jit(solution)/shard_map/ppermute | solution.py:555
  50.2 24.7 %collective-permute-start.9 = (f32[64,2304]{1,0:T(8,128)S(1)}, f32[64,2304]{1,0:T(8,128)S(1)}, u32[]{:S(2)}, u32[]{:S(2)}) collective-permute-start(f32[64,2304]{1,0:T(8,128)S(1)} %collective-permute-done.8.refs_2_), channel_id=1, source_target_pairs={{0,1},{1,0},{2,3},{3,2},{4,5},{5,4},{6,7},{7,6},{8,9},{9,8},{10,11... | collective-permute-start | bytes 1769480 | tf_op jit(solution)/shard_map/ppermute | solution.py:567
  50.2 3.5 %collective-permute-start.10 = (f32[64,512]{1,0:T(8,128)S(1)}, f32[64,512]{1,0:T(8,128)S(1)}, u32[]{:S(2)}, u32[]{:S(2)}) collective-permute-start(f32[64,512]{1,0:T(8,128)S(1)} %get-tuple-element.75.refs_3_), channel_id=1, source_target_pairs={{0,1},{1,0},{2,3},{3,2},{4,5},{5,4},{6,7},{7,6},{8,9},{9,8},{10,11... | collective-permute-start | bytes 393224 | tf_op jit(solution)/shard_map/ppermute | solution.py:555
  50.7 8.9 %collective-permute-start.11 = (f32[64,1280]{1,0:T(8,128)S(1)}, f32[64,1280]{1,0:T(8,128)S(1)}, u32[]{:S(2)}, u32[]{:S(2)}) collective-permute-start(f32[64,1280]{1,0:T(8,128)S(1)} %get-tuple-element.76.refs_4_), channel_id=1, source_target_pairs={{0,1},{1,0},{2,3},{3,2},{4,5},{5,4},{6,7},{7,6},{8,9},{9,8},{10,11... | collective-permute-start | bytes 983048 | tf_op jit(solution)/shard_map/ppermute | solution.py:555
  53.7 7.3 %collective-permute-start.15 = (f32[64,1280]{1,0:T(8,128)S(1)}, f32[64,1280]{1,0:T(8,128)S(1)}, u32[]{:S(2)}, u32[]{:S(2)}) collective-permute-start(f32[64,1280]{1,0:T(8,128)S(1)} %collective-permute-done.14.refs_5_), channel_id=1, source_target_pairs={{0,1},{1,0},{2,3},{3,2},{4,5},{5,4},{6,7},{7,6},{8,9},{9,8},{10,11... | collective-permute-start | bytes 983048 | tf_op jit(solution)/shard_map/ppermute | solution.py:567
  53.7 5.9 %collective-permute-start.12 = (f32[64,512]{1,0:T(8,128)S(1)}, f32[64,512]{1,0:T(8,128)S(1)}, u32[]{:S(2)}, u32[]{:S(2)}) collective-permute-start(f32[64,512]{1,0:T(8,128)S(1)} %get-tuple-element.75.refs_3_), channel_id=1, source_target_pairs={{0,2},{1,3},{2,0},{3,1},{4,6},{5,7},{6,4},{7,5},{8,10},{9,11},{10,... | collective-permute-start | bytes 393224 | tf_op jit(solution)/shard_map/ppermute | solution.py:554
  59.6 1.3 %collective-permute-start.13 = (f32[64,512]{1,0:T(8,128)S(1)}, f32[64,512]{1,0:T(8,128)S(1)}, u32[]{:S(2)}, u32[]{:S(2)}) collective-permute-start(f32[64,512]{1,0:T(8,128)S(1)} %collective-permute-done.12.refs_2_), channel_id=1, source_target_pairs={{0,1},{1,0},{2,3},{3,2},{4,5},{5,4},{6,7},{7,6},{8,9},{9,8},{10,11... | collective-permute-start | bytes 393224 | tf_op jit(solution)/shard_map/ppermute | solution.py:567
  62.0 9.0 %collective-permute-start.16 = (f32[64,256]{1,0:T(8,128)S(1)}, f32[64,256]{1,0:T(8,128)S(1)}, u32[]{:S(2)}, u32[]{:S(2)}) collective-permute-start(f32[64,256]{1,0:T(8,128)S(1)} %get-tuple-element.80), channel_id=1, source_target_pairs={{0,16},{4,20},{8,24},{12,28},{16,0},{20,4},{24,8},{28,12},{1,17},{... | collective-permute-start | bytes 196616 | tf_op jit(solution)/shard_map/ppermute | solution.py:537
  65.1 9.7 %collective-permute-start.17 = (f32[64,256]{1,0:T(8,128)S(1)}, f32[64,256]{1,0:T(8,128)S(1)}, u32[]{:S(2)}, u32[]{:S(2)}) collective-permute-start(f32[64,256]{1,0:T(8,128)S(1)} %get-tuple-element.81), channel_id=1, source_target_pairs={{0,20},{4,16},{8,28},{12,24},{16,4},{20,0},{24,12},{28,8},{1,21},{... | collective-permute-start | bytes 196616 | tf_op jit(solution)/shard_map/ppermute | solution.py:537
  66.2 10.7 %collective-permute-start.18 = (f32[64,256]{1,0:T(8,128)S(1)}, f32[64,256]{1,0:T(8,128)S(1)}, u32[]{:S(2)}, u32[]{:S(2)}) collective-permute-start(f32[64,256]{1,0:T(8,128)S(1)} %get-tuple-element.82), channel_id=1, source_target_pairs={{0,24},{4,28},{8,16},{12,20},{16,8},{20,12},{24,0},{28,4},{1,25},{... | collective-permute-start | bytes 196616 | tf_op jit(solution)/shard_map/ppermute | solution.py:537
  71.0 7.2 %collective-permute-start.19 = (f32[64,256]{1,0:T(8,128)S(1)}, f32[64,256]{1,0:T(8,128)S(1)}, u32[]{:S(2)}, u32[]{:S(2)}) collective-permute-start(f32[64,256]{1,0:T(8,128)S(1)} %get-tuple-element.83), channel_id=1, source_target_pairs={{0,28},{4,24},{8,20},{12,16},{16,12},{20,8},{24,4},{28,0},{1,29},{... | collective-permute-start | bytes 196616 | tf_op jit(solution)/shard_map/ppermute | solution.py:537
  71.0 7.3 %collective-permute-start.20 = (f32[64,256]{1,0:T(8,128)S(1)}, f32[64,256]{1,0:T(8,128)S(1)}, u32[]{:S(2)}, u32[]{:S(2)}) collective-permute-start(f32[64,256]{1,0:T(8,128)S(1)} %get-tuple-element.84), channel_id=1, source_target_pairs={{0,12},{4,8},{8,4},{12,0},{16,28},{20,24},{24,20},{28,16},{1,13},{... | collective-permute-start | bytes 196616 | tf_op jit(solution)/shard_map/ppermute | solution.py:537
  74.8 4.3 %collective-permute-start.21 = (f32[64,256]{1,0:T(8,128)S(1)}, f32[64,256]{1,0:T(8,128)S(1)}, u32[]{:S(2)}, u32[]{:S(2)}) collective-permute-start(f32[64,256]{1,0:T(8,128)S(1)} %get-tuple-element.85), channel_id=1, source_target_pairs={{0,8},{4,12},{8,0},{12,4},{16,24},{20,28},{24,16},{28,20},{1,9},{5... | collective-permute-start | bytes 196616 | tf_op jit(solution)/shard_map/ppermute | solution.py:537
  74.8 4.8 %collective-permute-start.22 = (f32[64,256]{1,0:T(8,128)S(1)}, f32[64,256]{1,0:T(8,128)S(1)}, u32[]{:S(2)}, u32[]{:S(2)}) collective-permute-start(f32[64,256]{1,0:T(8,128)S(1)} %get-tuple-element.86), channel_id=1, source_target_pairs={{0,4},{4,0},{8,12},{12,8},{16,20},{20,16},{24,28},{28,24},{1,5},{5... | collective-permute-start | bytes 196616 | tf_op jit(solution)/shard_map/ppermute | solution.py:537
  76.1 3.5 %copy-start.1 = (f32[64,4096]{1,0:T(8,128)S(1)}, f32[64,4096]{1,0:T(8,128)}, u32[]{:S(2)}) copy-start(f32[64,4096]{1,0:T(8,128)} %g_ref.11) | copy-start | bytes 3145732
  76.1 3.5 %copy-start.3 = (f32[64,4096]{1,0:T(8,128)S(1)}, f32[64,4096]{1,0:T(8,128)}, u32[]{:S(2)}) copy-start(f32[64,4096]{1,0:T(8,128)} %c_ref.11) | copy-start | bytes 3145732
  80.8 7.5 %collective-permute-start.23 = (f32[64,512]{1,0:T(8,128)S(1)}, f32[64,512]{1,0:T(8,128)S(1)}, u32[]{:S(2)}, u32[]{:S(2)}) collective-permute-start(f32[64,512]{1,0:T(8,128)S(1)} %get-tuple-element.93.refs_6_), channel_id=1, source_target_pairs={{0,1},{1,0},{2,3},{3,2},{4,5},{5,4},{6,7},{7,6},{8,9},{9,8},{10,11... | collective-permute-start | bytes 393224 | tf_op jit(solution)/shard_map/ppermute | solution.py:555
  82.1 9.5 %collective-permute-start.27 = (f32[64,512]{1,0:T(8,128)S(1)}, f32[64,512]{1,0:T(8,128)S(1)}, u32[]{:S(2)}, u32[]{:S(2)}) collective-permute-start(f32[64,512]{1,0:T(8,128)S(1)} %get-tuple-element.97.refs_10_), channel_id=1, source_target_pairs={{0,1},{1,0},{2,3},{3,2},{4,5},{5,4},{6,7},{7,6},{8,9},{9,8},{10,11... | collective-permute-start | bytes 393224 | tf_op jit(solution)/shard_map/ppermute | solution.py:555
  84.7 17.8 %collective-permute-start.30 = (f32[64,1280]{1,0:T(8,128)S(1)}, f32[64,1280]{1,0:T(8,128)S(1)}, u32[]{:S(2)}, u32[]{:S(2)}) collective-permute-start(f32[64,1280]{1,0:T(8,128)S(1)} %get-tuple-element.96.refs_9_), channel_id=1, source_target_pairs={{0,2},{1,3},{2,0},{3,1},{4,6},{5,7},{6,4},{7,5},{8,10},{9,11},{10,... | collective-permute-start | bytes 983048 | tf_op jit(solution)/shard_map/ppermute | solution.py:554
  87.6 13.3 %collective-permute-start.24 = (f32[64,768]{1,0:T(8,128)S(1)}, f32[64,768]{1,0:T(8,128)S(1)}, u32[]{:S(2)}, u32[]{:S(2)}) collective-permute-start(f32[64,768]{1,0:T(8,128)S(1)} %get-tuple-element.94.refs_7_), channel_id=1, source_target_pairs={{0,1},{1,0},{2,3},{3,2},{4,5},{5,4},{6,7},{7,6},{8,9},{9,8},{10,11... | collective-permute-start | bytes 589832 | tf_op jit(solution)/shard_map/ppermute | solution.py:555
  87.7 10.4 %collective-permute-start.28 = (f32[64,512]{1,0:T(8,128)S(1)}, f32[64,512]{1,0:T(8,128)S(1)}, u32[]{:S(2)}, u32[]{:S(2)}) collective-permute-start(f32[64,512]{1,0:T(8,128)S(1)} %get-tuple-element.97.refs_10_), channel_id=1, source_target_pairs={{0,2},{1,3},{2,0},{3,1},{4,6},{5,7},{6,4},{7,5},{8,10},{9,11},{10,... | collective-permute-start | bytes 393224 | tf_op jit(solution)/shard_map/ppermute | solution.py:554
  88.3 12.6 %collective-permute-start.32 = (f32[64,512]{1,0:T(8,128)S(1)}, f32[64,512]{1,0:T(8,128)S(1)}, u32[]{:S(2)}, u32[]{:S(2)}) collective-permute-start(f32[64,512]{1,0:T(8,128)S(1)} %get-tuple-element.93.refs_6_), channel_id=1, source_target_pairs={{0,2},{1,3},{2,0},{3,1},{4,6},{5,7},{6,4},{7,5},{8,10},{9,11},{10,... | collective-permute-start | bytes 393224 | tf_op jit(solution)/shard_map/ppermute | solution.py:554
  91.6 15.0 %collective-permute-start.36 = (f32[64,1024]{1,0:T(8,128)S(1)}, f32[64,1024]{1,0:T(8,128)S(1)}, u32[]{:S(2)}, u32[]{:S(2)}) collective-permute-start(f32[64,1024]{1,0:T(8,128)S(1)} %get-tuple-element.95.refs_8_), channel_id=1, source_target_pairs={{0,2},{1,3},{2,0},{3,1},{4,6},{5,7},{6,4},{7,5},{8,10},{9,11},{10,... | collective-permute-start | bytes 786440 | tf_op jit(solution)/shard_map/ppermute | solution.py:554
  98.2 12.2 %collective-permute-start.26 = (f32[64,1280]{1,0:T(8,128)S(1)}, f32[64,1280]{1,0:T(8,128)S(1)}, u32[]{:S(2)}, u32[]{:S(2)}) collective-permute-start(f32[64,1280]{1,0:T(8,128)S(1)} %get-tuple-element.96.refs_9_), channel_id=1, source_target_pairs={{0,1},{1,0},{2,3},{3,2},{4,5},{5,4},{6,7},{7,6},{8,9},{9,8},{10,11... | collective-permute-start | bytes 983048 | tf_op jit(solution)/shard_map/ppermute | solution.py:555
  101.0 8.9 %collective-permute-start.25 = (f32[64,1024]{1,0:T(8,128)S(1)}, f32[64,1024]{1,0:T(8,128)S(1)}, u32[]{:S(2)}, u32[]{:S(2)}) collective-permute-start(f32[64,1024]{1,0:T(8,128)S(1)} %get-tuple-element.95.refs_8_), channel_id=1, source_target_pairs={{0,1},{1,0},{2,3},{3,2},{4,5},{5,4},{6,7},{7,6},{8,9},{9,8},{10,11... | collective-permute-start | bytes 786440 | tf_op jit(solution)/shard_map/ppermute | solution.py:555
  101.0 8.9 %collective-permute-start.34 = (f32[64,768]{1,0:T(8,128)S(1)}, f32[64,768]{1,0:T(8,128)S(1)}, u32[]{:S(2)}, u32[]{:S(2)}) collective-permute-start(f32[64,768]{1,0:T(8,128)S(1)} %get-tuple-element.94.refs_7_), channel_id=1, source_target_pairs={{0,2},{1,3},{2,0},{3,1},{4,6},{5,7},{6,4},{7,5},{8,10},{9,11},{10,... | collective-permute-start | bytes 589832 | tf_op jit(solution)/shard_map/ppermute | solution.py:554
  102.5 10.3 %collective-permute-start.31 = (f32[64,1280]{1,0:T(8,128)S(1)}, f32[64,1280]{1,0:T(8,128)S(1)}, u32[]{:S(2)}, u32[]{:S(2)}) collective-permute-start(f32[64,1280]{1,0:T(8,128)S(1)} %collective-permute-done.30.refs_2_), channel_id=1, source_target_pairs={{0,1},{1,0},{2,3},{3,2},{4,5},{5,4},{6,7},{7,6},{8,9},{9,8},{10,11... | collective-permute-start | bytes 983048 | tf_op jit(solution)/shard_map/ppermute | solution.py:567
  106.6 5.7 %collective-permute-start.37 = (f32[64,1024]{1,0:T(8,128)S(1)}, f32[64,1024]{1,0:T(8,128)S(1)}, u32[]{:S(2)}, u32[]{:S(2)}) collective-permute-start(f32[64,1024]{1,0:T(8,128)S(1)} %collective-permute-done.36.refs_8_), channel_id=1, source_target_pairs={{0,1},{1,0},{2,3},{3,2},{4,5},{5,4},{6,7},{7,6},{8,9},{9,8},{10,11... | collective-permute-start | bytes 786440 | tf_op jit(solution)/shard_map/ppermute | solution.py:567
  109.9 2.4 %collective-permute-start.35 = (f32[64,768]{1,0:T(8,128)S(1)}, f32[64,768]{1,0:T(8,128)S(1)}, u32[]{:S(2)}, u32[]{:S(2)}) collective-permute-start(f32[64,768]{1,0:T(8,128)S(1)} %collective-permute-done.34.refs_5_), channel_id=1, source_target_pairs={{0,1},{1,0},{2,3},{3,2},{4,5},{5,4},{6,7},{7,6},{8,9},{9,8},{10,11... | collective-permute-start | bytes 589832 | tf_op jit(solution)/shard_map/ppermute | solution.py:567
  109.9 2.4 %collective-permute-start.33 = (f32[64,512]{1,0:T(8,128)S(1)}, f32[64,512]{1,0:T(8,128)S(1)}, u32[]{:S(2)}, u32[]{:S(2)}) collective-permute-start(f32[64,512]{1,0:T(8,128)S(1)} %collective-permute-done.32.refs_2_), channel_id=1, source_target_pairs={{0,1},{1,0},{2,3},{3,2},{4,5},{5,4},{6,7},{7,6},{8,9},{9,8},{10,11... | collective-permute-start | bytes 393224 | tf_op jit(solution)/shard_map/ppermute | solution.py:567
  110.4 2.8 %collective-permute-start.29 = (f32[64,512]{1,0:T(8,128)S(1)}, f32[64,512]{1,0:T(8,128)S(1)}, u32[]{:S(2)}, u32[]{:S(2)}) collective-permute-start(f32[64,512]{1,0:T(8,128)S(1)} %collective-permute-done.28.refs_2_), channel_id=1, source_target_pairs={{0,1},{1,0},{2,3},{3,2},{4,5},{5,4},{6,7},{7,6},{8,9},{9,8},{10,11... | collective-permute-start | bytes 393224 | tf_op jit(solution)/shard_map/ppermute | solution.py:567

commit v4 on v3

--- a/solution.py
+++ b/solution.py
@@ -110,12 +110,16 @@
     lax.fori_loop(first_row, last_row, convert, 0, unroll=2)
 
 
-def fetch_kernel(order_ref, stamps_hbm, out_ref, buffer, sems):
+def fetch_kernel(domains, groups, send_ref, field_ref, stamps_hbm, order_ref, out_ref, *refs):
+    ext, near_ref, far_ref, buffer, sems = refs
+    order_rows(domains, send_ref, order_ref)
     rows, _, width = buffer.shape
     copies = []
     for n in range(rows):
         copies.append(pltpu.make_async_copy(stamps_hbm.at[order_ref[0, n]], buffer.at[n], sems.at[n]))
         copies[-1].start()
+    extend_kernel(field_ref, ext)
+    tables_kernel(groups, near_ref, far_ref)
     for n, copy in enumerate(copies):
         copy.wait()
         high, low = split(buffer[n])
@@ -123,17 +127,21 @@
         out_ref[n, :, width:] = low
 
 
-def fetch(order, stamps, rows):
+def fetch(send, field, stamps, rows, domains, groups, outputs):
     total, depth, width = stamps.shape
     return pl.pallas_call(
-        fetch_kernel,
-        in_specs=[scalars(), pl.BlockSpec(memory_space=pl.ANY)],
-        out_specs=whole(),
-        out_shape=pltpu.VMEM((total, depth, 2 * width), jnp.bfloat16),
+        functools.partial(fetch_kernel, domains, groups),
+        in_specs=[scalars(), whole(), pl.BlockSpec(memory_space=pl.ANY)],
+        out_specs=[scalars()] + [whole()] * (1 + len(outputs)),
+        out_shape=[
+            jax.ShapeDtypeStruct((2, total), jnp.int32),
+            pltpu.VMEM((total, depth, 2 * width), jnp.bfloat16),
+            *[pltpu.VMEM(shape, dtype) for shape, dtype in outputs],
+        ],
         scratch_shapes=[pltpu.VMEM((rows, depth, width), stamps.dtype), pltpu.SemaphoreType.DMA((rows,))],
         compiler_params=pltpu.CompilerParams(vmem_limit_bytes=LIMIT),
         name="prepare_0",
-    )(order, far_memory(stamps))
+    )(far_memory(send), near_memory(field), far_memory(stamps))
 
 
 def pair_tile(ref, first, second):
@@ -202,7 +210,7 @@
         later = later + 1 - flag
 
 
-def gather_kernel(domains, send_hbm, field_hbm, field_ref, order_ref, *refs):
+def gather_kernel(domains, send_hbm, field_hbm, field_ref, *refs):
     *out_refs, field_sem, send_ref, send_sem = refs
     table = pltpu.make_async_copy(send_hbm, send_ref, send_sem)
     table.start()
@@ -216,20 +224,14 @@
     for copy in copies:
         copy.wait()
     gather_all(domains, send_ref, field_ref, out_refs)
-    order_rows(domains, send_ref, order_ref)
-
-
-def gather(send, field, rows, domains, outputs):
-    table = jax.ShapeDtypeStruct((2, rows), jnp.int32)
+
+
+def gather(send, field, domains, outputs):
     return pl.pallas_call(
         functools.partial(gather_kernel, domains),
         in_specs=[pl.BlockSpec(memory_space=pl.ANY)] * 2,
-        out_specs=[whole(), scalars()] + [whole()] * len(outputs),
-        out_shape=[
-            pltpu.VMEM(field.shape, field.dtype),
-            table,
-            *[pltpu.VMEM(shape, dtype) for shape, dtype in outputs],
-        ],
+        out_specs=[whole()] * (1 + len(outputs)),
+        out_shape=[pltpu.VMEM(shape, dtype) for shape, dtype in ((field.shape, field.dtype), *outputs)],
         scratch_shapes=[
             pltpu.SemaphoreType.DMA((COPIES,)),
             pltpu.SMEM(send.shape, send.dtype),
@@ -269,11 +271,6 @@
     for i in range(u_ref.shape[1] // LANES):
         inside = slice(i * LANES, (i + 1) * LANES)
         out_ref[:, inside] = pair_tile(u_ref, order_ref[1, 2 * i], order_ref[1, 2 * i + 1])
-
-
-def first_extend_kernel(groups, field_ref, ext, near_ref, far_ref):
-    extend_kernel(field_ref, ext)
-    tables_kernel(groups, near_ref, far_ref)
 
 
 def extend_kernel(field_ref, ext):
@@ -567,24 +564,25 @@
             charges += [x, lax.ppermute(x, "samp", pairs)]
         return [half, *charges]
 
-    field, order, *outgoing = gather(send, residual, rows, domains, outgoing_shapes)
+    field, *outgoing = gather(send, residual, domains, outgoing_shapes)
     incoming = exchange(outgoing)
     blocks = stamps.reshape(rows, per_entry * width, 2 * width)
-    ext, near_matrix, far_matrix = kernel_call(
-        functools.partial(first_extend_kernel, groups),
-        (field,),
+    order, weights, ext, near_matrix, far_matrix = fetch(
+        send,
+        field,
+        blocks,
+        early,
+        domains,
+        groups,
         [
             ext_shape,
             ((2 * samples, 2 * samples), jnp.bfloat16),
             ((2 * samples, count * samples), jnp.bfloat16),
         ],
     )
-    weights = None
     own = []
     for n, (low, high) in enumerate(((0, early), (early, rows))):
-        if n == 0:
-            weights = fetch(order, blocks, early)
-        else:
+        if n:
             (weights,) = kernel_call(
                 functools.partial(prepare_kernel, low, high), (order, blocks, weights), [weight_shape], aliases={2: 0}
             )

time: 127 us -> 119 us (0.937)
  waiting for transfers between devices: 46.2 us -> 41.9 us
  local copies, waits for them, and re-layouts: 2.49 us -> 0.04 us
    ppermute x8, waiting for transfers between devices: 37.4 us -> 31.8 us  [spread(): lax.ppermute(q, 'samp', [(i, (i + k) % groups) for i in range(groups)])]
    unnamed x16 -> x12, local copies, waits for them, and re-layouts: 2.49 us -> 0.04 us
    pallas_call x1, Pallas kernels: 3.15 us -> 4.66 us  [fetch(): pl.pallas_call(functools.partial(fetch_kernel, domains, groups), in_specs...]
    ppermute x8, waiting for transfers between devices: 0.02 us -> 1.36 us  [spread(): return (far, lax.ppermute(q, 'samp', pairs))]
    pallas_call x22 -> x21, Pallas kernels: 23.3 us -> 22.5 us  [kernel_call(): pl.pallas_call(kernel, in_specs=specs, out_specs=[scalars() if number els...]
  transfers between devices with their start and end apart: 38 -> 38, of which waited for: 14 -> 13; matrix products, arithmetic and copies ran while one was open for 0% -> 0% of each run, Pallas kernels for 14% -> 16%
where the time goes in v4:
time: 119 us
  waiting for transfers between devices  41.9 us (35%)
  starting transfers between devices  36 us (30%)
  Pallas kernels  29.9 us (25%)
  blocking collectives  10.8 us (9%)
    ppermute x8, waiting for transfers between devices, spread(): lax.ppermute(q, 'samp', [(i, (i + k) % groups) for i in range(groups)])  31.8 us
    ppermute x14, starting transfers between devices, exchange(): lax.ppermute(x, 'dom', [(i, i ^ k) for i in range(domains)])  24.2 us
    pallas_call x21, Pallas kernels, kernel_call(): pl.pallas_call(kernel, in_specs=specs, out_specs=[scalars() if number els...  22.5 us
    all_to_all x1, blocking collectives, body(): lax.all_to_all(sums, ('dom', 'samp'), split_axis=0, concat_axis=0, tiled=...  10.8 us
    ppermute x8, starting transfers between devices, spread(): lax.ppermute(q, 'samp', [(i, (i + k) % groups) for i in range(groups)])  9.45 us
    ppermute x14, waiting for transfers between devices, exchange(): lax.ppermute(x, 'dom', [(i, i ^ k) for i in range(domains)])  7.84 us
    pallas_call x1, Pallas kernels, fetch(): pl.pallas_call(functools.partial(fetch_kernel, domains, groups), in_specs...  4.66 us
  transfers between devices with their start and end apart: 38, of which 13 were waited for; matrix products, arithmetic and copies ran while one was open for 0% of the time, Pallas kernels for 16%

profile of v4, /device:TPU:0, one launch (start us, length us, event | category | flops | bytes accessed | tf_op | source)
XLA Modules:
  0.0 119.2 jit_solution(782370082561667079)
XLA Ops:
  0.0 1.5 %gather.1 = (f32[64,4096]{1,0:T(8,128)S(1)}, f32[64,256]{1,0:T(8,128)S(1)}, f32[64,256]{1,0:T(8,128)S(1)}, f32[64,256]{1,0:T(8,128)S(1)}, f32[64,256]{1,0:T(8,12...) custom-call(s32[4,8]{1,0:T(4,128)} %bitcast.17, f32[64,4096]{1,0:T(8,128)} %field_hbm.1), custom_call_target="tpu_custom_call" | custom-call | tf_op jit(solution)/shard_map/gather/pallas_call | solution.py:230
  1.5 4.1 %collective-permute-start = (f32[64,256]{1,0:T(8,128)S(1)}, f32[64,256]{1,0:T(8,128)S(1)}, u32[]{:S(2)}, u32[]{:S(2)}) collective-permute-start(f32[64,256]{1,0:T(8,128)S(1)} %get-tuple-element.63), channel_id=1, source_target_pairs={{0,16},{4,20},{8,24},{12,28},{16,0},{20,4},{24,8},{28,12},{1,17},{... | collective-permute-start | bytes 196616 | tf_op jit(solution)/shard_map/ppermute | solution.py:534
  5.7 1.3 %collective-permute-start.1 = (f32[64,256]{1,0:T(8,128)S(1)}, f32[64,256]{1,0:T(8,128)S(1)}, u32[]{:S(2)}, u32[]{:S(2)}) collective-permute-start(f32[64,256]{1,0:T(8,128)S(1)} %get-tuple-element.64), channel_id=1, source_target_pairs={{0,20},{4,16},{8,28},{12,24},{16,4},{20,0},{24,12},{28,8},{1,21},{... | collective-permute-start | bytes 196616 | tf_op jit(solution)/shard_map/ppermute | solution.py:534
  7.0 3.6 %collective-permute-start.2 = (f32[64,256]{1,0:T(8,128)S(1)}, f32[64,256]{1,0:T(8,128)S(1)}, u32[]{:S(2)}, u32[]{:S(2)}) collective-permute-start(f32[64,256]{1,0:T(8,128)S(1)} %get-tuple-element.65), channel_id=1, source_target_pairs={{0,24},{4,28},{8,16},{12,20},{16,8},{20,12},{24,0},{28,4},{1,25},{... | collective-permute-start | bytes 196616 | tf_op jit(solution)/shard_map/ppermute | solution.py:534
  10.6 0.9 collective-permute-start.4
  11.5 2.2 %collective-permute-start.5 = (f32[64,256]{1,0:T(8,128)S(1)}, f32[64,256]{1,0:T(8,128)S(1)}, u32[]{:S(2)}, u32[]{:S(2)}) collective-permute-start(f32[64,256]{1,0:T(8,128)S(1)} %get-tuple-element.68), channel_id=1, source_target_pairs={{0,8},{4,12},{8,0},{12,4},{16,24},{20,28},{24,16},{28,20},{1,9},{5... | collective-permute-start | bytes 196616 | tf_op jit(solution)/shard_map/ppermute | solution.py:534
  13.7 2.0 %collective-permute-done.1.refs_5_ = f32[64,256]{1,0:T(8,128)S(1)} collective-permute-done((f32[64,256]{1,0:T(8,128)S(1)}, f32[64,256]{1,0:T(8,128)S(1)}, u32[]{:S(2)}, u32[]{:S(2)}) %collective-permute-start.1) | collective-permute-done | bytes 65568 | tf_op jit(solution)/shard_map/ppermute | solution.py:534
  15.7 1.5 %collective-permute-start.6 = (f32[64,256]{1,0:T(8,128)S(1)}, f32[64,256]{1,0:T(8,128)S(1)}, u32[]{:S(2)}, u32[]{:S(2)}) collective-permute-start(f32[64,256]{1,0:T(8,128)S(1)} %get-tuple-element.69), channel_id=1, source_target_pairs={{0,4},{4,0},{8,12},{12,8},{16,20},{20,16},{24,28},{28,24},{1,5},{5... | collective-permute-start | bytes 196616 | tf_op jit(solution)/shard_map/ppermute | solution.py:534
  17.2 4.7 %prepare_0.1 = (s32[2,64]{1,0:T(2,128)S(1)}, bf16[64,256,256]{2,1,0:T(8,128)(2,1)S(1)}, bf16[2,48,128,128]{3,2,1,0:T(8,128)(2,1)S(1)}, bf16[128,128]{1,0:T(8,128)(2,1)S(1)}, bf16[128,128]{1,0:T(8,128)(2,1)S(1)}) custom-call(s32[4,8]{1,0:T(4,128)} %bitcast.18, f32[64,4096]{1,0:T(8,128)S(1)} %get-tuple-element.55.field_ref.refs_10_.refs_4_.r_ref, ...), custom_call_target="tpu_custom_call" | custom-call | tf_op jit(solution)/shard_map/prepare_0/pallas_call | solution.py:132
  21.9 1.1 shard_map.64
  23.0 1.3 %shard_map.67 = (f32[64,2304]{1,0:T(8,128)S(1)}, f32[64,2304]{1,0:T(8,128)S(1)}) custom-call(s32[2,64]{1,0:T(2,128)S(1)} %get-tuple-element.58.order_ref.order_near, f32[64,4096]{1,0:T(8,128)S(1)} %get-tuple-element.55.field_ref.refs_10_.refs_4_.r_ref, f32[64,4096]{1,0:T(8,128)S(1)} %copy-done, f32[64,4096]{1,0:T(8,128)S(1)} %copy-done.1), custom_call_target="tpu_custom_call" | custom-call | tf_op jit(solution)/shard_map/pallas_call | solution.py:55
  24.3 1.2 shard_map.65
  25.5 1.9 %shard_map.70 = (f32[64,1280]{1,0:T(8,128)S(1)}, f32[64,1280]{1,0:T(8,128)S(1)}) custom-call(s32[4,64]{1,0:T(4,128)S(1)} %bitcast.10, s32[2,64]{1,0:T(2,128)S(1)} %get-tuple-element.58.order_ref.order_near, bf16[2,48,128,128]{3,2,1,0:T(8,128)(2,1)S(1)} %get-tuple-element.70.ext, bf16[64,256,256]{2,1,0:T(8,128)(2,1)S(1)} %get-tuple-element.60.refs_1_.refs_0_.w_ref, ...), custom_call_target="tpu_custom_call" | custom-call | tf_op jit(solution)/shard_map/pallas_call | solution.py:55
  27.4 1.4 %shard_map.66.w_ref.refs_1_ = bf16[64,256,256]{2,1,0:T(8,128)(2,1)S(1)} custom-call(s32[2,64]{1,0:T(2,128)S(1)} %get-tuple-element.58.order_ref.order_near, f32[64,256,128]{2,1,0:T(8,128)S(1)} %bitcast.8, bf16[64,256,256]{2,1,0:T(8,128)(2,1)S(1)} %get-tuple-element.60.refs_1_.refs_0_.w_ref), custom_call_target="tpu_custom_call", output_to_operand_aliasing={{}: (2, {})} | custom-call | tf_op jit(solution)/shard_map/pallas_call | solution.py:55
  28.9 2.5 %shard_map.68 = (f32[64,2304]{1,0:T(8,128)S(1)}, f32[64,2304]{1,0:T(8,128)S(1)}) custom-call(s32[4,64]{1,0:T(4,128)S(1)} %bitcast.11, s32[2,64]{1,0:T(2,128)S(1)} %get-tuple-element.58.order_ref.order_near, bf16[2,48,128,128]{3,2,1,0:T(8,128)(2,1)S(1)} %get-tuple-element.70.ext, bf16[64,256,256]{2,1,0:T(8,128)(2,1)S(1)} %shard_map.66.w_ref.refs_1_, ...), custom_call_target="tpu_custom_call" | custom-call | tf_op jit(solution)/shard_map/pallas_call | solution.py:55
  31.3 1.6 %collective-permute-start.8 = (f32[64,2304]{1,0:T(8,128)S(1)}, f32[64,2304]{1,0:T(8,128)S(1)}, u32[]{:S(2)}, u32[]{:S(2)}) collective-permute-start(f32[64,2304]{1,0:T(8,128)S(1)} %get-tuple-element.74.refs_2_), channel_id=1, source_target_pairs={{0,2},{1,3},{2,0},{3,1},{4,6},{5,7},{6,4},{7,5},{8,10},{9,11},{10,... | collective-permute-start | bytes 1769480 | tf_op jit(solution)/shard_map/ppermute | solution.py:551
  32.9 0.5 collective-permute-start.14
  33.4 14.1 %collective-permute-done.8.refs_2_ = f32[64,2304]{1,0:T(8,128)S(1)} collective-permute-done((f32[64,2304]{1,0:T(8,128)S(1)}, f32[64,2304]{1,0:T(8,128)S(1)}, u32[]{:S(2)}, u32[]{:S(2)}) %collective-permute-start.8) | collective-permute-done | bytes 589856 | tf_op jit(solution)/shard_map/ppermute | solution.py:551
  47.5 1.5 %collective-permute-start.12 = (f32[64,512]{1,0:T(8,128)S(1)}, f32[64,512]{1,0:T(8,128)S(1)}, u32[]{:S(2)}, u32[]{:S(2)}) collective-permute-start(f32[64,512]{1,0:T(8,128)S(1)} %get-tuple-element.77.refs_3_), channel_id=1, source_target_pairs={{0,2},{1,3},{2,0},{3,1},{4,6},{5,7},{6,4},{7,5},{8,10},{9,11},{10,... | collective-permute-start | bytes 393224 | tf_op jit(solution)/shard_map/ppermute | solution.py:551
  49.0 0.2 collective-permute-start.11
  49.3 2.2 %collective-permute-done.14.refs_5_ = f32[64,1280]{1,0:T(8,128)S(1)} collective-permute-done((f32[64,1280]{1,0:T(8,128)S(1)}, f32[64,1280]{1,0:T(8,128)S(1)}, u32[]{:S(2)}, u32[]{:S(2)}) %collective-permute-start.14) | collective-permute-done | bytes 327712 | tf_op jit(solution)/shard_map/ppermute | solution.py:551
  51.5 2.4 %collective-permute-done.12.refs_2_ = f32[64,512]{1,0:T(8,128)S(1)} collective-permute-done((f32[64,512]{1,0:T(8,128)S(1)}, f32[64,512]{1,0:T(8,128)S(1)}, u32[]{:S(2)}, u32[]{:S(2)}) %collective-permute-start.12) | collective-permute-done | bytes 131104 | tf_op jit(solution)/shard_map/ppermute | solution.py:551
  53.9 1.3 %collective-permute-done.10.refs_5_ = f32[64,512]{1,0:T(8,128)S(1)} collective-permute-done((f32[64,512]{1,0:T(8,128)S(1)}, f32[64,512]{1,0:T(8,128)S(1)}, u32[]{:S(2)}, u32[]{:S(2)}) %collective-permute-start.10) | collective-permute-done | bytes 131104 | tf_op jit(solution)/shard_map/ppermute | solution.py:552
  55.2 0.1 collective-permute-start.13
  55.4 0.3 shard_map.71
  55.7 0.8 collective-permute-done.13.refs_3_
  56.6 1.1 shard_map.72
  57.7 3.1 %collective-permute-start.16 = (f32[64,256]{1,0:T(8,128)S(1)}, f32[64,256]{1,0:T(8,128)S(1)}, u32[]{:S(2)}, u32[]{:S(2)}) collective-permute-start(f32[64,256]{1,0:T(8,128)S(1)} %get-tuple-element.82), channel_id=1, source_target_pairs={{0,16},{4,20},{8,24},{12,28},{16,0},{20,4},{24,8},{28,12},{1,17},{... | collective-permute-start | bytes 196616 | tf_op jit(solution)/shard_map/ppermute | solution.py:534
  60.7 1.1 collective-permute-start.17
  61.8 4.8 %collective-permute-start.18 = (f32[64,256]{1,0:T(8,128)S(1)}, f32[64,256]{1,0:T(8,128)S(1)}, u32[]{:S(2)}, u32[]{:S(2)}) collective-permute-start(f32[64,256]{1,0:T(8,128)S(1)} %get-tuple-element.84), channel_id=1, source_target_pairs={{0,24},{4,28},{8,16},{12,20},{16,8},{20,12},{24,0},{28,4},{1,25},{... | collective-permute-start | bytes 196616 | tf_op jit(solution)/shard_map/ppermute | solution.py:534
  66.7 0.6 collective-permute-start.20
  67.3 3.1 %collective-permute-done.17.refs_6_ = f32[64,256]{1,0:T(8,128)S(1)} collective-permute-done((f32[64,256]{1,0:T(8,128)S(1)}, f32[64,256]{1,0:T(8,128)S(1)}, u32[]{:S(2)}, u32[]{:S(2)}) %collective-permute-start.17) | collective-permute-done | bytes 65568 | tf_op jit(solution)/shard_map/ppermute | solution.py:534
  70.4 0.9 collective-permute-start.22
  71.3 0.4 shard_map.69.refs_1_
  71.7 0.4 shard_map.73.field_ref.refs_2_.u_ref
  72.1 0.3 shard_map.74.refs_0_
  72.5 1.3 %collective-permute-done.19.refs_8_ = f32[64,256]{1,0:T(8,128)S(1)} collective-permute-done((f32[64,256]{1,0:T(8,128)S(1)}, f32[64,256]{1,0:T(8,128)S(1)}, u32[]{:S(2)}, u32[]{:S(2)}) %collective-permute-start.19) | collective-permute-done | bytes 65568 | tf_op jit(solution)/shard_map/ppermute | solution.py:534
  73.8 0.1 collective-permute-done.20.refs_9_
  73.9 0.7 collective-permute-done.21.refs_10_
  74.7 0.5 collective-permute-done.22.refs_11_
  75.2 1.2 %shard_map.75 = (bf16[2,48,128,128]{3,2,1,0:T(8,128)(2,1)S(1)}, f32[64,512]{1,0:T(8,128)S(1)}, f32[64,512]{1,0:T(8,128)S(1)}) custom-call(s32[4,64]{1,0:T(4,128)S(1)} %bitcast.12, s32[2,64]{1,0:T(2,128)S(1)} %get-tuple-element.58.order_ref.order_near, bf16[2,48,128,128]{3,2,1,0:T(8,128)(2,1)S(1)} %shard_map.74.refs_0_, ...), custom_call_target="tpu_custom_call", output_to_operand_aliasing={{0}: (2, {})} | custom-call | tf_op jit(solution)/shard_map/pallas_call | solution.py:55
  76.4 1.6 %collective-permute-start.32 = (f32[64,512]{1,0:T(8,128)S(1)}, f32[64,512]{1,0:T(8,128)S(1)}, u32[]{:S(2)}, u32[]{:S(2)}) collective-permute-start(f32[64,512]{1,0:T(8,128)S(1)} %get-tuple-element.95.refs_6_), channel_id=1, source_target_pairs={{0,2},{1,3},{2,0},{3,1},{4,6},{5,7},{6,4},{7,5},{8,10},{9,11},{10,... | collective-permute-start | bytes 393224 | tf_op jit(solution)/shard_map/ppermute | solution.py:551
  78.0 2.1 %shard_map.78 = (f32[64,1280]{1,0:T(8,128)S(1)}, f32[64,1280]{1,0:T(8,128)S(1)}) custom-call(s32[4,64]{1,0:T(4,128)S(1)} %bitcast.13, s32[2,64]{1,0:T(2,128)S(1)} %get-tuple-element.58.order_ref.order_near, bf16[2,48,128,128]{3,2,1,0:T(8,128)(2,1)S(1)} %get-tuple-element.90.ext, bf16[64,256,256]{2,1,0:T(8,128)(2,1)S(1)} %shard_map.66.w_ref.refs_1_, ...), custom_call_target="tpu_custom_call" | custom-call | tf_op jit(solution)/shard_map/pallas_call | solution.py:55
  80.1 0.6 collective-permute-start.30
  80.7 1.4 %shard_map.76 = (f32[64,768]{1,0:T(8,128)S(1)}, f32[64,768]{1,0:T(8,128)S(1)}) custom-call(s32[4,64]{1,0:T(4,128)S(1)} %bitcast.14, s32[2,64]{1,0:T(2,128)S(1)} %get-tuple-element.58.order_ref.order_near, bf16[2,48,128,128]{3,2,1,0:T(8,128)(2,1)S(1)} %get-tuple-element.90.ext, bf16[64,256,256]{2,1,0:T(8,128)(2,1)S(1)} %shard_map.66.w_ref.refs_1_, ...), custom_call_target="tpu_custom_call" | custom-call | tf_op jit(solution)/shard_map/pallas_call | solution.py:55
  82.1 1.6 %collective-permute-start.34 = (f32[64,768]{1,0:T(8,128)S(1)}, f32[64,768]{1,0:T(8,128)S(1)}, u32[]{:S(2)}, u32[]{:S(2)}) collective-permute-start(f32[64,768]{1,0:T(8,128)S(1)} %get-tuple-element.96.refs_7_), channel_id=1, source_target_pairs={{0,2},{1,3},{2,0},{3,1},{4,6},{5,7},{6,4},{7,5},{8,10},{9,11},{10,... | collective-permute-start | bytes 589832 | tf_op jit(solution)/shard_map/ppermute | solution.py:551
  83.6 1.2 shard_map.79
  84.8 0.6 collective-permute-start.28
  85.4 1.8 %shard_map.77 = (f32[64,1024]{1,0:T(8,128)S(1)}, f32[64,1024]{1,0:T(8,128)S(1)}) custom-call(s32[4,64]{1,0:T(4,128)S(1)} %bitcast.16, s32[2,64]{1,0:T(2,128)S(1)} %get-tuple-element.58.order_ref.order_near, bf16[2,48,128,128]{3,2,1,0:T(8,128)(2,1)S(1)} %get-tuple-element.90.ext, bf16[64,256,256]{2,1,0:T(8,128)(2,1)S(1)} %shard_map.66.w_ref.refs_1_, ...), custom_call_target="tpu_custom_call" | custom-call | tf_op jit(solution)/shard_map/pallas_call | solution.py:55
  87.2 1.6 %collective-permute-start.36 = (f32[64,1024]{1,0:T(8,128)S(1)}, f32[64,1024]{1,0:T(8,128)S(1)}, u32[]{:S(2)}, u32[]{:S(2)}) collective-permute-start(f32[64,1024]{1,0:T(8,128)S(1)} %get-tuple-element.97.refs_8_), channel_id=1, source_target_pairs={{0,2},{1,3},{2,0},{3,1},{4,6},{5,7},{6,4},{7,5},{8,10},{9,11},{10,... | collective-permute-start | bytes 786440 | tf_op jit(solution)/shard_map/ppermute | solution.py:551
  88.8 9.0 %collective-permute-done.28.refs_2_ = f32[64,512]{1,0:T(8,128)S(1)} collective-permute-done((f32[64,512]{1,0:T(8,128)S(1)}, f32[64,512]{1,0:T(8,128)S(1)}, u32[]{:S(2)}, u32[]{:S(2)}) %collective-permute-start.28) | collective-permute-done | bytes 131104 | tf_op jit(solution)/shard_map/ppermute | solution.py:551
  97.7 0.5 collective-permute-start.25
  98.3 0.1 collective-permute-start.24
  98.3 0.4 collective-permute-start.31
  98.8 4.1 %collective-permute-done.36.refs_8_ = f32[64,1024]{1,0:T(8,128)S(1)} collective-permute-done((f32[64,1024]{1,0:T(8,128)S(1)}, f32[64,1024]{1,0:T(8,128)S(1)}, u32[]{:S(2)}, u32[]{:S(2)}) %collective-permute-start.36) | collective-permute-done | bytes 262176 | tf_op jit(solution)/shard_map/ppermute | solution.py:551
  102.9 0.5 collective-permute-start.35
  103.5 0.4 collective-permute-start.29
  103.9 1.2 shard_map.81.refs_11_.refs_5_.u_ref
  105.1 0.6 shard_map.80
  105.7 0.6 shard_map.82.refs_6_
  106.3 0.3 shard_map.83.refs_6_
  106.7 0.4 shard_map.84
  107.0 10.8 %all_to_all.5.sums_ref = f32[32,1,128]{2,1,0:T(1,128)S(1)} all-to-all(f32[32,1,128]{2,1,0:T(1,128)S(1)} %shard_map.84), channel_id=1, replica_groups=mesh['dom'=8,'samp'=4] {'dom','samp'}, dimensions={0} | all-to-all | bytes 32768 | tf_op jit(solution)/shard_map/all_to_all | solution.py:642
  117.9 1.2 update.1
  (50 shorter events, 0.2 us)
Async XLA Ops:
  1.5 9.9 %collective-permute-start = (f32[64,256]{1,0:T(8,128)S(1)}, f32[64,256]{1,0:T(8,128)S(1)}, u32[]{:S(2)}, u32[]{:S(2)}) collective-permute-start(f32[64,256]{1,0:T(8,128)S(1)} %get-tuple-element.63), channel_id=1, source_target_pairs={{0,16},{4,20},{8,24},{12,28},{16,0},{20,4},{24,8},{28,12},{1,17},{... | collective-permute-start | bytes 196616 | tf_op jit(solution)/shard_map/ppermute | solution.py:534
  5.7 10.0 %collective-permute-start.1 = (f32[64,256]{1,0:T(8,128)S(1)}, f32[64,256]{1,0:T(8,128)S(1)}, u32[]{:S(2)}, u32[]{:S(2)}) collective-permute-start(f32[64,256]{1,0:T(8,128)S(1)} %get-tuple-element.64), channel_id=1, source_target_pairs={{0,20},{4,16},{8,28},{12,24},{16,4},{20,0},{24,12},{28,8},{1,21},{... | collective-permute-start | bytes 196616 | tf_op jit(solution)/shard_map/ppermute | solution.py:534
  7.0 17.3 %collective-permute-start.2 = (f32[64,256]{1,0:T(8,128)S(1)}, f32[64,256]{1,0:T(8,128)S(1)}, u32[]{:S(2)}, u32[]{:S(2)}) collective-permute-start(f32[64,256]{1,0:T(8,128)S(1)} %get-tuple-element.65), channel_id=1, source_target_pairs={{0,24},{4,28},{8,16},{12,20},{16,8},{20,12},{24,0},{28,4},{1,25},{... | collective-permute-start | bytes 196616 | tf_op jit(solution)/shard_map/ppermute | solution.py:534
  10.6 13.7 %collective-permute-start.3 = (f32[64,256]{1,0:T(8,128)S(1)}, f32[64,256]{1,0:T(8,128)S(1)}, u32[]{:S(2)}, u32[]{:S(2)}) collective-permute-start(f32[64,256]{1,0:T(8,128)S(1)} %get-tuple-element.66), channel_id=1, source_target_pairs={{0,28},{4,24},{8,20},{12,16},{16,12},{20,8},{24,4},{28,0},{1,29},{... | collective-permute-start | bytes 196616 | tf_op jit(solution)/shard_map/ppermute | solution.py:534
  10.6 13.7 %collective-permute-start.4 = (f32[64,256]{1,0:T(8,128)S(1)}, f32[64,256]{1,0:T(8,128)S(1)}, u32[]{:S(2)}, u32[]{:S(2)}) collective-permute-start(f32[64,256]{1,0:T(8,128)S(1)} %get-tuple-element.67), channel_id=1, source_target_pairs={{0,12},{4,8},{8,4},{12,0},{16,28},{20,24},{24,20},{28,16},{1,13},{... | collective-permute-start | bytes 196616 | tf_op jit(solution)/shard_map/ppermute | solution.py:534
  11.5 12.8 %collective-permute-start.5 = (f32[64,256]{1,0:T(8,128)S(1)}, f32[64,256]{1,0:T(8,128)S(1)}, u32[]{:S(2)}, u32[]{:S(2)}) collective-permute-start(f32[64,256]{1,0:T(8,128)S(1)} %get-tuple-element.68), channel_id=1, source_target_pairs={{0,8},{4,12},{8,0},{12,4},{16,24},{20,28},{24,16},{28,20},{1,9},{5... | collective-permute-start | bytes 196616 | tf_op jit(solution)/shard_map/ppermute | solution.py:534
  15.7 8.6 %collective-permute-start.6 = (f32[64,256]{1,0:T(8,128)S(1)}, f32[64,256]{1,0:T(8,128)S(1)}, u32[]{:S(2)}, u32[]{:S(2)}) collective-permute-start(f32[64,256]{1,0:T(8,128)S(1)} %get-tuple-element.69), channel_id=1, source_target_pairs={{0,4},{4,0},{8,12},{12,8},{16,20},{20,16},{24,28},{28,24},{1,5},{5... | collective-permute-start | bytes 196616 | tf_op jit(solution)/shard_map/ppermute | solution.py:534
  17.2 4.7 %copy-start = (f32[64,4096]{1,0:T(8,128)S(1)}, f32[64,4096]{1,0:T(8,128)}, u32[]{:S(2)}) copy-start(f32[64,4096]{1,0:T(8,128)} %g_ref.11) | copy-start | bytes 3145732
  17.2 4.7 %copy-start.1 = (f32[64,4096]{1,0:T(8,128)S(1)}, f32[64,4096]{1,0:T(8,128)}, u32[]{:S(2)}) copy-start(f32[64,4096]{1,0:T(8,128)} %c_ref.11) | copy-start | bytes 3145732
  21.9 2.5 %copy-start.2 = (s32[64,4]{0,1:T(4,128)S(1)}, s32[64,4]{0,1:T(4,128)}, u32[]{:S(2)}) copy-start(s32[64,4]{0,1:T(4,128)} %param.10) | copy-start | bytes 3076
  23.0 4.4 %slice-start = ((s8[8388608]{0:T(1024)(128)(4,1)}), s8[4194304]{0:T(1024)(128)(4,1)S(1)}, s32[]{:S(2)}) async-start(s8[8388608]{0:T(1024)(128)(4,1)} %bitcast.6), calls=%async_computation.1 | async-start | bytes 8388608
  24.3 3.1 %slice-start.1 = ((s8[8388608]{0:T(1024)(128)(4,1)}), s8[4194304]{0:T(1024)(128)(4,1)S(1)}, s32[]{:S(2)}) async-start(s8[8388608]{0:T(1024)(128)(4,1)} %bitcast.6), calls=%async_computation.2 | async-start | bytes 8388608
  28.9 27.7 %copy-start.3 = (s32[1,8,4]{1,2,0:T(4,128)S(1)}, s32[1,8,4]{1,2,0:T(4,128)}, u32[]{:S(2)}) copy-start(s32[1,8,4]{1,2,0:T(4,128)} %param.11) | copy-start | bytes 388
  31.3 16.2 %collective-permute-start.8 = (f32[64,2304]{1,0:T(8,128)S(1)}, f32[64,2304]{1,0:T(8,128)S(1)}, u32[]{:S(2)}, u32[]{:S(2)}) collective-permute-start(f32[64,2304]{1,0:T(8,128)S(1)} %get-tuple-element.74.refs_2_), channel_id=1, source_target_pairs={{0,2},{1,3},{2,0},{3,1},{4,6},{5,7},{6,4},{7,5},{8,10},{9,11},{10,... | collective-permute-start | bytes 1769480 | tf_op jit(solution)/shard_map/ppermute | solution.py:551
  32.9 18.5 %collective-permute-start.14 = (f32[64,1280]{1,0:T(8,128)S(1)}, f32[64,1280]{1,0:T(8,128)S(1)}, u32[]{:S(2)}, u32[]{:S(2)}) collective-permute-start(f32[64,1280]{1,0:T(8,128)S(1)} %get-tuple-element.78.refs_4_), channel_id=1, source_target_pairs={{0,2},{1,3},{2,0},{3,1},{4,6},{5,7},{6,4},{7,5},{8,10},{9,11},{10,... | collective-permute-start | bytes 983048 | tf_op jit(solution)/shard_map/ppermute | solution.py:551
  33.4 33.2 %collective-permute-start.7 = (f32[64,2304]{1,0:T(8,128)S(1)}, f32[64,2304]{1,0:T(8,128)S(1)}, u32[]{:S(2)}, u32[]{:S(2)}) collective-permute-start(f32[64,2304]{1,0:T(8,128)S(1)} %get-tuple-element.74.refs_2_), channel_id=1, source_target_pairs={{0,1},{1,0},{2,3},{3,2},{4,5},{5,4},{6,7},{7,6},{8,9},{9,8},{10,11... | collective-permute-start | bytes 1769480 | tf_op jit(solution)/shard_map/ppermute | solution.py:552
  47.5 22.9 %collective-permute-start.9 = (f32[64,2304]{1,0:T(8,128)S(1)}, f32[64,2304]{1,0:T(8,128)S(1)}, u32[]{:S(2)}, u32[]{:S(2)}) collective-permute-start(f32[64,2304]{1,0:T(8,128)S(1)} %collective-permute-done.8.refs_2_), channel_id=1, source_target_pairs={{0,1},{1,0},{2,3},{3,2},{4,5},{5,4},{6,7},{7,6},{8,9},{9,8},{10,11... | collective-permute-start | bytes 1769480 | tf_op jit(solution)/shard_map/ppermute | solution.py:564
  47.5 6.3 %collective-permute-start.12 = (f32[64,512]{1,0:T(8,128)S(1)}, f32[64,512]{1,0:T(8,128)S(1)}, u32[]{:S(2)}, u32[]{:S(2)}) collective-permute-start(f32[64,512]{1,0:T(8,128)S(1)} %get-tuple-element.77.refs_3_), channel_id=1, source_target_pairs={{0,2},{1,3},{2,0},{3,1},{4,6},{5,7},{6,4},{7,5},{8,10},{9,11},{10,... | collective-permute-start | bytes 393224 | tf_op jit(solution)/shard_map/ppermute | solution.py:551
  49.0 6.3 %collective-permute-start.11 = (f32[64,1280]{1,0:T(8,128)S(1)}, f32[64,1280]{1,0:T(8,128)S(1)}, u32[]{:S(2)}, u32[]{:S(2)}) collective-permute-start(f32[64,1280]{1,0:T(8,128)S(1)} %get-tuple-element.78.refs_4_), channel_id=1, source_target_pairs={{0,1},{1,0},{2,3},{3,2},{4,5},{5,4},{6,7},{7,6},{8,9},{9,8},{10,11... | collective-permute-start | bytes 983048 | tf_op jit(solution)/shard_map/ppermute | solution.py:552
  51.5 5.1 %collective-permute-start.15 = (f32[64,1280]{1,0:T(8,128)S(1)}, f32[64,1280]{1,0:T(8,128)S(1)}, u32[]{:S(2)}, u32[]{:S(2)}) collective-permute-start(f32[64,1280]{1,0:T(8,128)S(1)} %collective-permute-done.14.refs_5_), channel_id=1, source_target_pairs={{0,1},{1,0},{2,3},{3,2},{4,5},{5,4},{6,7},{7,6},{8,9},{9,8},{10,11... | collective-permute-start | bytes 983048 | tf_op jit(solution)/shard_map/ppermute | solution.py:564
  53.9 1.3 %collective-permute-start.10 = (f32[64,512]{1,0:T(8,128)S(1)}, f32[64,512]{1,0:T(8,128)S(1)}, u32[]{:S(2)}, u32[]{:S(2)}) collective-permute-start(f32[64,512]{1,0:T(8,128)S(1)} %get-tuple-element.77.refs_3_), channel_id=1, source_target_pairs={{0,1},{1,0},{2,3},{3,2},{4,5},{5,4},{6,7},{7,6},{8,9},{9,8},{10,11... | collective-permute-start | bytes 393224 | tf_op jit(solution)/shard_map/ppermute | solution.py:552
  55.2 1.3 %collective-permute-start.13 = (f32[64,512]{1,0:T(8,128)S(1)}, f32[64,512]{1,0:T(8,128)S(1)}, u32[]{:S(2)}, u32[]{:S(2)}) collective-permute-start(f32[64,512]{1,0:T(8,128)S(1)} %collective-permute-done.12.refs_2_), channel_id=1, source_target_pairs={{0,1},{1,0},{2,3},{3,2},{4,5},{5,4},{6,7},{7,6},{8,9},{9,8},{10,11... | collective-permute-start | bytes 393224 | tf_op jit(solution)/shard_map/ppermute | solution.py:564
  57.7 9.0 %collective-permute-start.16 = (f32[64,256]{1,0:T(8,128)S(1)}, f32[64,256]{1,0:T(8,128)S(1)}, u32[]{:S(2)}, u32[]{:S(2)}) collective-permute-start(f32[64,256]{1,0:T(8,128)S(1)} %get-tuple-element.82), channel_id=1, source_target_pairs={{0,16},{4,20},{8,24},{12,28},{16,0},{20,4},{24,8},{28,12},{1,17},{... | collective-permute-start | bytes 196616 | tf_op jit(solution)/shard_map/ppermute | solution.py:534
  60.7 9.7 %collective-permute-start.17 = (f32[64,256]{1,0:T(8,128)S(1)}, f32[64,256]{1,0:T(8,128)S(1)}, u32[]{:S(2)}, u32[]{:S(2)}) collective-permute-start(f32[64,256]{1,0:T(8,128)S(1)} %get-tuple-element.83), channel_id=1, source_target_pairs={{0,20},{4,16},{8,28},{12,24},{16,4},{20,0},{24,12},{28,8},{1,21},{... | collective-permute-start | bytes 196616 | tf_op jit(solution)/shard_map/ppermute | solution.py:534
  61.8 10.6 %collective-permute-start.18 = (f32[64,256]{1,0:T(8,128)S(1)}, f32[64,256]{1,0:T(8,128)S(1)}, u32[]{:S(2)}, u32[]{:S(2)}) collective-permute-start(f32[64,256]{1,0:T(8,128)S(1)} %get-tuple-element.84), channel_id=1, source_target_pairs={{0,24},{4,28},{8,16},{12,20},{16,8},{20,12},{24,0},{28,4},{1,25},{... | collective-permute-start | bytes 196616 | tf_op jit(solution)/shard_map/ppermute | solution.py:534
  66.6 7.2 %collective-permute-start.19 = (f32[64,256]{1,0:T(8,128)S(1)}, f32[64,256]{1,0:T(8,128)S(1)}, u32[]{:S(2)}, u32[]{:S(2)}) collective-permute-start(f32[64,256]{1,0:T(8,128)S(1)} %get-tuple-element.85), channel_id=1, source_target_pairs={{0,28},{4,24},{8,20},{12,16},{16,12},{20,8},{24,4},{28,0},{1,29},{... | collective-permute-start | bytes 196616 | tf_op jit(solution)/shard_map/ppermute | solution.py:534
  66.7 7.3 %collective-permute-start.20 = (f32[64,256]{1,0:T(8,128)S(1)}, f32[64,256]{1,0:T(8,128)S(1)}, u32[]{:S(2)}, u32[]{:S(2)}) collective-permute-start(f32[64,256]{1,0:T(8,128)S(1)} %get-tuple-element.86), channel_id=1, source_target_pairs={{0,12},{4,8},{8,4},{12,0},{16,28},{20,24},{24,20},{28,16},{1,13},{... | collective-permute-start | bytes 196616 | tf_op jit(solution)/shard_map/ppermute | solution.py:534
  70.4 4.3 %collective-permute-start.21 = (f32[64,256]{1,0:T(8,128)S(1)}, f32[64,256]{1,0:T(8,128)S(1)}, u32[]{:S(2)}, u32[]{:S(2)}) collective-permute-start(f32[64,256]{1,0:T(8,128)S(1)} %get-tuple-element.87), channel_id=1, source_target_pairs={{0,8},{4,12},{8,0},{12,4},{16,24},{20,28},{24,16},{28,20},{1,9},{5... | collective-permute-start | bytes 196616 | tf_op jit(solution)/shard_map/ppermute | solution.py:534
  70.4 4.8 %collective-permute-start.22 = (f32[64,256]{1,0:T(8,128)S(1)}, f32[64,256]{1,0:T(8,128)S(1)}, u32[]{:S(2)}, u32[]{:S(2)}) collective-permute-start(f32[64,256]{1,0:T(8,128)S(1)} %get-tuple-element.88), channel_id=1, source_target_pairs={{0,4},{4,0},{8,12},{12,8},{16,20},{20,16},{24,28},{28,24},{1,5},{5... | collective-permute-start | bytes 196616 | tf_op jit(solution)/shard_map/ppermute | solution.py:534
  76.4 8.9 %collective-permute-start.32 = (f32[64,512]{1,0:T(8,128)S(1)}, f32[64,512]{1,0:T(8,128)S(1)}, u32[]{:S(2)}, u32[]{:S(2)}) collective-permute-start(f32[64,512]{1,0:T(8,128)S(1)} %get-tuple-element.95.refs_6_), channel_id=1, source_target_pairs={{0,2},{1,3},{2,0},{3,1},{4,6},{5,7},{6,4},{7,5},{8,10},{9,11},{10,... | collective-permute-start | bytes 393224 | tf_op jit(solution)/shard_map/ppermute | solution.py:551
  78.0 9.2 %collective-permute-start.23 = (f32[64,512]{1,0:T(8,128)S(1)}, f32[64,512]{1,0:T(8,128)S(1)}, u32[]{:S(2)}, u32[]{:S(2)}) collective-permute-start(f32[64,512]{1,0:T(8,128)S(1)} %get-tuple-element.95.refs_6_), channel_id=1, source_target_pairs={{0,1},{1,0},{2,3},{3,2},{4,5},{5,4},{6,7},{7,6},{8,9},{9,8},{10,11... | collective-permute-start | bytes 393224 | tf_op jit(solution)/shard_map/ppermute | solution.py:552
  80.1 18.3 %collective-permute-start.30 = (f32[64,1280]{1,0:T(8,128)S(1)}, f32[64,1280]{1,0:T(8,128)S(1)}, u32[]{:S(2)}, u32[]{:S(2)}) collective-permute-start(f32[64,1280]{1,0:T(8,128)S(1)} %get-tuple-element.98.refs_9_), channel_id=1, source_target_pairs={{0,2},{1,3},{2,0},{3,1},{4,6},{5,7},{6,4},{7,5},{8,10},{9,11},{10,... | collective-permute-start | bytes 983048 | tf_op jit(solution)/shard_map/ppermute | solution.py:551
  82.1 16.2 %collective-permute-start.34 = (f32[64,768]{1,0:T(8,128)S(1)}, f32[64,768]{1,0:T(8,128)S(1)}, u32[]{:S(2)}, u32[]{:S(2)}) collective-permute-start(f32[64,768]{1,0:T(8,128)S(1)} %get-tuple-element.96.refs_7_), channel_id=1, source_target_pairs={{0,2},{1,3},{2,0},{3,1},{4,6},{5,7},{6,4},{7,5},{8,10},{9,11},{10,... | collective-permute-start | bytes 589832 | tf_op jit(solution)/shard_map/ppermute | solution.py:551
  84.8 13.0 %collective-permute-start.28 = (f32[64,512]{1,0:T(8,128)S(1)}, f32[64,512]{1,0:T(8,128)S(1)}, u32[]{:S(2)}, u32[]{:S(2)}) collective-permute-start(f32[64,512]{1,0:T(8,128)S(1)} %get-tuple-element.99.refs_10_), channel_id=1, source_target_pairs={{0,2},{1,3},{2,0},{3,1},{4,6},{5,7},{6,4},{7,5},{8,10},{9,11},{10,... | collective-permute-start | bytes 393224 | tf_op jit(solution)/shard_map/ppermute | solution.py:551
  85.4 12.4 %collective-permute-start.27 = (f32[64,512]{1,0:T(8,128)S(1)}, f32[64,512]{1,0:T(8,128)S(1)}, u32[]{:S(2)}, u32[]{:S(2)}) collective-permute-start(f32[64,512]{1,0:T(8,128)S(1)} %get-tuple-element.99.refs_10_), channel_id=1, source_target_pairs={{0,1},{1,0},{2,3},{3,2},{4,5},{5,4},{6,7},{7,6},{8,9},{9,8},{10,11... | collective-permute-start | bytes 393224 | tf_op jit(solution)/shard_map/ppermute | solution.py:552
  87.2 15.7 %collective-permute-start.36 = (f32[64,1024]{1,0:T(8,128)S(1)}, f32[64,1024]{1,0:T(8,128)S(1)}, u32[]{:S(2)}, u32[]{:S(2)}) collective-permute-start(f32[64,1024]{1,0:T(8,128)S(1)} %get-tuple-element.97.refs_8_), channel_id=1, source_target_pairs={{0,2},{1,3},{2,0},{3,1},{4,6},{5,7},{6,4},{7,5},{8,10},{9,11},{10,... | collective-permute-start | bytes 786440 | tf_op jit(solution)/shard_map/ppermute | solution.py:551
  97.7 5.8 %collective-permute-start.26 = (f32[64,1280]{1,0:T(8,128)S(1)}, f32[64,1280]{1,0:T(8,128)S(1)}, u32[]{:S(2)}, u32[]{:S(2)}) collective-permute-start(f32[64,1280]{1,0:T(8,128)S(1)} %get-tuple-element.98.refs_9_), channel_id=1, source_target_pairs={{0,1},{1,0},{2,3},{3,2},{4,5},{5,4},{6,7},{7,6},{8,9},{9,8},{10,11... | collective-permute-start | bytes 983048 | tf_op jit(solution)/shard_map/ppermute | solution.py:552
  97.7 5.7 %collective-permute-start.25 = (f32[64,1024]{1,0:T(8,128)S(1)}, f32[64,1024]{1,0:T(8,128)S(1)}, u32[]{:S(2)}, u32[]{:S(2)}) collective-permute-start(f32[64,1024]{1,0:T(8,128)S(1)} %get-tuple-element.97.refs_8_), channel_id=1, source_target_pairs={{0,1},{1,0},{2,3},{3,2},{4,5},{5,4},{6,7},{7,6},{8,9},{9,8},{10,11... | collective-permute-start | bytes 786440 | tf_op jit(solution)/shard_map/ppermute | solution.py:552
  98.3 4.7 %collective-permute-start.24 = (f32[64,768]{1,0:T(8,128)S(1)}, f32[64,768]{1,0:T(8,128)S(1)}, u32[]{:S(2)}, u32[]{:S(2)}) collective-permute-start(f32[64,768]{1,0:T(8,128)S(1)} %get-tuple-element.96.refs_7_), channel_id=1, source_target_pairs={{0,1},{1,0},{2,3},{3,2},{4,5},{5,4},{6,7},{7,6},{8,9},{9,8},{10,11... | collective-permute-start | bytes 589832 | tf_op jit(solution)/shard_map/ppermute | solution.py:552
  98.3 8.0 %collective-permute-start.31 = (f32[64,1280]{1,0:T(8,128)S(1)}, f32[64,1280]{1,0:T(8,128)S(1)}, u32[]{:S(2)}, u32[]{:S(2)}) collective-permute-start(f32[64,1280]{1,0:T(8,128)S(1)} %collective-permute-done.30.refs_2_), channel_id=1, source_target_pairs={{0,1},{1,0},{2,3},{3,2},{4,5},{5,4},{6,7},{7,6},{8,9},{9,8},{10,11... | collective-permute-start | bytes 983048 | tf_op jit(solution)/shard_map/ppermute | solution.py:564
  102.9 2.8 %collective-permute-start.37 = (f32[64,1024]{1,0:T(8,128)S(1)}, f32[64,1024]{1,0:T(8,128)S(1)}, u32[]{:S(2)}, u32[]{:S(2)}) collective-permute-start(f32[64,1024]{1,0:T(8,128)S(1)} %collective-permute-done.36.refs_8_), channel_id=1, source_target_pairs={{0,1},{1,0},{2,3},{3,2},{4,5},{5,4},{6,7},{7,6},{8,9},{9,8},{10,11... | collective-permute-start | bytes 786440 | tf_op jit(solution)/shard_map/ppermute | solution.py:564
  102.9 2.8 %collective-permute-start.35 = (f32[64,768]{1,0:T(8,128)S(1)}, f32[64,768]{1,0:T(8,128)S(1)}, u32[]{:S(2)}, u32[]{:S(2)}) collective-permute-start(f32[64,768]{1,0:T(8,128)S(1)} %collective-permute-done.34.refs_5_), channel_id=1, source_target_pairs={{0,1},{1,0},{2,3},{3,2},{4,5},{5,4},{6,7},{7,6},{8,9},{9,8},{10,11... | collective-permute-start | bytes 589832 | tf_op jit(solution)/shard_map/ppermute | solution.py:564
  103.4 2.3 %collective-permute-start.33 = (f32[64,512]{1,0:T(8,128)S(1)}, f32[64,512]{1,0:T(8,128)S(1)}, u32[]{:S(2)}, u32[]{:S(2)}) collective-permute-start(f32[64,512]{1,0:T(8,128)S(1)} %collective-permute-done.32.refs_2_), channel_id=1, source_target_pairs={{0,1},{1,0},{2,3},{3,2},{4,5},{5,4},{6,7},{7,6},{8,9},{9,8},{10,11... | collective-permute-start | bytes 393224 | tf_op jit(solution)/shard_map/ppermute | solution.py:564
  103.5 3.2 %collective-permute-start.29 = (f32[64,512]{1,0:T(8,128)S(1)}, f32[64,512]{1,0:T(8,128)S(1)}, u32[]{:S(2)}, u32[]{:S(2)}) collective-permute-start(f32[64,512]{1,0:T(8,128)S(1)} %collective-permute-done.28.refs_2_), channel_id=1, source_target_pairs={{0,1},{1,0},{2,3},{3,2},{4,5},{5,4},{6,7},{7,6},{8,9},{9,8},{10,11... | collective-permute-start | bytes 393224 | tf_op jit(solution)/shard_map/ppermute | solution.py:564

commit v5 on v4

--- a/solution.py
+++ b/solution.py
@@ -354,9 +354,9 @@
     lax.fori_loop(0, count // group, block, 0)
 
 
-def permuted_product(first_row, base_row, cols_ref, order_ref, ext, w_ref, g_ref, c_ref, p_ref, q_ref):
+def permuted_product(first_row, cols_ref, order_ref, ext, w_ref, g_ref, c_ref, p_ref, q_ref):
     def own_terms(row):
-        there = pl.ds(pl.multiple_of((first_row - base_row + row) * HALF, LANES), LANES)
+        there = pl.ds(pl.multiple_of(row * HALF, LANES), LANES)
         return g_ref[:, there], c_ref[:, there]
 
     product_rows(first_row, True, cols_ref, order_ref, ext, w_ref, p_ref, q_ref, own_terms)
@@ -580,27 +580,22 @@
             ((2 * samples, count * samples), jnp.bfloat16),
         ],
     )
-    own = []
-    for n, (low, high) in enumerate(((0, early), (early, rows))):
-        if n:
-            (weights,) = kernel_call(
-                functools.partial(prepare_kernel, low, high), (order, blocks, weights), [weight_shape], aliases={2: 0}
-            )
-        terms = kernel_call(
-            functools.partial(arrange_kernel, low),
-            (order, field, conductance, capacitance),
-            [((samples, (high - low) * width), f32)] * 2,
-        )
-        own.append((low, weights, terms))
+    (all_weights,) = kernel_call(
+        functools.partial(prepare_kernel, early, rows), (order, blocks, weights), [weight_shape], aliases={2: 0}
+    )
     chunks = []
     first = 0
     for n, size in enumerate(sizes_one):
-        base, w, terms = own[first >= early]
-        ext, p, q = product_call(
-            n, size, functools.partial(permuted_product, first, base), (cols, order, ext, w, *terms), incoming
+        terms = kernel_call(
+            functools.partial(arrange_kernel, first),
+            (order, field, conductance, capacitance),
+            [((samples, size * width), f32)] * 2,
         )
+        operands = (cols, order, ext, weights if first < early else all_weights, *terms)
+        ext, p, q = product_call(n, size, functools.partial(permuted_product, first), operands, incoming)
         chunks.append((p, q, *spread(q)))
         first += size
+    weights = all_weights
     half = near_call(chunks[:2]) + near_call(chunks[2:])
     pieces = [forward(half[n], chunk[2]) for n, chunk in enumerate(chunks)]
     ready = 2 if few(domains) else len(chunks)

time: 119 us -> 125 us (1.050)
  waiting for transfers between devices: 41.9 us -> 46.3 us
    ppermute x8, waiting for transfers between devices: 31.8 us -> 37.4 us  [spread(): lax.ppermute(q, 'samp', [(i, (i + k) % groups) for i in range(groups)])]
    ppermute x8, waiting for transfers between devices: 1.36 us -> 0.02 us  [spread(): return (far, lax.ppermute(q, 'samp', pairs))]
    pallas_call x21 -> x22, Pallas kernels: 22.5 us -> 23.1 us  [kernel_call(): pl.pallas_call(kernel, in_specs=specs, out_specs=[scalars() if number els...]
  transfers between devices with their start and end apart: 38 -> 38, of which waited for: 13 -> 14; matrix products, arithmetic and copies ran while one was open for 0% -> 0% of each run, Pallas kernels for 16% -> 15%
where the time goes in v5:
time: 125 us
  waiting for transfers between devices  46.3 us (37%)
  starting transfers between devices  35.5 us (28%)
  Pallas kernels  30.5 us (24%)
  blocking collectives  11.8 us (9%)
    ppermute x8, waiting for transfers between devices, spread(): lax.ppermute(q, 'samp', [(i, (i + k) % groups) for i in range(groups)])  37.4 us
    ppermute x14, starting transfers between devices, exchange(): lax.ppermute(x, 'dom', [(i, i ^ k) for i in range(domains)])  24.2 us
    pallas_call x22, Pallas kernels, kernel_call(): pl.pallas_call(kernel, in_specs=specs, out_specs=[scalars() if number els...  23.1 us
    all_to_all x1, blocking collectives, body(): lax.all_to_all(sums, ('dom', 'samp'), split_axis=0, concat_axis=0, tiled=...  11.8 us
    ppermute x8, starting transfers between devices, spread(): lax.ppermute(q, 'samp', [(i, (i + k) % groups) for i in range(groups)])  9.34 us
    ppermute x14, waiting for transfers between devices, exchange(): lax.ppermute(x, 'dom', [(i, i ^ k) for i in range(domains)])  7.85 us
    pallas_call x1, Pallas kernels, fetch(): pl.pallas_call(functools.partial(fetch_kernel, domains, groups), in_specs...  4.66 us
  transfers between devices with their start and end apart: 38, of which 14 were waited for; matrix products, arithmetic and copies ran while one was open for 0% of the time, Pallas kernels for 15%

profile of v5, /device:TPU:0, one launch (start us, length us, event | category | flops | bytes accessed | tf_op | source)
XLA Modules:
  0.0 124.7 jit_solution(3166175717445635428)
XLA Ops:
  0.0 1.5 %gather.1 = (f32[64,4096]{1,0:T(8,128)S(1)}, f32[64,256]{1,0:T(8,128)S(1)}, f32[64,256]{1,0:T(8,128)S(1)}, f32[64,256]{1,0:T(8,128)S(1)}, f32[64,256]{1,0:T(8,12...) custom-call(s32[4,8]{1,0:T(4,128)} %bitcast.17, f32[64,4096]{1,0:T(8,128)} %field_hbm.1), custom_call_target="tpu_custom_call" | custom-call | tf_op jit(solution)/shard_map/gather/pallas_call | solution.py:230
  1.5 4.1 %collective-permute-start = (f32[64,256]{1,0:T(8,128)S(1)}, f32[64,256]{1,0:T(8,128)S(1)}, u32[]{:S(2)}, u32[]{:S(2)}) collective-permute-start(f32[64,256]{1,0:T(8,128)S(1)} %get-tuple-element.65), channel_id=1, source_target_pairs={{0,16},{4,20},{8,24},{12,28},{16,0},{20,4},{24,8},{28,12},{1,17},{... | collective-permute-start | bytes 196616 | tf_op jit(solution)/shard_map/ppermute | solution.py:534
  5.7 1.3 %collective-permute-start.1 = (f32[64,256]{1,0:T(8,128)S(1)}, f32[64,256]{1,0:T(8,128)S(1)}, u32[]{:S(2)}, u32[]{:S(2)}) collective-permute-start(f32[64,256]{1,0:T(8,128)S(1)} %get-tuple-element.66), channel_id=1, source_target_pairs={{0,20},{4,16},{8,28},{12,24},{16,4},{20,0},{24,12},{28,8},{1,21},{... | collective-permute-start | bytes 196616 | tf_op jit(solution)/shard_map/ppermute | solution.py:534
  7.0 3.6 %collective-permute-start.2 = (f32[64,256]{1,0:T(8,128)S(1)}, f32[64,256]{1,0:T(8,128)S(1)}, u32[]{:S(2)}, u32[]{:S(2)}) collective-permute-start(f32[64,256]{1,0:T(8,128)S(1)} %get-tuple-element.67), channel_id=1, source_target_pairs={{0,24},{4,28},{8,16},{12,20},{16,8},{20,12},{24,0},{28,4},{1,25},{... | collective-permute-start | bytes 196616 | tf_op jit(solution)/shard_map/ppermute | solution.py:534
  10.6 0.9 collective-permute-start.4
  11.5 2.2 %collective-permute-start.5 = (f32[64,256]{1,0:T(8,128)S(1)}, f32[64,256]{1,0:T(8,128)S(1)}, u32[]{:S(2)}, u32[]{:S(2)}) collective-permute-start(f32[64,256]{1,0:T(8,128)S(1)} %get-tuple-element.70), channel_id=1, source_target_pairs={{0,8},{4,12},{8,0},{12,4},{16,24},{20,28},{24,16},{28,20},{1,9},{5... | collective-permute-start | bytes 196616 | tf_op jit(solution)/shard_map/ppermute | solution.py:534
  13.7 2.0 %collective-permute-done.1.refs_5_ = f32[64,256]{1,0:T(8,128)S(1)} collective-permute-done((f32[64,256]{1,0:T(8,128)S(1)}, f32[64,256]{1,0:T(8,128)S(1)}, u32[]{:S(2)}, u32[]{:S(2)}) %collective-permute-start.1) | collective-permute-done | bytes 65568 | tf_op jit(solution)/shard_map/ppermute | solution.py:534
  15.7 1.5 %collective-permute-start.6 = (f32[64,256]{1,0:T(8,128)S(1)}, f32[64,256]{1,0:T(8,128)S(1)}, u32[]{:S(2)}, u32[]{:S(2)}) collective-permute-start(f32[64,256]{1,0:T(8,128)S(1)} %get-tuple-element.71), channel_id=1, source_target_pairs={{0,4},{4,0},{8,12},{12,8},{16,20},{20,16},{24,28},{28,24},{1,5},{5... | collective-permute-start | bytes 196616 | tf_op jit(solution)/shard_map/ppermute | solution.py:534
  17.2 4.7 %prepare_0.1 = (s32[2,64]{1,0:T(2,128)S(1)}, bf16[64,256,256]{2,1,0:T(8,128)(2,1)S(1)}, bf16[2,48,128,128]{3,2,1,0:T(8,128)(2,1)S(1)}, bf16[128,128]{1,0:T(8,128)(2,1)S(1)}, bf16[128,128]{1,0:T(8,128)(2,1)S(1)}) custom-call(s32[4,8]{1,0:T(4,128)} %bitcast.18, f32[64,4096]{1,0:T(8,128)S(1)} %get-tuple-element.57.field_ref.refs_10_.refs_4_.r_ref, ...), custom_call_target="tpu_custom_call" | custom-call | tf_op jit(solution)/shard_map/prepare_0/pallas_call | solution.py:132
  21.9 0.8 shard_map.64
  22.6 1.0 shard_map.70
  23.6 1.3 %shard_map.67 = (f32[64,2304]{1,0:T(8,128)S(1)}, f32[64,2304]{1,0:T(8,128)S(1)}) custom-call(s32[2,64]{1,0:T(2,128)S(1)} %get-tuple-element.60.order_ref.order_near, f32[64,4096]{1,0:T(8,128)S(1)} %get-tuple-element.57.field_ref.refs_10_.refs_4_.r_ref, f32[64,4096]{1,0:T(8,128)S(1)} %copy-done, f32[64,4096]{1,0:T(8,128)S(1)} %copy-done.1), custom_call_target="tpu_custom_call" | custom-call | tf_op jit(solution)/shard_map/pallas_call | solution.py:55
  25.0 1.2 shard_map.65
  26.2 1.9 %shard_map.71 = (f32[64,1280]{1,0:T(8,128)S(1)}, f32[64,1280]{1,0:T(8,128)S(1)}) custom-call(s32[4,64]{1,0:T(4,128)S(1)} %bitcast.10, s32[2,64]{1,0:T(2,128)S(1)} %get-tuple-element.60.order_ref.order_near, bf16[2,48,128,128]{3,2,1,0:T(8,128)(2,1)S(1)} %get-tuple-element.72.ext, bf16[64,256,256]{2,1,0:T(8,128)(2,1)S(1)} %get-tuple-element.62.refs_1_.refs_0_.w_ref, ...), custom_call_target="tpu_custom_call" | custom-call | tf_op jit(solution)/shard_map/pallas_call | solution.py:55
  28.1 1.4 %shard_map.66.w_ref.refs_1_ = bf16[64,256,256]{2,1,0:T(8,128)(2,1)S(1)} custom-call(s32[2,64]{1,0:T(2,128)S(1)} %get-tuple-element.60.order_ref.order_near, f32[64,256,128]{2,1,0:T(8,128)S(1)} %bitcast.8, bf16[64,256,256]{2,1,0:T(8,128)(2,1)S(1)} %get-tuple-element.62.refs_1_.refs_0_.w_ref), custom_call_target="tpu_custom_call", output_to_operand_aliasing={{}: (2, {})} | custom-call | tf_op jit(solution)/shard_map/pallas_call | solution.py:55
  29.5 2.5 %shard_map.68 = (f32[64,2304]{1,0:T(8,128)S(1)}, f32[64,2304]{1,0:T(8,128)S(1)}) custom-call(s32[4,64]{1,0:T(4,128)S(1)} %bitcast.11, s32[2,64]{1,0:T(2,128)S(1)} %get-tuple-element.60.order_ref.order_near, bf16[2,48,128,128]{3,2,1,0:T(8,128)(2,1)S(1)} %get-tuple-element.72.ext, bf16[64,256,256]{2,1,0:T(8,128)(2,1)S(1)} %shard_map.66.w_ref.refs_1_, ...), custom_call_target="tpu_custom_call" | custom-call | tf_op jit(solution)/shard_map/pallas_call | solution.py:55
  32.0 1.6 %collective-permute-start.8 = (f32[64,2304]{1,0:T(8,128)S(1)}, f32[64,2304]{1,0:T(8,128)S(1)}, u32[]{:S(2)}, u32[]{:S(2)}) collective-permute-start(f32[64,2304]{1,0:T(8,128)S(1)} %get-tuple-element.76.refs_2_), channel_id=1, source_target_pairs={{0,2},{1,3},{2,0},{3,1},{4,6},{5,7},{6,4},{7,5},{8,10},{9,11},{10,... | collective-permute-start | bytes 1769480 | tf_op jit(solution)/shard_map/ppermute | solution.py:551
  33.5 0.5 collective-permute-start.14
  34.1 14.1 %collective-permute-done.8.refs_2_ = f32[64,2304]{1,0:T(8,128)S(1)} collective-permute-done((f32[64,2304]{1,0:T(8,128)S(1)}, f32[64,2304]{1,0:T(8,128)S(1)}, u32[]{:S(2)}, u32[]{:S(2)}) %collective-permute-start.8) | collective-permute-done | bytes 589856 | tf_op jit(solution)/shard_map/ppermute | solution.py:551
  48.2 0.5 collective-permute-start.10
  48.7 3.0 %collective-permute-done.14.refs_5_ = f32[64,1280]{1,0:T(8,128)S(1)} collective-permute-done((f32[64,1280]{1,0:T(8,128)S(1)}, f32[64,1280]{1,0:T(8,128)S(1)}, u32[]{:S(2)}, u32[]{:S(2)}) %collective-permute-start.14) | collective-permute-done | bytes 327712 | tf_op jit(solution)/shard_map/ppermute | solution.py:551
  51.7 1.5 %collective-permute-start.12 = (f32[64,512]{1,0:T(8,128)S(1)}, f32[64,512]{1,0:T(8,128)S(1)}, u32[]{:S(2)}, u32[]{:S(2)}) collective-permute-start(f32[64,512]{1,0:T(8,128)S(1)} %get-tuple-element.81.refs_3_), channel_id=1, source_target_pairs={{0,2},{1,3},{2,0},{3,1},{4,6},{5,7},{6,4},{7,5},{8,10},{9,11},{10,... | collective-permute-start | bytes 393224 | tf_op jit(solution)/shard_map/ppermute | solution.py:551
  53.2 4.4 %collective-permute-done.12.refs_2_ = f32[64,512]{1,0:T(8,128)S(1)} collective-permute-done((f32[64,512]{1,0:T(8,128)S(1)}, f32[64,512]{1,0:T(8,128)S(1)}, u32[]{:S(2)}, u32[]{:S(2)}) %collective-permute-start.12) | collective-permute-done | bytes 131104 | tf_op jit(solution)/shard_map/ppermute | solution.py:551
  57.6 0.3 shard_map.72
  58.0 1.0 collective-permute-done.13.refs_3_
  59.0 1.1 shard_map.73
  60.1 3.1 %collective-permute-start.16 = (f32[64,256]{1,0:T(8,128)S(1)}, f32[64,256]{1,0:T(8,128)S(1)}, u32[]{:S(2)}, u32[]{:S(2)}) collective-permute-start(f32[64,256]{1,0:T(8,128)S(1)} %get-tuple-element.86), channel_id=1, source_target_pairs={{0,16},{4,20},{8,24},{12,28},{16,0},{20,4},{24,8},{28,12},{1,17},{... | collective-permute-start | bytes 196616 | tf_op jit(solution)/shard_map/ppermute | solution.py:534
  63.1 1.1 collective-permute-start.17
  64.2 4.8 %collective-permute-start.18 = (f32[64,256]{1,0:T(8,128)S(1)}, f32[64,256]{1,0:T(8,128)S(1)}, u32[]{:S(2)}, u32[]{:S(2)}) collective-permute-start(f32[64,256]{1,0:T(8,128)S(1)} %get-tuple-element.88), channel_id=1, source_target_pairs={{0,24},{4,28},{8,16},{12,20},{16,8},{20,12},{24,0},{28,4},{1,25},{... | collective-permute-start | bytes 196616 | tf_op jit(solution)/shard_map/ppermute | solution.py:534
  69.0 0.6 collective-permute-start.20
  69.7 3.1 %collective-permute-done.17.refs_6_ = f32[64,256]{1,0:T(8,128)S(1)} collective-permute-done((f32[64,256]{1,0:T(8,128)S(1)}, f32[64,256]{1,0:T(8,128)S(1)}, u32[]{:S(2)}, u32[]{:S(2)}) %collective-permute-start.17) | collective-permute-done | bytes 65568 | tf_op jit(solution)/shard_map/ppermute | solution.py:534
  72.8 0.9 collective-permute-start.22
  73.7 0.4 shard_map.69.refs_1_
  74.1 0.4 shard_map.74.field_ref.refs_2_.u_ref
  74.5 0.3 shard_map.75.refs_0_
  74.9 1.3 %collective-permute-done.19.refs_8_ = f32[64,256]{1,0:T(8,128)S(1)} collective-permute-done((f32[64,256]{1,0:T(8,128)S(1)}, f32[64,256]{1,0:T(8,128)S(1)}, u32[]{:S(2)}, u32[]{:S(2)}) %collective-permute-start.19) | collective-permute-done | bytes 65568 | tf_op jit(solution)/shard_map/ppermute | solution.py:534
  76.2 0.1 collective-permute-done.20.refs_9_
  76.3 0.7 collective-permute-done.21.refs_10_
  77.1 0.5 collective-permute-done.22.refs_11_
  77.6 1.2 shard_map.76
  78.8 0.1 collective-permute-start.23
  78.9 1.2 shard_map.80
  80.1 0.6 collective-permute-start.27
  80.6 2.1 %shard_map.79 = (f32[64,1280]{1,0:T(8,128)S(1)}, f32[64,1280]{1,0:T(8,128)S(1)}) custom-call(s32[4,64]{1,0:T(4,128)S(1)} %bitcast.14, s32[2,64]{1,0:T(2,128)S(1)} %get-tuple-element.60.order_ref.order_near, bf16[2,48,128,128]{3,2,1,0:T(8,128)(2,1)S(1)} %get-tuple-element.94.ext, bf16[64,256,256]{2,1,0:T(8,128)(2,1)S(1)} %shard_map.66.w_ref.refs_1_, ...), custom_call_target="tpu_custom_call" | custom-call | tf_op jit(solution)/shard_map/pallas_call | solution.py:55
  82.7 1.6 %collective-permute-start.30 = (f32[64,1280]{1,0:T(8,128)S(1)}, f32[64,1280]{1,0:T(8,128)S(1)}, u32[]{:S(2)}, u32[]{:S(2)}) collective-permute-start(f32[64,1280]{1,0:T(8,128)S(1)} %get-tuple-element.102.refs_9_), channel_id=1, source_target_pairs={{0,2},{1,3},{2,0},{3,1},{4,6},{5,7},{6,4},{7,5},{8,10},{9,11},{10,... | collective-permute-start | bytes 983048 | tf_op jit(solution)/shard_map/ppermute | solution.py:551
  84.3 1.4 %shard_map.77 = (f32[64,768]{1,0:T(8,128)S(1)}, f32[64,768]{1,0:T(8,128)S(1)}) custom-call(s32[4,64]{1,0:T(4,128)S(1)} %bitcast.15, s32[2,64]{1,0:T(2,128)S(1)} %get-tuple-element.60.order_ref.order_near, bf16[2,48,128,128]{3,2,1,0:T(8,128)(2,1)S(1)} %get-tuple-element.94.ext, bf16[64,256,256]{2,1,0:T(8,128)(2,1)S(1)} %shard_map.66.w_ref.refs_1_, ...), custom_call_target="tpu_custom_call" | custom-call | tf_op jit(solution)/shard_map/pallas_call | solution.py:55
  85.7 0.6 collective-permute-start.28
  86.3 1.5 %collective-permute-start.32 = (f32[64,512]{1,0:T(8,128)S(1)}, f32[64,512]{1,0:T(8,128)S(1)}, u32[]{:S(2)}, u32[]{:S(2)}) collective-permute-start(f32[64,512]{1,0:T(8,128)S(1)} %get-tuple-element.99.refs_6_), channel_id=1, source_target_pairs={{0,2},{1,3},{2,0},{3,1},{4,6},{5,7},{6,4},{7,5},{8,10},{9,11},{10,... | collective-permute-start | bytes 393224 | tf_op jit(solution)/shard_map/ppermute | solution.py:551
  87.8 1.8 %shard_map.78 = (f32[64,1024]{1,0:T(8,128)S(1)}, f32[64,1024]{1,0:T(8,128)S(1)}) custom-call(s32[4,64]{1,0:T(4,128)S(1)} %bitcast.16, s32[2,64]{1,0:T(2,128)S(1)} %get-tuple-element.60.order_ref.order_near, bf16[2,48,128,128]{3,2,1,0:T(8,128)(2,1)S(1)} %get-tuple-element.94.ext, bf16[64,256,256]{2,1,0:T(8,128)(2,1)S(1)} %shard_map.66.w_ref.refs_1_, ...), custom_call_target="tpu_custom_call" | custom-call | tf_op jit(solution)/shard_map/pallas_call | solution.py:55
  89.6 0.6 collective-permute-start.36
  90.2 5.9 %collective-permute-done.28.refs_2_ = f32[64,512]{1,0:T(8,128)S(1)} collective-permute-done((f32[64,512]{1,0:T(8,128)S(1)}, f32[64,512]{1,0:T(8,128)S(1)}, u32[]{:S(2)}, u32[]{:S(2)}) %collective-permute-start.28) | collective-permute-done | bytes 131104 | tf_op jit(solution)/shard_map/ppermute | solution.py:551
  96.2 2.8 %collective-permute-done.32.refs_2_ = f32[64,512]{1,0:T(8,128)S(1)} collective-permute-done((f32[64,512]{1,0:T(8,128)S(1)}, f32[64,512]{1,0:T(8,128)S(1)}, u32[]{:S(2)}, u32[]{:S(2)}) %collective-permute-start.32) | collective-permute-done | bytes 131104 | tf_op jit(solution)/shard_map/ppermute | solution.py:551
  99.0 1.5 %collective-permute-start.34 = (f32[64,768]{1,0:T(8,128)S(1)}, f32[64,768]{1,0:T(8,128)S(1)}, u32[]{:S(2)}, u32[]{:S(2)}) collective-permute-start(f32[64,768]{1,0:T(8,128)S(1)} %get-tuple-element.100.refs_7_), channel_id=1, source_target_pairs={{0,2},{1,3},{2,0},{3,1},{4,6},{5,7},{6,4},{7,5},{8,10},{9,11},{10,... | collective-permute-start | bytes 589832 | tf_op jit(solution)/shard_map/ppermute | solution.py:551
  100.5 0.2 collective-permute-start.31
  100.7 3.9 %collective-permute-done.36.refs_8_ = f32[64,1024]{1,0:T(8,128)S(1)} collective-permute-done((f32[64,1024]{1,0:T(8,128)S(1)}, f32[64,1024]{1,0:T(8,128)S(1)}, u32[]{:S(2)}, u32[]{:S(2)}) %collective-permute-start.36) | collective-permute-done | bytes 262176 | tf_op jit(solution)/shard_map/ppermute | solution.py:551
  104.6 3.3 %collective-permute-done.34.refs_5_ = f32[64,768]{1,0:T(8,128)S(1)} collective-permute-done((f32[64,768]{1,0:T(8,128)S(1)}, f32[64,768]{1,0:T(8,128)S(1)}, u32[]{:S(2)}, u32[]{:S(2)}) %collective-permute-start.34) | collective-permute-done | bytes 196640 | tf_op jit(solution)/shard_map/ppermute | solution.py:551
  107.9 0.5 collective-permute-start.33
  108.4 1.2 shard_map.82.refs_11_.refs_5_.u_ref
  109.6 0.6 shard_map.81
  110.3 0.6 shard_map.83.refs_6_
  110.8 0.3 shard_map.84.refs_6_
  111.2 0.4 shard_map.85
  111.5 11.8 %all_to_all.5.sums_ref = f32[32,1,128]{2,1,0:T(1,128)S(1)} all-to-all(f32[32,1,128]{2,1,0:T(1,128)S(1)} %shard_map.85), channel_id=1, replica_groups=mesh['dom'=8,'samp'=4] {'dom','samp'}, dimensions={0} | all-to-all | bytes 32768 | tf_op jit(solution)/shard_map/all_to_all | solution.py:637
  123.3 1.2 update.1
  (51 shorter events, 0.3 us)
Async XLA Ops:
  1.5 9.9 %collective-permute-start = (f32[64,256]{1,0:T(8,128)S(1)}, f32[64,256]{1,0:T(8,128)S(1)}, u32[]{:S(2)}, u32[]{:S(2)}) collective-permute-start(f32[64,256]{1,0:T(8,128)S(1)} %get-tuple-element.65), channel_id=1, source_target_pairs={{0,16},{4,20},{8,24},{12,28},{16,0},{20,4},{24,8},{28,12},{1,17},{... | collective-permute-start | bytes 196616 | tf_op jit(solution)/shard_map/ppermute | solution.py:534
  5.7 10.0 %collective-permute-start.1 = (f32[64,256]{1,0:T(8,128)S(1)}, f32[64,256]{1,0:T(8,128)S(1)}, u32[]{:S(2)}, u32[]{:S(2)}) collective-permute-start(f32[64,256]{1,0:T(8,128)S(1)} %get-tuple-element.66), channel_id=1, source_target_pairs={{0,20},{4,16},{8,28},{12,24},{16,4},{20,0},{24,12},{28,8},{1,21},{... | collective-permute-start | bytes 196616 | tf_op jit(solution)/shard_map/ppermute | solution.py:534
  7.0 17.9 %collective-permute-start.2 = (f32[64,256]{1,0:T(8,128)S(1)}, f32[64,256]{1,0:T(8,128)S(1)}, u32[]{:S(2)}, u32[]{:S(2)}) collective-permute-start(f32[64,256]{1,0:T(8,128)S(1)} %get-tuple-element.67), channel_id=1, source_target_pairs={{0,24},{4,28},{8,16},{12,20},{16,8},{20,12},{24,0},{28,4},{1,25},{... | collective-permute-start | bytes 196616 | tf_op jit(solution)/shard_map/ppermute | solution.py:534
  10.6 14.3 %collective-permute-start.3 = (f32[64,256]{1,0:T(8,128)S(1)}, f32[64,256]{1,0:T(8,128)S(1)}, u32[]{:S(2)}, u32[]{:S(2)}) collective-permute-start(f32[64,256]{1,0:T(8,128)S(1)} %get-tuple-element.68), channel_id=1, source_target_pairs={{0,28},{4,24},{8,20},{12,16},{16,12},{20,8},{24,4},{28,0},{1,29},{... | collective-permute-start | bytes 196616 | tf_op jit(solution)/shard_map/ppermute | solution.py:534
  10.6 14.3 %collective-permute-start.4 = (f32[64,256]{1,0:T(8,128)S(1)}, f32[64,256]{1,0:T(8,128)S(1)}, u32[]{:S(2)}, u32[]{:S(2)}) collective-permute-start(f32[64,256]{1,0:T(8,128)S(1)} %get-tuple-element.69), channel_id=1, source_target_pairs={{0,12},{4,8},{8,4},{12,0},{16,28},{20,24},{24,20},{28,16},{1,13},{... | collective-permute-start | bytes 196616 | tf_op jit(solution)/shard_map/ppermute | solution.py:534
  11.5 13.5 %collective-permute-start.5 = (f32[64,256]{1,0:T(8,128)S(1)}, f32[64,256]{1,0:T(8,128)S(1)}, u32[]{:S(2)}, u32[]{:S(2)}) collective-permute-start(f32[64,256]{1,0:T(8,128)S(1)} %get-tuple-element.70), channel_id=1, source_target_pairs={{0,8},{4,12},{8,0},{12,4},{16,24},{20,28},{24,16},{28,20},{1,9},{5... | collective-permute-start | bytes 196616 | tf_op jit(solution)/shard_map/ppermute | solution.py:534
  15.7 9.3 %collective-permute-start.6 = (f32[64,256]{1,0:T(8,128)S(1)}, f32[64,256]{1,0:T(8,128)S(1)}, u32[]{:S(2)}, u32[]{:S(2)}) collective-permute-start(f32[64,256]{1,0:T(8,128)S(1)} %get-tuple-element.71), channel_id=1, source_target_pairs={{0,4},{4,0},{8,12},{12,8},{16,20},{20,16},{24,28},{28,24},{1,5},{5... | collective-permute-start | bytes 196616 | tf_op jit(solution)/shard_map/ppermute | solution.py:534
  17.2 4.7 %copy-start = (f32[64,4096]{1,0:T(8,128)S(1)}, f32[64,4096]{1,0:T(8,128)}, u32[]{:S(2)}) copy-start(f32[64,4096]{1,0:T(8,128)} %g_ref.13) | copy-start | bytes 3145732
  17.2 4.7 %copy-start.1 = (f32[64,4096]{1,0:T(8,128)S(1)}, f32[64,4096]{1,0:T(8,128)}, u32[]{:S(2)}) copy-start(f32[64,4096]{1,0:T(8,128)} %c_ref.13) | copy-start | bytes 3145732
  22.6 2.3 %copy-start.2 = (s32[64,4]{0,1:T(4,128)S(1)}, s32[64,4]{0,1:T(4,128)}, u32[]{:S(2)}) copy-start(s32[64,4]{0,1:T(4,128)} %param.10) | copy-start | bytes 3076
  23.6 4.4 %slice-start = ((s8[8388608]{0:T(1024)(128)(4,1)}), s8[4194304]{0:T(1024)(128)(4,1)S(1)}, s32[]{:S(2)}) async-start(s8[8388608]{0:T(1024)(128)(4,1)} %bitcast.6), calls=%async_computation.1 | async-start | bytes 8388608
  25.0 3.1 %slice-start.1 = ((s8[8388608]{0:T(1024)(128)(4,1)}), s8[4194304]{0:T(1024)(128)(4,1)S(1)}, s32[]{:S(2)}) async-start(s8[8388608]{0:T(1024)(128)(4,1)} %bitcast.6), calls=%async_computation.2 | async-start | bytes 8388608
  29.5 29.4 %copy-start.3 = (s32[1,8,4]{1,2,0:T(4,128)S(1)}, s32[1,8,4]{1,2,0:T(4,128)}, u32[]{:S(2)}) copy-start(s32[1,8,4]{1,2,0:T(4,128)} %param.11) | copy-start | bytes 388
  32.0 16.2 %collective-permute-start.8 = (f32[64,2304]{1,0:T(8,128)S(1)}, f32[64,2304]{1,0:T(8,128)S(1)}, u32[]{:S(2)}, u32[]{:S(2)}) collective-permute-start(f32[64,2304]{1,0:T(8,128)S(1)} %get-tuple-element.76.refs_2_), channel_id=1, source_target_pairs={{0,2},{1,3},{2,0},{3,1},{4,6},{5,7},{6,4},{7,5},{8,10},{9,11},{10,... | collective-permute-start | bytes 1769480 | tf_op jit(solution)/shard_map/ppermute | solution.py:551
  33.5 18.1 %collective-permute-start.14 = (f32[64,1280]{1,0:T(8,128)S(1)}, f32[64,1280]{1,0:T(8,128)S(1)}, u32[]{:S(2)}, u32[]{:S(2)}) collective-permute-start(f32[64,1280]{1,0:T(8,128)S(1)} %get-tuple-element.82.refs_4_), channel_id=1, source_target_pairs={{0,2},{1,3},{2,0},{3,1},{4,6},{5,7},{6,4},{7,5},{8,10},{9,11},{10,... | collective-permute-start | bytes 983048 | tf_op jit(solution)/shard_map/ppermute | solution.py:551
  34.1 35.0 %collective-permute-start.7 = (f32[64,2304]{1,0:T(8,128)S(1)}, f32[64,2304]{1,0:T(8,128)S(1)}, u32[]{:S(2)}, u32[]{:S(2)}) collective-permute-start(f32[64,2304]{1,0:T(8,128)S(1)} %get-tuple-element.76.refs_2_), channel_id=1, source_target_pairs={{0,1},{1,0},{2,3},{3,2},{4,5},{5,4},{6,7},{7,6},{8,9},{9,8},{10,11... | collective-permute-start | bytes 1769480 | tf_op jit(solution)/shard_map/ppermute | solution.py:552
  48.2 24.7 %collective-permute-start.9 = (f32[64,2304]{1,0:T(8,128)S(1)}, f32[64,2304]{1,0:T(8,128)S(1)}, u32[]{:S(2)}, u32[]{:S(2)}) collective-permute-start(f32[64,2304]{1,0:T(8,128)S(1)} %collective-permute-done.8.refs_2_), channel_id=1, source_target_pairs={{0,1},{1,0},{2,3},{3,2},{4,5},{5,4},{6,7},{7,6},{8,9},{9,8},{10,11... | collective-permute-start | bytes 1769480 | tf_op jit(solution)/shard_map/ppermute | solution.py:564
  48.2 3.5 %collective-permute-start.10 = (f32[64,512]{1,0:T(8,128)S(1)}, f32[64,512]{1,0:T(8,128)S(1)}, u32[]{:S(2)}, u32[]{:S(2)}) collective-permute-start(f32[64,512]{1,0:T(8,128)S(1)} %get-tuple-element.81.refs_3_), channel_id=1, source_target_pairs={{0,1},{1,0},{2,3},{3,2},{4,5},{5,4},{6,7},{7,6},{8,9},{9,8},{10,11... | collective-permute-start | bytes 393224 | tf_op jit(solution)/shard_map/ppermute | solution.py:552
  48.7 8.9 %collective-permute-start.11 = (f32[64,1280]{1,0:T(8,128)S(1)}, f32[64,1280]{1,0:T(8,128)S(1)}, u32[]{:S(2)}, u32[]{:S(2)}) collective-permute-start(f32[64,1280]{1,0:T(8,128)S(1)} %get-tuple-element.82.refs_4_), channel_id=1, source_target_pairs={{0,1},{1,0},{2,3},{3,2},{4,5},{5,4},{6,7},{7,6},{8,9},{9,8},{10,11... | collective-permute-start | bytes 983048 | tf_op jit(solution)/shard_map/ppermute | solution.py:552
  51.7 7.3 %collective-permute-start.15 = (f32[64,1280]{1,0:T(8,128)S(1)}, f32[64,1280]{1,0:T(8,128)S(1)}, u32[]{:S(2)}, u32[]{:S(2)}) collective-permute-start(f32[64,1280]{1,0:T(8,128)S(1)} %collective-permute-done.14.refs_5_), channel_id=1, source_target_pairs={{0,1},{1,0},{2,3},{3,2},{4,5},{5,4},{6,7},{7,6},{8,9},{9,8},{10,11... | collective-permute-start | bytes 983048 | tf_op jit(solution)/shard_map/ppermute | solution.py:564
  51.7 5.9 %collective-permute-start.12 = (f32[64,512]{1,0:T(8,128)S(1)}, f32[64,512]{1,0:T(8,128)S(1)}, u32[]{:S(2)}, u32[]{:S(2)}) collective-permute-start(f32[64,512]{1,0:T(8,128)S(1)} %get-tuple-element.81.refs_3_), channel_id=1, source_target_pairs={{0,2},{1,3},{2,0},{3,1},{4,6},{5,7},{6,4},{7,5},{8,10},{9,11},{10,... | collective-permute-start | bytes 393224 | tf_op jit(solution)/shard_map/ppermute | solution.py:551
  57.6 1.3 %collective-permute-start.13 = (f32[64,512]{1,0:T(8,128)S(1)}, f32[64,512]{1,0:T(8,128)S(1)}, u32[]{:S(2)}, u32[]{:S(2)}) collective-permute-start(f32[64,512]{1,0:T(8,128)S(1)} %collective-permute-done.12.refs_2_), channel_id=1, source_target_pairs={{0,1},{1,0},{2,3},{3,2},{4,5},{5,4},{6,7},{7,6},{8,9},{9,8},{10,11... | collective-permute-start | bytes 393224 | tf_op jit(solution)/shard_map/ppermute | solution.py:564
  60.1 9.0 %collective-permute-start.16 = (f32[64,256]{1,0:T(8,128)S(1)}, f32[64,256]{1,0:T(8,128)S(1)}, u32[]{:S(2)}, u32[]{:S(2)}) collective-permute-start(f32[64,256]{1,0:T(8,128)S(1)} %get-tuple-element.86), channel_id=1, source_target_pairs={{0,16},{4,20},{8,24},{12,28},{16,0},{20,4},{24,8},{28,12},{1,17},{... | collective-permute-start | bytes 196616 | tf_op jit(solution)/shard_map/ppermute | solution.py:534
  63.1 9.7 %collective-permute-start.17 = (f32[64,256]{1,0:T(8,128)S(1)}, f32[64,256]{1,0:T(8,128)S(1)}, u32[]{:S(2)}, u32[]{:S(2)}) collective-permute-start(f32[64,256]{1,0:T(8,128)S(1)} %get-tuple-element.87), channel_id=1, source_target_pairs={{0,20},{4,16},{8,28},{12,24},{16,4},{20,0},{24,12},{28,8},{1,21},{... | collective-permute-start | bytes 196616 | tf_op jit(solution)/shard_map/ppermute | solution.py:534
  64.2 10.6 %collective-permute-start.18 = (f32[64,256]{1,0:T(8,128)S(1)}, f32[64,256]{1,0:T(8,128)S(1)}, u32[]{:S(2)}, u32[]{:S(2)}) collective-permute-start(f32[64,256]{1,0:T(8,128)S(1)} %get-tuple-element.88), channel_id=1, source_target_pairs={{0,24},{4,28},{8,16},{12,20},{16,8},{20,12},{24,0},{28,4},{1,25},{... | collective-permute-start | bytes 196616 | tf_op jit(solution)/shard_map/ppermute | solution.py:534
  69.0 7.2 %collective-permute-start.19 = (f32[64,256]{1,0:T(8,128)S(1)}, f32[64,256]{1,0:T(8,128)S(1)}, u32[]{:S(2)}, u32[]{:S(2)}) collective-permute-start(f32[64,256]{1,0:T(8,128)S(1)} %get-tuple-element.89), channel_id=1, source_target_pairs={{0,28},{4,24},{8,20},{12,16},{16,12},{20,8},{24,4},{28,0},{1,29},{... | collective-permute-start | bytes 196616 | tf_op jit(solution)/shard_map/ppermute | solution.py:534
  69.0 7.3 %collective-permute-start.20 = (f32[64,256]{1,0:T(8,128)S(1)}, f32[64,256]{1,0:T(8,128)S(1)}, u32[]{:S(2)}, u32[]{:S(2)}) collective-permute-start(f32[64,256]{1,0:T(8,128)S(1)} %get-tuple-element.90), channel_id=1, source_target_pairs={{0,12},{4,8},{8,4},{12,0},{16,28},{20,24},{24,20},{28,16},{1,13},{... | collective-permute-start | bytes 196616 | tf_op jit(solution)/shard_map/ppermute | solution.py:534
  72.8 4.3 %collective-permute-start.21 = (f32[64,256]{1,0:T(8,128)S(1)}, f32[64,256]{1,0:T(8,128)S(1)}, u32[]{:S(2)}, u32[]{:S(2)}) collective-permute-start(f32[64,256]{1,0:T(8,128)S(1)} %get-tuple-element.91), channel_id=1, source_target_pairs={{0,8},{4,12},{8,0},{12,4},{16,24},{20,28},{24,16},{28,20},{1,9},{5... | collective-permute-start | bytes 196616 | tf_op jit(solution)/shard_map/ppermute | solution.py:534
  72.8 4.8 %collective-permute-start.22 = (f32[64,256]{1,0:T(8,128)S(1)}, f32[64,256]{1,0:T(8,128)S(1)}, u32[]{:S(2)}, u32[]{:S(2)}) collective-permute-start(f32[64,256]{1,0:T(8,128)S(1)} %get-tuple-element.92), channel_id=1, source_target_pairs={{0,4},{4,0},{8,12},{12,8},{16,20},{20,16},{24,28},{28,24},{1,5},{5... | collective-permute-start | bytes 196616 | tf_op jit(solution)/shard_map/ppermute | solution.py:534
  78.8 7.5 %collective-permute-start.23 = (f32[64,512]{1,0:T(8,128)S(1)}, f32[64,512]{1,0:T(8,128)S(1)}, u32[]{:S(2)}, u32[]{:S(2)}) collective-permute-start(f32[64,512]{1,0:T(8,128)S(1)} %get-tuple-element.99.refs_6_), channel_id=1, source_target_pairs={{0,1},{1,0},{2,3},{3,2},{4,5},{5,4},{6,7},{7,6},{8,9},{9,8},{10,11... | collective-permute-start | bytes 393224 | tf_op jit(solution)/shard_map/ppermute | solution.py:552
  80.1 9.5 %collective-permute-start.27 = (f32[64,512]{1,0:T(8,128)S(1)}, f32[64,512]{1,0:T(8,128)S(1)}, u32[]{:S(2)}, u32[]{:S(2)}) collective-permute-start(f32[64,512]{1,0:T(8,128)S(1)} %get-tuple-element.103.refs_10_), channel_id=1, source_target_pairs={{0,1},{1,0},{2,3},{3,2},{4,5},{5,4},{6,7},{7,6},{8,9},{9,8},{10,11... | collective-permute-start | bytes 393224 | tf_op jit(solution)/shard_map/ppermute | solution.py:552
  82.7 17.8 %collective-permute-start.30 = (f32[64,1280]{1,0:T(8,128)S(1)}, f32[64,1280]{1,0:T(8,128)S(1)}, u32[]{:S(2)}, u32[]{:S(2)}) collective-permute-start(f32[64,1280]{1,0:T(8,128)S(1)} %get-tuple-element.102.refs_9_), channel_id=1, source_target_pairs={{0,2},{1,3},{2,0},{3,1},{4,6},{5,7},{6,4},{7,5},{8,10},{9,11},{10,... | collective-permute-start | bytes 983048 | tf_op jit(solution)/shard_map/ppermute | solution.py:551
  85.7 13.3 %collective-permute-start.24 = (f32[64,768]{1,0:T(8,128)S(1)}, f32[64,768]{1,0:T(8,128)S(1)}, u32[]{:S(2)}, u32[]{:S(2)}) collective-permute-start(f32[64,768]{1,0:T(8,128)S(1)} %get-tuple-element.100.refs_7_), channel_id=1, source_target_pairs={{0,1},{1,0},{2,3},{3,2},{4,5},{5,4},{6,7},{7,6},{8,9},{9,8},{10,11... | collective-permute-start | bytes 589832 | tf_op jit(solution)/shard_map/ppermute | solution.py:552
  85.7 10.4 %collective-permute-start.28 = (f32[64,512]{1,0:T(8,128)S(1)}, f32[64,512]{1,0:T(8,128)S(1)}, u32[]{:S(2)}, u32[]{:S(2)}) collective-permute-start(f32[64,512]{1,0:T(8,128)S(1)} %get-tuple-element.103.refs_10_), channel_id=1, source_target_pairs={{0,2},{1,3},{2,0},{3,1},{4,6},{5,7},{6,4},{7,5},{8,10},{9,11},{10,... | collective-permute-start | bytes 393224 | tf_op jit(solution)/shard_map/ppermute | solution.py:551
  86.3 12.6 %collective-permute-start.32 = (f32[64,512]{1,0:T(8,128)S(1)}, f32[64,512]{1,0:T(8,128)S(1)}, u32[]{:S(2)}, u32[]{:S(2)}) collective-permute-start(f32[64,512]{1,0:T(8,128)S(1)} %get-tuple-element.99.refs_6_), channel_id=1, source_target_pairs={{0,2},{1,3},{2,0},{3,1},{4,6},{5,7},{6,4},{7,5},{8,10},{9,11},{10,... | collective-permute-start | bytes 393224 | tf_op jit(solution)/shard_map/ppermute | solution.py:551
  89.6 14.9 %collective-permute-start.36 = (f32[64,1024]{1,0:T(8,128)S(1)}, f32[64,1024]{1,0:T(8,128)S(1)}, u32[]{:S(2)}, u32[]{:S(2)}) collective-permute-start(f32[64,1024]{1,0:T(8,128)S(1)} %get-tuple-element.101.refs_8_), channel_id=1, source_target_pairs={{0,2},{1,3},{2,0},{3,1},{4,6},{5,7},{6,4},{7,5},{8,10},{9,11},{10,... | collective-permute-start | bytes 786440 | tf_op jit(solution)/shard_map/ppermute | solution.py:551
  96.2 12.2 %collective-permute-start.26 = (f32[64,1280]{1,0:T(8,128)S(1)}, f32[64,1280]{1,0:T(8,128)S(1)}, u32[]{:S(2)}, u32[]{:S(2)}) collective-permute-start(f32[64,1280]{1,0:T(8,128)S(1)} %get-tuple-element.102.refs_9_), channel_id=1, source_target_pairs={{0,1},{1,0},{2,3},{3,2},{4,5},{5,4},{6,7},{7,6},{8,9},{9,8},{10,11... | collective-permute-start | bytes 983048 | tf_op jit(solution)/shard_map/ppermute | solution.py:552
  99.0 8.9 %collective-permute-start.25 = (f32[64,1024]{1,0:T(8,128)S(1)}, f32[64,1024]{1,0:T(8,128)S(1)}, u32[]{:S(2)}, u32[]{:S(2)}) collective-permute-start(f32[64,1024]{1,0:T(8,128)S(1)} %get-tuple-element.101.refs_8_), channel_id=1, source_target_pairs={{0,1},{1,0},{2,3},{3,2},{4,5},{5,4},{6,7},{7,6},{8,9},{9,8},{10,11... | collective-permute-start | bytes 786440 | tf_op jit(solution)/shard_map/ppermute | solution.py:552
  99.0 8.9 %collective-permute-start.34 = (f32[64,768]{1,0:T(8,128)S(1)}, f32[64,768]{1,0:T(8,128)S(1)}, u32[]{:S(2)}, u32[]{:S(2)}) collective-permute-start(f32[64,768]{1,0:T(8,128)S(1)} %get-tuple-element.100.refs_7_), channel_id=1, source_target_pairs={{0,2},{1,3},{2,0},{3,1},{4,6},{5,7},{6,4},{7,5},{8,10},{9,11},{10,... | collective-permute-start | bytes 589832 | tf_op jit(solution)/shard_map/ppermute | solution.py:551
  100.5 10.3 %collective-permute-start.31 = (f32[64,1280]{1,0:T(8,128)S(1)}, f32[64,1280]{1,0:T(8,128)S(1)}, u32[]{:S(2)}, u32[]{:S(2)}) collective-permute-start(f32[64,1280]{1,0:T(8,128)S(1)} %collective-permute-done.30.refs_2_), channel_id=1, source_target_pairs={{0,1},{1,0},{2,3},{3,2},{4,5},{5,4},{6,7},{7,6},{8,9},{9,8},{10,11... | collective-permute-start | bytes 983048 | tf_op jit(solution)/shard_map/ppermute | solution.py:564
  104.6 5.7 %collective-permute-start.37 = (f32[64,1024]{1,0:T(8,128)S(1)}, f32[64,1024]{1,0:T(8,128)S(1)}, u32[]{:S(2)}, u32[]{:S(2)}) collective-permute-start(f32[64,1024]{1,0:T(8,128)S(1)} %collective-permute-done.36.refs_8_), channel_id=1, source_target_pairs={{0,1},{1,0},{2,3},{3,2},{4,5},{5,4},{6,7},{7,6},{8,9},{9,8},{10,11... | collective-permute-start | bytes 786440 | tf_op jit(solution)/shard_map/ppermute | solution.py:564
  107.9 2.4 %collective-permute-start.35 = (f32[64,768]{1,0:T(8,128)S(1)}, f32[64,768]{1,0:T(8,128)S(1)}, u32[]{:S(2)}, u32[]{:S(2)}) collective-permute-start(f32[64,768]{1,0:T(8,128)S(1)} %collective-permute-done.34.refs_5_), channel_id=1, source_target_pairs={{0,1},{1,0},{2,3},{3,2},{4,5},{5,4},{6,7},{7,6},{8,9},{9,8},{10,11... | collective-permute-start | bytes 589832 | tf_op jit(solution)/shard_map/ppermute | solution.py:564
  107.9 2.4 %collective-permute-start.33 = (f32[64,512]{1,0:T(8,128)S(1)}, f32[64,512]{1,0:T(8,128)S(1)}, u32[]{:S(2)}, u32[]{:S(2)}) collective-permute-start(f32[64,512]{1,0:T(8,128)S(1)} %collective-permute-done.32.refs_2_), channel_id=1, source_target_pairs={{0,1},{1,0},{2,3},{3,2},{4,5},{5,4},{6,7},{7,6},{8,9},{9,8},{10,11... | collective-permute-start | bytes 393224 | tf_op jit(solution)/shard_map/ppermute | solution.py:564
  108.4 2.8 %collective-permute-start.29 = (f32[64,512]{1,0:T(8,128)S(1)}, f32[64,512]{1,0:T(8,128)S(1)}, u32[]{:S(2)}, u32[]{:S(2)}) collective-permute-start(f32[64,512]{1,0:T(8,128)S(1)} %collective-permute-done.28.refs_2_), channel_id=1, source_target_pairs={{0,1},{1,0},{2,3},{3,2},{4,5},{5,4},{6,7},{7,6},{8,9},{9,8},{10,11... | collective-permute-start | bytes 393224 | tf_op jit(solution)/shard_map/ppermute | solution.py:564

commit v6 on v4

--- a/solution.py
+++ b/solution.py
@@ -110,9 +110,8 @@
     lax.fori_loop(first_row, last_row, convert, 0, unroll=2)
 
 
-def fetch_kernel(domains, groups, send_ref, field_ref, stamps_hbm, order_ref, out_ref, *refs):
+def fetch_kernel(groups, order_ref, field_ref, stamps_hbm, out_ref, *refs):
     ext, near_ref, far_ref, buffer, sems = refs
-    order_rows(domains, send_ref, order_ref)
     rows, _, width = buffer.shape
     copies = []
     for n in range(rows):
@@ -127,21 +126,20 @@
         out_ref[n, :, width:] = low
 
 
-def fetch(send, field, stamps, rows, domains, groups, outputs):
+def fetch(order, field, stamps, rows, groups, outputs):
     total, depth, width = stamps.shape
     return pl.pallas_call(
-        functools.partial(fetch_kernel, domains, groups),
+        functools.partial(fetch_kernel, groups),
         in_specs=[scalars(), whole(), pl.BlockSpec(memory_space=pl.ANY)],
-        out_specs=[scalars()] + [whole()] * (1 + len(outputs)),
+        out_specs=[whole()] * (1 + len(outputs)),
         out_shape=[
-            jax.ShapeDtypeStruct((2, total), jnp.int32),
             pltpu.VMEM((total, depth, 2 * width), jnp.bfloat16),
             *[pltpu.VMEM(shape, dtype) for shape, dtype in outputs],
         ],
         scratch_shapes=[pltpu.VMEM((rows, depth, width), stamps.dtype), pltpu.SemaphoreType.DMA((rows,))],
         compiler_params=pltpu.CompilerParams(vmem_limit_bytes=LIMIT),
         name="prepare_0",
-    )(far_memory(send), near_memory(field), far_memory(stamps))
+    )(order, near_memory(field), far_memory(stamps))
 
 
 def pair_tile(ref, first, second):
@@ -210,7 +208,7 @@
         later = later + 1 - flag
 
 
-def gather_kernel(domains, send_hbm, field_hbm, field_ref, *refs):
+def gather_kernel(domains, send_hbm, field_hbm, order_ref, field_ref, *refs):
     *out_refs, field_sem, send_ref, send_sem = refs
     table = pltpu.make_async_copy(send_hbm, send_ref, send_sem)
     table.start()
@@ -221,17 +219,21 @@
         copies.append(pltpu.make_async_copy(field_hbm.at[:, inside], field_ref.at[:, inside], field_sem.at[n]))
         copies[-1].start()
     table.wait()
+    order_rows(domains, send_ref, order_ref)
     for copy in copies:
         copy.wait()
     gather_all(domains, send_ref, field_ref, out_refs)
 
 
-def gather(send, field, domains, outputs):
+def gather(send, field, rows, domains, outputs):
     return pl.pallas_call(
         functools.partial(gather_kernel, domains),
         in_specs=[pl.BlockSpec(memory_space=pl.ANY)] * 2,
-        out_specs=[whole()] * (1 + len(outputs)),
-        out_shape=[pltpu.VMEM(shape, dtype) for shape, dtype in ((field.shape, field.dtype), *outputs)],
+        out_specs=[scalars()] + [whole()] * (1 + len(outputs)),
+        out_shape=[
+            jax.ShapeDtypeStruct((2, rows), jnp.int32),
+            *[pltpu.VMEM(shape, dtype) for shape, dtype in ((field.shape, field.dtype), *outputs)],
+        ],
         scratch_shapes=[
             pltpu.SemaphoreType.DMA((COPIES,)),
             pltpu.SMEM(send.shape, send.dtype),
@@ -564,15 +566,14 @@
             charges += [x, lax.ppermute(x, "samp", pairs)]
         return [half, *charges]
 
-    field, *outgoing = gather(send, residual, domains, outgoing_shapes)
+    order, field, *outgoing = gather(send, residual, rows, domains, outgoing_shapes)
     incoming = exchange(outgoing)
     blocks = stamps.reshape(rows, per_entry * width, 2 * width)
-    order, weights, ext, near_matrix, far_matrix = fetch(
-        send,
+    weights, ext, near_matrix, far_matrix = fetch(
+        order,
         field,
         blocks,
         early,
-        domains,
         groups,
         [
             ext_shape,

time: 119 us -> 126 us (1.059)
  waiting for transfers between devices: 41.9 us -> 46.2 us
  local copies, waits for them, and re-layouts: 0.04 us -> 2.49 us
    ppermute x8, waiting for transfers between devices: 31.8 us -> 37.4 us  [spread(): lax.ppermute(q, 'samp', [(i, (i + k) % groups) for i in range(groups)])]
    unnamed x12 -> x16, local copies, waits for them, and re-layouts: 0.04 us -> 2.49 us
    ppermute x8, waiting for transfers between devices: 1.36 us -> 0.02 us  [spread(): return (far, lax.ppermute(q, 'samp', pairs))]
  transfers between devices with their start and end apart: 38 -> 38, of which waited for: 13 -> 14; matrix products, arithmetic and copies ran while one was open for 0% -> 0% of each run, Pallas kernels for 16% -> 14%
where the time goes in v6:
time: 126 us
  waiting for transfers between devices  46.2 us (37%)
  starting transfers between devices  35.5 us (28%)
  Pallas kernels  29.5 us (23%)
  blocking collectives  11.8 us (9%)
  local copies, waits for them, and re-layouts  2.49 us (2%)
    ppermute x8, waiting for transfers between devices, spread(): lax.ppermute(q, 'samp', [(i, (i + k) % groups) for i in range(groups)])  37.4 us
    ppermute x14, starting transfers between devices, exchange(): lax.ppermute(x, 'dom', [(i, i ^ k) for i in range(domains)])  24.2 us
    pallas_call x21, Pallas kernels, kernel_call(): pl.pallas_call(kernel, in_specs=specs, out_specs=[scalars() if number els...  22.5 us
    all_to_all x1, blocking collectives, body(): lax.all_to_all(sums, ('dom', 'samp'), split_axis=0, concat_axis=0, tiled=...  11.8 us
    ppermute x8, starting transfers between devices, spread(): lax.ppermute(q, 'samp', [(i, (i + k) % groups) for i in range(groups)])  9.33 us
    ppermute x14, waiting for transfers between devices, exchange(): lax.ppermute(x, 'dom', [(i, i ^ k) for i in range(domains)])  7.82 us
    pallas_call x1, Pallas kernels, fetch(): pl.pallas_call(functools.partial(fetch_kernel, groups), in_specs=[scalars...  3.6 us
  transfers between devices with their start and end apart: 38, of which 14 were waited for; matrix products, arithmetic and copies ran while one was open for 0% of the time, Pallas kernels for 14%

profile of v6, /device:TPU:0, one launch (start us, length us, event | category | flops | bytes accessed | tf_op | source)
XLA Modules:
  0.0 126.1 jit_solution(3143603772185717323)
XLA Ops:
  0.0 2.2 %gather.1 = (s32[2,64]{1,0:T(2,128)S(1)}, f32[64,4096]{1,0:T(8,128)S(1)}, f32[64,256]{1,0:T(8,128)S(1)}, f32[64,256]{1,0:T(8,128)S(1)}, f32[64,256]{1,0:T(8,128)...) custom-call(s32[4,8]{1,0:T(4,128)} %bitcast.17, ...), custom_call_target="tpu_custom_call" | custom-call | tf_op jit(solution)/shard_map/gather/pallas_call | solution.py:229
  2.2 4.1 %collective-permute-start = (f32[64,256]{1,0:T(8,128)S(1)}, f32[64,256]{1,0:T(8,128)S(1)}, u32[]{:S(2)}, u32[]{:S(2)}) collective-permute-start(f32[64,256]{1,0:T(8,128)S(1)} %get-tuple-element.63), channel_id=1, source_target_pairs={{0,16},{4,20},{8,24},{12,28},{16,0},{20,4},{24,8},{28,12},{1,17},{... | collective-permute-start | bytes 196616 | tf_op jit(solution)/shard_map/ppermute | solution.py:536
  6.4 1.3 %collective-permute-start.1 = (f32[64,256]{1,0:T(8,128)S(1)}, f32[64,256]{1,0:T(8,128)S(1)}, u32[]{:S(2)}, u32[]{:S(2)}) collective-permute-start(f32[64,256]{1,0:T(8,128)S(1)} %get-tuple-element.64), channel_id=1, source_target_pairs={{0,20},{4,16},{8,28},{12,24},{16,4},{20,0},{24,12},{28,8},{1,21},{... | collective-permute-start | bytes 196616 | tf_op jit(solution)/shard_map/ppermute | solution.py:536
  7.7 3.6 %collective-permute-start.2 = (f32[64,256]{1,0:T(8,128)S(1)}, f32[64,256]{1,0:T(8,128)S(1)}, u32[]{:S(2)}, u32[]{:S(2)}) collective-permute-start(f32[64,256]{1,0:T(8,128)S(1)} %get-tuple-element.65), channel_id=1, source_target_pairs={{0,24},{4,28},{8,16},{12,20},{16,8},{20,12},{24,0},{28,4},{1,25},{... | collective-permute-start | bytes 196616 | tf_op jit(solution)/shard_map/ppermute | solution.py:536
  11.3 0.9 collective-permute-start.4
  12.2 2.2 %collective-permute-start.5 = (f32[64,256]{1,0:T(8,128)S(1)}, f32[64,256]{1,0:T(8,128)S(1)}, u32[]{:S(2)}, u32[]{:S(2)}) collective-permute-start(f32[64,256]{1,0:T(8,128)S(1)} %get-tuple-element.68), channel_id=1, source_target_pairs={{0,8},{4,12},{8,0},{12,4},{16,24},{20,28},{24,16},{28,20},{1,9},{5... | collective-permute-start | bytes 196616 | tf_op jit(solution)/shard_map/ppermute | solution.py:536
  14.4 2.0 %collective-permute-done.1.refs_5_ = f32[64,256]{1,0:T(8,128)S(1)} collective-permute-done((f32[64,256]{1,0:T(8,128)S(1)}, f32[64,256]{1,0:T(8,128)S(1)}, u32[]{:S(2)}, u32[]{:S(2)}) %collective-permute-start.1) | collective-permute-done | bytes 65568 | tf_op jit(solution)/shard_map/ppermute | solution.py:536
  16.4 1.5 %collective-permute-start.6 = (f32[64,256]{1,0:T(8,128)S(1)}, f32[64,256]{1,0:T(8,128)S(1)}, u32[]{:S(2)}, u32[]{:S(2)}) collective-permute-start(f32[64,256]{1,0:T(8,128)S(1)} %get-tuple-element.69), channel_id=1, source_target_pairs={{0,4},{4,0},{8,12},{12,8},{16,20},{20,16},{24,28},{28,24},{1,5},{5... | collective-permute-start | bytes 196616 | tf_op jit(solution)/shard_map/ppermute | solution.py:536
  17.9 1.2 copy-done
  19.1 1.2 copy-done.2
  20.3 1.1 shard_map.64
  21.4 1.3 shard_map.67
  22.7 3.6 %prepare_0.1 = (bf16[64,256,256]{2,1,0:T(8,128)(2,1)S(1)}, bf16[2,48,128,128]{3,2,1,0:T(8,128)(2,1)S(1)}, bf16[128,128]{1,0:T(8,128)(2,1)S(1)}, bf16[128,128]{1,0:T(8,128)(2,1)S(1)}) custom-call(s32[2,64]{1,0:T(2,128)S(1)} %get-tuple-element.55.order_ref.order_near, f32[64,4096]{1,0:T(8,128)S(1)} %get-tuple-element.56.field_ref.refs_10_.refs_4_.r_ref, ...), custom_call_target="tpu_custom_call" | custom-call | tf_op jit(solution)/shard_map/prepare_0/pallas_call | solution.py:131
  26.4 1.2 shard_map.65
  27.6 1.9 %shard_map.70 = (f32[64,1280]{1,0:T(8,128)S(1)}, f32[64,1280]{1,0:T(8,128)S(1)}) custom-call(s32[4,64]{1,0:T(4,128)S(1)} %bitcast.10, s32[2,64]{1,0:T(2,128)S(1)} %get-tuple-element.55.order_ref.order_near, bf16[2,48,128,128]{3,2,1,0:T(8,128)(2,1)S(1)} %get-tuple-element.70.ext, bf16[64,256,256]{2,1,0:T(8,128)(2,1)S(1)} %get-tuple-element.60.refs_1_.refs_0_.w_ref, ...), custom_call_target="tpu_custom_call" | custom-call | tf_op jit(solution)/shard_map/pallas_call | solution.py:55
  29.5 1.4 %shard_map.66.w_ref.refs_1_ = bf16[64,256,256]{2,1,0:T(8,128)(2,1)S(1)} custom-call(s32[2,64]{1,0:T(2,128)S(1)} %get-tuple-element.55.order_ref.order_near, f32[64,256,128]{2,1,0:T(8,128)S(1)} %bitcast.8, bf16[64,256,256]{2,1,0:T(8,128)(2,1)S(1)} %get-tuple-element.60.refs_1_.refs_0_.w_ref), custom_call_target="tpu_custom_call", output_to_operand_aliasing={{}: (2, {})} | custom-call | tf_op jit(solution)/shard_map/pallas_call | solution.py:55
  30.9 2.5 %shard_map.68 = (f32[64,2304]{1,0:T(8,128)S(1)}, f32[64,2304]{1,0:T(8,128)S(1)}) custom-call(s32[4,64]{1,0:T(4,128)S(1)} %bitcast.11, s32[2,64]{1,0:T(2,128)S(1)} %get-tuple-element.55.order_ref.order_near, bf16[2,48,128,128]{3,2,1,0:T(8,128)(2,1)S(1)} %get-tuple-element.70.ext, bf16[64,256,256]{2,1,0:T(8,128)(2,1)S(1)} %shard_map.66.w_ref.refs_1_, ...), custom_call_target="tpu_custom_call" | custom-call | tf_op jit(solution)/shard_map/pallas_call | solution.py:55
  33.4 1.6 %collective-permute-start.8 = (f32[64,2304]{1,0:T(8,128)S(1)}, f32[64,2304]{1,0:T(8,128)S(1)}, u32[]{:S(2)}, u32[]{:S(2)}) collective-permute-start(f32[64,2304]{1,0:T(8,128)S(1)} %get-tuple-element.74.refs_2_), channel_id=1, source_target_pairs={{0,2},{1,3},{2,0},{3,1},{4,6},{5,7},{6,4},{7,5},{8,10},{9,11},{10,... | collective-permute-start | bytes 1769480 | tf_op jit(solution)/shard_map/ppermute | solution.py:553
  35.0 0.5 collective-permute-start.14
  35.5 14.1 %collective-permute-done.8.refs_2_ = f32[64,2304]{1,0:T(8,128)S(1)} collective-permute-done((f32[64,2304]{1,0:T(8,128)S(1)}, f32[64,2304]{1,0:T(8,128)S(1)}, u32[]{:S(2)}, u32[]{:S(2)}) %collective-permute-start.8) | collective-permute-done | bytes 589856 | tf_op jit(solution)/shard_map/ppermute | solution.py:553
  49.6 0.5 collective-permute-start.10
  50.1 3.0 %collective-permute-done.14.refs_5_ = f32[64,1280]{1,0:T(8,128)S(1)} collective-permute-done((f32[64,1280]{1,0:T(8,128)S(1)}, f32[64,1280]{1,0:T(8,128)S(1)}, u32[]{:S(2)}, u32[]{:S(2)}) %collective-permute-start.14) | collective-permute-done | bytes 327712 | tf_op jit(solution)/shard_map/ppermute | solution.py:553
  53.1 1.5 %collective-permute-start.12 = (f32[64,512]{1,0:T(8,128)S(1)}, f32[64,512]{1,0:T(8,128)S(1)}, u32[]{:S(2)}, u32[]{:S(2)}) collective-permute-start(f32[64,512]{1,0:T(8,128)S(1)} %get-tuple-element.77.refs_3_), channel_id=1, source_target_pairs={{0,2},{1,3},{2,0},{3,1},{4,6},{5,7},{6,4},{7,5},{8,10},{9,11},{10,... | collective-permute-start | bytes 393224 | tf_op jit(solution)/shard_map/ppermute | solution.py:553
  54.6 4.4 %collective-permute-done.12.refs_2_ = f32[64,512]{1,0:T(8,128)S(1)} collective-permute-done((f32[64,512]{1,0:T(8,128)S(1)}, f32[64,512]{1,0:T(8,128)S(1)}, u32[]{:S(2)}, u32[]{:S(2)}) %collective-permute-start.12) | collective-permute-done | bytes 131104 | tf_op jit(solution)/shard_map/ppermute | solution.py:553
  59.0 0.4 shard_map.71
  59.4 1.0 collective-permute-done.13.refs_3_
  60.4 1.1 shard_map.72
  61.5 3.1 %collective-permute-start.16 = (f32[64,256]{1,0:T(8,128)S(1)}, f32[64,256]{1,0:T(8,128)S(1)}, u32[]{:S(2)}, u32[]{:S(2)}) collective-permute-start(f32[64,256]{1,0:T(8,128)S(1)} %get-tuple-element.82), channel_id=1, source_target_pairs={{0,16},{4,20},{8,24},{12,28},{16,0},{20,4},{24,8},{28,12},{1,17},{... | collective-permute-start | bytes 196616 | tf_op jit(solution)/shard_map/ppermute | solution.py:536
  64.6 1.1 collective-permute-start.17
  65.7 4.8 %collective-permute-start.18 = (f32[64,256]{1,0:T(8,128)S(1)}, f32[64,256]{1,0:T(8,128)S(1)}, u32[]{:S(2)}, u32[]{:S(2)}) collective-permute-start(f32[64,256]{1,0:T(8,128)S(1)} %get-tuple-element.84), channel_id=1, source_target_pairs={{0,24},{4,28},{8,16},{12,20},{16,8},{20,12},{24,0},{28,4},{1,25},{... | collective-permute-start | bytes 196616 | tf_op jit(solution)/shard_map/ppermute | solution.py:536
  70.5 0.6 collective-permute-start.20
  71.1 3.1 %collective-permute-done.17.refs_6_ = f32[64,256]{1,0:T(8,128)S(1)} collective-permute-done((f32[64,256]{1,0:T(8,128)S(1)}, f32[64,256]{1,0:T(8,128)S(1)}, u32[]{:S(2)}, u32[]{:S(2)}) %collective-permute-start.17) | collective-permute-done | bytes 65568 | tf_op jit(solution)/shard_map/ppermute | solution.py:536
  74.2 0.9 collective-permute-start.22
  75.1 0.4 shard_map.69.refs_1_
  75.5 0.4 shard_map.73.field_ref.refs_2_.u_ref
  76.0 0.3 shard_map.74.refs_0_
  76.3 1.3 %collective-permute-done.19.refs_8_ = f32[64,256]{1,0:T(8,128)S(1)} collective-permute-done((f32[64,256]{1,0:T(8,128)S(1)}, f32[64,256]{1,0:T(8,128)S(1)}, u32[]{:S(2)}, u32[]{:S(2)}) %collective-permute-start.19) | collective-permute-done | bytes 65568 | tf_op jit(solution)/shard_map/ppermute | solution.py:536
  77.6 0.1 collective-permute-done.20.refs_9_
  77.8 0.7 collective-permute-done.21.refs_10_
  78.5 0.5 collective-permute-done.22.refs_11_
  79.0 1.2 shard_map.75
  80.3 1.2 shard_map.79
  81.5 0.6 collective-permute-start.27
  82.1 2.1 %shard_map.78 = (f32[64,1280]{1,0:T(8,128)S(1)}, f32[64,1280]{1,0:T(8,128)S(1)}) custom-call(s32[4,64]{1,0:T(4,128)S(1)} %bitcast.14, s32[2,64]{1,0:T(2,128)S(1)} %get-tuple-element.55.order_ref.order_near, bf16[2,48,128,128]{3,2,1,0:T(8,128)(2,1)S(1)} %get-tuple-element.90.ext, bf16[64,256,256]{2,1,0:T(8,128)(2,1)S(1)} %shard_map.66.w_ref.refs_1_, ...), custom_call_target="tpu_custom_call" | custom-call | tf_op jit(solution)/shard_map/pallas_call | solution.py:55
  84.1 1.6 %collective-permute-start.30 = (f32[64,1280]{1,0:T(8,128)S(1)}, f32[64,1280]{1,0:T(8,128)S(1)}, u32[]{:S(2)}, u32[]{:S(2)}) collective-permute-start(f32[64,1280]{1,0:T(8,128)S(1)} %get-tuple-element.98.refs_9_), channel_id=1, source_target_pairs={{0,2},{1,3},{2,0},{3,1},{4,6},{5,7},{6,4},{7,5},{8,10},{9,11},{10,... | collective-permute-start | bytes 983048 | tf_op jit(solution)/shard_map/ppermute | solution.py:553
  85.7 1.4 %shard_map.76 = (f32[64,768]{1,0:T(8,128)S(1)}, f32[64,768]{1,0:T(8,128)S(1)}) custom-call(s32[4,64]{1,0:T(4,128)S(1)} %bitcast.15, s32[2,64]{1,0:T(2,128)S(1)} %get-tuple-element.55.order_ref.order_near, bf16[2,48,128,128]{3,2,1,0:T(8,128)(2,1)S(1)} %get-tuple-element.90.ext, bf16[64,256,256]{2,1,0:T(8,128)(2,1)S(1)} %shard_map.66.w_ref.refs_1_, ...), custom_call_target="tpu_custom_call" | custom-call | tf_op jit(solution)/shard_map/pallas_call | solution.py:55
  87.2 0.6 collective-permute-start.28
  87.8 1.5 %collective-permute-start.32 = (f32[64,512]{1,0:T(8,128)S(1)}, f32[64,512]{1,0:T(8,128)S(1)}, u32[]{:S(2)}, u32[]{:S(2)}) collective-permute-start(f32[64,512]{1,0:T(8,128)S(1)} %get-tuple-element.95.refs_6_), channel_id=1, source_target_pairs={{0,2},{1,3},{2,0},{3,1},{4,6},{5,7},{6,4},{7,5},{8,10},{9,11},{10,... | collective-permute-start | bytes 393224 | tf_op jit(solution)/shard_map/ppermute | solution.py:553
  89.3 1.8 %shard_map.77 = (f32[64,1024]{1,0:T(8,128)S(1)}, f32[64,1024]{1,0:T(8,128)S(1)}) custom-call(s32[4,64]{1,0:T(4,128)S(1)} %bitcast.16, s32[2,64]{1,0:T(2,128)S(1)} %get-tuple-element.55.order_ref.order_near, bf16[2,48,128,128]{3,2,1,0:T(8,128)(2,1)S(1)} %get-tuple-element.90.ext, bf16[64,256,256]{2,1,0:T(8,128)(2,1)S(1)} %shard_map.66.w_ref.refs_1_, ...), custom_call_target="tpu_custom_call" | custom-call | tf_op jit(solution)/shard_map/pallas_call | solution.py:55
  91.1 0.6 collective-permute-start.36
  91.7 5.9 %collective-permute-done.28.refs_2_ = f32[64,512]{1,0:T(8,128)S(1)} collective-permute-done((f32[64,512]{1,0:T(8,128)S(1)}, f32[64,512]{1,0:T(8,128)S(1)}, u32[]{:S(2)}, u32[]{:S(2)}) %collective-permute-start.28) | collective-permute-done | bytes 131104 | tf_op jit(solution)/shard_map/ppermute | solution.py:553
  97.6 2.8 %collective-permute-done.32.refs_2_ = f32[64,512]{1,0:T(8,128)S(1)} collective-permute-done((f32[64,512]{1,0:T(8,128)S(1)}, f32[64,512]{1,0:T(8,128)S(1)}, u32[]{:S(2)}, u32[]{:S(2)}) %collective-permute-start.32) | collective-permute-done | bytes 131104 | tf_op jit(solution)/shard_map/ppermute | solution.py:553
  100.4 1.5 %collective-permute-start.34 = (f32[64,768]{1,0:T(8,128)S(1)}, f32[64,768]{1,0:T(8,128)S(1)}, u32[]{:S(2)}, u32[]{:S(2)}) collective-permute-start(f32[64,768]{1,0:T(8,128)S(1)} %get-tuple-element.96.refs_7_), channel_id=1, source_target_pairs={{0,2},{1,3},{2,0},{3,1},{4,6},{5,7},{6,4},{7,5},{8,10},{9,11},{10,... | collective-permute-start | bytes 589832 | tf_op jit(solution)/shard_map/ppermute | solution.py:553
  101.9 0.2 collective-permute-start.31
  102.1 3.9 %collective-permute-done.36.refs_8_ = f32[64,1024]{1,0:T(8,128)S(1)} collective-permute-done((f32[64,1024]{1,0:T(8,128)S(1)}, f32[64,1024]{1,0:T(8,128)S(1)}, u32[]{:S(2)}, u32[]{:S(2)}) %collective-permute-start.36) | collective-permute-done | bytes 262176 | tf_op jit(solution)/shard_map/ppermute | solution.py:553
  106.0 3.3 %collective-permute-done.34.refs_5_ = f32[64,768]{1,0:T(8,128)S(1)} collective-permute-done((f32[64,768]{1,0:T(8,128)S(1)}, f32[64,768]{1,0:T(8,128)S(1)}, u32[]{:S(2)}, u32[]{:S(2)}) %collective-permute-start.34) | collective-permute-done | bytes 196640 | tf_op jit(solution)/shard_map/ppermute | solution.py:553
  109.3 0.5 collective-permute-start.33
  109.9 1.2 shard_map.81.refs_11_.refs_5_.u_ref
  111.0 0.6 shard_map.80
  111.7 0.6 shard_map.82.refs_6_
  112.3 0.3 shard_map.83.refs_6_
  112.6 0.4 shard_map.84
  113.0 11.8 %all_to_all.5.sums_ref = f32[32,1,128]{2,1,0:T(1,128)S(1)} all-to-all(f32[32,1,128]{2,1,0:T(1,128)S(1)} %shard_map.84), channel_id=1, replica_groups=mesh['dom'=8,'samp'=4] {'dom','samp'}, dimensions={0} | all-to-all | bytes 32768 | tf_op jit(solution)/shard_map/all_to_all | solution.py:643
  124.8 1.2 update.1
  (54 shorter events, 0.4 us)
Async XLA Ops:
  2.2 9.9 %collective-permute-start = (f32[64,256]{1,0:T(8,128)S(1)}, f32[64,256]{1,0:T(8,128)S(1)}, u32[]{:S(2)}, u32[]{:S(2)}) collective-permute-start(f32[64,256]{1,0:T(8,128)S(1)} %get-tuple-element.63), channel_id=1, source_target_pairs={{0,16},{4,20},{8,24},{12,28},{16,0},{20,4},{24,8},{28,12},{1,17},{... | collective-permute-start | bytes 196616 | tf_op jit(solution)/shard_map/ppermute | solution.py:536
  6.4 10.0 %collective-permute-start.1 = (f32[64,256]{1,0:T(8,128)S(1)}, f32[64,256]{1,0:T(8,128)S(1)}, u32[]{:S(2)}, u32[]{:S(2)}) collective-permute-start(f32[64,256]{1,0:T(8,128)S(1)} %get-tuple-element.64), channel_id=1, source_target_pairs={{0,20},{4,16},{8,28},{12,24},{16,4},{20,0},{24,12},{28,8},{1,21},{... | collective-permute-start | bytes 196616 | tf_op jit(solution)/shard_map/ppermute | solution.py:536
  7.7 18.7 %collective-permute-start.2 = (f32[64,256]{1,0:T(8,128)S(1)}, f32[64,256]{1,0:T(8,128)S(1)}, u32[]{:S(2)}, u32[]{:S(2)}) collective-permute-start(f32[64,256]{1,0:T(8,128)S(1)} %get-tuple-element.65), channel_id=1, source_target_pairs={{0,24},{4,28},{8,16},{12,20},{16,8},{20,12},{24,0},{28,4},{1,25},{... | collective-permute-start | bytes 196616 | tf_op jit(solution)/shard_map/ppermute | solution.py:536
  11.3 15.1 %collective-permute-start.3 = (f32[64,256]{1,0:T(8,128)S(1)}, f32[64,256]{1,0:T(8,128)S(1)}, u32[]{:S(2)}, u32[]{:S(2)}) collective-permute-start(f32[64,256]{1,0:T(8,128)S(1)} %get-tuple-element.66), channel_id=1, source_target_pairs={{0,28},{4,24},{8,20},{12,16},{16,12},{20,8},{24,4},{28,0},{1,29},{... | collective-permute-start | bytes 196616 | tf_op jit(solution)/shard_map/ppermute | solution.py:536
  11.3 15.1 %collective-permute-start.4 = (f32[64,256]{1,0:T(8,128)S(1)}, f32[64,256]{1,0:T(8,128)S(1)}, u32[]{:S(2)}, u32[]{:S(2)}) collective-permute-start(f32[64,256]{1,0:T(8,128)S(1)} %get-tuple-element.67), channel_id=1, source_target_pairs={{0,12},{4,8},{8,4},{12,0},{16,28},{20,24},{24,20},{28,16},{1,13},{... | collective-permute-start | bytes 196616 | tf_op jit(solution)/shard_map/ppermute | solution.py:536
  12.2 14.2 %collective-permute-start.5 = (f32[64,256]{1,0:T(8,128)S(1)}, f32[64,256]{1,0:T(8,128)S(1)}, u32[]{:S(2)}, u32[]{:S(2)}) collective-permute-start(f32[64,256]{1,0:T(8,128)S(1)} %get-tuple-element.68), channel_id=1, source_target_pairs={{0,8},{4,12},{8,0},{12,4},{16,24},{20,28},{24,16},{28,20},{1,9},{5... | collective-permute-start | bytes 196616 | tf_op jit(solution)/shard_map/ppermute | solution.py:536
  16.4 10.0 %collective-permute-start.6 = (f32[64,256]{1,0:T(8,128)S(1)}, f32[64,256]{1,0:T(8,128)S(1)}, u32[]{:S(2)}, u32[]{:S(2)}) collective-permute-start(f32[64,256]{1,0:T(8,128)S(1)} %get-tuple-element.69), channel_id=1, source_target_pairs={{0,4},{4,0},{8,12},{12,8},{16,20},{20,16},{24,28},{28,24},{1,5},{5... | collective-permute-start | bytes 196616 | tf_op jit(solution)/shard_map/ppermute | solution.py:536
  17.9 1.2 copy-start
  19.1 1.2 copy-start.2
  22.7 3.7 %copy-start.4 = (s32[64,4]{0,1:T(4,128)S(1)}, s32[64,4]{0,1:T(4,128)}, u32[]{:S(2)}) copy-start(s32[64,4]{0,1:T(4,128)} %param.10) | copy-start | bytes 3076
  22.7 6.8 %slice-start = ((s8[8388608]{0:T(1024)(128)(4,1)}), s8[4194304]{0:T(1024)(128)(4,1)S(1)}, s32[]{:S(2)}) async-start(s8[8388608]{0:T(1024)(128)(4,1)} %bitcast.6), calls=%async_computation.1 | async-start | bytes 8388608
  26.4 3.1 %slice-start.1 = ((s8[8388608]{0:T(1024)(128)(4,1)}), s8[4194304]{0:T(1024)(128)(4,1)S(1)}, s32[]{:S(2)}) async-start(s8[8388608]{0:T(1024)(128)(4,1)} %bitcast.6), calls=%async_computation.2 | async-start | bytes 8388608
  30.9 29.4 %copy-start.5 = (s32[1,8,4]{1,2,0:T(4,128)S(1)}, s32[1,8,4]{1,2,0:T(4,128)}, u32[]{:S(2)}) copy-start(s32[1,8,4]{1,2,0:T(4,128)} %param.11) | copy-start | bytes 388
  33.4 16.2 %collective-permute-start.8 = (f32[64,2304]{1,0:T(8,128)S(1)}, f32[64,2304]{1,0:T(8,128)S(1)}, u32[]{:S(2)}, u32[]{:S(2)}) collective-permute-start(f32[64,2304]{1,0:T(8,128)S(1)} %get-tuple-element.74.refs_2_), channel_id=1, source_target_pairs={{0,2},{1,3},{2,0},{3,1},{4,6},{5,7},{6,4},{7,5},{8,10},{9,11},{10,... | collective-permute-start | bytes 1769480 | tf_op jit(solution)/shard_map/ppermute | solution.py:553
  35.0 18.2 %collective-permute-start.14 = (f32[64,1280]{1,0:T(8,128)S(1)}, f32[64,1280]{1,0:T(8,128)S(1)}, u32[]{:S(2)}, u32[]{:S(2)}) collective-permute-start(f32[64,1280]{1,0:T(8,128)S(1)} %get-tuple-element.78.refs_4_), channel_id=1, source_target_pairs={{0,2},{1,3},{2,0},{3,1},{4,6},{5,7},{6,4},{7,5},{8,10},{9,11},{10,... | collective-permute-start | bytes 983048 | tf_op jit(solution)/shard_map/ppermute | solution.py:553
  35.5 35.0 %collective-permute-start.7 = (f32[64,2304]{1,0:T(8,128)S(1)}, f32[64,2304]{1,0:T(8,128)S(1)}, u32[]{:S(2)}, u32[]{:S(2)}) collective-permute-start(f32[64,2304]{1,0:T(8,128)S(1)} %get-tuple-element.74.refs_2_), channel_id=1, source_target_pairs={{0,1},{1,0},{2,3},{3,2},{4,5},{5,4},{6,7},{7,6},{8,9},{9,8},{10,11... | collective-permute-start | bytes 1769480 | tf_op jit(solution)/shard_map/ppermute | solution.py:554
  49.6 24.6 %collective-permute-start.9 = (f32[64,2304]{1,0:T(8,128)S(1)}, f32[64,2304]{1,0:T(8,128)S(1)}, u32[]{:S(2)}, u32[]{:S(2)}) collective-permute-start(f32[64,2304]{1,0:T(8,128)S(1)} %collective-permute-done.8.refs_2_), channel_id=1, source_target_pairs={{0,1},{1,0},{2,3},{3,2},{4,5},{5,4},{6,7},{7,6},{8,9},{9,8},{10,11... | collective-permute-start | bytes 1769480 | tf_op jit(solution)/shard_map/ppermute | solution.py:566
  49.6 3.5 %collective-permute-start.10 = (f32[64,512]{1,0:T(8,128)S(1)}, f32[64,512]{1,0:T(8,128)S(1)}, u32[]{:S(2)}, u32[]{:S(2)}) collective-permute-start(f32[64,512]{1,0:T(8,128)S(1)} %get-tuple-element.77.refs_3_), channel_id=1, source_target_pairs={{0,1},{1,0},{2,3},{3,2},{4,5},{5,4},{6,7},{7,6},{8,9},{9,8},{10,11... | collective-permute-start | bytes 393224 | tf_op jit(solution)/shard_map/ppermute | solution.py:554
  50.1 8.9 %collective-permute-start.11 = (f32[64,1280]{1,0:T(8,128)S(1)}, f32[64,1280]{1,0:T(8,128)S(1)}, u32[]{:S(2)}, u32[]{:S(2)}) collective-permute-start(f32[64,1280]{1,0:T(8,128)S(1)} %get-tuple-element.78.refs_4_), channel_id=1, source_target_pairs={{0,1},{1,0},{2,3},{3,2},{4,5},{5,4},{6,7},{7,6},{8,9},{9,8},{10,11... | collective-permute-start | bytes 983048 | tf_op jit(solution)/shard_map/ppermute | solution.py:554
  53.1 7.3 %collective-permute-start.15 = (f32[64,1280]{1,0:T(8,128)S(1)}, f32[64,1280]{1,0:T(8,128)S(1)}, u32[]{:S(2)}, u32[]{:S(2)}) collective-permute-start(f32[64,1280]{1,0:T(8,128)S(1)} %collective-permute-done.14.refs_5_), channel_id=1, source_target_pairs={{0,1},{1,0},{2,3},{3,2},{4,5},{5,4},{6,7},{7,6},{8,9},{9,8},{10,11... | collective-permute-start | bytes 983048 | tf_op jit(solution)/shard_map/ppermute | solution.py:566
  53.1 5.9 %collective-permute-start.12 = (f32[64,512]{1,0:T(8,128)S(1)}, f32[64,512]{1,0:T(8,128)S(1)}, u32[]{:S(2)}, u32[]{:S(2)}) collective-permute-start(f32[64,512]{1,0:T(8,128)S(1)} %get-tuple-element.77.refs_3_), channel_id=1, source_target_pairs={{0,2},{1,3},{2,0},{3,1},{4,6},{5,7},{6,4},{7,5},{8,10},{9,11},{10,... | collective-permute-start | bytes 393224 | tf_op jit(solution)/shard_map/ppermute | solution.py:553
  59.0 1.3 %collective-permute-start.13 = (f32[64,512]{1,0:T(8,128)S(1)}, f32[64,512]{1,0:T(8,128)S(1)}, u32[]{:S(2)}, u32[]{:S(2)}) collective-permute-start(f32[64,512]{1,0:T(8,128)S(1)} %collective-permute-done.12.refs_2_), channel_id=1, source_target_pairs={{0,1},{1,0},{2,3},{3,2},{4,5},{5,4},{6,7},{7,6},{8,9},{9,8},{10,11... | collective-permute-start | bytes 393224 | tf_op jit(solution)/shard_map/ppermute | solution.py:566
  61.5 9.0 %collective-permute-start.16 = (f32[64,256]{1,0:T(8,128)S(1)}, f32[64,256]{1,0:T(8,128)S(1)}, u32[]{:S(2)}, u32[]{:S(2)}) collective-permute-start(f32[64,256]{1,0:T(8,128)S(1)} %get-tuple-element.82), channel_id=1, source_target_pairs={{0,16},{4,20},{8,24},{12,28},{16,0},{20,4},{24,8},{28,12},{1,17},{... | collective-permute-start | bytes 196616 | tf_op jit(solution)/shard_map/ppermute | solution.py:536
  64.6 9.7 %collective-permute-start.17 = (f32[64,256]{1,0:T(8,128)S(1)}, f32[64,256]{1,0:T(8,128)S(1)}, u32[]{:S(2)}, u32[]{:S(2)}) collective-permute-start(f32[64,256]{1,0:T(8,128)S(1)} %get-tuple-element.83), channel_id=1, source_target_pairs={{0,20},{4,16},{8,28},{12,24},{16,4},{20,0},{24,12},{28,8},{1,21},{... | collective-permute-start | bytes 196616 | tf_op jit(solution)/shard_map/ppermute | solution.py:536
  65.7 10.6 %collective-permute-start.18 = (f32[64,256]{1,0:T(8,128)S(1)}, f32[64,256]{1,0:T(8,128)S(1)}, u32[]{:S(2)}, u32[]{:S(2)}) collective-permute-start(f32[64,256]{1,0:T(8,128)S(1)} %get-tuple-element.84), channel_id=1, source_target_pairs={{0,24},{4,28},{8,16},{12,20},{16,8},{20,12},{24,0},{28,4},{1,25},{... | collective-permute-start | bytes 196616 | tf_op jit(solution)/shard_map/ppermute | solution.py:536
  70.5 7.2 %collective-permute-start.19 = (f32[64,256]{1,0:T(8,128)S(1)}, f32[64,256]{1,0:T(8,128)S(1)}, u32[]{:S(2)}, u32[]{:S(2)}) collective-permute-start(f32[64,256]{1,0:T(8,128)S(1)} %get-tuple-element.85), channel_id=1, source_target_pairs={{0,28},{4,24},{8,20},{12,16},{16,12},{20,8},{24,4},{28,0},{1,29},{... | collective-permute-start | bytes 196616 | tf_op jit(solution)/shard_map/ppermute | solution.py:536
  70.5 7.3 %collective-permute-start.20 = (f32[64,256]{1,0:T(8,128)S(1)}, f32[64,256]{1,0:T(8,128)S(1)}, u32[]{:S(2)}, u32[]{:S(2)}) collective-permute-start(f32[64,256]{1,0:T(8,128)S(1)} %get-tuple-element.86), channel_id=1, source_target_pairs={{0,12},{4,8},{8,4},{12,0},{16,28},{20,24},{24,20},{28,16},{1,13},{... | collective-permute-start | bytes 196616 | tf_op jit(solution)/shard_map/ppermute | solution.py:536
  74.2 4.3 %collective-permute-start.21 = (f32[64,256]{1,0:T(8,128)S(1)}, f32[64,256]{1,0:T(8,128)S(1)}, u32[]{:S(2)}, u32[]{:S(2)}) collective-permute-start(f32[64,256]{1,0:T(8,128)S(1)} %get-tuple-element.87), channel_id=1, source_target_pairs={{0,8},{4,12},{8,0},{12,4},{16,24},{20,28},{24,16},{28,20},{1,9},{5... | collective-permute-start | bytes 196616 | tf_op jit(solution)/shard_map/ppermute | solution.py:536
  74.2 4.8 %collective-permute-start.22 = (f32[64,256]{1,0:T(8,128)S(1)}, f32[64,256]{1,0:T(8,128)S(1)}, u32[]{:S(2)}, u32[]{:S(2)}) collective-permute-start(f32[64,256]{1,0:T(8,128)S(1)} %get-tuple-element.88), channel_id=1, source_target_pairs={{0,4},{4,0},{8,12},{12,8},{16,20},{20,16},{24,28},{28,24},{1,5},{5... | collective-permute-start | bytes 196616 | tf_op jit(solution)/shard_map/ppermute | solution.py:536
  75.5 3.5 %copy-start.1 = (f32[64,4096]{1,0:T(8,128)S(1)}, f32[64,4096]{1,0:T(8,128)}, u32[]{:S(2)}) copy-start(f32[64,4096]{1,0:T(8,128)} %g_ref.11) | copy-start | bytes 3145732
  75.5 3.5 %copy-start.3 = (f32[64,4096]{1,0:T(8,128)S(1)}, f32[64,4096]{1,0:T(8,128)}, u32[]{:S(2)}) copy-start(f32[64,4096]{1,0:T(8,128)} %c_ref.11) | copy-start | bytes 3145732
  80.3 7.5 %collective-permute-start.23 = (f32[64,512]{1,0:T(8,128)S(1)}, f32[64,512]{1,0:T(8,128)S(1)}, u32[]{:S(2)}, u32[]{:S(2)}) collective-permute-start(f32[64,512]{1,0:T(8,128)S(1)} %get-tuple-element.95.refs_6_), channel_id=1, source_target_pairs={{0,1},{1,0},{2,3},{3,2},{4,5},{5,4},{6,7},{7,6},{8,9},{9,8},{10,11... | collective-permute-start | bytes 393224 | tf_op jit(solution)/shard_map/ppermute | solution.py:554
  81.5 9.5 %collective-permute-start.27 = (f32[64,512]{1,0:T(8,128)S(1)}, f32[64,512]{1,0:T(8,128)S(1)}, u32[]{:S(2)}, u32[]{:S(2)}) collective-permute-start(f32[64,512]{1,0:T(8,128)S(1)} %get-tuple-element.99.refs_10_), channel_id=1, source_target_pairs={{0,1},{1,0},{2,3},{3,2},{4,5},{5,4},{6,7},{7,6},{8,9},{9,8},{10,11... | collective-permute-start | bytes 393224 | tf_op jit(solution)/shard_map/ppermute | solution.py:554
  84.1 17.8 %collective-permute-start.30 = (f32[64,1280]{1,0:T(8,128)S(1)}, f32[64,1280]{1,0:T(8,128)S(1)}, u32[]{:S(2)}, u32[]{:S(2)}) collective-permute-start(f32[64,1280]{1,0:T(8,128)S(1)} %get-tuple-element.98.refs_9_), channel_id=1, source_target_pairs={{0,2},{1,3},{2,0},{3,1},{4,6},{5,7},{6,4},{7,5},{8,10},{9,11},{10,... | collective-permute-start | bytes 983048 | tf_op jit(solution)/shard_map/ppermute | solution.py:553
  87.1 13.3 %collective-permute-start.24 = (f32[64,768]{1,0:T(8,128)S(1)}, f32[64,768]{1,0:T(8,128)S(1)}, u32[]{:S(2)}, u32[]{:S(2)}) collective-permute-start(f32[64,768]{1,0:T(8,128)S(1)} %get-tuple-element.96.refs_7_), channel_id=1, source_target_pairs={{0,1},{1,0},{2,3},{3,2},{4,5},{5,4},{6,7},{7,6},{8,9},{9,8},{10,11... | collective-permute-start | bytes 589832 | tf_op jit(solution)/shard_map/ppermute | solution.py:554
  87.2 10.4 %collective-permute-start.28 = (f32[64,512]{1,0:T(8,128)S(1)}, f32[64,512]{1,0:T(8,128)S(1)}, u32[]{:S(2)}, u32[]{:S(2)}) collective-permute-start(f32[64,512]{1,0:T(8,128)S(1)} %get-tuple-element.99.refs_10_), channel_id=1, source_target_pairs={{0,2},{1,3},{2,0},{3,1},{4,6},{5,7},{6,4},{7,5},{8,10},{9,11},{10,... | collective-permute-start | bytes 393224 | tf_op jit(solution)/shard_map/ppermute | solution.py:553
  87.8 12.6 %collective-permute-start.32 = (f32[64,512]{1,0:T(8,128)S(1)}, f32[64,512]{1,0:T(8,128)S(1)}, u32[]{:S(2)}, u32[]{:S(2)}) collective-permute-start(f32[64,512]{1,0:T(8,128)S(1)} %get-tuple-element.95.refs_6_), channel_id=1, source_target_pairs={{0,2},{1,3},{2,0},{3,1},{4,6},{5,7},{6,4},{7,5},{8,10},{9,11},{10,... | collective-permute-start | bytes 393224 | tf_op jit(solution)/shard_map/ppermute | solution.py:553
  91.1 14.9 %collective-permute-start.36 = (f32[64,1024]{1,0:T(8,128)S(1)}, f32[64,1024]{1,0:T(8,128)S(1)}, u32[]{:S(2)}, u32[]{:S(2)}) collective-permute-start(f32[64,1024]{1,0:T(8,128)S(1)} %get-tuple-element.97.refs_8_), channel_id=1, source_target_pairs={{0,2},{1,3},{2,0},{3,1},{4,6},{5,7},{6,4},{7,5},{8,10},{9,11},{10,... | collective-permute-start | bytes 786440 | tf_op jit(solution)/shard_map/ppermute | solution.py:553
  97.6 12.2 %collective-permute-start.26 = (f32[64,1280]{1,0:T(8,128)S(1)}, f32[64,1280]{1,0:T(8,128)S(1)}, u32[]{:S(2)}, u32[]{:S(2)}) collective-permute-start(f32[64,1280]{1,0:T(8,128)S(1)} %get-tuple-element.98.refs_9_), channel_id=1, source_target_pairs={{0,1},{1,0},{2,3},{3,2},{4,5},{5,4},{6,7},{7,6},{8,9},{9,8},{10,11... | collective-permute-start | bytes 983048 | tf_op jit(solution)/shard_map/ppermute | solution.py:554
  100.4 8.9 %collective-permute-start.25 = (f32[64,1024]{1,0:T(8,128)S(1)}, f32[64,1024]{1,0:T(8,128)S(1)}, u32[]{:S(2)}, u32[]{:S(2)}) collective-permute-start(f32[64,1024]{1,0:T(8,128)S(1)} %get-tuple-element.97.refs_8_), channel_id=1, source_target_pairs={{0,1},{1,0},{2,3},{3,2},{4,5},{5,4},{6,7},{7,6},{8,9},{9,8},{10,11... | collective-permute-start | bytes 786440 | tf_op jit(solution)/shard_map/ppermute | solution.py:554
  100.4 8.9 %collective-permute-start.34 = (f32[64,768]{1,0:T(8,128)S(1)}, f32[64,768]{1,0:T(8,128)S(1)}, u32[]{:S(2)}, u32[]{:S(2)}) collective-permute-start(f32[64,768]{1,0:T(8,128)S(1)} %get-tuple-element.96.refs_7_), channel_id=1, source_target_pairs={{0,2},{1,3},{2,0},{3,1},{4,6},{5,7},{6,4},{7,5},{8,10},{9,11},{10,... | collective-permute-start | bytes 589832 | tf_op jit(solution)/shard_map/ppermute | solution.py:553
  101.9 10.3 %collective-permute-start.31 = (f32[64,1280]{1,0:T(8,128)S(1)}, f32[64,1280]{1,0:T(8,128)S(1)}, u32[]{:S(2)}, u32[]{:S(2)}) collective-permute-start(f32[64,1280]{1,0:T(8,128)S(1)} %collective-permute-done.30.refs_2_), channel_id=1, source_target_pairs={{0,1},{1,0},{2,3},{3,2},{4,5},{5,4},{6,7},{7,6},{8,9},{9,8},{10,11... | collective-permute-start | bytes 983048 | tf_op jit(solution)/shard_map/ppermute | solution.py:566
  106.0 5.7 %collective-permute-start.37 = (f32[64,1024]{1,0:T(8,128)S(1)}, f32[64,1024]{1,0:T(8,128)S(1)}, u32[]{:S(2)}, u32[]{:S(2)}) collective-permute-start(f32[64,1024]{1,0:T(8,128)S(1)} %collective-permute-done.36.refs_8_), channel_id=1, source_target_pairs={{0,1},{1,0},{2,3},{3,2},{4,5},{5,4},{6,7},{7,6},{8,9},{9,8},{10,11... | collective-permute-start | bytes 786440 | tf_op jit(solution)/shard_map/ppermute | solution.py:566
  109.3 2.4 %collective-permute-start.35 = (f32[64,768]{1,0:T(8,128)S(1)}, f32[64,768]{1,0:T(8,128)S(1)}, u32[]{:S(2)}, u32[]{:S(2)}) collective-permute-start(f32[64,768]{1,0:T(8,128)S(1)} %collective-permute-done.34.refs_5_), channel_id=1, source_target_pairs={{0,1},{1,0},{2,3},{3,2},{4,5},{5,4},{6,7},{7,6},{8,9},{9,8},{10,11... | collective-permute-start | bytes 589832 | tf_op jit(solution)/shard_map/ppermute | solution.py:566
  109.3 2.4 %collective-permute-start.33 = (f32[64,512]{1,0:T(8,128)S(1)}, f32[64,512]{1,0:T(8,128)S(1)}, u32[]{:S(2)}, u32[]{:S(2)}) collective-permute-start(f32[64,512]{1,0:T(8,128)S(1)} %collective-permute-done.32.refs_2_), channel_id=1, source_target_pairs={{0,1},{1,0},{2,3},{3,2},{4,5},{5,4},{6,7},{7,6},{8,9},{9,8},{10,11... | collective-permute-start | bytes 393224 | tf_op jit(solution)/shard_map/ppermute | solution.py:566
  109.8 2.8 %collective-permute-start.29 = (f32[64,512]{1,0:T(8,128)S(1)}, f32[64,512]{1,0:T(8,128)S(1)}, u32[]{:S(2)}, u32[]{:S(2)}) collective-permute-start(f32[64,512]{1,0:T(8,128)S(1)} %collective-permute-done.28.refs_2_), channel_id=1, source_target_pairs={{0,1},{1,0},{2,3},{3,2},{4,5},{5,4},{6,7},{7,6},{8,9},{9,8},{10,11... | collective-permute-start | bytes 393224 | tf_op jit(solution)/shard_map/ppermute | solution.py:566
